TPU v7x, 32 devices: a whole 2x2x4 slice. The times are simulated.
32 devices in a mesh: dp: 2 (over y), seq: 16 (over z, x, core).
Axes of the slice: x: 2, y: 2, z: 4, core: 2. Of those that a mesh axis runs over, the one named last changes fastest.
Arguments:
- inputs: bfloat16 [2, 2, 1024, 1024], P(None, 'dp', 'seq'), may hold values from -6 to 6
- teacher: bfloat16 [2, 2, 1024, 1024], P(None, 'dp', 'seq')
- valid_mask: int32 [2, 2, 1024], P(None, 'dp', 'seq'), may hold values from 0 to 1
- prefix: int32 [2, 2], P(None, 'dp'), may hold values from 1 to 512, as said below
- attn_in: bfloat16 [3072, 1024], P(('dp', 'seq')), may hold values from -0.1875 to 0.1875
- attn_out: bfloat16 [1024, 1024], P(('dp', 'seq')), may hold values from -2.5 to 2.5
- mlp_in: bfloat16 [8192, 1024], P(('dp', 'seq')), may hold values from -0.1875 to 0.1875
- mlp_out: bfloat16 [4096, 1024], P(('dp', 'seq')), may hold values from -0.09375 to 0.09375
- norm_gains: float32 [2, 1024], replicated, may hold values from 0.1 to 1.9
Outputs:
- output: bfloat16 [2, 2, 1024, 1024], P(None, 'dp', 'seq')
- losses: float32 [2], replicated
- input_grad: float32 [2, 2, 1024, 1024], P(None, 'dp', 'seq')
- attn_in_grad: float32 [3072, 1024], P(('dp', 'seq'))
- attn_out_grad: float32 [1024, 1024], P(('dp', 'seq'))
- mlp_in_grad: float32 [8192, 1024], P(('dp', 'seq'))
- mlp_out_grad: float32 [4096, 1024], P(('dp', 'seq'))
- gain_grad: float32 [2, 1024], replicated
Inputs may be any that keep to these rules, and one draw needn't show every extreme that they name: Each sequence's prefix length is drawn evenly from 1 to 512, and one sequence has a prefix of exactly 512.
All inputs are finite; a program needn't handle non-finite values.
Results may differ from a plain program's by a relative error of at most 0.017.
Values may be sent and summed in bfloat16 or wider, within the bound.
No kernel may reach another device: no remote copies, remote signals or barrier semaphores. Data moves between devices by JAX's collectives and lax.ppermute only.
A program may use at most 256 MiB of HBM per device.

v0:
```python
import math

import jax
import jax.numpy as jnp
from jax import lax
from jax.sharding import PartitionSpec as P

HEADS = 16
HEAD_DIM = 64


EPS = 1e-05
NEG = -1e30


def rms_scale(rows):
    return lax.rsqrt(jnp.mean(rows * rows, axis=-1, keepdims=True) + EPS)


def right_product(left, right):
    return lax.dot_general(
        left, right, (((1,), (1,)), ((), ())), preferred_element_type=jnp.float32
    )


def left_product(left, right):
    return lax.dot_general(
        left, right, (((0,), (0,)), ((), ())), preferred_element_type=jnp.float32
    )


def norm_back(grad_norm, normed, scale_rows, gain):
    scaled = grad_norm * gain
    return scale_rows * (scaled - normed * jnp.mean(scaled * normed, axis=-1, keepdims=True))


def visible(query_pos, key_pos, prefix_len):
    causal = key_pos[None, :] <= query_pos[:, None]
    inside = key_pos[None, None, :] < prefix_len[:, None, None]
    return causal[None] | inside


def forward_fold(queries, query_pos, prefix_len, score_scale, state_now, pieces):
    group_size, tok_rows, head_count, head_size = queries.shape
    key_rows, value_rows = pieces
    piece_rows = key_rows.shape[1]
    block_size = math.gcd(piece_rows, 512)
    key_heads = key_rows.reshape(group_size, piece_rows, head_count, head_size)
    value_heads = value_rows.reshape(group_size, piece_rows, head_count, head_size)

    def sub_block(block_index, state_in):
        offset = block_index * block_size
        key_block = lax.dynamic_slice_in_dim(key_heads, offset, block_size, 1)
        value_block = lax.dynamic_slice_in_dim(value_heads, offset, block_size, 1)
        key_pos = offset + jnp.arange(block_size, dtype=jnp.int32)
        allowed = visible(query_pos, key_pos, prefix_len)[:, None]

        def compute(current):
            running_max, running_sum, weighted = current
            scores = (
                jnp.einsum(
                    "gqhd,gkhd->ghqk", queries, key_block, preferred_element_type=jnp.float32
                )
                * score_scale
            )
            scores = jnp.where(allowed, scores, NEG)
            new_max = jnp.maximum(running_max, jnp.max(scores, axis=-1))
            shrink = jnp.exp(running_max - new_max)
            soft_weights = jnp.where(allowed, jnp.exp(scores - new_max[..., None]), 0.0)
            running_sum = running_sum * shrink + jnp.sum(soft_weights, axis=-1)
            update = jnp.einsum(
                "ghqk,gkhd->gqhd",
                soft_weights.astype(jnp.bfloat16),
                value_block,
                preferred_element_type=jnp.float32,
            )
            weighted = weighted * jnp.transpose(shrink, (0, 2, 1))[..., None] + update
            return (new_max, running_sum, weighted)

        return lax.cond(jnp.any(allowed), compute, lambda current: current, state_in)

    return lax.fori_loop(0, piece_rows // block_size, sub_block, state_now)


def query_grad_fold(queries, grad_heads, log_sums, row_delta, query_pos, prefix_len, score_scale):
    group_size, tok_rows, head_count, head_size = queries.shape

    def fold(state_now, pieces, first_row):
        key_rows, value_rows = pieces
        piece_rows = key_rows.shape[1]
        block_size = math.gcd(piece_rows, 512)
        key_heads = key_rows.reshape(group_size, piece_rows, head_count, head_size)
        value_heads = value_rows.reshape(group_size, piece_rows, head_count, head_size)

        def sub_block(block_index, state_in):
            offset = block_index * block_size
            key_block = lax.dynamic_slice_in_dim(key_heads, offset, block_size, 1)
            value_block = lax.dynamic_slice_in_dim(value_heads, offset, block_size, 1)
            key_pos = offset + jnp.arange(block_size, dtype=jnp.int32)
            allowed = visible(query_pos, key_pos, prefix_len)[:, None]

            def compute(current):
                scores = (
                    jnp.einsum(
                        "gqhd,gkhd->ghqk", queries, key_block, preferred_element_type=jnp.float32
                    )
                    * score_scale
                )
                soft_weights = jnp.where(allowed, jnp.exp(scores - log_sums[..., None]), 0.0)
                grad_weights = jnp.einsum(
                    "gqhd,gkhd->ghqk", grad_heads, value_block, preferred_element_type=jnp.float32
                )
                grad_scores = (soft_weights * (grad_weights - row_delta[..., None])).astype(
                    jnp.bfloat16
                )
                return (
                    current
                    + jnp.einsum(
                        "ghqk,gkhd->gqhd",
                        grad_scores,
                        key_block,
                        preferred_element_type=jnp.float32,
                    )
                    * score_scale
                )

            return lax.cond(jnp.any(allowed), compute, lambda current: current, state_in)

        return lax.fori_loop(0, piece_rows // block_size, sub_block, state_now)

    return fold


def key_grad_fold(key_heads, value_heads, all_logs, all_deltas, key_pos, prefix_len, score_scale):
    group_size, tok_rows, head_count, head_size = key_heads.shape

    def fold(state_now, pieces, first_row):
        query_rows, grad_rows = pieces
        piece_rows = query_rows.shape[1]
        block_size = math.gcd(piece_rows, 512)
        query_heads = query_rows.reshape(group_size, piece_rows, head_count, head_size)
        grad_heads = grad_rows.reshape(group_size, piece_rows, head_count, head_size)

        def sub_block(block_index, state_in):
            offset = block_index * block_size
            query_block = lax.dynamic_slice_in_dim(query_heads, offset, block_size, 1)
            grad_block = lax.dynamic_slice_in_dim(grad_heads, offset, block_size, 1)
            log_block = jnp.transpose(
                lax.dynamic_slice_in_dim(all_logs, offset, block_size, 1), (0, 2, 1)
            )
            delta_block = jnp.transpose(
                lax.dynamic_slice_in_dim(all_deltas, offset, block_size, 1), (0, 2, 1)
            )
            query_pos = offset + jnp.arange(block_size, dtype=jnp.int32)
            allowed = visible(query_pos, key_pos, prefix_len)[:, None]

            def compute(current):
                key_grad, value_grad = current
                scores = (
                    jnp.einsum(
                        "gqhd,gkhd->ghqk",
                        query_block,
                        key_heads,
                        preferred_element_type=jnp.float32,
                    )
                    * score_scale
                )
                soft_weights = jnp.where(allowed, jnp.exp(scores - log_block[..., None]), 0.0)
                value_grad = value_grad + jnp.einsum(
                    "ghqk,gqhd->gkhd",
                    soft_weights.astype(jnp.bfloat16),
                    grad_block,
                    preferred_element_type=jnp.float32,
                )
                grad_weights = jnp.einsum(
                    "gqhd,gkhd->ghqk", grad_block, value_heads, preferred_element_type=jnp.float32
                )
                grad_scores = (soft_weights * (grad_weights - delta_block[..., None])).astype(
                    jnp.bfloat16
                )
                key_grad = (
                    key_grad
                    + jnp.einsum(
                        "ghqk,gqhd->gkhd",
                        grad_scores,
                        query_block,
                        preferred_element_type=jnp.float32,
                    )
                    * score_scale
                )
                return (key_grad, value_grad)

            return lax.cond(jnp.any(allowed), compute, lambda current: current, state_in)

        return lax.fori_loop(0, piece_rows // block_size, sub_block, state_now)

    return fold


def shards(inputs, teacher, valid_mask, prefix, attn_in, attn_out, mlp_in, mlp_out, norm_gains):
    n_micro = inputs.shape[0]
    tok_rows = inputs.shape[2]
    model_width = inputs.shape[3]
    head_count = HEADS
    head_size = HEAD_DIM
    score_scale = HEAD_DIM ** (-0.5)
    gain_one = norm_gains[0]
    gain_two = norm_gains[1]
    query_pos = lax.axis_index("seq") * tok_rows + jnp.arange(tok_rows, dtype=jnp.int32)
    kept_first, kept_mixed, kept_attended, kept_middle = ([], [], [], [])
    kept_second, kept_gate_up, kept_hidden, kept_error = ([], [], [], [])
    outputs, input_grads, error_parts = ([], [], [])
    gain_one_grad = jnp.zeros((model_width,), jnp.float32)
    gain_two_grad = jnp.zeros((model_width,), jnp.float32)
    for micro in range(n_micro):
        whole_weights = (
            lax.all_gather(attn_in, ("dp", "seq"), axis=0, tiled=True),
            lax.all_gather(attn_out, ("dp", "seq"), axis=0, tiled=True),
            lax.all_gather(mlp_in, ("dp", "seq"), axis=0, tiled=True),
            lax.all_gather(mlp_out, ("dp", "seq"), axis=0, tiled=True),
        )
        attn_in_full, attn_out_full, mlp_in_full, mlp_out_full = whole_weights
        group_size = 1
        source = inputs[micro, 0].astype(jnp.float32)
        target = teacher[micro, 0].astype(jnp.float32)
        weight_rows = valid_mask[micro, 0].astype(jnp.float32).reshape(tok_rows, 1)
        prefix_len = prefix[micro : micro + 1, 0]
        scale_one = rms_scale(source)
        normed_one = source * scale_one
        first_in = (normed_one * gain_one).astype(jnp.bfloat16)
        mixed = right_product(first_in, attn_in_full).astype(jnp.bfloat16)
        query_rows = mixed[:, :model_width].reshape(group_size, tok_rows, model_width)
        key_rows = mixed[:, model_width : 2 * model_width].reshape(
            group_size, tok_rows, model_width
        )
        value_rows = mixed[:, 2 * model_width :].reshape(group_size, tok_rows, model_width)
        queries = query_rows.reshape(group_size, tok_rows, head_count, head_size)
        head_shape = (group_size, head_count, tok_rows)
        start_state = (
            jnp.full(head_shape, NEG, jnp.float32),
            jnp.zeros(head_shape, jnp.float32),
            jnp.zeros((group_size, tok_rows, head_count, head_size), jnp.float32),
        )
        running_max, running_sum, weighted = forward_fold(
            queries,
            query_pos,
            prefix_len,
            score_scale,
            start_state,
            (
                lax.all_gather(key_rows, "seq", axis=1, tiled=True),
                lax.all_gather(value_rows, "seq", axis=1, tiled=True),
            ),
        )
        attended = weighted / jnp.transpose(running_sum, (0, 2, 1))[..., None]
        log_sums = running_max + jnp.log(running_sum)
        attended_low = attended.reshape(tok_rows, model_width).astype(jnp.bfloat16)
        middle = source + jnp.dot(attended_low, attn_out_full, preferred_element_type=jnp.float32)
        scale_two = rms_scale(middle)
        normed_two = middle * scale_two
        second_in = (normed_two * gain_two).astype(jnp.bfloat16)
        gate_up = right_product(second_in, mlp_in_full)
        hidden_width = gate_up.shape[1] // 2
        gate = gate_up[:, :hidden_width]
        up_part = gate_up[:, hidden_width:]
        sigmoid_gate = jax.nn.sigmoid(gate)
        silu_gate = gate * sigmoid_gate
        hidden = (silu_gate * up_part).astype(jnp.bfloat16)
        result = middle + jnp.dot(hidden, mlp_out_full, preferred_element_type=jnp.float32)
        outputs.append(result.astype(jnp.bfloat16).reshape(1, 1, tok_rows, model_width))
        error = weight_rows * (result - target)
        error_parts.append(jnp.sum(error * error).reshape(1))
        error_low = error.astype(jnp.bfloat16)
        grad_hidden = right_product(error_low, mlp_out_full)
        grad_gate = grad_hidden * up_part * sigmoid_gate * (1.0 + gate * (1.0 - sigmoid_gate))
        grad_up = grad_hidden * silu_gate
        grad_gate_up = jnp.concatenate([grad_gate, grad_up], axis=1).astype(jnp.bfloat16)
        grad_second = jnp.dot(grad_gate_up, mlp_in_full, preferred_element_type=jnp.float32)
        gain_two_grad = gain_two_grad + jnp.sum(grad_second * normed_two, axis=0)
        grad_middle = error + norm_back(grad_second, normed_two, scale_two, gain_two)
        middle_low = grad_middle.astype(jnp.bfloat16)
        grad_att = right_product(middle_low, attn_out_full).astype(jnp.bfloat16)
        grad_heads = grad_att.reshape(group_size, tok_rows, head_count, head_size)
        row_delta = jnp.sum(grad_heads.astype(jnp.float32) * attended, axis=-1)
        log_rows = jnp.transpose(log_sums, (0, 2, 1))
        all_logs, all_deltas = (
            lax.all_gather(log_rows, "seq", axis=1, tiled=True),
            lax.all_gather(row_delta, "seq", axis=1, tiled=True),
        )
        query_fold = query_grad_fold(
            queries,
            grad_heads,
            log_sums,
            jnp.transpose(row_delta, (0, 2, 1)),
            query_pos,
            prefix_len,
            score_scale,
        )
        head_zeros = jnp.zeros((group_size, tok_rows, head_count, head_size), jnp.float32)
        grad_queries = query_fold(
            head_zeros,
            (
                lax.all_gather(key_rows, "seq", axis=1, tiled=True),
                lax.all_gather(value_rows, "seq", axis=1, tiled=True),
            ),
            jnp.int32(0),
        )
        key_heads = key_rows.reshape(group_size, tok_rows, head_count, head_size)
        value_heads = value_rows.reshape(group_size, tok_rows, head_count, head_size)
        key_fold = key_grad_fold(
            key_heads, value_heads, all_logs, all_deltas, query_pos, prefix_len, score_scale
        )
        key_grad, value_grad = key_fold(
            (head_zeros, head_zeros),
            (
                lax.all_gather(query_rows, "seq", axis=1, tiled=True),
                lax.all_gather(
                    grad_att.reshape(group_size, tok_rows, model_width), "seq", axis=1, tiled=True
                ),
            ),
            jnp.int32(0),
        )
        grad_mixed = jnp.concatenate(
            [
                grad_queries.reshape(tok_rows, model_width),
                key_grad.reshape(tok_rows, model_width),
                value_grad.reshape(tok_rows, model_width),
            ],
            axis=1,
        ).astype(jnp.bfloat16)
        grad_first = jnp.dot(grad_mixed, attn_in_full, preferred_element_type=jnp.float32)
        gain_one_grad = gain_one_grad + jnp.sum(grad_first * normed_one, axis=0)
        grad_source = grad_middle + norm_back(grad_first, normed_one, scale_one, gain_one)
        input_grads.append(grad_source.reshape(1, 1, tok_rows, model_width))
        kept_first.append(first_in)
        kept_mixed.append(grad_mixed)
        kept_attended.append(attended_low)
        kept_middle.append(middle_low)
        kept_second.append(second_in)
        kept_gate_up.append(grad_gate_up)
        kept_hidden.append(hidden)
        kept_error.append(error_low)
    weight_terms = (
        left_product(jnp.concatenate(kept_mixed, 0), jnp.concatenate(kept_first, 0)),
        left_product(jnp.concatenate(kept_attended, 0), jnp.concatenate(kept_middle, 0)),
        left_product(jnp.concatenate(kept_gate_up, 0), jnp.concatenate(kept_second, 0)),
        left_product(jnp.concatenate(kept_hidden, 0), jnp.concatenate(kept_error, 0)),
    )
    attn_in_grad, attn_out_grad, mlp_in_grad, mlp_out_grad = (
        lax.psum_scatter(weight_terms[0], ("dp", "seq"), scatter_dimension=0, tiled=True),
        lax.psum_scatter(weight_terms[1], ("dp", "seq"), scatter_dimension=0, tiled=True),
        lax.psum_scatter(weight_terms[2], ("dp", "seq"), scatter_dimension=0, tiled=True),
        lax.psum_scatter(weight_terms[3], ("dp", "seq"), scatter_dimension=0, tiled=True),
    )
    local_count = jnp.sum(valid_mask.astype(jnp.float32))
    gain_total, error_total, count_total = lax.psum(
        (jnp.stack([gain_one_grad, gain_two_grad]), jnp.concatenate(error_parts, 0), local_count),
        ("dp", "seq"),
    )
    losses = error_total / (model_width * count_total)
    return (
        jnp.concatenate(outputs, 0),
        losses,
        jnp.concatenate(input_grads, 0),
        attn_in_grad,
        attn_out_grad,
        mlp_in_grad,
        mlp_out_grad,
        gain_total,
    )


def solution(mesh):
    placed = (
        P(None, "dp", "seq", None),
        P(None, "dp", "seq", None),
        P(None, "dp", "seq"),
        P(None, "dp"),
        P(("dp", "seq"), None),
        P(("dp", "seq"), None),
        P(("dp", "seq"), None),
        P(("dp", "seq"), None),
        P(),
    )
    return jax.shard_map(
        shards,
        mesh=mesh,
        in_specs=placed,
        out_specs=(
            P(None, "dp", "seq", None),
            P(),
            P(None, "dp", "seq", None),
            P(("dp", "seq"), None),
            P(("dp", "seq"), None),
            P(("dp", "seq"), None),
            P(("dp", "seq"), None),
            P(),
        ),
        check_vma=False,
    )
```

profile of v0, /device:TPU:2, one launch (start us, length us, event | category | flops | bytes accessed | tf_op | source)
XLA Modules:
  0.0 1534.3 jit_solution(10062458132997378033)
XLA Ops:
  11.6 70.0 %all-gather.25.cloned.1.call-done = bf16[3072,1024]{1,0:T(8,128)(2,1)} async-done(((bf16[96,1024]{1,0:T(8,128)(2,1)}), bf16[3072,1024]{1,0:T(8,128)(2,1)}) %all-gather.25.cloned.1.call-update) | async-done | bytes 6291472 | tf_op jit(solution)/shard_map/all_gather | solution.py:217
  81.6 4.8 convolution_convert_fusion
  88.7 4.8 convolution_convert_fusion.1
  98.4 28.0 %all-gather.37.cloned.1.call-done = bf16[1024,1024]{1,0:T(8,128)(2,1)} async-done(((bf16[64,1024]{1,0:T(8,128)(2,1)}), bf16[1024,1024]{1,0:T(8,128)(2,1)}) %all-gather.37.cloned.1.call-update) | async-done | bytes 2097168 | tf_op jit(solution)/shard_map/all_gather | solution.py:251
  126.4 2.9 copy.140
  129.2 39.5 %all-gather.39.cloned.1.call-done = bf16[1024,1024]{1,0:T(8,128)(2,1)} async-done(((bf16[64,1024]{1,0:T(8,128)(2,1)}), bf16[1024,1024]{1,0:T(8,128)(2,1)}) %all-gather.39.cloned.1.call-update) | async-done | bytes 2097168 | tf_op jit(solution)/shard_map/all_gather | solution.py:252
  168.7 4.0 copy.141
  173.6 7.6 while.103
  175.6 3.5 conditional.19
  182.4 45.3 %all-gather.27.cloned.1.call-done = bf16[1024,1024]{1,0:T(8,128)(2,1)} async-done(((bf16[32,1024]{1,0:T(8,128)(2,1)}), bf16[1024,1024]{1,0:T(8,128)(2,1)}) %all-gather.27.cloned.1.call-update) | async-done | bytes 2097168 | tf_op jit(solution)/shard_map/all_gather | solution.py:218
  230.0 39.2 %all-gather.33.cloned.1.call-done = bf16[1024,1024]{1,0:T(8,128)(2,1)} async-done(((bf16[64,1024]{1,0:T(8,128)(2,1)}), bf16[1024,1024]{1,0:T(8,128)(2,1)}) %all-gather.33.cloned.1.call-update) | async-done | bytes 2097168 | tf_op jit(solution)/shard_map/all_gather | solution.py:251
  269.2 3.9 copy.136
  273.1 38.3 %all-gather.35.cloned.1.call-done = bf16[1024,1024]{1,0:T(8,128)(2,1)} async-done(((bf16[64,1024]{1,0:T(8,128)(2,1)}), bf16[1024,1024]{1,0:T(8,128)(2,1)}) %all-gather.35.cloned.1.call-update) | async-done | bytes 2097168 | tf_op jit(solution)/shard_map/all_gather | solution.py:252
  311.4 3.9 copy.137
  316.2 8.6 while.102
  318.2 4.4 conditional.18
  328.5 100.1 %all-gather.29.cloned.1.call-done = bf16[8192,1024]{1,0:T(8,128)(2,1)} async-done(((bf16[256,1024]{1,0:T(8,128)(2,1)}), bf16[8192,1024]{1,0:T(8,128)(2,1)}) %all-gather.29.cloned.1.call-update) | async-done | bytes 16777232 | tf_op jit(solution)/shard_map/all_gather | solution.py:219
  428.6 12.3 fusion.264
  440.9 2.6 multiply_convert_fusion.7
  443.5 12.3 fusion.265
  455.8 2.8 multiply_convert_fusion.6
  458.6 48.5 %all-gather.31.cloned.1.call-done = bf16[4096,1024]{1,0:T(8,128)(2,1)} async-done(((bf16[128,1024]{1,0:T(8,128)(2,1)}), bf16[4096,1024]{1,0:T(8,128)(2,1)}) %all-gather.31.cloned.1.call-update) | async-done | bytes 8388624 | tf_op jit(solution)/shard_map/all_gather | solution.py:220
  507.0 5.2 convolution_add_fusion.3
  513.3 2.7 fusion.257
  516.1 3.7 multiply_convert_fusion.5
  519.8 5.5 multiply_convert_fusion.3
  525.3 4.3 fusion.166
  529.8 3.7 multiply_reduce_fusion.2
  536.9 3.0 convolution_convert_fusion.3
  540.0 2.7 fusion.231
  547.8 19.3 %all_gather.68 = f32[1,1024,16]{2,0,1:T(1,128)S(1)} all-gather(f32[1,64,16]{2,0,1:T(1,128)S(1)} %bitcast.426), channel_id=1, replica_groups=mesh['dp'=2,'seq'=16] {'seq'}, dimensions={1}, use_global_device_ids=true | all-gather | bytes 69632 | tf_op jit(solution)/shard_map/all_gather | solution.py:287
  568.8 21.6 %all_gather.64 = f32[1,1024,16]{2,0,1:T(1,128)S(1)} all-gather(f32[1,64,16]{2,0,1:T(1,128)S(1)} %bitcast.427), channel_id=1, replica_groups=mesh['dp'=2,'seq'=16] {'seq'}, dimensions={1}, use_global_device_ids=true | all-gather | bytes 69632 | tf_op jit(solution)/shard_map/all_gather | solution.py:287
  590.7 3.9 copy.168
  594.6 4.0 copy.153
  603.8 18.0 %all-gather.11 = f32[16,64,16]{1,2,0:T(8,128)S(1)} all-gather(f32[1,64,16]{1,2,0:T(8,128)S(1)} %copy.166), channel_id=9, replica_groups=mesh['dp'=2,'seq'=16] {'seq'}, dimensions={0}, use_global_device_ids=true | all-gather | bytes 69632 | tf_op jit(solution)/shard_map/all_gather | solution.py:288
  623.4 9.6 while.106
  625.3 5.7 conditional.22
  627.2 3.9 fusion.111
  636.5 21.4 %all-gather.10 = f32[16,64,16]{1,2,0:T(8,128)S(1)} all-gather(f32[1,64,16]{1,2,0:T(8,128)S(1)} %copy.151), channel_id=6, replica_groups=mesh['dp'=2,'seq'=16] {'seq'}, dimensions={0}, use_global_device_ids=true | all-gather | bytes 69632 | tf_op jit(solution)/shard_map/all_gather | solution.py:288
  658.8 9.3 while.104
  660.9 5.1 conditional.20
  662.7 3.3 fusion.60
  668.9 4.0 copy.169
  673.0 17.9 %while.107 = (s32[]{:T(128)}, f32[1,64,16,64]{1,3,2,0:T(8,128)S(1)}, f32[1,64,16,64]{1,3,2,0:T(8,128)S(1)}, s32[1,1]{1,0:T(1,128)}, f32[1,1024,16]{1,2,0:T(8,128...) while((s32[]{:T(128)}, f32[1,64,16,64]{1,3,2,0:T(8,128)S(1)}, ...), condition=%wide.region_47.48_spmd.clone, body=%wide.region_43.47_spmd.clone.sunk | while | flops 272466624 | bytes 12199205 | solution.py:195
  675.8 6.1 conditional.23
  677.8 2.3 fusion.138
  684.7 6.1 conditional.23
  686.6 2.4 fusion.138
  692.3 4.0 copy.154
  696.4 17.7 %while.105 = (s32[]{:T(128)}, f32[1,64,16,64]{1,3,2,0:T(8,128)S(1)}, f32[1,64,16,64]{1,3,2,0:T(8,128)S(1)}, s32[1,1]{1,0:T(1,128)}, f32[1,1024,16]{1,2,0:T(8,128...) while((s32[]{:T(128)}, f32[1,64,16,64]{1,3,2,0:T(8,128)S(1)}, ...), condition=%wide.region_34.35_spmd.clone, body=%wide.region_30.34_spmd.clone.sunk | while | flops 272466624 | bytes 12199205 | solution.py:195
  699.3 6.0 conditional.21
  701.2 2.3 fusion.87
  708.1 6.0 conditional.21
  710.0 2.3 fusion.87
  714.3 7.7 fusion.192
  723.2 8.2 fusion.174
  733.1 15.7 %fusion.158 = f32[8192,1024]{1,0:T(8,128)} fusion(bf16[64,4096]{1,0:T(8,128)(2,1)S(1)} %copy-done.40, bf16[64,4096]{1,0:T(8,128)(2,1)S(1)} %copy-done.38, bf16[64,4096]{1,0:T(8,128)(2,1)S(1)} %copy-done.36, bf16[64,4096]{1,0:T(8,128)(2,1)S(1)} %copy-done.35, bf16[64,1024]{1,0:T(8,128)(2,1)S(1)} %copy-done.46, bf16[64,1024]{1,0:T(8,128)(2,1)S(1)} %copy-done.44), kind=kOutput, calls=%fused_computation.192 | convolution fusion | flops 2156396544 | bytes 35913728 | tf_op jit(solution)/shard_map/dot_general | solution.py:27
  751.5 4.1 fusion.186
  755.7 4.3 fusion.218
  760.7 41.2 %all-reduce = (f32[2]{0:T(128)S(1)}, f32[]{:T(128)}, f32[2,1024]{1,0:T(2,128)}) all-reduce(f32[2]{0:T(128)S(1)} %pad_maximum_fusion.3, f32[]{:T(128)} %convert_reduce_fusion, f32[2,1024]{1,0:T(2,128)S(1)} %pad_maximum_fusion.2), channel_id=1, replica_groups=mesh['dp'=2,'seq'=16] {'dp','seq'}, use_global_device_ids=true, to_apply=%region_20.0 | all-reduce | flops 2051 | bytes 16408 | tf_op jit(solution)/shard_map/psum | solution.py:356
  804.2 12.8 reduce-scatter.7.cloned.1.call-done
  817.1 164.3 %reduce-scatter.5.cloned.1.call-done = f32[96,1024]{1,0:T(8,128)} async-done(((f32[3072,1024]{1,0:T(8,128)}), f32[96,1024]{1,0:T(8,128)}) %reduce-scatter.5.cloned.1.call-update) | async-done | bytes 393232 | tf_op jit(solution)/shard_map/reduce_scatter | solution.py:350
  981.4 184.6 %reduce-scatter.11.cloned.1.call-done = f32[128,1024]{1,0:T(8,128)} async-done(((f32[4096,1024]{1,0:T(8,128)}), f32[128,1024]{1,0:T(8,128)}) %reduce-scatter.11.cloned.1.call-update) | async-done | bytes 524304 | tf_op jit(solution)/shard_map/reduce_scatter | solution.py:353
  1165.9 361.6 %reduce-scatter.9.cloned.1.call-done = f32[256,1024]{1,0:T(8,128)} async-done(((f32[8192,1024]{1,0:T(8,128)}), f32[256,1024]{1,0:T(8,128)}) %reduce-scatter.9.cloned.1.call-update) | async-done | bytes 1048592 | tf_op jit(solution)/shard_map/reduce_scatter | solution.py:352
  (383 shorter events, 98.3 us)
Async XLA Ops:
  7.2 74.5 %all-gather.25.cloned.1.call-start = ((), (), s32[]{:S(2)}) async-start(), calls=%async_computation.4 | async-start | bytes 6488064 | tf_op jit(solution)/shard_map/all_gather | solution.py:217
  7.9 118.5 %all-gather.37.cloned.1.call-start = ((), (), s32[]{:S(2)}) async-start(), calls=%async_computation.14 | async-start | bytes 2228224 | tf_op jit(solution)/shard_map/all_gather | solution.py:251
  9.1 77.3 %copy-start.74 = (f32[64]{0:T(128)}, f32[64]{0:T(128)S(1)}, u32[]{:S(2)}) copy-start(f32[64]{0:T(128)S(1)} %get-tuple-element.2420) | copy-start | bytes 772
  9.1 77.3 %copy-start.76 = (f32[64]{0:T(128)}, f32[64]{0:T(128)S(1)}, u32[]{:S(2)}) copy-start(f32[64]{0:T(128)S(1)} %get-tuple-element.2421) | copy-start | bytes 772
  11.6 74.9 %copy-start.50 = (bf16[64,1024]{1,0:T(8,128)(2,1)}, bf16[64,1024]{1,0:T(8,128)(2,1)S(1)}, u32[]{:S(2)}) copy-start(bf16[64,1024]{1,0:T(8,128)(2,1)S(1)} %get-tuple-element.2398) | copy-start | bytes 393220
  11.6 77.0 %copy-start.49 = (bf16[64,1024]{1,0:T(8,128)(2,1)}, bf16[64,1024]{1,0:T(8,128)(2,1)S(1)}, u32[]{:S(2)}) copy-start(bf16[64,1024]{1,0:T(8,128)(2,1)S(1)} %get-tuple-element.2397) | copy-start | bytes 393220
  87.2 81.5 %all-gather.39.cloned.1.call-start = ((), (), s32[]{:S(2)}) async-start(), calls=%async_computation.15 | async-start | bytes 2228224 | tf_op jit(solution)/shard_map/all_gather | solution.py:252
  88.0 139.7 %all-gather.27.cloned.1.call-start = ((), (), s32[]{:S(2)}) async-start(), calls=%async_computation.5 | async-start | bytes 2162688 | tf_op jit(solution)/shard_map/all_gather | solution.py:218
  88.6 180.6 %all-gather.33.cloned.1.call-start = ((), (), s32[]{:S(2)}) async-start(), calls=%async_computation.12 | async-start | bytes 2228224 | tf_op jit(solution)/shard_map/all_gather | solution.py:251
  88.6 8.5 copy-start.78
  88.6 9.1 copy-start.79
  88.6 9.1 copy-start.51
  94.2 4.1 copy-start.52
  94.3 217.1 %all-gather.35.cloned.1.call-start = ((), (), s32[]{:S(2)}) async-start(), calls=%async_computation.13 | async-start | bytes 2228224 | tf_op jit(solution)/shard_map/all_gather | solution.py:252
  94.8 333.8 %all-gather.29.cloned.1.call-start = ((), (), s32[]{:S(2)}) async-start(), calls=%async_computation.6 | async-start | bytes 17301504 | tf_op jit(solution)/shard_map/all_gather | solution.py:219
  95.6 411.4 %all-gather.31.cloned.1.call-start = ((), (), s32[]{:S(2)}) async-start(), calls=%async_computation.7 | async-start | bytes 8650752 | tf_op jit(solution)/shard_map/all_gather | solution.py:220
  96.3 494.3 %all-gather.45.cloned.1.call-start = ((), (), s32[]{:S(2)}) async-start(), calls=%async_computation.18 | async-start | bytes 2228224 | tf_op jit(solution)/shard_map/all_gather | solution.py:316
  97.1 497.6 %all-gather.41.cloned.1.call-start = ((), (), s32[]{:S(2)}) async-start(), calls=%async_computation.16 | async-start | bytes 2228224 | tf_op jit(solution)/shard_map/all_gather | solution.py:316
  98.3 570.5 %all-gather.47.cloned.1.call-start = ((), (), s32[]{:S(2)}) async-start(), calls=%async_computation.19 | async-start | bytes 2228224 | tf_op jit(solution)/shard_map/all_gather | solution.py:317
  173.6 54.2 %copy-start.18 = (bf16[2,1,64,1024]{3,2,1,0:T(8,128)(2,1)S(1)}, bf16[2,1,64,1024]{3,2,1,0:T(8,128)(2,1)}, u32[]{:S(2)}) copy-start(bf16[2,1,64,1024]{3,2,1,0:T(8,128)(2,1)} %param.33) | copy-start | bytes 786436
  181.2 91.9 %copy-start.5 = (bf16[1,64,16,64]{3,1,2,0:T(8,128)(2,1)}, bf16[1,64,16,64]{3,1,2,0:T(8,128)(2,1)S(1)}, u32[]{:S(2)}) copy-start(bf16[1,64,16,64]{3,1,2,0:T(8,128)(2,1)S(1)} %get-tuple-element.3099) | copy-start | bytes 393220
  182.4 90.7 %copy-start.31 = (bf16[1,64,16,64]{1,3,2,0:T(8,128)(2,1)}, bf16[1,64,16,64]{1,3,2,0:T(8,128)(2,1)S(1)}, u32[]{:S(2)}) copy-start(bf16[1,64,16,64]{1,3,2,0:T(8,128)(2,1)S(1)} %fusion.247) | copy-start | bytes 393220
  229.9 98.4 %copy-start.13 = (f32[64,1024]{1,0:T(8,128)}, f32[64,1024]{1,0:T(8,128)S(1)}, u32[]{:S(2)}) copy-start(f32[64,1024]{1,0:T(8,128)S(1)} %get-tuple-element.2416) | copy-start | bytes 786436
  326.0 114.9 %copy-start.33 = (bf16[1,64,16,64]{1,3,2,0:T(8,128)(2,1)}, bf16[1,64,16,64]{1,3,2,0:T(8,128)(2,1)S(1)}, u32[]{:S(2)}) copy-start(bf16[1,64,16,64]{1,3,2,0:T(8,128)(2,1)S(1)} %fusion.246) | copy-start | bytes 393220
  328.3 112.6 %copy-start.16 = (f32[64,1024]{1,0:T(8,128)}, f32[64,1024]{1,0:T(8,128)S(1)}, u32[]{:S(2)}) copy-start(f32[64,1024]{1,0:T(8,128)S(1)} %get-tuple-element.2414) | copy-start | bytes 786436
  328.5 112.4 %copy-start.43 = (bf16[64,1024]{1,0:T(8,128)(2,1)}, bf16[64,1024]{1,0:T(8,128)(2,1)S(1)}, u32[]{:S(2)}) copy-start(bf16[64,1024]{1,0:T(8,128)(2,1)S(1)} %get-tuple-element.2407) | copy-start | bytes 393220
  328.5 115.0 %copy-start.45 = (bf16[64,1024]{1,0:T(8,128)(2,1)}, bf16[64,1024]{1,0:T(8,128)(2,1)S(1)}, u32[]{:S(2)}) copy-start(bf16[64,1024]{1,0:T(8,128)(2,1)S(1)} %get-tuple-element.2408) | copy-start | bytes 393220
  507.0 6.0 copy-start
  507.0 6.0 copy-start.11
  507.0 6.1 copy-start.14
  507.0 6.3 copy-start.60
  513.3 12.0 slice-start
  513.3 12.0 slice-start.1
  516.0 9.2 slice-start.2
  519.8 5.5 slice-start.3
  525.3 4.4 copy-start.15
  525.3 4.4 copy-start.17
  525.3 4.4 copy-start.37
  525.3 4.4 copy-start.39
  535.4 4.6 copy-start.32
  535.4 4.6 copy-start.34
  536.8 155.5 %all-gather.43.cloned.1.call-start = ((), (), s32[]{:S(2)}) async-start(), calls=%async_computation.17 | async-start | bytes 2228224 | tf_op jit(solution)/shard_map/all_gather | solution.py:317
  539.9 277.1 %reduce-scatter.7.cloned.1.call-start = ((), (), s32[]{:S(2)}) async-start(), calls=%async_computation.9 | async-start | bytes 4325376 | tf_op jit(solution)/shard_map/reduce_scatter | solution.py:351
  542.8 438.6 %reduce-scatter.5.cloned.1.call-start = ((), (), s32[]{:S(2)}) async-start(), calls=%async_computation.8 | async-start | bytes 12976128 | tf_op jit(solution)/shard_map/reduce_scatter | solution.py:350
  594.6 5.9 copy-start.47
  599.8 23.6 %copy-start.6 = (bf16[1,64,16,64]{3,1,2,0:T(8,128)(2,1)S(1)}, bf16[1,64,16,64]{3,1,2,0:T(8,128)(2,1)}, u32[]{:S(2)}) copy-start(bf16[1,64,16,64]{3,1,2,0:T(8,128)(2,1)} %copy-done.5) | copy-start | bytes 393220
  600.8 22.6 %copy-start.68 = (bf16[1,64,16,64]{3,1,2,0:T(8,128)(2,1)S(1)}, bf16[1,64,16,64]{3,1,2,0:T(8,128)(2,1)}, u32[]{:S(2)}) copy-start(bf16[1,64,16,64]{3,1,2,0:T(8,128)(2,1)} %copy.164) | copy-start | bytes 393220
  633.0 25.8 %copy-start.1 = (bf16[1,1024,16,64]{1,3,2,0:T(8,128)(2,1)S(1)}, bf16[1,1024,16,64]{1,3,2,0:T(8,128)(2,1)}, u32[]{:S(2)}) copy-start(bf16[1,1024,16,64]{1,3,2,0:T(8,128)(2,1)} %get-tuple-element.3094) | copy-start | bytes 6291460
  633.0 25.8 %copy-start.4 = (bf16[1,64,16,64]{3,1,2,0:T(8,128)(2,1)S(1)}, bf16[1,64,16,64]{3,1,2,0:T(8,128)(2,1)}, u32[]{:S(2)}) copy-start(bf16[1,64,16,64]{3,1,2,0:T(8,128)(2,1)} %copy-done.3) | copy-start | bytes 393220
  633.1 25.8 %copy-start.67 = (bf16[1,64,16,64]{3,1,2,0:T(8,128)(2,1)S(1)}, bf16[1,64,16,64]{3,1,2,0:T(8,128)(2,1)}, u32[]{:S(2)}) copy-start(bf16[1,64,16,64]{3,1,2,0:T(8,128)(2,1)} %copy.149) | copy-start | bytes 393220
  633.1 25.8 %copy-start.73 = (f32[1,16,64]{2,1,0:T(8,128)S(1)}, f32[1,16,64]{2,1,0:T(8,128)}, u32[]{:S(2)}) copy-start(f32[1,16,64]{2,1,0:T(8,128)} %copy.148) | copy-start | bytes 12292
  668.9 4.1 copy-start.8
  692.3 4.1 copy-start.7
  722.0 443.9 %reduce-scatter.11.cloned.1.call-start = ((), (), s32[]{:S(2)}) async-start(), calls=%async_computation.11 | async-start | bytes 17301504 | tf_op jit(solution)/shard_map/reduce_scatter | solution.py:353
  731.5 796.0 %reduce-scatter.9.cloned.1.call-start = ((), (), s32[]{:S(2)}) async-start(), calls=%async_computation.10 | async-start | bytes 34603008 | tf_op jit(solution)/shard_map/reduce_scatter | solution.py:352
  751.4 4.1 copy-start.19
  751.4 4.1 copy-start.28
  751.5 4.1 copy-start.70
  751.5 4.1 copy-start.75
  751.5 4.1 copy-start.77
  755.6 4.4 copy-start.65
  755.6 4.4 copy-start.66
  755.6 47.0 %copy-start.58 = (f32[64,1024]{1,0:T(8,128)S(1)}, f32[64,1024]{1,0:T(8,128)}, u32[]{:S(2)}) copy-start(f32[64,1024]{1,0:T(8,128)} %get-tuple-element.2370) | copy-start | bytes 786436
  755.6 47.0 %copy-start.59 = (f32[64,1024]{1,0:T(8,128)S(1)}, f32[64,1024]{1,0:T(8,128)}, u32[]{:S(2)}) copy-start(f32[64,1024]{1,0:T(8,128)} %get-tuple-element.2388) | copy-start | bytes 786436
  (37 other events, 74.4 us)
Sparse Core Ops, SparseCore 0:
  10.9 70.7 all-gather.24
  87.4 38.9 all-gather.36
  128.5 40.1 all-gather.38
  171.4 56.2 all-gather.26
  229.7 39.3 all-gather.32
  271.2 40.1 all-gather.34
  314.2 114.3 all-gather.28
  431.4 75.5 all-gather.30
  509.2 39.1 all-gather.44
  550.4 43.4 all-gather.40
  596.0 40.2 all-gather.46
  638.4 40.3 all-gather.42
  681.6 135.3 reduce-scatter.6
  823.5 157.8 reduce-scatter.4
  984.2 181.6 reduce-scatter.10
  1168.8 358.7 reduce-scatter.8
where the time goes:
time: 1550 us; the launch traced here: 1530 us
  waiting for transfers between devices  1140 us (74%)
  matrix products  149 us (10%)
  blocking collectives  121 us (8%)
  local copies, waits for them, and re-layouts  59.4 us (4%)
  other arithmetic  41.5 us (3%)
  between operations  15.9 us (1%)
    reduce_scatter x1, waiting for transfers between devices, shards(): lax.psum_scatter(weight_terms[2], ('dp', 'seq'), scatter_dimension=0, til...  362 us
    reduce_scatter x1, waiting for transfers between devices, shards(): lax.psum_scatter(weight_terms[3], ('dp', 'seq'), scatter_dimension=0, til...  185 us
    reduce_scatter x1, waiting for transfers between devices, shards(): lax.psum_scatter(weight_terms[0], ('dp', 'seq'), scatter_dimension=0, til...  164 us
    all_gather x1, waiting for transfers between devices, shards(): lax.all_gather(mlp_in, ('dp', 'seq'), axis=0, tiled=True)  100 us
    all_gather x2, waiting for transfers between devices, shards(): lax.all_gather(value_rows, 'seq', axis=1, tiled=True)  77.8 us
    all_gather x1, waiting for transfers between devices, shards(): lax.all_gather(attn_in, ('dp', 'seq'), axis=0, tiled=True)  70 us
    all_gather x2, waiting for transfers between devices, shards(): lax.all_gather(key_rows, 'seq', axis=1, tiled=True)  67.2 us
    all_gather x1, waiting for transfers between devices, shards(): lax.all_gather(mlp_out, ('dp', 'seq'), axis=0, tiled=True)  48.5 us
  transfers between devices with their start and end apart: 16, of which 12 were waited for; matrix products, arithmetic and copies ran while one was open for 15% of the time, Pallas kernels for 0%

commit v1 on v0

v1 whole, which is shorter than its diff:
```python
import functools

import jax
import jax.numpy as jnp
from jax import lax
from jax.experimental import pallas as pl
from jax.experimental.pallas import tpu as pltpu
from jax.sharding import PartitionSpec as P

HEADS = 16
HEAD_DIM = 64
PAIR_DIM = 2 * HEAD_DIM
EPS = 1e-05
NEG = -1e30
F32 = jnp.float32
BF16 = jnp.bfloat16
BOTH = ("dp", "seq")
BLOCK = 256


def rms_scale(rows):
    return lax.rsqrt(jnp.mean(rows * rows, axis=-1, keepdims=True) + EPS)


def nt(left, right):
    return lax.dot_general(left, right, (((1,), (1,)), ((), ())), preferred_element_type=F32)


def tn(left, right):
    return lax.dot_general(left, right, (((0,), (0,)), ((), ())), preferred_element_type=F32)


def nn(left, right):
    return jnp.dot(left, right, preferred_element_type=F32)


def norm_back(grad_norm, normed, scale_rows, gain):
    scaled = grad_norm * gain
    return scale_rows * (scaled - normed * jnp.mean(scaled * normed, axis=-1, keepdims=True))


def swap_seq(value, bits, n_seq):
    return lax.ppermute(value, "seq", [(i, i ^ bits) for i in range(n_seq)])


def swap_dp(value):
    return lax.ppermute(value, "dp", [(0, 1), (1, 0)])


def cube_gather(own, n_seq):
    half = own.shape[0] // 2
    by_x = swap_seq(own, 2, n_seq)
    by_dp = swap_dp(own)
    by_core = swap_seq(own, 1, n_seq)
    far = jnp.concatenate([swap_seq(by_dp[:half], 2, n_seq), swap_dp(by_x[half:])], 0)
    others = [swap_seq(v, 1, n_seq) for v in (by_x, by_dp, far)]
    return jnp.concatenate([own, by_x, by_dp, far, by_core] + others, 0)


def cube_reduce(parts, n_seq):
    rows = parts.shape[1]
    half = rows // 2
    got = swap_seq(parts[4:].astype(BF16), 1, n_seq).astype(F32)
    here, for_x, for_dp, for_far = (parts[i] + got[i] for i in range(4))
    far_low = for_far.astype(BF16)
    via_x = swap_seq(far_low[:half], 2, n_seq).astype(F32)
    via_dp = swap_dp(far_low[half:]).astype(F32)
    for_dp = jnp.concatenate([for_dp[:half] + via_x, for_dp[half:]], 0)
    for_x = jnp.concatenate([for_x[:half], for_x[half:] + via_dp], 0)
    from_x = swap_seq(for_x.astype(BF16), 2, n_seq).astype(F32)
    from_dp = swap_dp(for_dp.astype(BF16)).astype(F32)
    return here + from_x + from_dp


def micro_gather(rows, core, n_seq):
    keep = jnp.where(core == 0, rows[0], rows[1])
    send = jnp.where(core == 0, rows[1], rows[0])
    got = swap_seq(send, 1, n_seq)
    own = jnp.where(core == 0, jnp.concatenate([keep, got], 0), jnp.concatenate([got, keep], 0))
    lines = [own] + [swap_seq(own, 4 * j, n_seq) for j in range(1, n_seq // 4)]
    blocks = []
    for value in lines:
        blocks += [value, swap_seq(value, 2, n_seq)]
    return blocks


def matchings(edges, count):
    left = list(edges)
    rounds = []
    for _ in range(count):
        by_source = {}
        for edge in left:
            by_source.setdefault(edge[0], []).append(edge)
        taken = {}

        def place(source, seen):
            for edge in by_source[source]:
                if edge[1] in seen:
                    continue
                seen.add(edge[1])
                if edge[1] not in taken or place(taken[edge[1]][0], seen):
                    taken[edge[1]] = edge
                    return True
            return False

        for source in sorted(by_source):
            place(source, set())
        chosen = sorted(taken.values())
        rounds.append(chosen)
        for edge in chosen:
            left.remove(edge)
    return rounds


def spans(rows_q, rows_k):
    for start in range(0, rows_q, BLOCK):
        if rows_q == rows_k:
            yield start, max(start + BLOCK, rows_k // 2)
        else:
            yield start, rows_k


def attend_kernel(where_ref, *refs):
    n_blocks = len(refs) - 5
    x_refs = refs[:n_blocks]
    w_ref, gain_ref, first_ref, mixed_ref, att_ref = refs[n_blocks:]
    my_block, first_query, prefix_len = where_ref[0], where_ref[1], where_ref[2]
    rows = x_refs[0].shape[0]
    for j in range(n_blocks):
        at = pl.multiple_of((my_block ^ j) * rows, rows)
        source = x_refs[j][...].astype(F32)
        first = (source * rms_scale(source) * gain_ref[...]).astype(BF16)
        first_ref[pl.ds(at, rows), :] = first
        mixed_ref[pl.ds(at, rows), :] = nt(first, w_ref[...]).astype(BF16)
    rows_q, rows_k = att_ref.shape[0], mixed_ref.shape[0]
    lanes = lax.broadcasted_iota(jnp.int32, (BLOCK, PAIR_DIM), 1)
    for start, width in spans(rows_q, rows_k):
        at = pl.multiple_of(first_query + start, BLOCK)
        query = mixed_ref[pl.ds(at, BLOCK), 0:PAIR_DIM]
        keys = mixed_ref[0:width, PAIR_DIM : 2 * PAIR_DIM]
        values = mixed_ref[0:width, 2 * PAIR_DIM :]
        key_pos = lax.broadcasted_iota(jnp.int32, (BLOCK, width), 1)
        query_pos = at + lax.broadcasted_iota(jnp.int32, (BLOCK, width), 0)
        allowed = (key_pos <= query_pos) | (key_pos < prefix_len)
        outs = []
        for head in range(2):
            mine = (lanes // HEAD_DIM) == head
            scores = nt(jnp.where(mine, query, jnp.zeros_like(query)), keys) * HEAD_DIM**-0.5
            scores = jnp.where(allowed, scores, NEG)
            top = jnp.max(scores, axis=-1, keepdims=True)
            weights = jnp.exp(scores - top)
            total = jnp.sum(weights, axis=-1, keepdims=True)
            probs = (weights / total).astype(BF16)
            outs.append(nn(probs, values))
        att_ref[start : start + BLOCK, :] = jnp.where(lanes < HEAD_DIM, outs[0], outs[1]).astype(BF16)


def attend(where, blocks, weights, gain, rows_q):
    rows_k = blocks[0].shape[0] * len(blocks)
    width = blocks[0].shape[1]
    n_in = len(blocks) + 2
    return pl.pallas_call(
        attend_kernel,
        out_shape=(
            jax.ShapeDtypeStruct((rows_k, width), BF16),
            jax.ShapeDtypeStruct((rows_k, 3 * PAIR_DIM), BF16),
            jax.ShapeDtypeStruct((rows_q, PAIR_DIM), BF16),
        ),
        in_specs=[pl.BlockSpec(memory_space=pltpu.SMEM)] + [pl.BlockSpec(memory_space=pltpu.VMEM)] * n_in,
        out_specs=(pl.BlockSpec(memory_space=pltpu.VMEM),) * 3,
        compiler_params=pltpu.CompilerParams(vmem_limit_bytes=56 << 20),
        cost_estimate=pl.CostEstimate(
            flops=2 * rows_k * width * 3 * PAIR_DIM + 4 * rows_q * rows_k * PAIR_DIM,
            bytes_accessed=4 * rows_k * width,
            transcendentals=2 * rows_q * rows_k,
        ),
    )(where, *blocks, weights, gain)


def attend_back_kernel(where_ref, mixed_ref, grad_ref, gq_ref, gk_ref, gv_ref):
    first_query, prefix_len = where_ref[1], where_ref[2]
    rows_q, rows_k = grad_ref.shape[0], mixed_ref.shape[0]
    lanes = lax.broadcasted_iota(jnp.int32, (BLOCK, PAIR_DIM), 1)
    gk_ref[...] = jnp.zeros_like(gk_ref)
    gv_ref[...] = jnp.zeros_like(gv_ref)
    for start, width in spans(rows_q, rows_k):
        at = pl.multiple_of(first_query + start, BLOCK)
        query = mixed_ref[pl.ds(at, BLOCK), 0:PAIR_DIM]
        grad = grad_ref[start : start + BLOCK, :]
        keys = mixed_ref[0:width, PAIR_DIM : 2 * PAIR_DIM]
        values = mixed_ref[0:width, 2 * PAIR_DIM :]
        key_pos = lax.broadcasted_iota(jnp.int32, (width, BLOCK), 0)
        query_pos = at + lax.broadcasted_iota(jnp.int32, (width, BLOCK), 1)
        allowed = (key_pos <= query_pos) | (key_pos < prefix_len)
        outs = []
        for head in range(2):
            mine = (lanes // HEAD_DIM) == head
            own_query = jnp.where(mine, query, jnp.zeros_like(query))
            own_grad = jnp.where(mine, grad, jnp.zeros_like(grad))
            scores = nt(keys, own_query) * HEAD_DIM**-0.5
            scores = jnp.where(allowed, scores, NEG)
            top = jnp.max(scores, axis=0, keepdims=True)
            weights = jnp.exp(scores - top)
            probs = weights / jnp.sum(weights, axis=0, keepdims=True)
            grad_probs = nt(values, own_grad)
            delta = jnp.sum(probs * grad_probs, axis=0, keepdims=True)
            grad_scores = (probs * (grad_probs - delta)).astype(BF16)
            gv_ref[0:width, :] += nn(probs.astype(BF16), own_grad)
            gk_ref[0:width, :] += nn(grad_scores, own_query) * HEAD_DIM**-0.5
            outs.append(tn(grad_scores, keys) * HEAD_DIM**-0.5)
        gq_ref[start : start + BLOCK, :] = jnp.where(lanes < HEAD_DIM, outs[0], outs[1])


def attend_back(where, mixed, grad):
    rows_q, rows_k = grad.shape[0], mixed.shape[0]
    return pl.pallas_call(
        attend_back_kernel,
        out_shape=(
            jax.ShapeDtypeStruct((rows_q, PAIR_DIM), F32),
            jax.ShapeDtypeStruct((rows_k, PAIR_DIM), F32),
            jax.ShapeDtypeStruct((rows_k, PAIR_DIM), F32),
        ),
        in_specs=[pl.BlockSpec(memory_space=pltpu.SMEM)] + [pl.BlockSpec(memory_space=pltpu.VMEM)] * 2,
        out_specs=(pl.BlockSpec(memory_space=pltpu.VMEM),) * 3,
        compiler_params=pltpu.CompilerParams(vmem_limit_bytes=56 << 20),
        cost_estimate=pl.CostEstimate(
            flops=10 * rows_q * rows_k * PAIR_DIM,
            bytes_accessed=8 * rows_k * PAIR_DIM * 4,
            transcendentals=2 * rows_q * rows_k,
        ),
    )(where, mixed, grad)


def shards(n_dp, n_seq, inputs, teacher, valid_mask, prefix, attn_in, attn_out, mlp_in, mlp_out, norm_gains):
    n_micro, _, tok_rows, width = inputs.shape
    rows = n_micro * tok_rows
    dp = lax.axis_index("dp")
    seq = lax.axis_index("seq")
    me = dp * n_seq + seq
    core = seq % 2
    n_dev = n_dp * n_seq
    n_pairs = HEADS // 2
    group = n_micro * n_pairs
    n_parts = n_seq // group
    part = seq // group
    n_line = n_seq // 4
    seq_len = n_seq * tok_rows
    rows_q = seq_len // n_parts
    part_groups = [[p * group + g for p in range(n_parts)] for g in range(group)]
    in_groups = [[p * group + g for g in range(group)] for p in range(n_parts)] if n_parts > 1 else None
    gain_one = norm_gains[0:1]
    gain_two = norm_gains[1:2]

    x_blocks = micro_gather(inputs[:, 0], core, n_seq)

    unit = attn_in.shape[0] // 3
    n_share = PAIR_DIM // unit
    edges = []
    for block in range(3 * n_dev):
        third, rest = divmod(block, n_pairs * n_share)
        pair, share = divmod(rest, n_share)
        to_dp, rest = divmod(share, 2 * n_parts)
        to_part, to_core = divmod(rest, 2)
        to_seq = to_part * group + 2 * pair + to_core
        edges.append((block // 3, to_dp * n_seq + to_seq, block % 3, third))
    rounds = matchings(edges, 3)
    own_units = attn_in.reshape(3, unit, width)
    arrived = []
    for chosen in rounds:
        slot = jnp.array([edge[2] for edge in chosen], jnp.int32)[me]
        value = lax.dynamic_index_in_dim(own_units, slot, 0, keepdims=False)
        arrived.append(lax.ppermute(value, BOTH, [(edge[0], edge[1]) for edge in chosen]))
    thirds = []
    for chosen in rounds:
        order = sorted((edge[1], edge[3]) for edge in chosen)
        thirds.append(jnp.array([third for _, third in order], jnp.int32)[me])
    my_thirds = jnp.stack(
        [
            jnp.where(thirds[0] == third, arrived[0], jnp.where(thirds[1] == third, arrived[1], arrived[2]))
            for third in range(3)
        ]
    )
    got = swap_seq(my_thirds, 1, n_seq)
    both = jnp.where(core == 0, jnp.stack([my_thirds, got], 1), jnp.stack([got, my_thirds], 1))
    if n_parts > 1:
        both = lax.all_gather(both, "seq", axis=1, axis_index_groups=part_groups, tiled=True)
    got = swap_dp(both)
    pair_weights = jnp.where(dp == 0, jnp.stack([both, got], 1), jnp.stack([got, both], 1))
    pair_weights = pair_weights.reshape(3 * PAIR_DIM, width)

    attn_out_full = lax.all_gather(attn_out, BOTH, axis=0, tiled=True)
    attn_in_full = lax.all_gather(attn_in, BOTH, axis=0, tiled=True)

    ff_half = mlp_in.shape[0] // 2
    given = swap_dp(jnp.where(dp == 0, mlp_in[ff_half:], mlp_in[:ff_half]))
    gate_rows = jnp.where(dp == 0, mlp_in[:ff_half], given)
    up_rows = jnp.where(dp == 0, given, mlp_in[ff_half:])
    down_rows = lax.ppermute(mlp_out, BOTH, [(b, (b % 2) * n_seq + b // 2) for b in range(n_dev)])
    line_own = jnp.concatenate([gate_rows, up_rows, down_rows], 0)
    line = jnp.stack([line_own] + [swap_seq(line_own, 4 * j, n_seq) for j in range(1, n_line)])
    gate_w = line[:, :ff_half].reshape(n_line * ff_half, width)
    up_w = line[:, ff_half : 2 * ff_half].reshape(n_line * ff_half, width)
    down_w = line[:, 2 * ff_half :].reshape(n_line * ff_half, width)

    prefix_len = jnp.where(core == 0, prefix[0, 0], prefix[1, 0])
    where = jnp.stack([seq // 2, part * rows_q, prefix_len]).astype(jnp.int32)
    first_in, mixed, attended = attend(where, x_blocks, pair_weights, gain_one, rows_q)

    def to_rows(by_device, n_kinds):
        moved = lax.all_to_all(by_device, "seq", 0, 0, axis_index_groups=in_groups)
        moved = moved.reshape(n_pairs, n_micro, tok_rows, n_kinds, PAIR_DIM)
        return moved.transpose(1, 2, 3, 0, 4).reshape(rows, n_kinds * width)

    attended_low = to_rows(attended.reshape(group, tok_rows, PAIR_DIM), 1)

    source = inputs[:, 0].reshape(rows, width).astype(F32)
    target = teacher[:, 0].reshape(rows, width).astype(F32)
    row_mask = valid_mask[:, 0].reshape(rows, 1).astype(F32)
    middle = source + nn(attended_low, attn_out_full)
    scale_two = rms_scale(middle)
    normed_two = middle * scale_two
    second_in = cube_gather((normed_two * gain_two).astype(BF16), n_seq)

    gate = nt(second_in, gate_w)
    up_part = nt(second_in, up_w)
    sigmoid_gate = jax.nn.sigmoid(gate)
    silu_gate = gate * sigmoid_gate
    hidden = (silu_gate * up_part).astype(BF16)
    result = middle + cube_reduce(nn(hidden, down_w).reshape(8, rows, width), n_seq)
    output = result.astype(BF16).reshape(n_micro, 1, tok_rows, width)
    error = row_mask * (result - target)
    error_low = cube_gather(error.astype(BF16), n_seq)
    grad_hidden = nt(error_low, down_w)
    grad_gate = (grad_hidden * up_part * sigmoid_gate * (1.0 + gate * (1.0 - sigmoid_gate))).astype(BF16)
    grad_up = (grad_hidden * silu_gate).astype(BF16)
    grad_second = cube_reduce((nn(grad_gate, gate_w) + nn(grad_up, up_w)).reshape(8, rows, width), n_seq)

    terms = jnp.concatenate(
        [
            tn(grad_gate, second_in).astype(BF16).reshape(n_line, ff_half, width),
            tn(grad_up, second_in).astype(BF16).reshape(n_line, ff_half, width),
            tn(hidden, error_low).astype(BF16).reshape(n_line, ff_half, width),
        ],
        1,
    )
    line_sum = terms[0].astype(F32)
    for j in range(1, n_line):
        line_sum = line_sum + swap_seq(terms[j], 4 * j, n_seq).astype(F32)
    gate_sum, up_sum, down_sum = line_sum[:ff_half], line_sum[ff_half : 2 * ff_half], line_sum[2 * ff_half :]
    given = swap_dp(jnp.where(dp == 0, up_sum, gate_sum))
    mlp_in_grad = jnp.where(
        dp == 0, jnp.concatenate([gate_sum, given], 0), jnp.concatenate([given, up_sum], 0)
    )
    mlp_out_grad = lax.ppermute(down_sum, BOTH, [((b % 2) * n_seq + b // 2, b) for b in range(n_dev)])

    gain_two_term = jnp.sum(grad_second * normed_two, axis=0)
    grad_middle = error + norm_back(grad_second, normed_two, scale_two, gain_two)
    middle_low = grad_middle.astype(BF16)
    grad_att = nt(middle_low, attn_out_full).astype(BF16)
    grad_att = grad_att.reshape(n_micro, tok_rows, n_pairs, PAIR_DIM).transpose(2, 0, 1, 3)
    grad_att = lax.all_to_all(
        grad_att.reshape(group, tok_rows, PAIR_DIM), "seq", 0, 0, axis_index_groups=in_groups
    ).reshape(rows_q, PAIR_DIM)
    middle_blocks = micro_gather(middle_low.reshape(n_micro, tok_rows, width), core, n_seq)

    grad_q, grad_k, grad_v = attend_back(where, mixed, grad_att)
    first_part = first_in
    if n_parts > 1:
        grad_k, grad_v = (
            lax.psum_scatter(v, "seq", scatter_dimension=0, axis_index_groups=part_groups, tiled=True)
            for v in (grad_k, grad_v)
        )
        first_part = lax.dynamic_slice_in_dim(first_in, part * rows_q, rows_q, 0)
    grad_mixed = jnp.concatenate([grad_q, grad_k, grad_v], 1).astype(BF16)
    pair_grad = tn(grad_mixed, first_part)
    own_grad_mixed = to_rows(grad_mixed.reshape(group, tok_rows, 3 * PAIR_DIM), 3)

    gain_one_term = jnp.sum(pair_grad * pair_weights.astype(F32), axis=0) / gain_one[0]
    n_blocks = len(middle_blocks)
    stacked = jnp.stack(middle_blocks)
    order = (jnp.arange(n_blocks, dtype=jnp.int32) ^ (seq // 2)).astype(jnp.int32)
    middle_rows = stacked[order].reshape(seq_len, width)
    middle_part = middle_rows
    if n_parts > 1:
        middle_part = lax.dynamic_slice_in_dim(middle_rows, part * rows_q, rows_q, 0)
    out_grad = tn(attended, middle_part)
    all_grad = jnp.concatenate([pair_grad, out_grad], 0).reshape(4, n_dp, n_parts, 2, unit, width)
    keep = jnp.where(core == 0, all_grad[:, :, :, 0], all_grad[:, :, :, 1])
    give = jnp.where(core == 0, all_grad[:, :, :, 1], all_grad[:, :, :, 0])
    all_grad = keep + swap_seq(give, 1, n_seq)
    if n_parts > 1:
        all_grad = lax.psum_scatter(
            all_grad, "seq", scatter_dimension=2, axis_index_groups=part_groups, tiled=True
        )
    all_grad = all_grad[:, :, 0]
    keep = jnp.where(dp == 0, all_grad[:, 0], all_grad[:, 1])
    give = jnp.where(dp == 0, all_grad[:, 1], all_grad[:, 0])
    all_grad = keep + swap_dp(give)
    returned = []
    for chosen in rounds:
        order = sorted((edge[1], edge[3]) for edge in chosen)
        third = jnp.array([t for _, t in order], jnp.int32)[me]
        value = lax.dynamic_index_in_dim(all_grad[:3], third, 0, keepdims=False)
        returned.append(lax.ppermute(value, BOTH, [(edge[1], edge[0]) for edge in chosen]))
    slots = [jnp.array([edge[2] for edge in chosen], jnp.int32)[me] for chosen in rounds]
    attn_in_grad = jnp.stack(
        [
            jnp.where(slots[0] == slot, returned[0], jnp.where(slots[1] == slot, returned[1], returned[2]))
            for slot in range(3)
        ]
    ).reshape(3 * unit, width)
    moves = []
    for block in range(n_dev):
        pair, share = divmod(block, n_share)
        to_dp, rest = divmod(share, 2 * n_parts)
        to_part, to_core = divmod(rest, 2)
        moves.append((to_dp * n_seq + to_part * group + 2 * pair + to_core, block))
    attn_out_grad = lax.ppermute(all_grad[3], BOTH, moves)

    scale_one = rms_scale(source)
    normed_one = source * scale_one
    grad_first = nn(own_grad_mixed, attn_in_full)
    input_grad = grad_middle + norm_back(grad_first, normed_one, scale_one, gain_one)

    squares = jnp.sum((error * error).reshape(n_micro, tok_rows * width), axis=1)
    count = jnp.sum(row_mask)
    scalars = jnp.zeros((width,), F32).at[0:2].set(squares).at[2].set(count)
    sums = jnp.stack([gain_one_term, gain_two_term, scalars])
    bits = 1
    while bits < n_seq:
        sums = sums + swap_seq(sums, bits, n_seq)
        bits *= 2
    sums = sums + swap_dp(sums)
    losses = sums[2, 0:2] / (width * sums[2, 2])
    return (
        output,
        losses,
        input_grad.reshape(n_micro, 1, tok_rows, width),
        attn_in_grad,
        attn_out_grad,
        mlp_in_grad,
        mlp_out_grad,
        sums[0:2],
    )


def solution(mesh):
    n_dp, n_seq = mesh.shape["dp"], mesh.shape["seq"]
    placed = (
        P(None, "dp", "seq", None),
        P(None, "dp", "seq", None),
        P(None, "dp", "seq"),
        P(None, "dp"),
        P(BOTH, None),
        P(BOTH, None),
        P(BOTH, None),
        P(BOTH, None),
        P(),
    )
    return jax.shard_map(
        functools.partial(shards, n_dp, n_seq),
        mesh=mesh,
        in_specs=placed,
        out_specs=(
            P(None, "dp", "seq", None),
            P(),
            P(None, "dp", "seq", None),
            P(BOTH, None),
            P(BOTH, None),
            P(BOTH, None),
            P(BOTH, None),
            P(),
        ),
        check_vma=False,
    )
```

time: 1550 us -> 446 us (0.29)
  waiting for transfers between devices: 1140 us -> 173 us
  blocking collectives: 121 us -> 0 us
  starting transfers between devices: 1.02 us -> 122 us
  matrix products: 149 us -> 35.2 us
  local copies, waits for them, and re-layouts: 59.4 us -> 32.4 us
  Pallas kernels: 0 us -> 18.6 us
    reduce_scatter x4 -> x0, waiting for transfers between devices: 723 us -> none  [the longest x1 362 us: shards(): lax.psum_scatter(weight_terms[2], ('dp', 'seq'), scatter_dimension=0, til...]
    all_gather x12 -> x2, waiting for transfers between devices: 409 us -> 0.02 us  [the longest x1 0.02 us: shards(): attn_out_full = lax.all_gather(attn_out, BOTH, axis=0, tiled=True)]
    ppermute x0 -> x68, waiting for transfers between devices: none -> 156 us  [the longest x46 120 us: swap_seq(): return lax.ppermute(value, 'seq', [(i, i ^ bits) for i in range(n_seq)])]
    dot_general x40 -> x14, matrix products: 149 us -> 35.2 us  [the longest x5 18.3 us: tn(): lax.dot_general(left, right, (((0,), (0,)), ((), ())), preferred_element_...]
    ppermute x0 -> x68, starting transfers between devices: none -> 106 us  [the longest x46 50.8 us: swap_seq(): return lax.ppermute(value, 'seq', [(i, i ^ bits) for i in range(n_seq)])]
    all_gather x4 -> x0, blocking collectives: 80.2 us -> none  [the longest x2 40.9 us: shards(): lax.all_gather(log_rows, 'seq', axis=1, tiled=True)]
    psum x1 -> x0, blocking collectives: 41.2 us -> none  [shards(): lax.psum((jnp.stack([gain_one_grad, gain_two_grad]), jnp.concatenate(erro...]
    all_gather x12 -> x0, local copies, waits for them, and re-layouts: 32.1 us -> none  [the longest x2 7.96 us: shards(): lax.all_gather(grad_att.reshape(group_size, tok_rows, model_width), 'seq'...]
  transfers between devices with their start and end apart: 16 -> 73, of which waited for: 12 -> 31; matrix products, arithmetic and copies ran while one was open for 15% -> 17% of each run, Pallas kernels for 0% -> 4%
where the time goes in v1:
time: 446 us; the launch traced here: 441 us
  waiting for transfers between devices  173 us (39%)
  starting transfers between devices  122 us (27%)
  matrix products  35.2 us (8%)
  local copies, waits for them, and re-layouts  32.4 us (7%)
  other arithmetic  32.1 us (7%)
  between operations  27 us (6%)
  Pallas kernels  18.6 us (4%)
    ppermute x46, waiting for transfers between devices, swap_seq(): return lax.ppermute(value, 'seq', [(i, i ^ bits) for i in range(n_seq)])  120 us
    ppermute x46, starting transfers between devices, swap_seq(): return lax.ppermute(value, 'seq', [(i, i ^ bits) for i in range(n_seq)])  50.8 us
    ppermute x13, waiting for transfers between devices, swap_dp(): return lax.ppermute(value, 'dp', [(0, 1), (1, 0)])  27.7 us
    dot_general x5, matrix products, tn(): lax.dot_general(left, right, (((0,), (0,)), ((), ())), preferred_element_...  18.3 us
    ppermute x13, starting transfers between devices, swap_dp(): return lax.ppermute(value, 'dp', [(0, 1), (1, 0)])  16.9 us
    ppermute x1, starting transfers between devices, shards(): lax.ppermute(down_sum, BOTH, [(b % 2 * n_seq + b // 2, b) for b in range(...  16.4 us
    all_to_all x2, waiting for transfers between devices, to_rows(): moved = lax.all_to_all(by_device, 'seq', 0, 0, axis_index_groups=in_groups)  15.9 us
    unnamed x100, local copies, waits for them, and re-layouts  13.8 us
  transfers between devices with their start and end apart: 73, of which 31 were waited for; matrix products, arithmetic and copies ran while one was open for 17% of the time, Pallas kernels for 4%

profile of v1, /device:TPU:2, one launch (start us, length us, event | category | flops | bytes accessed | tf_op | source)
XLA Modules:
  0.0 440.6 jit_solution(6320771744560148269)
XLA Ops:
  8.9 3.5 collective-permute-start.10
  12.4 5.4 %collective-permute-start.8 = (bf16[32,1024]{1,0:T(8,128)(2,1)S(1)}, bf16[32,1024]{1,0:T(8,128)(2,1)S(1)}, u32[]{:S(2)}, u32[]{:S(2)}) collective-permute-start(bf16[32,1024]{1,0:T(8,128)(2,1)S(1)} %get-tuple-element.124), channel_id=1, source_target_pairs={{0,0},{1,17},{2,18},{3,5},{4,6},{5,23},{6,24},{7,11},{8,12},{9,29}... | collective-permute-start | bytes 196616 | tf_op jit(solution)/shard_map/ppermute | solution.py:272
  27.9 3.3 collective-permute-start.22
  33.8 2.9 collective-permute-start.6
  39.6 3.5 collective-permute-start.12
  43.2 2.6 collective-permute-done.2.refs_2_
  45.7 1.5 collective-permute-start.3
  48.4 15.8 %collective-permute-done.4.refs_4_ = bf16[128,1024]{1,0:T(8,128)(2,1)S(1)} collective-permute-done((bf16[128,1024]{1,0:T(8,128)(2,1)S(1)}, bf16[128,1024]{1,0:T(8,128)(2,1)S(1)}, u32[]{:S(2)}, u32[]{:S(2)}) %collective-permute-start.4) | collective-permute-done | bytes 262176 | tf_op jit(solution)/shard_map/ppermute | solution.py:43
  64.9 4.4 collective-permute-start.24
  69.3 3.5 collective-permute-start.25
  74.7 3.3 collective-permute-start.5
  79.8 5.5 %collective-permute-done.5.refs_5_ = bf16[128,1024]{1,0:T(8,128)(2,1)S(1)} collective-permute-done((bf16[128,1024]{1,0:T(8,128)(2,1)}, bf16[128,1024]{1,0:T(8,128)(2,1)S(1)}, u32[]{:S(2)}, u32[]{:S(2)}) %collective-permute-start.5) | collective-permute-done | bytes 262176 | tf_op jit(solution)/shard_map/ppermute | solution.py:43
  85.4 4.0 collective-permute-done.7.refs_7_
  90.0 9.1 %shard_map.242 = (bf16[1024,1024]{1,0:T(8,128)(2,1)}, bf16[1024,384]{1,0:T(8,128)(2,1)}, bf16[1024,128]{1,0:T(8,128)(2,1)}) custom-call(s32[3]{0:T(128)} %pad_add_fusion.where_ref, bf16[128,1024]{1,0:T(8,128)(2,1)} %copy-done.23, bf16[128,1024]{1,0:T(8,128)(2,1)} %copy-done.30, bf16[128,1024]{1,0:T(8,128)(2,1)} %collective-permute-done.2.refs_2_, ...), custom_call_target="tpu_custom_call" | custom-call | flops 1342177280 | bytes 4194304 | tf_op jit(solution)/shard_map/pallas_call | solution.py:162
  99.2 5.1 %all-to-all-start = ((bf16[16,64,128]{2,1,0:T(8,128)(2,1)}), bf16[16,64,128]{2,1,0:T(8,128)(2,1)S(1)}, u32[]{:S(2)}, u32[]{:S(2)}) async-start(bf16[16,64,128]{2,1,0:T(8,128)(2,1)} %bitcast.256), calls=%async_computation | async-start | bytes 524288 | tf_op jit(solution)/shard_map/all_to_all | solution.py:310
  104.3 24.9 %collective-permute-done.24 = bf16[384,1024]{1,0:T(8,128)(2,1)S(1)} collective-permute-done((bf16[384,1024]{1,0:T(8,128)(2,1)}, bf16[384,1024]{1,0:T(8,128)(2,1)S(1)}, u32[]{:S(2)}, u32[]{:S(2)}) %collective-permute-start.24) | collective-permute-done | bytes 786464 | tf_op jit(solution)/shard_map/ppermute | solution.py:43
  129.2 3.2 pad_maximum_fusion
  132.4 15.9 %all-to-all-done = bf16[16,64,128]{2,1,0:T(8,128)(2,1)S(1)} async-done(((bf16[16,64,128]{2,1,0:T(8,128)(2,1)}), bf16[16,64,128]{2,1,0:T(8,128)(2,1)S(1)}, u32[]{:S(2)}, u32[]{:S(2)}) %all-to-all-start) | async-done | bytes 262176 | tf_op jit(solution)/shard_map/all_to_all | solution.py:310
  148.5 2.3 multiply_reduce_fusion.6
  151.6 4.3 collective-permute-start.14
  156.4 6.3 %collective-permute-done.14 = bf16[128,1024]{1,0:T(8,128)(2,1)S(1)} collective-permute-done((bf16[128,1024]{1,0:T(8,128)(2,1)S(1)}, bf16[128,1024]{1,0:T(8,128)(2,1)S(1)}, u32[]{:S(2)}, u32[]{:S(2)}) %collective-permute-start.14) | collective-permute-done | bytes 262176 | tf_op jit(solution)/shard_map/ppermute | solution.py:47
  162.8 1.7 collective-permute-start.15
  164.5 1.8 collective-permute-start.16
  168.0 1.5 collective-permute-done.16
  172.5 2.8 multiply_convert_fusion.2
  178.0 2.5 collective-permute-done.26
  182.1 1.8 collective-permute-start.27
  184.4 3.3 collective-permute-done.27
  191.4 4.0 collective-permute-done.28
  195.5 2.1 collective-permute-done.30
  197.6 1.6 fusion.38
  200.0 1.7 collective-permute-start.31
  201.8 5.1 %collective-permute-done.32 = bf16[128,1024]{1,0:T(8,128)(2,1)S(1)} collective-permute-done((bf16[128,1024]{1,0:T(8,128)(2,1)S(1)}, bf16[128,1024]{1,0:T(8,128)(2,1)S(1)}, u32[]{:S(2)}, u32[]{:S(2)}) %collective-permute-start.32) | collective-permute-done | bytes 262176 | tf_op jit(solution)/shard_map/ppermute | solution.py:47
  209.3 2.7 collective-permute-done.33
  214.4 2.0 multiply_convert_fusion.1
  220.2 13.1 %convolution_convert_fusion = bf16[512,1024]{1,0:T(8,128)(2,1)S(1)} fusion(bf16[1024,512]{1,0:T(8,128)(2,1)S(1)} %copy-done.19, bf16[1024,1024]{1,0:T(8,128)(2,1)S(1)} %constant_dynamic-update-slice_fusion.9), kind=kOutput, calls=%fused_computation.16 | convolution fusion | flops 1074266112 | bytes 4194304 | tf_op jit(solution)/shard_map/dot_general | solution.py:30
  239.2 6.3 %collective-permute-done.40 = bf16[64,1024]{1,0:T(8,128)(2,1)S(1)} collective-permute-done((bf16[64,1024]{1,0:T(8,128)(2,1)S(1)}, bf16[64,1024]{1,0:T(8,128)(2,1)S(1)}, u32[]{:S(2)}, u32[]{:S(2)}) %collective-permute-start.40) | collective-permute-done | bytes 131104 | tf_op jit(solution)/shard_map/ppermute | solution.py:47
  252.2 3.4 collective-permute-done.41
  262.9 5.2 %all-to-all-start.1 = ((bf16[16,64,128]{2,1,0:T(8,128)(2,1)}), bf16[16,64,128]{2,1,0:T(8,128)(2,1)S(1)}, u32[]{:S(2)}, u32[]{:S(2)}) async-start(bf16[16,64,128]{2,1,0:T(8,128)(2,1)} %bitcast.48), calls=%async_computation.1 | async-start | bytes 524288 | tf_op jit(solution)/shard_map/all_to_all | solution.py:361
  268.1 2.4 collective-permute-start.53
  272.6 32.0 %collective-permute-done.51 = bf16[128,1024]{1,0:T(8,128)(2,1)S(1)} collective-permute-done((bf16[128,1024]{1,0:T(8,128)(2,1)S(1)}, bf16[128,1024]{1,0:T(8,128)(2,1)S(1)}, u32[]{:S(2)}, u32[]{:S(2)}) %collective-permute-start.51) | collective-permute-done | bytes 262176 | tf_op jit(solution)/shard_map/ppermute | solution.py:43
  307.6 9.5 %shard_map.243 = (f32[1024,128]{1,0:T(8,128)}, f32[1024,128]{1,0:T(8,128)}, f32[1024,128]{1,0:T(8,128)}) custom-call(s32[3]{0:T(128)} %pad_add_fusion.where_ref, bf16[1024,384]{1,0:T(8,128)(2,1)} %get-tuple-element.39.mixed_ref, bf16[1024,128]{1,0:T(8,128)(2,1)} %bitcast.268), custom_call_target="tpu_custom_call" | custom-call | flops 1342177280 | bytes 4194304 | tf_op jit(solution)/shard_map/pallas_call | solution.py:216
  320.6 2.2 multiply_reduce_fusion
  322.8 2.6 collective-permute-start.65
  328.9 5.8 %collective-permute-done.54 = bf16[128,1024]{1,0:T(8,128)(2,1)S(1)} collective-permute-done((bf16[128,1024]{1,0:T(8,128)(2,1)S(1)}, bf16[128,1024]{1,0:T(8,128)(2,1)S(1)}, u32[]{:S(2)}, u32[]{:S(2)}) %collective-permute-start.54) | collective-permute-done | bytes 262176 | tf_op jit(solution)/shard_map/ppermute | solution.py:43
  336.1 1.7 collective-permute-done.56
  338.5 2.3 gather_fusion
  343.4 2.4 fusion.2
  347.7 16.4 %collective-permute-start.67 = (f32[128,1024]{1,0:T(8,128)}, f32[128,1024]{1,0:T(8,128)}, u32[]{:S(2)}, u32[]{:S(2)}) collective-permute-start(f32[128,1024]{1,0:T(8,128)} %get-tuple-element.95), channel_id=1, source_target_pairs={{0,0},{16,1},{1,2},{17,3},{2,4},{18,5},{3,6},{19,7},{4,8},{20,9},{... | collective-permute-start | bytes 1572872 | tf_op jit(solution)/shard_map/ppermute | solution.py:354
  365.4 2.2 pad_maximum_fusion.4
  367.5 5.6 %all-to-all-start.2 = ((bf16[16,64,384]{2,1,0:T(8,128)(2,1)}), bf16[16,64,384]{2,1,0:T(8,128)(2,1)}, u32[]{:S(2)}, u32[]{:S(2)}) async-start(bf16[16,64,384]{2,1,0:T(8,128)(2,1)} %pad_maximum_fusion.4), calls=%async_computation.2 | async-start | bytes 1572864 | tf_op jit(solution)/shard_map/all_to_all | solution.py:310
  373.3 1.5 fusion.4
  375.0 2.7 collective-permute-done.45
  377.7 4.1 collective-permute-start.46
  381.9 7.3 %collective-permute-done.46 = f32[3,1024]{1,0:T(4,128)S(1)} collective-permute-done((f32[3,1024]{1,0:T(4,128)S(1)}, f32[3,1024]{1,0:T(4,128)S(1)}, u32[]{:S(2)}, u32[]{:S(2)}) %collective-permute-start.46) | collective-permute-done | bytes 12320 | tf_op jit(solution)/shard_map/ppermute | solution.py:43
  389.2 1.9 collective-permute-start.47
  397.7 2.7 maximum_select_fusion
  403.4 3.1 collective-permute-start.59
  406.9 4.3 collective-permute-start.61
  411.2 2.4 collective-permute-start.62
  414.1 2.4 reshape.438
  417.8 7.3 %collective-permute-done.62 = f32[32,1024]{1,0:T(8,128)S(1)} collective-permute-done((f32[32,1024]{1,0:T(8,128)S(1)}, f32[32,1024]{1,0:T(8,128)S(1)}, u32[]{:S(2)}, u32[]{:S(2)}) %collective-permute-start.62) | collective-permute-done | bytes 131104 | tf_op jit(solution)/shard_map/ppermute | solution.py:418
  426.0 3.9 multiply_reduce_fusion.1
  431.6 1.9 copy.89
  (307 shorter events, 90.2 us)
Async XLA Ops:
  7.2 141.3 %all-gather.3.cloned.1.call-start = ((), (), s32[]{:S(2)}) async-start(), calls=%async_computation.3 | async-start | bytes 2162688 | tf_op jit(solution)/shard_map/all_gather | solution.py:291
  8.9 19.0 %collective-permute-start.10 = (bf16[32,1024]{1,0:T(8,128)(2,1)S(1)}, bf16[32,1024]{1,0:T(8,128)(2,1)S(1)}, u32[]{:S(2)}, u32[]{:S(2)}) collective-permute-start(bf16[32,1024]{1,0:T(8,128)(2,1)S(1)} %get-tuple-element.122), channel_id=1, source_target_pairs={{0,16},{1,3},{2,4},{3,21},{4,22},{5,9},{6,10},{7,27},{8,28},{9,15}... | collective-permute-start | bytes 196616 | tf_op jit(solution)/shard_map/ppermute | solution.py:272
  12.4 18.9 %collective-permute-start.8 = (bf16[32,1024]{1,0:T(8,128)(2,1)S(1)}, bf16[32,1024]{1,0:T(8,128)(2,1)S(1)}, u32[]{:S(2)}, u32[]{:S(2)}) collective-permute-start(bf16[32,1024]{1,0:T(8,128)(2,1)S(1)} %get-tuple-element.124), channel_id=1, source_target_pairs={{0,0},{1,17},{2,18},{3,5},{4,6},{5,23},{6,24},{7,11},{8,12},{9,29}... | collective-permute-start | bytes 196616 | tf_op jit(solution)/shard_map/ppermute | solution.py:272
  17.8 13.5 %collective-permute-start.9 = (bf16[32,1024]{1,0:T(8,128)(2,1)S(1)}, bf16[32,1024]{1,0:T(8,128)(2,1)S(1)}, u32[]{:S(2)}, u32[]{:S(2)}) collective-permute-start(bf16[32,1024]{1,0:T(8,128)(2,1)S(1)} %get-tuple-element.123), channel_id=1, source_target_pairs={{0,1},{1,2},{2,19},{3,20},{4,7},{5,8},{6,25},{7,26},{8,13},{9,14},... | collective-permute-start | bytes 196616 | tf_op jit(solution)/shard_map/ppermute | solution.py:272
  18.8 12.7 %collective-permute-start = (bf16[64,1024]{1,0:T(8,128)(2,1)S(1)}, bf16[64,1024]{1,0:T(8,128)(2,1)S(1)}, u32[]{:S(2)}, u32[]{:S(2)}) collective-permute-start(bf16[64,1024]{1,0:T(8,128)(2,1)S(1)} %get-tuple-element.115), channel_id=1, source_target_pairs={{0,1},{1,0},{2,3},{3,2},{4,5},{5,4},{6,7},{7,6},{8,9},{9,8},{10,11... | collective-permute-start | bytes 393224 | tf_op jit(solution)/shard_map/ppermute | solution.py:43
  21.3 16.1 %collective-permute-start.21 = (bf16[128,1024]{1,0:T(8,128)(2,1)S(1)}, bf16[128,1024]{1,0:T(8,128)(2,1)S(1)}, u32[]{:S(2)}, u32[]{:S(2)}) collective-permute-start(bf16[128,1024]{1,0:T(8,128)(2,1)S(1)} %broadcast_select_fusion.3), channel_id=1, source_target_pairs={{0,16},{16,0},{1,17},{17,1},{2,18},{18,2},{3,19},{19,3},{4,20},{20... | collective-permute-start | bytes 786440 | tf_op jit(solution)/shard_map/ppermute | solution.py:47
  27.9 11.7 %collective-permute-start.22 = (bf16[128,1024]{1,0:T(8,128)(2,1)}, bf16[128,1024]{1,0:T(8,128)(2,1)S(1)}, u32[]{:S(2)}, u32[]{:S(2)}) collective-permute-start(bf16[128,1024]{1,0:T(8,128)(2,1)} %param.30), channel_id=1, source_target_pairs={{0,0},{1,16},{2,1},{3,17},{4,2},{5,18},{6,3},{7,19},{8,4},{9,20},{... | collective-permute-start | bytes 786440 | tf_op jit(solution)/shard_map/ppermute | solution.py:298
  31.6 14.1 %collective-permute-start.2 = (bf16[128,1024]{1,0:T(8,128)(2,1)S(1)}, bf16[128,1024]{1,0:T(8,128)(2,1)}, u32[]{:S(2)}, u32[]{:S(2)}) collective-permute-start(bf16[128,1024]{1,0:T(8,128)(2,1)S(1)} %maximum_select_fusion.4.refs_0_), channel_id=1, source_target_pairs={{0,4},{1,5},{2,6},{3,7},{4,0},{5,1},{6,2},{7,3},{8,12},{9,13},{10,... | collective-permute-start | bytes 786440 | tf_op jit(solution)/shard_map/ppermute | solution.py:43
  33.5 30.7 %collective-permute-start.4 = (bf16[128,1024]{1,0:T(8,128)(2,1)S(1)}, bf16[128,1024]{1,0:T(8,128)(2,1)S(1)}, u32[]{:S(2)}, u32[]{:S(2)}) collective-permute-start(bf16[128,1024]{1,0:T(8,128)(2,1)S(1)} %maximum_select_fusion.4.refs_0_), channel_id=1, source_target_pairs={{0,8},{1,9},{2,10},{3,11},{4,12},{5,13},{6,14},{7,15},{8,0},{9,1},... | collective-permute-start | bytes 786440 | tf_op jit(solution)/shard_map/ppermute | solution.py:43
  33.8 31.1 %collective-permute-start.6 = (bf16[128,1024]{1,0:T(8,128)(2,1)S(1)}, bf16[128,1024]{1,0:T(8,128)(2,1)}, u32[]{:S(2)}, u32[]{:S(2)}) collective-permute-start(bf16[128,1024]{1,0:T(8,128)(2,1)S(1)} %maximum_select_fusion.4.refs_0_), channel_id=1, source_target_pairs={{0,12},{1,13},{2,14},{3,15},{4,8},{5,9},{6,10},{7,11},{8,4},{9,5},... | collective-permute-start | bytes 786440 | tf_op jit(solution)/shard_map/ppermute | solution.py:43
  37.4 31.8 %collective-permute-start.1 = (bf16[128,1024]{1,0:T(8,128)(2,1)S(1)}, bf16[128,1024]{1,0:T(8,128)(2,1)S(1)}, u32[]{:S(2)}, u32[]{:S(2)}) collective-permute-start(bf16[128,1024]{1,0:T(8,128)(2,1)S(1)} %maximum_select_fusion.4.refs_0_), channel_id=1, source_target_pairs={{0,2},{1,3},{2,0},{3,1},{4,6},{5,7},{6,4},{7,5},{8,10},{9,11},{10,... | collective-permute-start | bytes 786440 | tf_op jit(solution)/shard_map/ppermute | solution.py:43
  39.6 35.0 %collective-permute-start.12 = (bf16[3,2,32,1024]{3,2,0,1:T(8,128)(2,1)}, bf16[3,2,32,1024]{3,2,0,1:T(8,128)(2,1)S(1)}, u32[]{:S(2)}, u32[]{:S(2)}) collective-permute-start(bf16[3,2,32,1024]{3,2,0,1:T(8,128)(2,1)} %maximum_select_fusion.3), channel_id=1, source_target_pairs={{0,16},{16,0},{1,17},{17,1},{2,18},{18,2},{3,19},{19,3},{4,20},{20... | collective-permute-start | bytes 1179656 | tf_op jit(solution)/shard_map/ppermute | solution.py:47
  45.7 32.2 %collective-permute-start.3 = (bf16[128,1024]{1,0:T(8,128)(2,1)}, bf16[128,1024]{1,0:T(8,128)(2,1)}, u32[]{:S(2)}, u32[]{:S(2)}) collective-permute-start(bf16[128,1024]{1,0:T(8,128)(2,1)} %collective-permute-done.2.refs_2_), channel_id=1, source_target_pairs={{0,2},{1,3},{2,0},{3,1},{4,6},{5,7},{6,4},{7,5},{8,10},{9,11},{10,... | collective-permute-start | bytes 786440 | tf_op jit(solution)/shard_map/ppermute | solution.py:43
  64.2 40.1 %collective-permute-start.23 = (bf16[384,1024]{1,0:T(8,128)(2,1)}, bf16[384,1024]{1,0:T(8,128)(2,1)S(1)}, u32[]{:S(2)}, u32[]{:S(2)}) collective-permute-start(bf16[384,1024]{1,0:T(8,128)(2,1)} %get-tuple-element.101), channel_id=1, source_target_pairs={{0,4},{1,5},{2,6},{3,7},{4,0},{5,1},{6,2},{7,3},{8,12},{9,13},{10,... | collective-permute-start | bytes 2359304 | tf_op jit(solution)/shard_map/ppermute | solution.py:43
  64.9 64.3 %collective-permute-start.24 = (bf16[384,1024]{1,0:T(8,128)(2,1)}, bf16[384,1024]{1,0:T(8,128)(2,1)S(1)}, u32[]{:S(2)}, u32[]{:S(2)}) collective-permute-start(bf16[384,1024]{1,0:T(8,128)(2,1)} %get-tuple-element.101), channel_id=1, source_target_pairs={{0,8},{1,9},{2,10},{3,11},{4,12},{5,13},{6,14},{7,15},{8,0},{9,1},... | collective-permute-start | bytes 2359304 | tf_op jit(solution)/shard_map/ppermute | solution.py:43
  69.3 59.9 %collective-permute-start.25 = (bf16[384,1024]{1,0:T(8,128)(2,1)}, bf16[384,1024]{1,0:T(8,128)(2,1)}, u32[]{:S(2)}, u32[]{:S(2)}) collective-permute-start(bf16[384,1024]{1,0:T(8,128)(2,1)} %get-tuple-element.101), channel_id=1, source_target_pairs={{0,12},{1,13},{2,14},{3,15},{4,8},{5,9},{6,10},{7,11},{8,4},{9,5},... | collective-permute-start | bytes 2359304 | tf_op jit(solution)/shard_map/ppermute | solution.py:43
  74.7 10.7 %collective-permute-start.5 = (bf16[128,1024]{1,0:T(8,128)(2,1)}, bf16[128,1024]{1,0:T(8,128)(2,1)S(1)}, u32[]{:S(2)}, u32[]{:S(2)}) collective-permute-start(bf16[128,1024]{1,0:T(8,128)(2,1)} %copy-done.29), channel_id=1, source_target_pairs={{0,2},{1,3},{2,0},{3,1},{4,6},{5,7},{6,4},{7,5},{8,10},{9,11},{10,... | collective-permute-start | bytes 786440 | tf_op jit(solution)/shard_map/ppermute | solution.py:43
  77.9 11.4 %collective-permute-start.7 = (bf16[128,1024]{1,0:T(8,128)(2,1)}, bf16[128,1024]{1,0:T(8,128)(2,1)S(1)}, u32[]{:S(2)}, u32[]{:S(2)}) collective-permute-start(bf16[128,1024]{1,0:T(8,128)(2,1)} %collective-permute-done.6.refs_6_), channel_id=1, source_target_pairs={{0,2},{1,3},{2,0},{3,1},{4,6},{5,7},{6,4},{7,5},{8,10},{9,11},{10,... | collective-permute-start | bytes 786440 | tf_op jit(solution)/shard_map/ppermute | solution.py:43
  99.2 49.1 %all-to-all-start = ((bf16[16,64,128]{2,1,0:T(8,128)(2,1)}), bf16[16,64,128]{2,1,0:T(8,128)(2,1)S(1)}, u32[]{:S(2)}, u32[]{:S(2)}) async-start(bf16[16,64,128]{2,1,0:T(8,128)(2,1)} %bitcast.256), calls=%async_computation | async-start | bytes 524288 | tf_op jit(solution)/shard_map/all_to_all | solution.py:310
  104.2 321.7 %all-gather.5.cloned.1.call-start = ((), (), s32[]{:S(2)}) async-start(), calls=%async_computation.4 | async-start | bytes 6488064 | tf_op jit(solution)/shard_map/all_gather | solution.py:292
  150.9 13.6 %collective-permute-start.13 = (bf16[128,1024]{1,0:T(8,128)(2,1)S(1)}, bf16[128,1024]{1,0:T(8,128)(2,1)S(1)}, u32[]{:S(2)}, u32[]{:S(2)}) collective-permute-start(bf16[128,1024]{1,0:T(8,128)(2,1)S(1)} %get-tuple-element.78), channel_id=1, source_target_pairs={{0,2},{1,3},{2,0},{3,1},{4,6},{5,7},{6,4},{7,5},{8,10},{9,11},{10,... | collective-permute-start | bytes 786440 | tf_op jit(solution)/shard_map/ppermute | solution.py:43
  151.6 11.2 %collective-permute-start.14 = (bf16[128,1024]{1,0:T(8,128)(2,1)S(1)}, bf16[128,1024]{1,0:T(8,128)(2,1)S(1)}, u32[]{:S(2)}, u32[]{:S(2)}) collective-permute-start(bf16[128,1024]{1,0:T(8,128)(2,1)S(1)} %get-tuple-element.78), channel_id=1, source_target_pairs={{0,16},{16,0},{1,17},{17,1},{2,18},{18,2},{3,19},{19,3},{4,20},{20... | collective-permute-start | bytes 786440 | tf_op jit(solution)/shard_map/ppermute | solution.py:47
  156.3 13.4 %collective-permute-start.17 = (bf16[128,1024]{1,0:T(8,128)(2,1)S(1)}, bf16[128,1024]{1,0:T(8,128)(2,1)S(1)}, u32[]{:S(2)}, u32[]{:S(2)}) collective-permute-start(bf16[128,1024]{1,0:T(8,128)(2,1)S(1)} %get-tuple-element.78), channel_id=1, source_target_pairs={{0,1},{1,0},{2,3},{3,2},{4,5},{5,4},{6,7},{7,6},{8,9},{9,8},{10,11... | collective-permute-start | bytes 786440 | tf_op jit(solution)/shard_map/ppermute | solution.py:43
  162.8 5.3 %collective-permute-start.15 = (bf16[64,1024]{1,0:T(8,128)(2,1)S(1)}, bf16[64,1024]{1,0:T(8,128)(2,1)S(1)}, u32[]{:S(2)}, u32[]{:S(2)}) collective-permute-start(bf16[64,1024]{1,0:T(8,128)(2,1)S(1)} %slice.313), channel_id=1, source_target_pairs={{0,2},{1,3},{2,0},{3,1},{4,6},{5,7},{6,4},{7,5},{8,10},{9,11},{10,... | collective-permute-start | bytes 393224 | tf_op jit(solution)/shard_map/ppermute | solution.py:43
  164.5 5.0 %collective-permute-start.16 = (bf16[64,1024]{1,0:T(8,128)(2,1)S(1)}, bf16[64,1024]{1,0:T(8,128)(2,1)S(1)}, u32[]{:S(2)}, u32[]{:S(2)}) collective-permute-start(bf16[64,1024]{1,0:T(8,128)(2,1)S(1)} %slice.314), channel_id=1, source_target_pairs={{0,16},{16,0},{1,17},{17,1},{2,18},{18,2},{3,19},{19,3},{4,20},{20... | collective-permute-start | bytes 393224 | tf_op jit(solution)/shard_map/ppermute | solution.py:47
  182.1 5.6 %collective-permute-start.27 = (bf16[64,1024]{1,0:T(8,128)(2,1)S(1)}, bf16[64,1024]{1,0:T(8,128)(2,1)S(1)}, u32[]{:S(2)}, u32[]{:S(2)}) collective-permute-start(bf16[64,1024]{1,0:T(8,128)(2,1)S(1)} %get-tuple-element.112), channel_id=1, source_target_pairs={{0,16},{16,0},{1,17},{17,1},{2,18},{18,2},{3,19},{19,3},{4,20},{20... | collective-permute-start | bytes 393224 | tf_op jit(solution)/shard_map/ppermute | solution.py:47
  183.9 5.3 %collective-permute-start.29 = (bf16[64,1024]{1,0:T(8,128)(2,1)S(1)}, bf16[64,1024]{1,0:T(8,128)(2,1)S(1)}, u32[]{:S(2)}, u32[]{:S(2)}) collective-permute-start(bf16[64,1024]{1,0:T(8,128)(2,1)S(1)} %get-tuple-element.113), channel_id=1, source_target_pairs={{0,2},{1,3},{2,0},{3,1},{4,6},{5,7},{6,4},{7,5},{8,10},{9,11},{10,... | collective-permute-start | bytes 393224 | tf_op jit(solution)/shard_map/ppermute | solution.py:43
  187.8 7.7 %collective-permute-start.28 = (bf16[128,1024]{1,0:T(8,128)(2,1)S(1)}, bf16[128,1024]{1,0:T(8,128)(2,1)}, u32[]{:S(2)}, u32[]{:S(2)}) collective-permute-start(bf16[128,1024]{1,0:T(8,128)(2,1)S(1)} %pad_maximum_fusion.7), channel_id=1, source_target_pairs={{0,2},{1,3},{2,0},{3,1},{4,6},{5,7},{6,4},{7,5},{8,10},{9,11},{10,... | collective-permute-start | bytes 786440 | tf_op jit(solution)/shard_map/ppermute | solution.py:43
  190.0 7.5 %collective-permute-start.30 = (bf16[128,1024]{1,0:T(8,128)(2,1)}, bf16[128,1024]{1,0:T(8,128)(2,1)}, u32[]{:S(2)}, u32[]{:S(2)}) collective-permute-start(bf16[128,1024]{1,0:T(8,128)(2,1)} %pad_maximum_fusion.8), channel_id=1, source_target_pairs={{0,16},{16,0},{1,17},{17,1},{2,18},{18,2},{3,19},{19,3},{4,20},{20... | collective-permute-start | bytes 786440 | tf_op jit(solution)/shard_map/ppermute | solution.py:47
  199.2 7.7 %collective-permute-start.32 = (bf16[128,1024]{1,0:T(8,128)(2,1)S(1)}, bf16[128,1024]{1,0:T(8,128)(2,1)S(1)}, u32[]{:S(2)}, u32[]{:S(2)}) collective-permute-start(bf16[128,1024]{1,0:T(8,128)(2,1)S(1)} %get-tuple-element.75), channel_id=1, source_target_pairs={{0,16},{16,0},{1,17},{17,1},{2,18},{18,2},{3,19},{19,3},{4,20},{20... | collective-permute-start | bytes 786440 | tf_op jit(solution)/shard_map/ppermute | solution.py:47
  200.0 7.7 %collective-permute-start.31 = (bf16[128,1024]{1,0:T(8,128)(2,1)S(1)}, bf16[128,1024]{1,0:T(8,128)(2,1)S(1)}, u32[]{:S(2)}, u32[]{:S(2)}) collective-permute-start(bf16[128,1024]{1,0:T(8,128)(2,1)S(1)} %get-tuple-element.75), channel_id=1, source_target_pairs={{0,2},{1,3},{2,0},{3,1},{4,6},{5,7},{6,4},{7,5},{8,10},{9,11},{10,... | collective-permute-start | bytes 786440 | tf_op jit(solution)/shard_map/ppermute | solution.py:43
  201.7 11.2 %collective-permute-start.35 = (bf16[128,1024]{1,0:T(8,128)(2,1)S(1)}, bf16[128,1024]{1,0:T(8,128)(2,1)S(1)}, u32[]{:S(2)}, u32[]{:S(2)}) collective-permute-start(bf16[128,1024]{1,0:T(8,128)(2,1)S(1)} %get-tuple-element.75), channel_id=1, source_target_pairs={{0,1},{1,0},{2,3},{3,2},{4,5},{5,4},{6,7},{7,6},{8,9},{9,8},{10,11... | collective-permute-start | bytes 786440 | tf_op jit(solution)/shard_map/ppermute | solution.py:43
  206.9 5.0 %collective-permute-start.33 = (bf16[64,1024]{1,0:T(8,128)(2,1)S(1)}, bf16[64,1024]{1,0:T(8,128)(2,1)S(1)}, u32[]{:S(2)}, u32[]{:S(2)}) collective-permute-start(bf16[64,1024]{1,0:T(8,128)(2,1)S(1)} %slice.333), channel_id=1, source_target_pairs={{0,2},{1,3},{2,0},{3,1},{4,6},{5,7},{6,4},{7,5},{8,10},{9,11},{10,... | collective-permute-start | bytes 393224 | tf_op jit(solution)/shard_map/ppermute | solution.py:43
  207.7 5.0 %collective-permute-start.34 = (bf16[64,1024]{1,0:T(8,128)(2,1)S(1)}, bf16[64,1024]{1,0:T(8,128)(2,1)S(1)}, u32[]{:S(2)}, u32[]{:S(2)}) collective-permute-start(bf16[64,1024]{1,0:T(8,128)(2,1)S(1)} %slice.334), channel_id=1, source_target_pairs={{0,16},{16,0},{1,17},{17,1},{2,18},{18,2},{3,19},{19,3},{4,20},{20... | collective-permute-start | bytes 393224 | tf_op jit(solution)/shard_map/ppermute | solution.py:47
  208.7 4.3 collective-permute-start.37
  219.2 16.7 %collective-permute-start.39 = (bf16[4,128,1024]{2,1,0:T(8,128)(2,1)S(1)}, bf16[4,128,1024]{2,1,0:T(8,128)(2,1)S(1)}, u32[]{:S(2)}, u32[]{:S(2)}) collective-permute-start(bf16[4,128,1024]{2,1,0:T(8,128)(2,1)S(1)} %bitcast.245), channel_id=1, source_target_pairs={{0,1},{1,0},{2,3},{3,2},{4,5},{5,4},{6,7},{7,6},{8,9},{9,8},{10,11... | collective-permute-start | bytes 3145736 | tf_op jit(solution)/shard_map/ppermute | solution.py:43
  236.5 8.9 %collective-permute-start.40 = (bf16[64,1024]{1,0:T(8,128)(2,1)S(1)}, bf16[64,1024]{1,0:T(8,128)(2,1)S(1)}, u32[]{:S(2)}, u32[]{:S(2)}) collective-permute-start(bf16[64,1024]{1,0:T(8,128)(2,1)S(1)} %get-tuple-element.110), channel_id=1, source_target_pairs={{0,16},{16,0},{1,17},{17,1},{2,18},{18,2},{3,19},{19,3},{4,20},{20... | collective-permute-start | bytes 393224 | tf_op jit(solution)/shard_map/ppermute | solution.py:47
  237.9 9.0 %collective-permute-start.42 = (bf16[64,1024]{1,0:T(8,128)(2,1)S(1)}, bf16[64,1024]{1,0:T(8,128)(2,1)S(1)}, u32[]{:S(2)}, u32[]{:S(2)}) collective-permute-start(bf16[64,1024]{1,0:T(8,128)(2,1)S(1)} %get-tuple-element.111), channel_id=1, source_target_pairs={{0,2},{1,3},{2,0},{3,1},{4,6},{5,7},{6,4},{7,5},{8,10},{9,11},{10,... | collective-permute-start | bytes 393224 | tf_op jit(solution)/shard_map/ppermute | solution.py:43
  245.5 10.2 %collective-permute-start.41 = (bf16[128,1024]{1,0:T(8,128)(2,1)S(1)}, bf16[128,1024]{1,0:T(8,128)(2,1)S(1)}, u32[]{:S(2)}, u32[]{:S(2)}) collective-permute-start(bf16[128,1024]{1,0:T(8,128)(2,1)S(1)} %pad_maximum_fusion.10), channel_id=1, source_target_pairs={{0,2},{1,3},{2,0},{3,1},{4,6},{5,7},{6,4},{7,5},{8,10},{9,11},{10,... | collective-permute-start | bytes 786440 | tf_op jit(solution)/shard_map/ppermute | solution.py:43
  246.9 9.9 %collective-permute-start.43 = (bf16[128,1024]{1,0:T(8,128)(2,1)S(1)}, bf16[128,1024]{1,0:T(8,128)(2,1)S(1)}, u32[]{:S(2)}, u32[]{:S(2)}) collective-permute-start(bf16[128,1024]{1,0:T(8,128)(2,1)S(1)} %pad_maximum_fusion.11), channel_id=1, source_target_pairs={{0,16},{16,0},{1,17},{17,1},{2,18},{18,2},{3,19},{19,3},{4,20},{20... | collective-permute-start | bytes 786440 | tf_op jit(solution)/shard_map/ppermute | solution.py:47
  249.4 93.5 %collective-permute-start.63 = (bf16[384,1024]{1,0:T(8,128)(2,1)}, bf16[384,1024]{1,0:T(8,128)(2,1)}, u32[]{:S(2)}, u32[]{:S(2)}) collective-permute-start(bf16[384,1024]{1,0:T(8,128)(2,1)} %get-tuple-element.87), channel_id=1, source_target_pairs={{0,4},{1,5},{2,6},{3,7},{4,0},{5,1},{6,2},{7,3},{8,12},{9,13},{10,... | collective-permute-start | bytes 2359304 | tf_op jit(solution)/shard_map/ppermute | solution.py:43
  250.8 92.1 %collective-permute-start.64 = (bf16[384,1024]{1,0:T(8,128)(2,1)}, bf16[384,1024]{1,0:T(8,128)(2,1)}, u32[]{:S(2)}, u32[]{:S(2)}) collective-permute-start(bf16[384,1024]{1,0:T(8,128)(2,1)} %get-tuple-element.89), channel_id=1, source_target_pairs={{0,8},{1,9},{2,10},{3,11},{4,12},{5,13},{6,14},{7,15},{8,0},{9,1},... | collective-permute-start | bytes 2359304 | tf_op jit(solution)/shard_map/ppermute | solution.py:43
  260.0 11.2 %collective-permute-start.50 = (bf16[128,1024]{1,0:T(8,128)(2,1)S(1)}, bf16[128,1024]{1,0:T(8,128)(2,1)S(1)}, u32[]{:S(2)}, u32[]{:S(2)}) collective-permute-start(bf16[128,1024]{1,0:T(8,128)(2,1)S(1)} %maximum_select_fusion.6), channel_id=1, source_target_pairs={{0,2},{1,3},{2,0},{3,1},{4,6},{5,7},{6,4},{7,5},{8,10},{9,11},{10,... | collective-permute-start | bytes 786440 | tf_op jit(solution)/shard_map/ppermute | solution.py:43
  260.6 44.0 %collective-permute-start.51 = (bf16[128,1024]{1,0:T(8,128)(2,1)S(1)}, bf16[128,1024]{1,0:T(8,128)(2,1)S(1)}, u32[]{:S(2)}, u32[]{:S(2)}) collective-permute-start(bf16[128,1024]{1,0:T(8,128)(2,1)S(1)} %maximum_select_fusion.6), channel_id=1, source_target_pairs={{0,4},{1,5},{2,6},{3,7},{4,0},{5,1},{6,2},{7,3},{8,12},{9,13},{10,... | collective-permute-start | bytes 786440 | tf_op jit(solution)/shard_map/ppermute | solution.py:43
  262.9 44.0 %all-to-all-start.1 = ((bf16[16,64,128]{2,1,0:T(8,128)(2,1)}), bf16[16,64,128]{2,1,0:T(8,128)(2,1)S(1)}, u32[]{:S(2)}, u32[]{:S(2)}) async-start(bf16[16,64,128]{2,1,0:T(8,128)(2,1)} %bitcast.48), calls=%async_computation.1 | async-start | bytes 524288 | tf_op jit(solution)/shard_map/all_to_all | solution.py:361
  268.1 54.8 %collective-permute-start.53 = (bf16[128,1024]{1,0:T(8,128)(2,1)S(1)}, bf16[128,1024]{1,0:T(8,128)(2,1)S(1)}, u32[]{:S(2)}, u32[]{:S(2)}) collective-permute-start(bf16[128,1024]{1,0:T(8,128)(2,1)S(1)} %maximum_select_fusion.6), channel_id=1, source_target_pairs={{0,8},{1,9},{2,10},{3,11},{4,12},{5,13},{6,14},{7,15},{8,0},{9,1},... | collective-permute-start | bytes 786440 | tf_op jit(solution)/shard_map/ppermute | solution.py:43
  271.2 54.3 %collective-permute-start.55 = (bf16[128,1024]{1,0:T(8,128)(2,1)S(1)}, bf16[128,1024]{1,0:T(8,128)(2,1)S(1)}, u32[]{:S(2)}, u32[]{:S(2)}) collective-permute-start(bf16[128,1024]{1,0:T(8,128)(2,1)S(1)} %maximum_select_fusion.6), channel_id=1, source_target_pairs={{0,12},{1,13},{2,14},{3,15},{4,8},{5,9},{6,10},{7,11},{8,4},{9,5},... | collective-permute-start | bytes 786440 | tf_op jit(solution)/shard_map/ppermute | solution.py:43
  304.7 21.6 %collective-permute-start.52 = (bf16[128,1024]{1,0:T(8,128)(2,1)S(1)}, bf16[128,1024]{1,0:T(8,128)(2,1)S(1)}, u32[]{:S(2)}, u32[]{:S(2)}) collective-permute-start(bf16[128,1024]{1,0:T(8,128)(2,1)S(1)} %collective-permute-done.51), channel_id=1, source_target_pairs={{0,2},{1,3},{2,0},{3,1},{4,6},{5,7},{6,4},{7,5},{8,10},{9,11},{10,... | collective-permute-start | bytes 786440 | tf_op jit(solution)/shard_map/ppermute | solution.py:43
  322.8 20.5 %collective-permute-start.65 = (bf16[384,1024]{1,0:T(8,128)(2,1)}, bf16[384,1024]{1,0:T(8,128)(2,1)}, u32[]{:S(2)}, u32[]{:S(2)}) collective-permute-start(bf16[384,1024]{1,0:T(8,128)(2,1)} %get-tuple-element.88), channel_id=1, source_target_pairs={{0,12},{1,13},{2,14},{3,15},{4,8},{5,9},{6,10},{7,11},{8,4},{9,5},... | collective-permute-start | bytes 2359304 | tf_op jit(solution)/shard_map/ppermute | solution.py:43
  325.4 9.2 %collective-permute-start.54 = (bf16[128,1024]{1,0:T(8,128)(2,1)S(1)}, bf16[128,1024]{1,0:T(8,128)(2,1)S(1)}, u32[]{:S(2)}, u32[]{:S(2)}) collective-permute-start(bf16[128,1024]{1,0:T(8,128)(2,1)S(1)} %collective-permute-done.53), channel_id=1, source_target_pairs={{0,2},{1,3},{2,0},{3,1},{4,6},{5,7},{6,4},{7,5},{8,10},{9,11},{10,... | collective-permute-start | bytes 786440 | tf_op jit(solution)/shard_map/ppermute | solution.py:43
  326.3 11.5 %collective-permute-start.56 = (bf16[128,1024]{1,0:T(8,128)(2,1)S(1)}, bf16[128,1024]{1,0:T(8,128)(2,1)S(1)}, u32[]{:S(2)}, u32[]{:S(2)}) collective-permute-start(bf16[128,1024]{1,0:T(8,128)(2,1)S(1)} %collective-permute-done.55), channel_id=1, source_target_pairs={{0,2},{1,3},{2,0},{3,1},{4,6},{5,7},{6,4},{7,5},{8,10},{9,11},{10,... | collective-permute-start | bytes 786440 | tf_op jit(solution)/shard_map/ppermute | solution.py:43
  342.8 30.5 %collective-permute-start.57 = (f32[4,2,1,32,1024]{4,3,0,1,2:T(8,128)S(1)}, f32[4,2,1,32,1024]{4,3,0,1,2:T(8,128)}, u32[]{:S(2)}, u32[]{:S(2)}) collective-permute-start(f32[4,2,1,32,1024]{4,3,0,1,2:T(8,128)S(1)} %select_bitcast_fusion), channel_id=1, source_target_pairs={{0,1},{1,0},{2,3},{3,2},{4,5},{5,4},{6,7},{7,6},{8,9},{9,8},{10,11... | collective-permute-start | bytes 3145736 | tf_op jit(solution)/shard_map/ppermute | solution.py:43
  347.2 50.5 %collective-permute-start.66 = (f32[128,1024]{1,0:T(8,128)}, f32[128,1024]{1,0:T(8,128)}, u32[]{:S(2)}, u32[]{:S(2)}) collective-permute-start(f32[128,1024]{1,0:T(8,128)} %get-tuple-element.96), channel_id=1, source_target_pairs={{0,16},{16,0},{1,17},{17,1},{2,18},{18,2},{3,19},{19,3},{4,20},{20... | collective-permute-start | bytes 1572872 | tf_op jit(solution)/shard_map/ppermute | solution.py:47
  347.7 52.6 %collective-permute-start.67 = (f32[128,1024]{1,0:T(8,128)}, f32[128,1024]{1,0:T(8,128)}, u32[]{:S(2)}, u32[]{:S(2)}) collective-permute-start(f32[128,1024]{1,0:T(8,128)} %get-tuple-element.95), channel_id=1, source_target_pairs={{0,0},{16,1},{1,2},{17,3},{2,4},{18,5},{3,6},{19,7},{4,8},{20,9},{... | collective-permute-start | bytes 1572872 | tf_op jit(solution)/shard_map/ppermute | solution.py:354
  365.1 8.1 %collective-permute-start.44 = (f32[3,1024]{1,0:T(4,128)S(1)}, f32[3,1024]{1,0:T(4,128)S(1)}, u32[]{:S(2)}, u32[]{:S(2)}) collective-permute-start(f32[3,1024]{1,0:T(4,128)S(1)} %pad_maximum_fusion.13), channel_id=1, source_target_pairs={{0,1},{1,0},{2,3},{3,2},{4,5},{5,4},{6,7},{7,6},{8,9},{9,8},{10,11... | collective-permute-start | bytes 36872 | tf_op jit(solution)/shard_map/ppermute | solution.py:43
  367.5 46.6 %all-to-all-start.2 = ((bf16[16,64,384]{2,1,0:T(8,128)(2,1)}), bf16[16,64,384]{2,1,0:T(8,128)(2,1)}, u32[]{:S(2)}, u32[]{:S(2)}) async-start(bf16[16,64,384]{2,1,0:T(8,128)(2,1)} %pad_maximum_fusion.4), calls=%async_computation.2 | async-start | bytes 1572864 | tf_op jit(solution)/shard_map/all_to_all | solution.py:310
  373.2 4.4 %collective-permute-start.45 = (f32[3,1024]{1,0:T(4,128)S(1)}, f32[3,1024]{1,0:T(4,128)S(1)}, u32[]{:S(2)}, u32[]{:S(2)}) collective-permute-start(f32[3,1024]{1,0:T(4,128)S(1)} %fusion.37), channel_id=1, source_target_pairs={{0,2},{1,3},{2,0},{3,1},{4,6},{5,7},{6,4},{7,5},{8,10},{9,11},{10,... | collective-permute-start | bytes 36872 | tf_op jit(solution)/shard_map/ppermute | solution.py:43
  374.9 28.3 %collective-permute-start.58 = (f32[4,32,1024]{2,1,0:T(8,128)S(1)}, f32[4,32,1024]{2,1,0:T(8,128)S(1)}, u32[]{:S(2)}, u32[]{:S(2)}) collective-permute-start(f32[4,32,1024]{2,1,0:T(8,128)S(1)} %select_bitcast_fusion.1), channel_id=1, source_target_pairs={{0,16},{16,0},{1,17},{17,1},{2,18},{18,2},{3,19},{19,3},{4,20},{20... | collective-permute-start | bytes 1572872 | tf_op jit(solution)/shard_map/ppermute | solution.py:47
  377.7 11.5 %collective-permute-start.46 = (f32[3,1024]{1,0:T(4,128)S(1)}, f32[3,1024]{1,0:T(4,128)S(1)}, u32[]{:S(2)}, u32[]{:S(2)}) collective-permute-start(f32[3,1024]{1,0:T(4,128)S(1)} %fusion.83), channel_id=1, source_target_pairs={{0,4},{1,5},{2,6},{3,7},{4,0},{5,1},{6,2},{7,3},{8,12},{9,13},{10,... | collective-permute-start | bytes 36872 | tf_op jit(solution)/shard_map/ppermute | solution.py:43
  389.2 8.3 %collective-permute-start.47 = (f32[3,1024]{1,0:T(4,128)S(1)}, f32[3,1024]{1,0:T(4,128)S(1)}, u32[]{:S(2)}, u32[]{:S(2)}) collective-permute-start(f32[3,1024]{1,0:T(4,128)S(1)} %add.204), channel_id=1, source_target_pairs={{0,8},{1,9},{2,10},{3,11},{4,12},{5,13},{6,14},{7,15},{8,0},{9,1},... | collective-permute-start | bytes 36872 | tf_op jit(solution)/shard_map/ppermute | solution.py:43
  403.4 21.8 %collective-permute-start.59 = (f32[32,1024]{1,0:T(8,128)S(1)}, f32[32,1024]{1,0:T(8,128)S(1)}, u32[]{:S(2)}, u32[]{:S(2)}) collective-permute-start(f32[32,1024]{1,0:T(8,128)S(1)} %get-tuple-element.105), channel_id=1, source_target_pairs={{0,0},{17,1},{18,2},{5,3},{6,4},{23,5},{24,6},{11,7},{12,8},{29,9}... | collective-permute-start | bytes 393224 | tf_op jit(solution)/shard_map/ppermute | solution.py:404
  406.5 18.7 %collective-permute-start.60 = (f32[32,1024]{1,0:T(8,128)S(1)}, f32[32,1024]{1,0:T(8,128)S(1)}, u32[]{:S(2)}, u32[]{:S(2)}) collective-permute-start(f32[32,1024]{1,0:T(8,128)S(1)} %get-tuple-element.107), channel_id=1, source_target_pairs={{1,0},{2,1},{19,2},{20,3},{7,4},{8,5},{25,6},{26,7},{13,8},{14,9},... | collective-permute-start | bytes 393224 | tf_op jit(solution)/shard_map/ppermute | solution.py:404
  406.9 18.3 %collective-permute-start.61 = (f32[32,1024]{1,0:T(8,128)S(1)}, f32[32,1024]{1,0:T(8,128)S(1)}, u32[]{:S(2)}, u32[]{:S(2)}) collective-permute-start(f32[32,1024]{1,0:T(8,128)S(1)} %get-tuple-element.106), channel_id=1, source_target_pairs={{16,0},{3,1},{4,2},{21,3},{22,4},{9,5},{10,6},{27,7},{28,8},{15,9}... | collective-permute-start | bytes 393224 | tf_op jit(solution)/shard_map/ppermute | solution.py:404
  411.2 14.0 %collective-permute-start.62 = (f32[32,1024]{1,0:T(8,128)S(1)}, f32[32,1024]{1,0:T(8,128)S(1)}, u32[]{:S(2)}, u32[]{:S(2)}) collective-permute-start(f32[32,1024]{1,0:T(8,128)S(1)} %slice_bitcast_fusion.12), channel_id=1, source_target_pairs={{0,0},{1,1},{16,2},{17,3},{2,4},{3,5},{18,6},{19,7},{4,8},{5,9},{2... | collective-permute-start | bytes 393224 | tf_op jit(solution)/shard_map/ppermute | solution.py:418
  (47 other events, 370.6 us)
Sparse Core Ops, SparseCore 0:
  10.8 80.9 all-gather.2
  190.9 90.0 all-gather.4

commit v2 on v1

v2 whole, which is shorter than its diff:
```python
import functools

import jax
import jax.numpy as jnp
from jax import lax
from jax.experimental import pallas as pl
from jax.experimental.pallas import tpu as pltpu
from jax.sharding import PartitionSpec as P

HEADS = 16
HEAD_DIM = 64
PAIR_DIM = 2 * HEAD_DIM
EPS = 1e-05
NEG = -1e30
F32 = jnp.float32
BF16 = jnp.bfloat16
BOTH = ("dp", "seq")
BLOCK = 256


def rms_scale(rows):
    return lax.rsqrt(jnp.mean(rows * rows, axis=-1, keepdims=True) + EPS)


def nt(left, right):
    return lax.dot_general(left, right, (((1,), (1,)), ((), ())), preferred_element_type=F32)


def tn(left, right):
    return lax.dot_general(left, right, (((0,), (0,)), ((), ())), preferred_element_type=F32)


def nn(left, right):
    return jnp.dot(left, right, preferred_element_type=F32)


def norm_back(grad_norm, normed, scale_rows, gain):
    scaled = grad_norm * gain
    return scale_rows * (scaled - normed * jnp.mean(scaled * normed, axis=-1, keepdims=True))


def swap_seq(value, bits, n_seq):
    return lax.ppermute(value, "seq", [(i, i ^ bits) for i in range(n_seq)])


def swap_dp(value):
    return lax.ppermute(value, "dp", [(0, 1), (1, 0)])


def cube_gather(own, n_seq):
    half = own.shape[0] // 2
    by_one = swap_seq(own, 2, n_seq)
    by_two = swap_seq(own, 4, n_seq)
    by_core = swap_seq(own, 1, n_seq)
    across = jnp.concatenate([swap_seq(by_two[:half], 2, n_seq), swap_seq(by_one[half:], 4, n_seq)], 0)
    others = [swap_seq(v, 1, n_seq) for v in (by_one, by_two, across)]
    return jnp.concatenate([own, by_one, by_two, across, by_core] + others, 0)


def cube_reduce(parts, n_seq):
    half = parts.shape[1] // 2
    got = swap_seq(parts[4:].astype(BF16), 1, n_seq).astype(F32)
    here, for_one, for_two, for_across = (parts[i] + got[i] for i in range(4))
    low = for_across.astype(BF16)
    via_one = swap_seq(low[:half], 2, n_seq).astype(F32)
    via_two = swap_seq(low[half:], 4, n_seq).astype(F32)
    for_two = jnp.concatenate([for_two[:half] + via_one, for_two[half:]], 0)
    for_one = jnp.concatenate([for_one[:half], for_one[half:] + via_two], 0)
    from_one = swap_seq(for_one.astype(BF16), 2, n_seq).astype(F32)
    from_two = swap_seq(for_two.astype(BF16), 4, n_seq).astype(F32)
    return here + from_one + from_two, got


def joint(*trees):
    leaves, shape = jax.tree.flatten(trees)
    return jax.tree.unflatten(shape, lax.optimization_barrier(tuple(leaves)))


def after(value, *others):
    return joint(value, *others)[0]


def micro_pair(rows, core, n_seq):
    keep = jnp.where(core == 0, rows[0], rows[1])
    send = jnp.where(core == 0, rows[1], rows[0])
    got = swap_seq(send, 1, n_seq)
    return jnp.where(core == 0, jnp.concatenate([keep, got], 0), jnp.concatenate([got, keep], 0))


def ones_of(number):
    return bin(number).count("1")


def spread(blocks, ones, unit_bits, count, n_seq):
    for j in range(1, count):
        if ones_of(j) == ones:
            blocks[j] = swap_seq(blocks[j & (j - 1)], unit_bits * (j & -j), n_seq)


def far_reduce(terms, gates, n_seq):
    bits = 8
    while terms.shape[0] > 1:
        pairs = terms.reshape((terms.shape[0] // 2, 2) + terms.shape[1:])
        got = swap_seq(pairs[:, 1].astype(BF16), bits, n_seq)
        terms = pairs[:, 0] + after(got, gates[0]).astype(F32)
        gates = gates[1:] or gates
        bits *= 2
    return terms[0]


def halve(terms, extra, mine, exchange):
    keep = jnp.where(mine == 0, terms[0], terms[1])
    give = jnp.where(mine == 0, terms[1], terms[0]).astype(BF16)
    high = extra.astype(BF16)
    low = (extra - high.astype(F32)).astype(BF16)
    rows = give.reshape(-1, give.shape[-1])
    got = exchange(jnp.concatenate([rows, high, low], 0)).astype(F32)
    n = extra.shape[0]
    keep = keep + got[: rows.shape[0]].reshape(keep.shape)
    return keep, (high.astype(F32) + low.astype(F32)) + (got[-2 * n : -n] + got[-n:])


def halve_seq(terms, extra, bits, n_seq):
    shape = terms.shape
    pairs = terms.reshape(shape[:-3] + (shape[-3] // 2, 2) + shape[-2:])
    mine = (lax.axis_index("seq") // bits) % 2
    return halve(jnp.moveaxis(pairs, -3, 0), extra, mine, lambda v: swap_seq(v, bits, n_seq))


def matchings(edges, count):
    left = list(edges)
    rounds = []
    for _ in range(count):
        by_source = {}
        for edge in left:
            by_source.setdefault(edge[0], []).append(edge)
        taken = {}

        def place(source, seen):
            for edge in by_source[source]:
                if edge[1] in seen:
                    continue
                seen.add(edge[1])
                if edge[1] not in taken or place(taken[edge[1]][0], seen):
                    taken[edge[1]] = edge
                    return True
            return False

        for source in sorted(by_source):
            place(source, set())
        chosen = sorted(taken.values())
        rounds.append(chosen)
        for edge in chosen:
            left.remove(edge)
    return rounds


def spans(rows_q, rows_k):
    for start in range(0, rows_q, BLOCK):
        if rows_q == rows_k:
            yield start, max(start + BLOCK, rows_k // 2)
        else:
            yield start, rows_k


def attend_kernel(where_ref, *refs):
    n_blocks = len(refs) - 5
    x_refs = refs[:n_blocks]
    w_ref, gain_ref, first_ref, mixed_ref, att_ref = refs[n_blocks:]
    my_block, first_query, prefix_len = where_ref[0], where_ref[1], where_ref[2]
    rows = x_refs[0].shape[0]
    for j in range(n_blocks):
        at = pl.multiple_of((my_block ^ j) * rows, rows)
        source = x_refs[j][...].astype(F32)
        first = (source * rms_scale(source) * gain_ref[...]).astype(BF16)
        first_ref[pl.ds(at, rows), :] = first
        mixed_ref[pl.ds(at, rows), :] = nt(first, w_ref[...]).astype(BF16)
    rows_q, rows_k = att_ref.shape[0], mixed_ref.shape[0]
    lanes = lax.broadcasted_iota(jnp.int32, (BLOCK, PAIR_DIM), 1)
    for start, width in spans(rows_q, rows_k):
        at = pl.multiple_of(first_query + start, BLOCK)
        query = mixed_ref[pl.ds(at, BLOCK), 0:PAIR_DIM]
        keys = mixed_ref[0:width, PAIR_DIM : 2 * PAIR_DIM]
        values = mixed_ref[0:width, 2 * PAIR_DIM :]
        key_pos = lax.broadcasted_iota(jnp.int32, (BLOCK, width), 1)
        query_pos = at + lax.broadcasted_iota(jnp.int32, (BLOCK, width), 0)
        allowed = (key_pos <= query_pos) | (key_pos < prefix_len)
        outs = []
        for head in range(2):
            mine = (lanes // HEAD_DIM) == head
            scores = nt(jnp.where(mine, query, jnp.zeros_like(query)), keys) * HEAD_DIM**-0.5
            scores = jnp.where(allowed, scores, NEG)
            top = jnp.max(scores, axis=-1, keepdims=True)
            weights = jnp.exp(scores - top)
            total = jnp.sum(weights, axis=-1, keepdims=True)
            probs = (weights / total).astype(BF16)
            outs.append(nn(probs, values))
        att_ref[start : start + BLOCK, :] = jnp.where(lanes < HEAD_DIM, outs[0], outs[1]).astype(BF16)


def attend(where, blocks, weights, gain, rows_q):
    rows_k = blocks[0].shape[0] * len(blocks)
    width = blocks[0].shape[1]
    n_in = len(blocks) + 2
    return pl.pallas_call(
        attend_kernel,
        out_shape=(
            jax.ShapeDtypeStruct((rows_k, width), BF16),
            jax.ShapeDtypeStruct((rows_k, 3 * PAIR_DIM), BF16),
            jax.ShapeDtypeStruct((rows_q, PAIR_DIM), BF16),
        ),
        in_specs=[pl.BlockSpec(memory_space=pltpu.SMEM)] + [pl.BlockSpec(memory_space=pltpu.VMEM)] * n_in,
        out_specs=(pl.BlockSpec(memory_space=pltpu.VMEM),) * 3,
        compiler_params=pltpu.CompilerParams(vmem_limit_bytes=56 << 20),
        cost_estimate=pl.CostEstimate(
            flops=2 * rows_k * width * 3 * PAIR_DIM + 4 * rows_q * rows_k * PAIR_DIM,
            bytes_accessed=4 * rows_k * width,
            transcendentals=2 * rows_q * rows_k,
        ),
    )(where, *blocks, weights, gain)


def attend_back_kernel(where_ref, mixed_ref, grad_ref, out_ref, gk_ref, gv_ref):
    first_query, prefix_len = where_ref[1], where_ref[2]
    rows_q, rows_k = grad_ref.shape[0], mixed_ref.shape[0]
    lanes = lax.broadcasted_iota(jnp.int32, (BLOCK, PAIR_DIM), 1)
    gk_ref[...] = jnp.zeros_like(gk_ref)
    gv_ref[...] = jnp.zeros_like(gv_ref)
    for start, width in spans(rows_q, rows_k):
        at = pl.multiple_of(first_query + start, BLOCK)
        query = mixed_ref[pl.ds(at, BLOCK), 0:PAIR_DIM]
        grad = grad_ref[start : start + BLOCK, :]
        keys = mixed_ref[0:width, PAIR_DIM : 2 * PAIR_DIM]
        values = mixed_ref[0:width, 2 * PAIR_DIM :]
        key_pos = lax.broadcasted_iota(jnp.int32, (width, BLOCK), 0)
        query_pos = at + lax.broadcasted_iota(jnp.int32, (width, BLOCK), 1)
        allowed = (key_pos <= query_pos) | (key_pos < prefix_len)
        outs = []
        for head in range(2):
            mine = (lanes // HEAD_DIM) == head
            own_query = jnp.where(mine, query, jnp.zeros_like(query))
            own_grad = jnp.where(mine, grad, jnp.zeros_like(grad))
            scores = nt(keys, own_query) * HEAD_DIM**-0.5
            scores = jnp.where(allowed, scores, NEG)
            top = jnp.max(scores, axis=0, keepdims=True)
            weights = jnp.exp(scores - top)
            probs = weights / jnp.sum(weights, axis=0, keepdims=True)
            grad_probs = nt(values, own_grad)
            delta = jnp.sum(probs * grad_probs, axis=0, keepdims=True)
            grad_scores = (probs * (grad_probs - delta)).astype(BF16)
            gv_ref[0:width, :] += nn(probs.astype(BF16), own_grad)
            gk_ref[0:width, :] += nn(grad_scores, own_query) * HEAD_DIM**-0.5
            outs.append(tn(grad_scores, keys) * HEAD_DIM**-0.5)
        grad_q = jnp.where(lanes < HEAD_DIM, outs[0], outs[1])
        out_ref[start : start + BLOCK, 0:PAIR_DIM] = grad_q.astype(BF16)
    if out_ref.shape[1] > PAIR_DIM:
        out_ref[:, PAIR_DIM : 2 * PAIR_DIM] = gk_ref[...].astype(BF16)
        out_ref[:, 2 * PAIR_DIM :] = gv_ref[...].astype(BF16)


def attend_back(where, mixed, grad):
    rows_q, rows_k = grad.shape[0], mixed.shape[0]
    whole = rows_q == rows_k
    keys = jax.ShapeDtypeStruct((rows_k, PAIR_DIM), F32)
    vmem = pl.BlockSpec(memory_space=pltpu.VMEM)
    return pl.pallas_call(
        attend_back_kernel,
        out_shape=(jax.ShapeDtypeStruct((rows_q, (3 if whole else 1) * PAIR_DIM), BF16),) + (() if whole else (keys, keys)),
        in_specs=[pl.BlockSpec(memory_space=pltpu.SMEM), vmem, vmem],
        out_specs=(vmem,) if whole else (vmem,) * 3,
        scratch_shapes=[pltpu.VMEM(keys.shape, F32)] * (2 if whole else 0),
        compiler_params=pltpu.CompilerParams(vmem_limit_bytes=56 << 20),
        cost_estimate=pl.CostEstimate(
            flops=10 * rows_q * rows_k * PAIR_DIM,
            bytes_accessed=8 * rows_k * PAIR_DIM * 4,
            transcendentals=2 * rows_q * rows_k,
        ),
    )(where, mixed, grad)


def project_kernel(moved_ref, w_ref, x_ref, gain_ref, att_ref, middle_ref, second_ref):
    n_micro = att_ref.shape[0] // moved_ref.shape[1]
    tok = moved_ref.shape[1]
    for i in range(moved_ref.shape[0]):
        pair, micro = divmod(i, n_micro)
        att_ref[micro * tok : (micro + 1) * tok, pair * PAIR_DIM : (pair + 1) * PAIR_DIM] = moved_ref[i]
    middle = x_ref[...].astype(F32) + nn(att_ref[...], w_ref[...])
    middle_ref[...] = middle
    second_ref[...] = (middle * rms_scale(middle) * gain_ref[...]).astype(BF16)


def project(moved, weights, rows_in, gain):
    rows, width = rows_in.shape
    vmem = pl.BlockSpec(memory_space=pltpu.VMEM)
    return pl.pallas_call(
        project_kernel,
        out_shape=(
            jax.ShapeDtypeStruct((rows, width), BF16),
            jax.ShapeDtypeStruct((rows, width), F32),
            jax.ShapeDtypeStruct((rows, width), BF16),
        ),
        in_specs=[vmem] * 4,
        out_specs=(vmem,) * 3,
        compiler_params=pltpu.CompilerParams(vmem_limit_bytes=32 << 20),
        cost_estimate=pl.CostEstimate(flops=2 * rows * width * width, bytes_accessed=4 * width * width, transcendentals=rows),
    )(moved, weights, rows_in, gain)


def input_grad_kernel(moved_ref, w_ref, x_ref, grad_ref, gain_ref, out_ref, mixed_ref):
    n_micro = out_ref.shape[0] // moved_ref.shape[1]
    tok = moved_ref.shape[1]
    width = x_ref.shape[1]
    for i in range(moved_ref.shape[0]):
        pair, micro = divmod(i, n_micro)
        for kind in range(3):
            at = kind * width + pair * PAIR_DIM
            mixed_ref[micro * tok : (micro + 1) * tok, at : at + PAIR_DIM] = moved_ref[
                i, :, kind * PAIR_DIM : (kind + 1) * PAIR_DIM
            ]
    source = x_ref[...].astype(F32)
    scale = rms_scale(source)
    grad_first = nn(mixed_ref[...], w_ref[...])
    out_ref[...] = grad_ref[...] + norm_back(grad_first, source * scale, scale, gain_ref[...])


def input_gradient(moved, weights, rows_in, grad_middle, gain):
    rows, width = rows_in.shape
    vmem = pl.BlockSpec(memory_space=pltpu.VMEM)
    return pl.pallas_call(
        input_grad_kernel,
        out_shape=jax.ShapeDtypeStruct((rows, width), F32),
        in_specs=[vmem] * 5,
        out_specs=vmem,
        scratch_shapes=[pltpu.VMEM((rows, 3 * width), BF16)],
        compiler_params=pltpu.CompilerParams(vmem_limit_bytes=32 << 20),
        cost_estimate=pl.CostEstimate(flops=200 * rows * width * width, bytes_accessed=8 * width * width, transcendentals=rows),
    )(moved, weights, rows_in, grad_middle, gain)


def shards(n_dp, n_seq, inputs, teacher, valid_mask, prefix, attn_in, attn_out, mlp_in, mlp_out, norm_gains):
    n_micro, _, tok_rows, width = inputs.shape
    rows = n_micro * tok_rows
    dp = lax.axis_index("dp")
    seq = lax.axis_index("seq")
    me = dp * n_seq + seq
    core = seq % 2
    n_dev = n_dp * n_seq
    n_pairs = HEADS // 2
    group = n_micro * n_pairs
    n_parts = n_seq // group
    part = seq // group
    n_far = n_seq // 8
    seq_len = n_seq * tok_rows
    rows_q = seq_len // n_parts
    part_groups = [[p * group + g for p in range(n_parts)] for g in range(group)]
    in_groups = [[p * group + g for g in range(group)] for p in range(n_parts)] if n_parts > 1 else None
    gain_one = norm_gains[0:1]
    gain_two = norm_gains[1:2]

    unit = attn_in.shape[0] // 3
    n_share = PAIR_DIM // unit
    edges = []
    for block in range(3 * n_dev):
        third, rest = divmod(block, n_pairs * n_share)
        pair, share = divmod(rest, n_share)
        to_dp, rest = divmod(share, 2 * n_parts)
        to_part, to_core = divmod(rest, 2)
        to_seq = to_part * group + 2 * pair + to_core
        edges.append((block // 3, to_dp * n_seq + to_seq, block % 3, third))
    rounds = matchings(edges, 3)
    own_units = attn_in.reshape(3, unit, width)
    arrived = []
    for chosen in rounds:
        slot = jnp.array([edge[2] for edge in chosen], jnp.int32)[me]
        value = lax.dynamic_index_in_dim(own_units, slot, 0, keepdims=False)
        arrived.append(lax.ppermute(value, BOTH, [(edge[0], edge[1]) for edge in chosen]))
    thirds = []
    for chosen in rounds:
        order = sorted((edge[1], edge[3]) for edge in chosen)
        thirds.append(jnp.array([third for _, third in order], jnp.int32)[me])

    attn_out_full = lax.all_gather(attn_out, BOTH, axis=0, tiled=True)
    attn_in_full = lax.all_gather(attn_in, BOTH, axis=0, tiled=True)

    down_rows = lax.ppermute(mlp_out, BOTH, [(b, (b % 2) * n_seq + b // 2) for b in range(n_dev)])

    n_line = n_seq // 4
    near = {0: micro_pair(inputs[:, 0], core, n_seq)}
    far = {}
    near, arrived, down_rows = joint(near, arrived, down_rows)
    spread(near, 1, 4, n_line, n_seq)
    far[0] = swap_seq(near[0], 2, n_seq)
    my_thirds = jnp.stack(
        [
            jnp.where(thirds[0] == third, arrived[0], jnp.where(thirds[1] == third, arrived[1], arrived[2]))
            for third in range(3)
        ]
    )
    got = swap_seq(my_thirds, 1, n_seq)
    both = jnp.where(core == 0, jnp.stack([my_thirds, got], 1), jnp.stack([got, my_thirds], 1))
    if n_parts > 1:
        both = lax.all_gather(both, "seq", axis=1, axis_index_groups=part_groups, tiled=True)
    near, far, both, ffn_own = joint(near, far, both, jnp.concatenate([mlp_in, down_rows], 0))
    ffn_here, ffn_there = {0: ffn_own}, {}
    ones = 2
    while True:
        before = [j for j in near if ones_of(j) == ones - 1]
        if not before:
            break
        spread(near, ones, 4, n_line, n_seq)
        for j in before:
            far[j] = swap_seq(near[j], 2, n_seq)
        if ones == 2:
            got = swap_dp(both)
            ffn_there[0] = swap_dp(ffn_own)
        near, far, got, ffn_here = joint(near, far, got, ffn_here)
        ones += 1
    spread(ffn_here, 1, 8, n_far, n_seq)
    pair_weights = jnp.where(dp == 0, jnp.stack([both, got], 1), jnp.stack([got, both], 1))
    pair_weights = pair_weights.reshape(3 * PAIR_DIM, width)
    x_blocks = [value for j in range(n_line) for value in (near[j], far[j])]

    prefix_len = jnp.where(core == 0, prefix[0, 0], prefix[1, 0])
    where = jnp.stack([seq // 2, part * rows_q, prefix_len]).astype(jnp.int32)
    first_in, mixed, attended = attend(where, x_blocks, pair_weights, gain_one, rows_q)

    def exchange(by_device):
        return lax.all_to_all(by_device, "seq", 0, 0, axis_index_groups=in_groups)

    own_in = inputs[:, 0].reshape(rows, width)
    target = teacher[:, 0].reshape(rows, width).astype(F32)
    row_mask = valid_mask[:, 0].reshape(rows, 1).astype(F32)
    attended_low, middle, second_own = project(
        exchange(attended.reshape(group, tok_rows, PAIR_DIM)), attn_out_full, own_in, gain_two
    )
    scale_two = rms_scale(middle)
    normed_two = middle * scale_two
    second_in = cube_gather(second_own, n_seq)

    ffn_here = after(ffn_here, second_own)
    for ones in range(1, n_far.bit_length()):
        if ones > 1:
            spread(ffn_here, ones, 8, n_far, n_seq)
        for j in range(1, n_far):
            if ones_of(j) == ones:
                ffn_there[j] = swap_dp(ffn_here[j])
    in_rows = mlp_in.shape[0]
    here_w, there_w = (
        jnp.concatenate([blocks[j][:in_rows] for j in range(n_far)], 0) for blocks in (ffn_here, ffn_there)
    )
    downs = [(ffn_here[j][in_rows:], ffn_there[j][in_rows:]) for j in range(n_far)]
    down_w = jnp.where(
        dp == 0,
        jnp.concatenate([block for here, there in downs for block in (here, there)], 0),
        jnp.concatenate([block for here, there in downs for block in (there, here)], 0),
    )

    by_here = nt(second_in, here_w)
    by_there = nt(second_in, there_w)
    gate = jnp.where(dp == 0, by_here, by_there)
    up_part = jnp.where(dp == 0, by_there, by_here)
    sigmoid_gate = jax.nn.sigmoid(gate)
    silu_gate = gate * sigmoid_gate
    hidden = (silu_gate * up_part).astype(BF16)
    result = middle + cube_reduce(nn(hidden, down_w).reshape(8, rows, width), n_seq)[0]
    output = result.astype(BF16).reshape(n_micro, 1, tok_rows, width)
    error = row_mask * (result - target)
    error_low = cube_gather(error.astype(BF16), n_seq)
    grad_hidden = nt(error_low, down_w)
    grad_gate = grad_hidden * up_part * sigmoid_gate * (1.0 + gate * (1.0 - sigmoid_gate))
    grad_up = grad_hidden * silu_gate
    grad_here = jnp.where(dp == 0, grad_gate, grad_up).astype(BF16)
    grad_there = jnp.where(dp == 0, grad_up, grad_gate).astype(BF16)
    grad_second, begun = cube_reduce(
        (nn(grad_here, here_w) + nn(grad_there, there_w)).reshape(8, rows, width), n_seq
    )

    hidden_late, grad_here, grad_there = after((hidden, grad_here, grad_there), begun)
    down_terms = tn(hidden_late, error_low).reshape(n_far, 2, mlp_out.shape[0], width)
    in_terms = tn(grad_here, second_in).reshape(n_far, in_rows, width)
    down_got = swap_dp(jnp.where(dp == 0, down_terms[:, 1], down_terms[:, 0]).astype(BF16))
    in_got = swap_dp(tn(grad_there, second_in).astype(BF16).reshape(n_far, in_rows, width))
    down_terms = jnp.where(dp == 0, down_terms[:, 0], down_terms[:, 1])

    grad_middle = error + norm_back(grad_second, normed_two, scale_two, gain_two)
    middle_low = grad_middle.astype(BF16)
    grad_att = nt(middle_low, attn_out_full).astype(BF16)
    grad_att = grad_att.reshape(n_micro, tok_rows, n_pairs, PAIR_DIM).transpose(2, 0, 1, 3)
    grad_att = exchange(grad_att.reshape(group, tok_rows, PAIR_DIM)).reshape(rows_q, PAIR_DIM)

    squares = jnp.sum((error * error).reshape(n_micro, tok_rows * width), axis=1)
    scalars = jnp.zeros((width,), F32).at[0:2].set(squares).at[2].set(jnp.sum(row_mask))
    extra = jnp.stack([jnp.sum(grad_second * normed_two, axis=0), scalars])
    out_terms = tn(attended_low, middle_low).reshape(n_dp, n_seq, width // n_dev, width)
    out_terms, extra = halve_seq(out_terms, extra, 1, n_seq)
    out_terms, extra = halve_seq(out_terms, extra, 2, n_seq)
    out_terms, extra = halve(out_terms, extra, dp, swap_dp)

    down_terms = down_terms + after(down_got, grad_second).astype(F32)
    down_sum = far_reduce(down_terms, [grad_att], n_seq)
    mlp_out_grad = lax.ppermute(
        down_sum.astype(BF16), BOTH, [((b % 2) * n_seq + b // 2, b) for b in range(n_dev)]
    )
    in_terms = in_terms + after(in_got, grad_att).astype(F32)

    grads = attend_back(where, mixed, grad_att)
    first_part = first_in
    grad_mixed = grads[0]
    if n_parts > 1:
        grad_k, grad_v = (
            lax.psum_scatter(v, "seq", scatter_dimension=0, axis_index_groups=part_groups, tiled=True).astype(BF16)
            for v in grads[1:]
        )
        grad_mixed = jnp.concatenate([grad_mixed, grad_k, grad_v], 1)
        first_part = lax.dynamic_slice_in_dim(first_in, part * rows_q, rows_q, 0)
    own_grad_mixed = exchange(grad_mixed.reshape(group, tok_rows, 3 * PAIR_DIM))
    mlp_in_grad = far_reduce(in_terms, [own_grad_mixed], n_seq)
    mlp_out_grad = after(mlp_out_grad, own_grad_mixed).astype(F32)

    pair_grad = tn(grad_mixed, first_part)
    gain_term = (jnp.sum(pair_grad * pair_weights.astype(F32), axis=0) / gain_one[0]).reshape(8, width // 8)
    pair_grad = pair_grad.reshape(3, n_dp, n_parts, 2, unit, width)
    keep = jnp.where(core == 0, pair_grad[:, :, :, 0], pair_grad[:, :, :, 1])
    give = jnp.where(core == 0, pair_grad[:, :, :, 1], pair_grad[:, :, :, 0])
    pair_grad = keep + swap_seq(give.astype(BF16), 1, n_seq).astype(F32)
    if n_parts > 1:
        pair_grad = lax.psum_scatter(
            pair_grad, "seq", scatter_dimension=2, axis_index_groups=part_groups, tiled=True
        )
    pair_grad = pair_grad[:, :, 0]
    keep = jnp.where(dp == 0, pair_grad[:, 0], pair_grad[:, 1])
    give = jnp.where(dp == 0, pair_grad[:, 1], pair_grad[:, 0])
    pair_grad = (keep + swap_dp(give.astype(BF16)).astype(F32)).astype(BF16)
    returned = []
    for chosen in rounds:
        order = sorted((edge[1], edge[3]) for edge in chosen)
        third = jnp.array([t for _, t in order], jnp.int32)[me]
        value = lax.dynamic_index_in_dim(pair_grad, third, 0, keepdims=False)
        returned.append(lax.ppermute(value, BOTH, [(edge[1], edge[0]) for edge in chosen]))
    slots = [jnp.array([edge[2] for edge in chosen], jnp.int32)[me] for chosen in rounds]
    attn_in_grad = jnp.concatenate(
        [
            jnp.where(slots[0] == slot, returned[0], jnp.where(slots[1] == slot, returned[1], returned[2]))
            for slot in range(3)
        ],
        0,
    ).astype(F32)

    gain_term = gain_term + swap_seq(gain_term, 1, n_seq)
    gain_term = gain_term + swap_seq(gain_term, 2, n_seq)
    gain_term = gain_term + swap_dp(gain_term)
    extra = jnp.concatenate([extra, gain_term.reshape(1, width)], 0)
    bits = 4
    while bits < n_seq:
        out_terms, extra = halve_seq(out_terms, extra, bits, n_seq)
        bits *= 2
    attn_out_grad = out_terms.reshape(attn_out.shape)
    losses = extra[1, 0:2] / (width * extra[1, 2])
    gain_grad = jnp.stack([extra[2], extra[0]])

    input_grad = input_gradient(own_grad_mixed, attn_in_full, own_in, grad_middle, gain_one)
    return (
        output,
        losses,
        input_grad.reshape(n_micro, 1, tok_rows, width),
        attn_in_grad,
        attn_out_grad,
        mlp_in_grad,
        mlp_out_grad,
        gain_grad,
    )


def solution(mesh):
    n_dp, n_seq = mesh.shape["dp"], mesh.shape["seq"]
    placed = (
        P(None, "dp", "seq", None),
        P(None, "dp", "seq", None),
        P(None, "dp", "seq"),
        P(None, "dp"),
        P(BOTH, None),
        P(BOTH, None),
        P(BOTH, None),
        P(BOTH, None),
        P(),
    )
    return jax.shard_map(
        functools.partial(shards, n_dp, n_seq),
        mesh=mesh,
        in_specs=placed,
        out_specs=(
            P(None, "dp", "seq", None),
            P(),
            P(None, "dp", "seq", None),
            P(BOTH, None),
            P(BOTH, None),
            P(BOTH, None),
            P(BOTH, None),
            P(),
        ),
        check_vma=False,
    )
```

time: 446 us -> 373 us (0.84)
  the two profiles are of different devices: /device:TPU:2 before, /device:TPU:0 now
where the time goes in v2:
time: 373 us; the launch traced here: 366 us
  waiting for transfers between devices  129 us (35%)
  starting transfers between devices  80.9 us (22%)
  other arithmetic  31.9 us (9%)
  local copies, waits for them, and re-layouts  27.6 us (7%)
  between operations  27.3 us (7%)
  blocking collectives  26.1 us (7%)
  matrix products  21.4 us (6%)
  Pallas kernels  21 us (6%)
    ppermute x45, waiting for transfers between devices, swap_seq(): return lax.ppermute(value, 'seq', [(i, i ^ bits) for i in range(n_seq)])  96.1 us
    ppermute x45, starting transfers between devices, swap_seq(): return lax.ppermute(value, 'seq', [(i, i ^ bits) for i in range(n_seq)])  41.2 us
    ppermute x8, waiting for transfers between devices, swap_dp(): return lax.ppermute(value, 'dp', [(0, 1), (1, 0)])  27.4 us
    all_to_all x1, blocking collectives, exchange(): return lax.all_to_all(by_device, 'seq', 0, 0, axis_index_groups=in_groups)  26.1 us
    ppermute x3, starting transfers between devices, shards(): lax.ppermute(value, BOTH, [(edge[0], edge[1]) for edge in chosen])  12.7 us
    unnamed x140, local copies, waits for them, and re-layouts  10.6 us
    ppermute x8, starting transfers between devices, swap_dp(): return lax.ppermute(value, 'dp', [(0, 1), (1, 0)])  10.5 us
    all_to_all x2, starting transfers between devices, exchange(): return lax.all_to_all(by_device, 'seq', 0, 0, axis_index_groups=in_groups)  9.59 us
  transfers between devices with their start and end apart: 65, of which 32 were waited for; matrix products, arithmetic and copies ran while one was open for 16% of the time, Pallas kernels for 5%

profile of v2, /device:TPU:0, one launch (start us, length us, event | category | flops | bytes accessed | tf_op | source)
XLA Modules:
  0.0 365.5 jit_solution(6037075678239161614)
XLA Ops:
  9.5 1.6 collective-permute-start.4
  12.7 6.6 %collective-permute-start.2 = (bf16[32,1024]{1,0:T(8,128)(2,1)S(1)}, bf16[32,1024]{1,0:T(8,128)(2,1)S(1)}, u32[]{:S(2)}, u32[]{:S(2)}) collective-permute-start(bf16[32,1024]{1,0:T(8,128)(2,1)S(1)} %get-tuple-element.187), channel_id=1, source_target_pairs={{0,1},{1,2},{2,19},{3,20},{4,7},{5,8},{6,25},{7,26},{8,13},{9,14},... | collective-permute-start | bytes 196616 | tf_op jit(solution)/shard_map/ppermute | solution.py:376
  19.3 5.5 %collective-permute-start.3 = (bf16[32,1024]{1,0:T(8,128)(2,1)S(1)}, bf16[32,1024]{1,0:T(8,128)(2,1)S(1)}, u32[]{:S(2)}, u32[]{:S(2)}) collective-permute-start(bf16[32,1024]{1,0:T(8,128)(2,1)S(1)} %get-tuple-element.186), channel_id=1, source_target_pairs={{0,16},{1,3},{2,4},{3,21},{4,22},{5,9},{6,10},{7,27},{8,28},{9,15}... | collective-permute-start | bytes 196616 | tf_op jit(solution)/shard_map/ppermute | solution.py:376
  31.2 5.0 %collective-permute-done.3 = bf16[32,1024]{1,0:T(8,128)(2,1)S(1)} collective-permute-done((bf16[32,1024]{1,0:T(8,128)(2,1)S(1)}, bf16[32,1024]{1,0:T(8,128)(2,1)S(1)}, u32[]{:S(2)}, u32[]{:S(2)}) %collective-permute-start.3) | collective-permute-done | bytes 65568 | tf_op jit(solution)/shard_map/ppermute | solution.py:376
  36.5 5.5 %collective-permute-start.7 = (bf16[128,1024]{1,0:T(8,128)(2,1)S(1)}, bf16[128,1024]{1,0:T(8,128)(2,1)S(1)}, u32[]{:S(2)}, u32[]{:S(2)}) collective-permute-start(bf16[128,1024]{1,0:T(8,128)(2,1)S(1)} %maximum_select_fusion.3.refs_0_), channel_id=1, source_target_pairs={{0,2},{1,3},{2,0},{3,1},{4,6},{5,7},{6,4},{7,5},{8,10},{9,11},{10,... | collective-permute-start | bytes 786440 | tf_op jit(solution)/shard_map/ppermute | solution.py:43
  42.1 5.2 %collective-permute-done.5.refs_2_ = bf16[128,1024]{1,0:T(8,128)(2,1)S(1)} collective-permute-done((bf16[128,1024]{1,0:T(8,128)(2,1)S(1)}, bf16[128,1024]{1,0:T(8,128)(2,1)S(1)}, u32[]{:S(2)}, u32[]{:S(2)}) %collective-permute-start.5) | collective-permute-done | bytes 262176 | tf_op jit(solution)/shard_map/ppermute | solution.py:43
  47.3 6.6 %collective-permute-done.6.refs_4_ = bf16[128,1024]{1,0:T(8,128)(2,1)S(1)} collective-permute-done((bf16[128,1024]{1,0:T(8,128)(2,1)S(1)}, bf16[128,1024]{1,0:T(8,128)(2,1)S(1)}, u32[]{:S(2)}, u32[]{:S(2)}) %collective-permute-start.6) | collective-permute-done | bytes 262176 | tf_op jit(solution)/shard_map/ppermute | solution.py:43
  53.9 3.0 collective-permute-start.12
  56.9 1.9 collective-permute-start.10
  60.8 5.0 %collective-permute-done.9.refs_6_ = bf16[128,1024]{1,0:T(8,128)(2,1)S(1)} collective-permute-done((bf16[128,1024]{1,0:T(8,128)(2,1)S(1)}, bf16[128,1024]{1,0:T(8,128)(2,1)S(1)}, u32[]{:S(2)}, u32[]{:S(2)}) %collective-permute-start.9) | collective-permute-done | bytes 262176 | tf_op jit(solution)/shard_map/ppermute | solution.py:43
  65.8 3.5 collective-permute-done.10.refs_3_
  69.3 4.2 %collective-permute-done.11.refs_5_ = bf16[128,1024]{1,0:T(8,128)(2,1)S(1)} collective-permute-done((bf16[128,1024]{1,0:T(8,128)(2,1)S(1)}, bf16[128,1024]{1,0:T(8,128)(2,1)S(1)}, u32[]{:S(2)}, u32[]{:S(2)}) %collective-permute-start.11) | collective-permute-done | bytes 262176 | tf_op jit(solution)/shard_map/ppermute | solution.py:43
  73.6 1.7 collective-permute-start.13
  76.8 3.2 collective-permute-done.13.refs_7_
  80.1 2.8 collective-permute-start.22
  84.0 9.1 %shard_map.242 = (bf16[1024,1024]{1,0:T(8,128)(2,1)}, bf16[1024,384]{1,0:T(8,128)(2,1)}, bf16[1024,128]{1,0:T(8,128)(2,1)}) custom-call(s32[3]{0:T(128)} %pad_add_fusion.where_ref, bf16[128,1024]{1,0:T(8,128)(2,1)} %copy-done.38, bf16[128,1024]{1,0:T(8,128)(2,1)} %copy-done.54, bf16[128,1024]{1,0:T(8,128)(2,1)} %copy-done.52, bf16[128,1024]{1,0:T(8,128)(2,1)} %copy-done.56, ...), custom_call_target="tpu_custom_call" | custom-call | flops 1342177280 | bytes 4194304 | tf_op jit(solution)/shard_map/pallas_call | solution.py:205
  93.1 26.1 %all_to_all.15.moved_ref = bf16[16,64,128]{2,1,0:T(8,128)(2,1)S(1)} all-to-all(bf16[16,64,128]{2,1,0:T(8,128)(2,1)} %bitcast.309), channel_id=1, replica_groups=mesh['dp'=2,'seq'=16] {'seq'}, dimensions={0} | all-to-all | bytes 524288 | tf_op jit(solution)/shard_map/all_to_all | solution.py:428
  119.2 1.6 copy-done
  122.7 1.7 collective-permute-start.14
  128.1 2.5 collective-permute-done.15
  133.1 3.1 collective-permute-done.16
  140.1 5.9 %collective-permute-done.24 = bf16[384,1024]{1,0:T(8,128)(2,1)S(1)} collective-permute-done((bf16[384,1024]{1,0:T(8,128)(2,1)}, bf16[384,1024]{1,0:T(8,128)(2,1)S(1)}, u32[]{:S(2)}, u32[]{:S(2)}) %collective-permute-start.24) | collective-permute-done | bytes 786464 | tf_op jit(solution)/shard_map/ppermute | solution.py:47
  146.0 2.9 multiply_convert_fusion
  150.6 2.6 collective-permute-done.25
  156.2 4.3 %collective-permute-done.28 = bf16[64,1024]{1,0:T(8,128)(2,1)S(1)} collective-permute-done((bf16[64,1024]{1,0:T(8,128)(2,1)S(1)}, bf16[64,1024]{1,0:T(8,128)(2,1)S(1)}, u32[]{:S(2)}, u32[]{:S(2)}) %collective-permute-start.28) | collective-permute-done | bytes 131104 | tf_op jit(solution)/shard_map/ppermute | solution.py:43
  163.8 5.2 %collective-permute-done.29 = bf16[128,1024]{1,0:T(8,128)(2,1)} collective-permute-done((bf16[128,1024]{1,0:T(8,128)(2,1)}, bf16[128,1024]{1,0:T(8,128)(2,1)}, u32[]{:S(2)}, u32[]{:S(2)}) %collective-permute-start.29) | collective-permute-done | bytes 262176 | tf_op jit(solution)/shard_map/ppermute | solution.py:43
  170.3 1.7 multiply_reduce_fusion.2
  173.7 4.8 %collective-permute-done.31 = bf16[128,1024]{1,0:T(8,128)(2,1)S(1)} collective-permute-done((bf16[128,1024]{1,0:T(8,128)(2,1)S(1)}, bf16[128,1024]{1,0:T(8,128)(2,1)S(1)}, u32[]{:S(2)}, u32[]{:S(2)}) %collective-permute-start.31) | collective-permute-done | bytes 262176 | tf_op jit(solution)/shard_map/ppermute | solution.py:43
  179.0 2.2 collective-permute-done.30
  183.6 2.7 collective-permute-done.33
  188.0 3.3 select_convert_fusion.1
  194.6 2.0 copy-done.5
  207.1 1.8 fusion.18
  209.9 2.2 convolution_convert_fusion
  212.2 1.6 collective-permute-start.56
  218.0 1.8 collective-permute-start.40
  219.8 2.7 fusion.83
  222.5 2.3 collective-permute-done.42
  225.3 1.5 multiply_reduce_fusion.3
  229.5 5.8 %all-to-all-start.1 = ((bf16[16,64,128]{2,1,0:T(8,128)(2,1)}), bf16[16,64,128]{2,1,0:T(8,128)(2,1)S(1)}, u32[]{:S(2)}, u32[]{:S(2)}) async-start(bf16[16,64,128]{2,1,0:T(8,128)(2,1)} %bitcast.51), calls=%async_computation.1 | async-start | bytes 524288 | tf_op jit(solution)/shard_map/all_to_all | solution.py:428
  239.6 15.0 %collective-permute-done.58 = bf16[2,128,1024]{2,1,0:T(8,128)(2,1)} collective-permute-done((bf16[2,128,1024]{2,1,0:T(8,128)(2,1)}, bf16[2,128,1024]{2,1,0:T(8,128)(2,1)}, u32[]{:S(2)}, u32[]{:S(2)}) %collective-permute-start.58) | collective-permute-done | bytes 524320 | tf_op jit(solution)/shard_map/ppermute | solution.py:47
  254.6 2.3 fusion.4
  257.7 9.4 %shard_map.244 = bf16[1024,384]{1,0:T(8,128)(2,1)} custom-call(s32[3]{0:T(128)} %pad_add_fusion.where_ref, bf16[1024,384]{1,0:T(8,128)(2,1)} %get-tuple-element.114.mixed_ref, bf16[1024,128]{1,0:T(8,128)(2,1)} %bitcast.308), custom_call_target="tpu_custom_call" | custom-call | flops 1342177280 | bytes 4194304 | tf_op jit(solution)/shard_map/pallas_call | solution.py:266
  267.0 2.3 multiply_reduce_fusion
  269.4 1.8 fusion.36
  271.2 5.3 %collective-permute-start.59 = (bf16[1,128,1024]{2,1,0:T(8,128)(2,1)}, bf16[1,128,1024]{2,1,0:T(8,128)(2,1)}, u32[]{:S(2)}, u32[]{:S(2)}) collective-permute-start(bf16[1,128,1024]{2,1,0:T(8,128)(2,1)} %fusion.36), channel_id=1, source_target_pairs={{0,8},{1,9},{2,10},{3,11},{4,12},{5,13},{6,14},{7,15},{8,0},{9,1},... | collective-permute-start | bytes 786440 | tf_op jit(solution)/shard_map/ppermute | solution.py:43
  277.0 3.2 collective-permute-done.47
  280.2 2.3 collective-permute-start.48
  282.5 1.8 slice_select_fusion
  284.3 3.8 %all-to-all-start.2 = ((bf16[16,64,384]{2,1,0:T(8,128)(2,1)}), bf16[16,64,384]{2,1,0:T(8,128)(2,1)S(1)}, u32[]{:S(2)}, u32[]{:S(2)}) async-start(bf16[16,64,384]{2,1,0:T(8,128)(2,1)} %bitcast.297), calls=%async_computation.2 | async-start | bytes 1572864 | tf_op jit(solution)/shard_map/all_to_all | solution.py:428
  288.9 2.2 add_bitcast_fusion
  294.0 1.6 slice.457
  296.6 2.0 collective-permute-start.44
  299.2 2.1 collective-permute-start.57
  301.3 4.1 %collective-permute-done.52 = bf16[3,32,1024]{2,1,0:T(8,128)(2,1)S(1)} collective-permute-done((bf16[3,32,1024]{2,1,0:T(8,128)(2,1)S(1)}, bf16[3,32,1024]{2,1,0:T(8,128)(2,1)S(1)}, u32[]{:S(2)}, u32[]{:S(2)}) %collective-permute-start.52) | collective-permute-done | bytes 196640 | tf_op jit(solution)/shard_map/ppermute | solution.py:47
  305.5 8.3 %collective-permute-done.44 = bf16[260,1024]{1,0:T(8,128)(2,1)S(1)} collective-permute-done((bf16[260,1024]{1,0:T(8,128)(2,1)S(1)}, bf16[260,1024]{1,0:T(8,128)(2,1)S(1)}, u32[]{:S(2)}, u32[]{:S(2)}) %collective-permute-start.44) | collective-permute-done | bytes 532512 | tf_op jit(solution)/shard_map/ppermute | solution.py:43
  315.7 3.9 %collective-permute-start.55 = (bf16[32,1024]{1,0:T(8,128)(2,1)S(1)}, bf16[32,1024]{1,0:T(8,128)(2,1)S(1)}, u32[]{:S(2)}, u32[]{:S(2)}) collective-permute-start(bf16[32,1024]{1,0:T(8,128)(2,1)S(1)} %get-tuple-element.179), channel_id=1, source_target_pairs={{16,0},{3,1},{4,2},{21,3},{22,4},{9,5},{10,6},{27,7},{28,8},{15,9}... | collective-permute-start | bytes 196616 | tf_op jit(solution)/shard_map/ppermute | solution.py:539
  320.4 2.5 collective-permute-done.45
  323.2 2.1 collective-permute-start.49
  327.8 5.5 %collective-permute-done.57 = bf16[1,256,1024]{2,1,0:T(8,128)(2,1)S(1)} collective-permute-done((bf16[1,256,1024]{2,1,0:T(8,128)(2,1)S(1)}, bf16[1,256,1024]{2,1,0:T(8,128)(2,1)S(1)}, u32[]{:S(2)}, u32[]{:S(2)}) %collective-permute-start.57) | collective-permute-done | bytes 524320 | tf_op jit(solution)/shard_map/ppermute | solution.py:43
  333.4 10.6 %collective-permute-done.49 = bf16[70,1024]{1,0:T(8,128)(2,1)S(1)} collective-permute-done((bf16[70,1024]{1,0:T(8,128)(2,1)S(1)}, bf16[70,1024]{1,0:T(8,128)(2,1)S(1)}, u32[]{:S(2)}, u32[]{:S(2)}) %collective-permute-start.49) | collective-permute-done | bytes 143392 | tf_op jit(solution)/shard_map/ppermute | solution.py:43
  346.2 4.4 %collective-permute-done.50 = bf16[38,1024]{1,0:T(8,128)(2,1)S(1)} collective-permute-done((bf16[38,1024]{1,0:T(8,128)(2,1)S(1)}, bf16[38,1024]{1,0:T(8,128)(2,1)S(1)}, u32[]{:S(2)}, u32[]{:S(2)}) %collective-permute-start.50) | collective-permute-done | bytes 77856 | tf_op jit(solution)/shard_map/ppermute | solution.py:43
  353.7 2.8 copy-done.4
  356.5 2.0 shard_map.245
  (351 shorter events, 74.2 us)
Async XLA Ops:
  7.2 112.0 %all-gather.3.cloned.1.call-start = ((), (), s32[]{:S(2)}) async-start(), calls=%async_computation.3 | async-start | bytes 2162688 | tf_op jit(solution)/shard_map/all_gather | solution.py:382
  7.9 345.8 %all-gather.5.cloned.1.call-start = ((), (), s32[]{:S(2)}) async-start(), calls=%async_computation.4 | async-start | bytes 6488064 | tf_op jit(solution)/shard_map/all_gather | solution.py:383
  9.0 22.1 %collective-permute-start = (bf16[64,1024]{1,0:T(8,128)(2,1)S(1)}, bf16[64,1024]{1,0:T(8,128)(2,1)S(1)}, u32[]{:S(2)}, u32[]{:S(2)}) collective-permute-start(bf16[64,1024]{1,0:T(8,128)(2,1)S(1)} %get-tuple-element.177), channel_id=1, source_target_pairs={{0,1},{1,0},{2,3},{3,2},{4,5},{5,4},{6,7},{7,6},{8,9},{9,8},{10,11... | collective-permute-start | bytes 393224 | tf_op jit(solution)/shard_map/ppermute | solution.py:43
  9.5 26.7 %collective-permute-start.4 = (bf16[128,1024]{1,0:T(8,128)(2,1)}, bf16[128,1024]{1,0:T(8,128)(2,1)S(1)}, u32[]{:S(2)}, u32[]{:S(2)}) collective-permute-start(bf16[128,1024]{1,0:T(8,128)(2,1)} %param.30), channel_id=1, source_target_pairs={{0,0},{1,16},{2,1},{3,17},{4,2},{5,18},{6,3},{7,19},{8,4},{9,20},{... | collective-permute-start | bytes 786440 | tf_op jit(solution)/shard_map/ppermute | solution.py:385
  12.0 19.2 %collective-permute-start.1 = (bf16[32,1024]{1,0:T(8,128)(2,1)S(1)}, bf16[32,1024]{1,0:T(8,128)(2,1)S(1)}, u32[]{:S(2)}, u32[]{:S(2)}) collective-permute-start(bf16[32,1024]{1,0:T(8,128)(2,1)S(1)} %get-tuple-element.188), channel_id=1, source_target_pairs={{0,0},{1,17},{2,18},{3,5},{4,6},{5,23},{6,24},{7,11},{8,12},{9,29}... | collective-permute-start | bytes 196616 | tf_op jit(solution)/shard_map/ppermute | solution.py:376
  12.7 18.5 %collective-permute-start.2 = (bf16[32,1024]{1,0:T(8,128)(2,1)S(1)}, bf16[32,1024]{1,0:T(8,128)(2,1)S(1)}, u32[]{:S(2)}, u32[]{:S(2)}) collective-permute-start(bf16[32,1024]{1,0:T(8,128)(2,1)S(1)} %get-tuple-element.187), channel_id=1, source_target_pairs={{0,1},{1,2},{2,19},{3,20},{4,7},{5,8},{6,25},{7,26},{8,13},{9,14},... | collective-permute-start | bytes 196616 | tf_op jit(solution)/shard_map/ppermute | solution.py:376
  19.3 16.9 %collective-permute-start.3 = (bf16[32,1024]{1,0:T(8,128)(2,1)S(1)}, bf16[32,1024]{1,0:T(8,128)(2,1)S(1)}, u32[]{:S(2)}, u32[]{:S(2)}) collective-permute-start(bf16[32,1024]{1,0:T(8,128)(2,1)S(1)} %get-tuple-element.186), channel_id=1, source_target_pairs={{0,16},{1,3},{2,4},{3,21},{4,22},{5,9},{6,10},{7,27},{8,28},{9,15}... | collective-permute-start | bytes 196616 | tf_op jit(solution)/shard_map/ppermute | solution.py:376
  36.2 5.8 %collective-permute-start.8 = (bf16[3,32,1024]{2,1,0:T(8,128)(2,1)S(1)}, bf16[3,32,1024]{2,1,0:T(8,128)(2,1)S(1)}, u32[]{:S(2)}, u32[]{:S(2)}) collective-permute-start(bf16[3,32,1024]{2,1,0:T(8,128)(2,1)S(1)} %get-tuple-element.182), channel_id=1, source_target_pairs={{0,1},{1,0},{2,3},{3,2},{4,5},{5,4},{6,7},{7,6},{8,9},{9,8},{10,11... | collective-permute-start | bytes 589832 | tf_op jit(solution)/shard_map/ppermute | solution.py:43
  36.4 10.9 %collective-permute-start.5 = (bf16[128,1024]{1,0:T(8,128)(2,1)S(1)}, bf16[128,1024]{1,0:T(8,128)(2,1)S(1)}, u32[]{:S(2)}, u32[]{:S(2)}) collective-permute-start(bf16[128,1024]{1,0:T(8,128)(2,1)S(1)} %maximum_select_fusion.3.refs_0_), channel_id=1, source_target_pairs={{0,4},{1,5},{2,6},{3,7},{4,0},{5,1},{6,2},{7,3},{8,12},{9,13},{10,... | collective-permute-start | bytes 786440 | tf_op jit(solution)/shard_map/ppermute | solution.py:43
  36.4 17.4 %collective-permute-start.6 = (bf16[128,1024]{1,0:T(8,128)(2,1)S(1)}, bf16[128,1024]{1,0:T(8,128)(2,1)S(1)}, u32[]{:S(2)}, u32[]{:S(2)}) collective-permute-start(bf16[128,1024]{1,0:T(8,128)(2,1)S(1)} %maximum_select_fusion.3.refs_0_), channel_id=1, source_target_pairs={{0,8},{1,9},{2,10},{3,11},{4,12},{5,13},{6,14},{7,15},{8,0},{9,1},... | collective-permute-start | bytes 786440 | tf_op jit(solution)/shard_map/ppermute | solution.py:43
  36.5 17.4 %collective-permute-start.7 = (bf16[128,1024]{1,0:T(8,128)(2,1)S(1)}, bf16[128,1024]{1,0:T(8,128)(2,1)S(1)}, u32[]{:S(2)}, u32[]{:S(2)}) collective-permute-start(bf16[128,1024]{1,0:T(8,128)(2,1)S(1)} %maximum_select_fusion.3.refs_0_), channel_id=1, source_target_pairs={{0,2},{1,3},{2,0},{3,1},{4,6},{5,7},{6,4},{7,5},{8,10},{9,11},{10,... | collective-permute-start | bytes 786440 | tf_op jit(solution)/shard_map/ppermute | solution.py:43
  53.9 19.7 %collective-permute-start.12 = (bf16[3,2,32,1024]{3,2,0,1:T(8,128)(2,1)S(1)}, bf16[3,2,32,1024]{3,2,0,1:T(8,128)(2,1)S(1)}, u32[]{:S(2)}, u32[]{:S(2)}) collective-permute-start(bf16[3,2,32,1024]{3,2,0,1:T(8,128)(2,1)S(1)} %maximum_select_fusion.2), channel_id=1, source_target_pairs={{0,16},{16,0},{1,17},{17,1},{2,18},{18,2},{3,19},{19,3},{4,20},{20... | collective-permute-start | bytes 1179656 | tf_op jit(solution)/shard_map/ppermute | solution.py:47
  56.9 8.9 %collective-permute-start.9 = (bf16[128,1024]{1,0:T(8,128)(2,1)S(1)}, bf16[128,1024]{1,0:T(8,128)(2,1)S(1)}, u32[]{:S(2)}, u32[]{:S(2)}) collective-permute-start(bf16[128,1024]{1,0:T(8,128)(2,1)S(1)} %collective-permute-done.6.refs_4_), channel_id=1, source_target_pairs={{0,4},{1,5},{2,6},{3,7},{4,0},{5,1},{6,2},{7,3},{8,12},{9,13},{10,... | collective-permute-start | bytes 786440 | tf_op jit(solution)/shard_map/ppermute | solution.py:43
  56.9 12.4 %collective-permute-start.10 = (bf16[128,1024]{1,0:T(8,128)(2,1)S(1)}, bf16[128,1024]{1,0:T(8,128)(2,1)S(1)}, u32[]{:S(2)}, u32[]{:S(2)}) collective-permute-start(bf16[128,1024]{1,0:T(8,128)(2,1)S(1)} %collective-permute-done.5.refs_2_), channel_id=1, source_target_pairs={{0,2},{1,3},{2,0},{3,1},{4,6},{5,7},{6,4},{7,5},{8,10},{9,11},{10,... | collective-permute-start | bytes 786440 | tf_op jit(solution)/shard_map/ppermute | solution.py:43
  58.9 14.7 %collective-permute-start.11 = (bf16[128,1024]{1,0:T(8,128)(2,1)S(1)}, bf16[128,1024]{1,0:T(8,128)(2,1)S(1)}, u32[]{:S(2)}, u32[]{:S(2)}) collective-permute-start(bf16[128,1024]{1,0:T(8,128)(2,1)S(1)} %collective-permute-done.6.refs_4_), channel_id=1, source_target_pairs={{0,2},{1,3},{2,0},{3,1},{4,6},{5,7},{6,4},{7,5},{8,10},{9,11},{10,... | collective-permute-start | bytes 786440 | tf_op jit(solution)/shard_map/ppermute | solution.py:43
  73.6 6.5 %collective-permute-start.13 = (bf16[128,1024]{1,0:T(8,128)(2,1)S(1)}, bf16[128,1024]{1,0:T(8,128)(2,1)}, u32[]{:S(2)}, u32[]{:S(2)}) collective-permute-start(bf16[128,1024]{1,0:T(8,128)(2,1)S(1)} %collective-permute-done.9.refs_6_), channel_id=1, source_target_pairs={{0,2},{1,3},{2,0},{3,1},{4,6},{5,7},{6,4},{7,5},{8,10},{9,11},{10,... | collective-permute-start | bytes 786440 | tf_op jit(solution)/shard_map/ppermute | solution.py:43
  76.5 47.9 %collective-permute-start.23 = (bf16[384,1024]{1,0:T(8,128)(2,1)S(1)}, bf16[384,1024]{1,0:T(8,128)(2,1)S(1)}, u32[]{:S(2)}, u32[]{:S(2)}) collective-permute-start(bf16[384,1024]{1,0:T(8,128)(2,1)S(1)} %pad_maximum_fusion.3), channel_id=1, source_target_pairs={{0,16},{16,0},{1,17},{17,1},{2,18},{18,2},{3,19},{19,3},{4,20},{20... | collective-permute-start | bytes 2359304 | tf_op jit(solution)/shard_map/ppermute | solution.py:47
  80.1 44.5 %collective-permute-start.22 = (bf16[384,1024]{1,0:T(8,128)(2,1)S(1)}, bf16[384,1024]{1,0:T(8,128)(2,1)}, u32[]{:S(2)}, u32[]{:S(2)}) collective-permute-start(bf16[384,1024]{1,0:T(8,128)(2,1)S(1)} %pad_maximum_fusion.3), channel_id=1, source_target_pairs={{0,8},{1,9},{2,10},{3,11},{4,12},{5,13},{6,14},{7,15},{8,0},{9,1},... | collective-permute-start | bytes 2359304 | tf_op jit(solution)/shard_map/ppermute | solution.py:43
  121.4 9.2 %collective-permute-start.15 = (bf16[128,1024]{1,0:T(8,128)(2,1)S(1)}, bf16[128,1024]{1,0:T(8,128)(2,1)S(1)}, u32[]{:S(2)}, u32[]{:S(2)}) collective-permute-start(bf16[128,1024]{1,0:T(8,128)(2,1)S(1)} %get-tuple-element.109), channel_id=1, source_target_pairs={{0,4},{1,5},{2,6},{3,7},{4,0},{5,1},{6,2},{7,3},{8,12},{9,13},{10,... | collective-permute-start | bytes 786440 | tf_op jit(solution)/shard_map/ppermute | solution.py:43
  122.7 9.4 %collective-permute-start.14 = (bf16[128,1024]{1,0:T(8,128)(2,1)S(1)}, bf16[128,1024]{1,0:T(8,128)(2,1)S(1)}, u32[]{:S(2)}, u32[]{:S(2)}) collective-permute-start(bf16[128,1024]{1,0:T(8,128)(2,1)S(1)} %get-tuple-element.109), channel_id=1, source_target_pairs={{0,2},{1,3},{2,0},{3,1},{4,6},{5,7},{6,4},{7,5},{8,10},{9,11},{10,... | collective-permute-start | bytes 786440 | tf_op jit(solution)/shard_map/ppermute | solution.py:43
  124.5 12.7 %collective-permute-start.18 = (bf16[128,1024]{1,0:T(8,128)(2,1)S(1)}, bf16[128,1024]{1,0:T(8,128)(2,1)S(1)}, u32[]{:S(2)}, u32[]{:S(2)}) collective-permute-start(bf16[128,1024]{1,0:T(8,128)(2,1)S(1)} %get-tuple-element.109), channel_id=1, source_target_pairs={{0,1},{1,0},{2,3},{3,2},{4,5},{5,4},{6,7},{7,6},{8,9},{9,8},{10,11... | collective-permute-start | bytes 786440 | tf_op jit(solution)/shard_map/ppermute | solution.py:43
  125.9 20.1 %collective-permute-start.24 = (bf16[384,1024]{1,0:T(8,128)(2,1)}, bf16[384,1024]{1,0:T(8,128)(2,1)S(1)}, u32[]{:S(2)}, u32[]{:S(2)}) collective-permute-start(bf16[384,1024]{1,0:T(8,128)(2,1)} %collective-permute-done.22), channel_id=1, source_target_pairs={{0,16},{16,0},{1,17},{17,1},{2,18},{18,2},{3,19},{19,3},{4,20},{20... | collective-permute-start | bytes 2359304 | tf_op jit(solution)/shard_map/ppermute | solution.py:47
  130.6 5.6 %collective-permute-start.16 = (bf16[64,1024]{1,0:T(8,128)(2,1)S(1)}, bf16[64,1024]{1,0:T(8,128)(2,1)S(1)}, u32[]{:S(2)}, u32[]{:S(2)}) collective-permute-start(bf16[64,1024]{1,0:T(8,128)(2,1)S(1)} %slice.415), channel_id=1, source_target_pairs={{0,2},{1,3},{2,0},{3,1},{4,6},{5,7},{6,4},{7,5},{8,10},{9,11},{10,... | collective-permute-start | bytes 393224 | tf_op jit(solution)/shard_map/ppermute | solution.py:43
  132.1 5.0 %collective-permute-start.17 = (bf16[64,1024]{1,0:T(8,128)(2,1)S(1)}, bf16[64,1024]{1,0:T(8,128)(2,1)S(1)}, u32[]{:S(2)}, u32[]{:S(2)}) collective-permute-start(bf16[64,1024]{1,0:T(8,128)(2,1)S(1)} %slice.416), channel_id=1, source_target_pairs={{0,4},{1,5},{2,6},{3,7},{4,0},{5,1},{6,2},{7,3},{8,12},{9,13},{10,... | collective-permute-start | bytes 393224 | tf_op jit(solution)/shard_map/ppermute | solution.py:43
  133.0 4.2 %collective-permute-start.19 = (bf16[128,1024]{1,0:T(8,128)(2,1)S(1)}, bf16[128,1024]{1,0:T(8,128)(2,1)S(1)}, u32[]{:S(2)}, u32[]{:S(2)}) collective-permute-start(bf16[128,1024]{1,0:T(8,128)(2,1)S(1)} %collective-permute-done.14), channel_id=1, source_target_pairs={{0,1},{1,0},{2,3},{3,2},{4,5},{5,4},{6,7},{7,6},{8,9},{9,8},{10,11... | collective-permute-start | bytes 786440 | tf_op jit(solution)/shard_map/ppermute | solution.py:43
  137.1 1.6 collective-permute-start.21
  150.5 2.7 collective-permute-start.25
  154.8 5.6 %collective-permute-start.28 = (bf16[64,1024]{1,0:T(8,128)(2,1)S(1)}, bf16[64,1024]{1,0:T(8,128)(2,1)S(1)}, u32[]{:S(2)}, u32[]{:S(2)}) collective-permute-start(bf16[64,1024]{1,0:T(8,128)(2,1)S(1)} %get-tuple-element.175), channel_id=1, source_target_pairs={{0,2},{1,3},{2,0},{3,1},{4,6},{5,7},{6,4},{7,5},{8,10},{9,11},{10,... | collective-permute-start | bytes 393224 | tf_op jit(solution)/shard_map/ppermute | solution.py:43
  155.2 6.7 %collective-permute-start.26 = (bf16[64,1024]{1,0:T(8,128)(2,1)S(1)}, bf16[64,1024]{1,0:T(8,128)(2,1)S(1)}, u32[]{:S(2)}, u32[]{:S(2)}) collective-permute-start(bf16[64,1024]{1,0:T(8,128)(2,1)S(1)} %get-tuple-element.174), channel_id=1, source_target_pairs={{0,4},{1,5},{2,6},{3,7},{4,0},{5,1},{6,2},{7,3},{8,12},{9,13},{10,... | collective-permute-start | bytes 393224 | tf_op jit(solution)/shard_map/ppermute | solution.py:43
  161.2 7.8 %collective-permute-start.29 = (bf16[128,1024]{1,0:T(8,128)(2,1)}, bf16[128,1024]{1,0:T(8,128)(2,1)}, u32[]{:S(2)}, u32[]{:S(2)}) collective-permute-start(bf16[128,1024]{1,0:T(8,128)(2,1)} %pad_maximum_fusion.12), channel_id=1, source_target_pairs={{0,4},{1,5},{2,6},{3,7},{4,0},{5,1},{6,2},{7,3},{8,12},{9,13},{10,... | collective-permute-start | bytes 786440 | tf_op jit(solution)/shard_map/ppermute | solution.py:43
  162.7 7.6 %collective-permute-start.27 = (bf16[128,1024]{1,0:T(8,128)(2,1)}, bf16[128,1024]{1,0:T(8,128)(2,1)}, u32[]{:S(2)}, u32[]{:S(2)}) collective-permute-start(bf16[128,1024]{1,0:T(8,128)(2,1)} %pad_maximum_fusion.11), channel_id=1, source_target_pairs={{0,2},{1,3},{2,0},{3,1},{4,6},{5,7},{6,4},{7,5},{8,10},{9,11},{10,... | collective-permute-start | bytes 786440 | tf_op jit(solution)/shard_map/ppermute | solution.py:43
  172.1 6.4 %collective-permute-start.31 = (bf16[128,1024]{1,0:T(8,128)(2,1)S(1)}, bf16[128,1024]{1,0:T(8,128)(2,1)S(1)}, u32[]{:S(2)}, u32[]{:S(2)}) collective-permute-start(bf16[128,1024]{1,0:T(8,128)(2,1)S(1)} %get-tuple-element.198), channel_id=1, source_target_pairs={{0,4},{1,5},{2,6},{3,7},{4,0},{5,1},{6,2},{7,3},{8,12},{9,13},{10,... | collective-permute-start | bytes 786440 | tf_op jit(solution)/shard_map/ppermute | solution.py:43
  173.4 7.8 %collective-permute-start.30 = (bf16[128,1024]{1,0:T(8,128)(2,1)S(1)}, bf16[128,1024]{1,0:T(8,128)(2,1)S(1)}, u32[]{:S(2)}, u32[]{:S(2)}) collective-permute-start(bf16[128,1024]{1,0:T(8,128)(2,1)S(1)} %get-tuple-element.198), channel_id=1, source_target_pairs={{0,2},{1,3},{2,0},{3,1},{4,6},{5,7},{6,4},{7,5},{8,10},{9,11},{10,... | collective-permute-start | bytes 786440 | tf_op jit(solution)/shard_map/ppermute | solution.py:43
  173.7 12.6 %collective-permute-start.34 = (bf16[128,1024]{1,0:T(8,128)(2,1)S(1)}, bf16[128,1024]{1,0:T(8,128)(2,1)S(1)}, u32[]{:S(2)}, u32[]{:S(2)}) collective-permute-start(bf16[128,1024]{1,0:T(8,128)(2,1)S(1)} %get-tuple-element.198), channel_id=1, source_target_pairs={{0,1},{1,0},{2,3},{3,2},{4,5},{5,4},{6,7},{7,6},{8,9},{9,8},{10,11... | collective-permute-start | bytes 786440 | tf_op jit(solution)/shard_map/ppermute | solution.py:43
  178.5 5.0 %collective-permute-start.32 = (bf16[64,1024]{1,0:T(8,128)(2,1)S(1)}, bf16[64,1024]{1,0:T(8,128)(2,1)S(1)}, u32[]{:S(2)}, u32[]{:S(2)}) collective-permute-start(bf16[64,1024]{1,0:T(8,128)(2,1)S(1)} %slice.436), channel_id=1, source_target_pairs={{0,2},{1,3},{2,0},{3,1},{4,6},{5,7},{6,4},{7,5},{8,10},{9,11},{10,... | collective-permute-start | bytes 393224 | tf_op jit(solution)/shard_map/ppermute | solution.py:43
  181.2 5.0 %collective-permute-start.33 = (bf16[64,1024]{1,0:T(8,128)(2,1)S(1)}, bf16[64,1024]{1,0:T(8,128)(2,1)S(1)}, u32[]{:S(2)}, u32[]{:S(2)}) collective-permute-start(bf16[64,1024]{1,0:T(8,128)(2,1)S(1)} %slice.437), channel_id=1, source_target_pairs={{0,4},{1,5},{2,6},{3,7},{4,0},{5,1},{6,2},{7,3},{8,12},{9,13},{10,... | collective-permute-start | bytes 393224 | tf_op jit(solution)/shard_map/ppermute | solution.py:43
  181.7 4.7 %collective-permute-start.35 = (bf16[128,1024]{1,0:T(8,128)(2,1)S(1)}, bf16[128,1024]{1,0:T(8,128)(2,1)S(1)}, u32[]{:S(2)}, u32[]{:S(2)}) collective-permute-start(bf16[128,1024]{1,0:T(8,128)(2,1)S(1)} %collective-permute-done.30), channel_id=1, source_target_pairs={{0,1},{1,0},{2,3},{3,2},{4,5},{5,4},{6,7},{7,6},{8,9},{9,8},{10,11... | collective-permute-start | bytes 786440 | tf_op jit(solution)/shard_map/ppermute | solution.py:43
  181.7 4.8 %collective-permute-start.36 = (bf16[128,1024]{1,0:T(8,128)(2,1)S(1)}, bf16[128,1024]{1,0:T(8,128)(2,1)S(1)}, u32[]{:S(2)}, u32[]{:S(2)}) collective-permute-start(bf16[128,1024]{1,0:T(8,128)(2,1)S(1)} %collective-permute-done.31), channel_id=1, source_target_pairs={{0,1},{1,0},{2,3},{3,2},{4,5},{5,4},{6,7},{7,6},{8,9},{9,8},{10,11... | collective-permute-start | bytes 786440 | tf_op jit(solution)/shard_map/ppermute | solution.py:43
  186.3 1.6 collective-permute-start.37
  197.7 7.9 %collective-permute-start.38 = (bf16[4,128,1024]{2,1,0:T(8,128)(2,1)}, bf16[4,128,1024]{2,1,0:T(8,128)(2,1)}, u32[]{:S(2)}, u32[]{:S(2)}) collective-permute-start(bf16[4,128,1024]{2,1,0:T(8,128)(2,1)} %bitcast.31), channel_id=1, source_target_pairs={{0,1},{1,0},{2,3},{3,2},{4,5},{5,4},{6,7},{7,6},{8,9},{9,8},{10,11... | collective-permute-start | bytes 3145736 | tf_op jit(solution)/shard_map/ppermute | solution.py:43
  208.9 7.5 %collective-permute-start.41 = (bf16[64,1024]{1,0:T(8,128)(2,1)S(1)}, bf16[64,1024]{1,0:T(8,128)(2,1)S(1)}, u32[]{:S(2)}, u32[]{:S(2)}) collective-permute-start(bf16[64,1024]{1,0:T(8,128)(2,1)S(1)} %get-tuple-element.173), channel_id=1, source_target_pairs={{0,2},{1,3},{2,0},{3,1},{4,6},{5,7},{6,4},{7,5},{8,10},{9,11},{10,... | collective-permute-start | bytes 393224 | tf_op jit(solution)/shard_map/ppermute | solution.py:43
  209.3 8.7 %collective-permute-start.39 = (bf16[64,1024]{1,0:T(8,128)(2,1)S(1)}, bf16[64,1024]{1,0:T(8,128)(2,1)S(1)}, u32[]{:S(2)}, u32[]{:S(2)}) collective-permute-start(bf16[64,1024]{1,0:T(8,128)(2,1)S(1)} %get-tuple-element.172), channel_id=1, source_target_pairs={{0,4},{1,5},{2,6},{3,7},{4,0},{5,1},{6,2},{7,3},{8,12},{9,13},{10,... | collective-permute-start | bytes 393224 | tf_op jit(solution)/shard_map/ppermute | solution.py:43
  212.2 76.7 %collective-permute-start.56 = (bf16[2,256,1024]{2,1,0:T(8,128)(2,1)}, bf16[2,256,1024]{2,1,0:T(8,128)(2,1)}, u32[]{:S(2)}, u32[]{:S(2)}) collective-permute-start(bf16[2,256,1024]{2,1,0:T(8,128)(2,1)} %bitcast.89), channel_id=1, source_target_pairs={{0,16},{16,0},{1,17},{17,1},{2,18},{18,2},{3,19},{19,3},{4,20},{20... | collective-permute-start | bytes 3145736 | tf_op jit(solution)/shard_map/ppermute | solution.py:47
  216.0 38.6 %collective-permute-start.58 = (bf16[2,128,1024]{2,1,0:T(8,128)(2,1)}, bf16[2,128,1024]{2,1,0:T(8,128)(2,1)}, u32[]{:S(2)}, u32[]{:S(2)}) collective-permute-start(bf16[2,128,1024]{2,1,0:T(8,128)(2,1)} %fusion.11), channel_id=1, source_target_pairs={{0,16},{16,0},{1,17},{17,1},{2,18},{18,2},{3,19},{19,3},{4,20},{20... | collective-permute-start | bytes 1572872 | tf_op jit(solution)/shard_map/ppermute | solution.py:47
  216.5 8.4 %collective-permute-start.42 = (bf16[128,1024]{1,0:T(8,128)(2,1)S(1)}, bf16[128,1024]{1,0:T(8,128)(2,1)S(1)}, u32[]{:S(2)}, u32[]{:S(2)}) collective-permute-start(bf16[128,1024]{1,0:T(8,128)(2,1)S(1)} %pad_maximum_fusion.15), channel_id=1, source_target_pairs={{0,4},{1,5},{2,6},{3,7},{4,0},{5,1},{6,2},{7,3},{8,12},{9,13},{10,... | collective-permute-start | bytes 786440 | tf_op jit(solution)/shard_map/ppermute | solution.py:43
  218.0 7.3 %collective-permute-start.40 = (bf16[128,1024]{1,0:T(8,128)(2,1)S(1)}, bf16[128,1024]{1,0:T(8,128)(2,1)S(1)}, u32[]{:S(2)}, u32[]{:S(2)}) collective-permute-start(bf16[128,1024]{1,0:T(8,128)(2,1)S(1)} %pad_maximum_fusion.14), channel_id=1, source_target_pairs={{0,2},{1,3},{2,0},{3,1},{4,6},{5,7},{6,4},{7,5},{8,10},{9,11},{10,... | collective-permute-start | bytes 786440 | tf_op jit(solution)/shard_map/ppermute | solution.py:43
  229.5 27.4 %all-to-all-start.1 = ((bf16[16,64,128]{2,1,0:T(8,128)(2,1)}), bf16[16,64,128]{2,1,0:T(8,128)(2,1)S(1)}, u32[]{:S(2)}, u32[]{:S(2)}) async-start(bf16[16,64,128]{2,1,0:T(8,128)(2,1)} %bitcast.51), calls=%async_computation.1 | async-start | bytes 524288 | tf_op jit(solution)/shard_map/all_to_all | solution.py:428
  239.1 53.4 %collective-permute-start.43 = (bf16[516,1024]{1,0:T(8,128)(2,1)}, bf16[516,1024]{1,0:T(8,128)(2,1)}, u32[]{:S(2)}, u32[]{:S(2)}) collective-permute-start(bf16[516,1024]{1,0:T(8,128)(2,1)} %pad_maximum_fusion), channel_id=1, source_target_pairs={{0,1},{1,0},{2,3},{3,2},{4,5},{5,4},{6,7},{7,6},{8,9},{9,8},{10,11... | collective-permute-start | bytes 3170312 | tf_op jit(solution)/shard_map/ppermute | solution.py:43
  269.4 7.2 %collective-permute-start.46 = (f32[8,128]{1,0:T(8,128)S(1)}, f32[8,128]{1,0:T(8,128)S(1)}, u32[]{:S(2)}, u32[]{:S(2)}) collective-permute-start(f32[8,128]{1,0:T(8,128)S(1)} %bitcast_divide_fusion), channel_id=1, source_target_pairs={{0,1},{1,0},{2,3},{3,2},{4,5},{5,4},{6,7},{7,6},{8,9},{9,8},{10,11... | collective-permute-start | bytes 12296 | tf_op jit(solution)/shard_map/ppermute | solution.py:43
  271.2 16.9 %collective-permute-start.59 = (bf16[1,128,1024]{2,1,0:T(8,128)(2,1)}, bf16[1,128,1024]{2,1,0:T(8,128)(2,1)}, u32[]{:S(2)}, u32[]{:S(2)}) collective-permute-start(bf16[1,128,1024]{2,1,0:T(8,128)(2,1)} %fusion.36), channel_id=1, source_target_pairs={{0,8},{1,9},{2,10},{3,11},{4,12},{5,13},{6,14},{7,15},{8,0},{9,1},... | collective-permute-start | bytes 786440 | tf_op jit(solution)/shard_map/ppermute | solution.py:43
  276.6 3.7 %collective-permute-start.47 = (f32[8,128]{1,0:T(8,128)S(1)}, f32[8,128]{1,0:T(8,128)S(1)}, u32[]{:S(2)}, u32[]{:S(2)}) collective-permute-start(f32[8,128]{1,0:T(8,128)S(1)} %fusion.101), channel_id=1, source_target_pairs={{0,2},{1,3},{2,0},{3,1},{4,6},{5,7},{6,4},{7,5},{8,10},{9,11},{10,... | collective-permute-start | bytes 12296 | tf_op jit(solution)/shard_map/ppermute | solution.py:43
  276.7 14.3 %collective-permute-start.51 = (bf16[3,2,1,32,1024]{4,3,1,0,2:T(8,128)(2,1)S(1)}, bf16[3,2,1,32,1024]{4,3,1,0,2:T(8,128)(2,1)}, u32[]{:S(2)}, u32[]{:S(2)}) collective-permute-start(bf16[3,2,1,32,1024]{4,3,1,0,2:T(8,128)(2,1)S(1)} %fusion.31), channel_id=1, source_target_pairs={{0,1},{1,0},{2,3},{3,2},{4,5},{5,4},{6,7},{7,6},{8,9},{9,8},{10,11... | collective-permute-start | bytes 1179656 | tf_op jit(solution)/shard_map/ppermute | solution.py:43
  280.2 7.9 %collective-permute-start.48 = (f32[8,128]{1,0:T(8,128)S(1)}, f32[8,128]{1,0:T(8,128)}, u32[]{:S(2)}, u32[]{:S(2)}) collective-permute-start(f32[8,128]{1,0:T(8,128)S(1)} %add.264), channel_id=1, source_target_pairs={{0,16},{16,0},{1,17},{17,1},{2,18},{18,2},{3,19},{19,3},{4,20},{20... | collective-permute-start | bytes 12296 | tf_op jit(solution)/shard_map/ppermute | solution.py:47
  284.3 49.1 %all-to-all-start.2 = ((bf16[16,64,384]{2,1,0:T(8,128)(2,1)}), bf16[16,64,384]{2,1,0:T(8,128)(2,1)S(1)}, u32[]{:S(2)}, u32[]{:S(2)}) async-start(bf16[16,64,384]{2,1,0:T(8,128)(2,1)} %bitcast.297), calls=%async_computation.2 | async-start | bytes 1572864 | tf_op jit(solution)/shard_map/all_to_all | solution.py:428
  296.6 17.1 %collective-permute-start.44 = (bf16[260,1024]{1,0:T(8,128)(2,1)S(1)}, bf16[260,1024]{1,0:T(8,128)(2,1)S(1)}, u32[]{:S(2)}, u32[]{:S(2)}) collective-permute-start(bf16[260,1024]{1,0:T(8,128)(2,1)S(1)} %pad_maximum_fusion.8), channel_id=1, source_target_pairs={{0,2},{1,3},{2,0},{3,1},{4,6},{5,7},{6,4},{7,5},{8,10},{9,11},{10,... | collective-permute-start | bytes 1597448 | tf_op jit(solution)/shard_map/ppermute | solution.py:43
  298.7 6.7 %collective-permute-start.52 = (bf16[3,32,1024]{2,1,0:T(8,128)(2,1)S(1)}, bf16[3,32,1024]{2,1,0:T(8,128)(2,1)S(1)}, u32[]{:S(2)}, u32[]{:S(2)}) collective-permute-start(bf16[3,32,1024]{2,1,0:T(8,128)(2,1)S(1)} %fusion.41), channel_id=1, source_target_pairs={{0,16},{16,0},{1,17},{17,1},{2,18},{18,2},{3,19},{19,3},{4,20},{20... | collective-permute-start | bytes 589832 | tf_op jit(solution)/shard_map/ppermute | solution.py:47
  299.2 34.2 %collective-permute-start.57 = (bf16[1,256,1024]{2,1,0:T(8,128)(2,1)S(1)}, bf16[1,256,1024]{2,1,0:T(8,128)(2,1)S(1)}, u32[]{:S(2)}, u32[]{:S(2)}) collective-permute-start(bf16[1,256,1024]{2,1,0:T(8,128)(2,1)S(1)} %fusion.12), channel_id=1, source_target_pairs={{0,8},{1,9},{2,10},{3,11},{4,12},{5,13},{6,14},{7,15},{8,0},{9,1},... | collective-permute-start | bytes 1572872 | tf_op jit(solution)/shard_map/ppermute | solution.py:43
  314.5 8.4 %collective-permute-start.45 = (bf16[132,1024]{1,0:T(8,128)(2,1)S(1)}, bf16[132,1024]{1,0:T(8,128)(2,1)S(1)}, u32[]{:S(2)}, u32[]{:S(2)}) collective-permute-start(bf16[132,1024]{1,0:T(8,128)(2,1)S(1)} %pad_maximum_fusion.9), channel_id=1, source_target_pairs={{0,16},{16,0},{1,17},{17,1},{2,18},{18,2},{3,19},{19,3},{4,20},{20... | collective-permute-start | bytes 811016 | tf_op jit(solution)/shard_map/ppermute | solution.py:47
  315.7 10.7 %collective-permute-start.55 = (bf16[32,1024]{1,0:T(8,128)(2,1)S(1)}, bf16[32,1024]{1,0:T(8,128)(2,1)S(1)}, u32[]{:S(2)}, u32[]{:S(2)}) collective-permute-start(bf16[32,1024]{1,0:T(8,128)(2,1)S(1)} %get-tuple-element.179), channel_id=1, source_target_pairs={{16,0},{3,1},{4,2},{21,3},{22,4},{9,5},{10,6},{27,7},{28,8},{15,9}... | collective-permute-start | bytes 196616 | tf_op jit(solution)/shard_map/ppermute | solution.py:539
  319.6 7.4 %collective-permute-start.54 = (bf16[32,1024]{1,0:T(8,128)(2,1)S(1)}, bf16[32,1024]{1,0:T(8,128)(2,1)S(1)}, u32[]{:S(2)}, u32[]{:S(2)}) collective-permute-start(bf16[32,1024]{1,0:T(8,128)(2,1)S(1)} %get-tuple-element.180), channel_id=1, source_target_pairs={{1,0},{2,1},{19,2},{20,3},{7,4},{8,5},{25,6},{26,7},{13,8},{14,9},... | collective-permute-start | bytes 196616 | tf_op jit(solution)/shard_map/ppermute | solution.py:539
  319.7 7.4 %collective-permute-start.53 = (bf16[32,1024]{1,0:T(8,128)(2,1)S(1)}, bf16[32,1024]{1,0:T(8,128)(2,1)S(1)}, u32[]{:S(2)}, u32[]{:S(2)}) collective-permute-start(bf16[32,1024]{1,0:T(8,128)(2,1)S(1)} %get-tuple-element.178), channel_id=1, source_target_pairs={{0,0},{17,1},{18,2},{5,3},{6,4},{23,5},{24,6},{11,7},{12,8},{29,9}... | collective-permute-start | bytes 196616 | tf_op jit(solution)/shard_map/ppermute | solution.py:539
  323.2 20.8 %collective-permute-start.49 = (bf16[70,1024]{1,0:T(8,128)(2,1)S(1)}, bf16[70,1024]{1,0:T(8,128)(2,1)S(1)}, u32[]{:S(2)}, u32[]{:S(2)}) collective-permute-start(bf16[70,1024]{1,0:T(8,128)(2,1)S(1)} %pad_maximum_fusion.17), channel_id=1, source_target_pairs={{0,4},{1,5},{2,6},{3,7},{4,0},{5,1},{6,2},{7,3},{8,12},{9,13},{10,... | collective-permute-start | bytes 430088 | tf_op jit(solution)/shard_map/ppermute | solution.py:43
  326.3 19.0 %collective-permute-start.60 = (bf16[128,1024]{1,0:T(8,128)(2,1)S(1)}, bf16[128,1024]{1,0:T(8,128)(2,1)S(1)}, u32[]{:S(2)}, u32[]{:S(2)}) collective-permute-start(bf16[128,1024]{1,0:T(8,128)(2,1)S(1)} %fusion.35), channel_id=1, source_target_pairs={{0,0},{16,1},{1,2},{17,3},{2,4},{18,5},{3,6},{19,7},{4,8},{20,9},{... | collective-permute-start | bytes 786440 | tf_op jit(solution)/shard_map/ppermute | solution.py:501
  344.1 6.5 %collective-permute-start.50 = (bf16[38,1024]{1,0:T(8,128)(2,1)S(1)}, bf16[38,1024]{1,0:T(8,128)(2,1)S(1)}, u32[]{:S(2)}, u32[]{:S(2)}) collective-permute-start(bf16[38,1024]{1,0:T(8,128)(2,1)S(1)} %pad_maximum_fusion.18), channel_id=1, source_target_pairs={{0,8},{1,9},{2,10},{3,11},{4,12},{5,13},{6,14},{7,15},{8,0},{9,1},... | collective-permute-start | bytes 233480 | tf_op jit(solution)/shard_map/ppermute | solution.py:43
  (63 other events, 683.5 us)
Sparse Core Ops, SparseCore 0:
  10.8 68.3 all-gather.2
  197.9 77.3 all-gather.4

commit v3 on v1

v3 whole, which is shorter than its diff:
```python
import functools

import jax
import jax.numpy as jnp
from jax import lax
from jax.experimental import pallas as pl
from jax.experimental.pallas import tpu as pltpu
from jax.sharding import PartitionSpec as P

HEADS = 16
HEAD_DIM = 64
PAIR_DIM = 2 * HEAD_DIM
EPS = 1e-05
NEG = -1e30
F32 = jnp.float32
BF16 = jnp.bfloat16
BOTH = ("dp", "seq")
BLOCK = 256
CUBE = (0, 2, 4, 6, 1, 3, 5, 7)


def rms_scale(rows):
    return lax.rsqrt(jnp.mean(rows * rows, axis=-1, keepdims=True) + EPS)


def nt(left, right):
    return lax.dot_general(left, right, (((1,), (1,)), ((), ())), preferred_element_type=F32)


def tn(left, right):
    return lax.dot_general(left, right, (((0,), (0,)), ((), ())), preferred_element_type=F32)


def nn(left, right):
    return jnp.dot(left, right, preferred_element_type=F32)


def norm_back(grad_norm, normed, scale_rows, gain):
    scaled = grad_norm * gain
    return scale_rows * (scaled - normed * jnp.mean(scaled * normed, axis=-1, keepdims=True))


def swap_seq(value, bits, n_seq):
    return lax.ppermute(value, "seq", [(i, i ^ bits) for i in range(n_seq)])


def swap_dp(value):
    return lax.ppermute(value, "dp", [(0, 1), (1, 0)])


def cube_gather(own, n_seq):
    half = own.shape[0] // 2
    by_one = swap_seq(own, 2, n_seq)
    by_two = swap_seq(own, 4, n_seq)
    by_core = swap_seq(own, 1, n_seq)
    across = jnp.concatenate([swap_seq(by_two[:half], 2, n_seq), swap_seq(by_one[half:], 4, n_seq)], 0)
    others = [swap_seq(v, 1, n_seq) for v in (by_one, by_two, across)]
    return [own, by_one, by_two, across, by_core] + others


def cube_rows(own, n_seq):
    return jnp.concatenate(cube_gather(own, n_seq), 0)


def cube_reduce(product, left, n_seq, hold=()):
    cut = left.shape[0] // 2
    got = swap_seq(product(left[cut:]).astype(BF16), 1, n_seq)
    got, hold = joint(got, hold)
    sums = product(left[:cut]) + got.astype(F32)
    here, for_one, for_two, for_across = sums.reshape(4, cut // 4, -1)
    half = cut // 8
    low = for_across.astype(BF16)
    via_one = swap_seq(low[:half], 2, n_seq).astype(F32)
    via_two = swap_seq(low[half:], 4, n_seq).astype(F32)
    for_two = jnp.concatenate([for_two[:half] + via_one, for_two[half:]], 0)
    for_one = jnp.concatenate([for_one[:half], for_one[half:] + via_two], 0)
    from_one = swap_seq(for_one.astype(BF16), 2, n_seq).astype(F32)
    from_two = swap_seq(for_two.astype(BF16), 4, n_seq).astype(F32)
    return here + from_one + from_two, (via_one, via_two), hold


def joint(*trees):
    leaves, shape = jax.tree.flatten(trees)
    return jax.tree.unflatten(shape, lax.optimization_barrier(tuple(leaves)))


def after(value, *others):
    return joint(value, *others)[0]


def ones_of(number):
    return bin(number).count("1")


def far_spread(own, n_seq):
    here = {0: own}
    for ones in range(1, (n_seq // 8).bit_length()):
        for j in range(1, n_seq // 8):
            if ones_of(j) == ones:
                here[j] = swap_seq(here[j & (j - 1)], 8 * (j & -j), n_seq)
    return [here[j] for j in range(n_seq // 8)]


def far_reduce(terms, gates, n_seq, bits=8):
    while terms.shape[0] > 1:
        pairs = terms.reshape((terms.shape[0] // 2, 2) + terms.shape[1:])
        got = swap_seq(pairs[:, 1].astype(BF16), bits, n_seq)
        terms = pairs[:, 0] + after(got, gates[0]).astype(F32)
        gates = gates[1:] or gates
        bits *= 2
    return terms[0]


def spans(rows_q, rows_k):
    if rows_q != rows_k:
        return [(0, rows_q, rows_k)]
    half = rows_k // 2
    return [(0, half, half)] + [(start, start + BLOCK, start + BLOCK) for start in range(half, rows_q, BLOCK)]


def place(micro, member, half, slot, tok):
    bits = (slot % 4) * 2 + slot // 4
    return pl.multiple_of(((micro ^ half) * 8 + (member ^ bits)) * tok, tok)


def attend_kernel(where_ref, *refs):
    x_refs = refs[:-8]
    w_ref, gain_ref, first_ref, mixed_ref, keep_ref, give_ref, att_ref, x_ref = refs[-8:]
    micro, member, first_query, prefix_len = where_ref[0], where_ref[1], where_ref[2], where_ref[3]
    rows_q, rows_k = att_ref.shape[0], mixed_ref.shape[0]
    tok = rows_q // 16
    for piece, ref in enumerate(x_refs):
        x_ref[2 * tok * piece : 2 * tok * (piece + 1), :] = ref[...]

    @pl.loop(0, rows_k // (4 * tok))
    def _(pair):
        rows = pl.ds(pl.multiple_of(4 * tok * pair, 4 * tok), 4 * tok)
        source = x_ref[rows, :].astype(F32)
        first = (source * rms_scale(source) * gain_ref[...]).astype(BF16)
        mixed = nt(first, w_ref[...]).astype(BF16)
        for piece in range(2):
            part, slot = (2 * pair + piece) // 8, (2 * pair + piece) % 8
            for half in range(2):
                at = part * rows_q + place(micro, member, half, slot, tok)
                here = slice((2 * piece + half) * tok, (2 * piece + half + 1) * tok)
                first_ref[pl.ds(at, tok), :] = first[here]
                mixed_ref[pl.ds(at, tok), :] = mixed[here]

    att_ref[...] = jnp.zeros_like(att_ref)
    lanes = lax.broadcasted_iota(jnp.int32, (BLOCK, PAIR_DIM), 1)
    for begin, end, width in spans(rows_q, rows_k):

        @pl.loop(0, 2 * (end - begin) // BLOCK)
        def _(step, begin=begin, width=width):
            start = pl.multiple_of(begin + (step // 2) * BLOCK, BLOCK)
            at = pl.multiple_of(first_query + start, BLOCK)
            mine = (lanes // HEAD_DIM) == step % 2
            query = mixed_ref[pl.ds(at, BLOCK), 0:PAIR_DIM]
            keys = mixed_ref[0:width, PAIR_DIM : 2 * PAIR_DIM]
            values = mixed_ref[0:width, 2 * PAIR_DIM :]
            key_pos = lax.broadcasted_iota(jnp.int32, (BLOCK, width), 1)
            query_pos = at + lax.broadcasted_iota(jnp.int32, (BLOCK, width), 0)
            allowed = (key_pos <= query_pos) | (key_pos < prefix_len)
            scores = nt(jnp.where(mine, query, jnp.zeros_like(query)), keys) * HEAD_DIM**-0.5
            scores = jnp.where(allowed, scores, NEG)
            top = jnp.max(scores, axis=-1, keepdims=True)
            weights = jnp.exp(scores - top)
            total = jnp.sum(weights, axis=-1, keepdims=True)
            probs = (weights / total).astype(BF16)
            before = att_ref[pl.ds(start, BLOCK), :]
            att_ref[pl.ds(start, BLOCK), :] = jnp.where(mine, nn(probs, values).astype(BF16), before)
    for slot in range(8):
        here = slice(slot * tok, (slot + 1) * tok)
        keep_ref[here, :] = att_ref[pl.ds(place(micro, member, 0, slot, tok), tok), :]
        give_ref[here, :] = att_ref[pl.ds(place(micro, member, 1, slot, tok), tok), :]


def attend(where, blocks, weights, gain, rows_q):
    rows_k, width = blocks[0].shape[0] * len(blocks), blocks[0].shape[1]
    vmem = pl.BlockSpec(memory_space=pltpu.VMEM)
    return pl.pallas_call(
        attend_kernel,
        out_shape=(
            jax.ShapeDtypeStruct((rows_k, width), BF16),
            jax.ShapeDtypeStruct((rows_k, 3 * PAIR_DIM), BF16),
            jax.ShapeDtypeStruct((rows_q // 2, PAIR_DIM), BF16),
            jax.ShapeDtypeStruct((rows_q // 2, PAIR_DIM), BF16),
        ),
        in_specs=[pl.BlockSpec(memory_space=pltpu.SMEM)] + [vmem] * (len(blocks) + 2),
        out_specs=(vmem,) * 4,
        scratch_shapes=[pltpu.VMEM((rows_q, PAIR_DIM), BF16), pltpu.VMEM((rows_k, width), BF16)],
        compiler_params=pltpu.CompilerParams(vmem_limit_bytes=56 << 20),
        cost_estimate=pl.CostEstimate(
            flops=2 * rows_k * width * 3 * PAIR_DIM + 4 * rows_q * rows_k * PAIR_DIM,
            bytes_accessed=4 * rows_k * width,
            transcendentals=2 * rows_q * rows_k,
        ),
    )(where, *blocks, weights, gain)


def attend_back_kernel(where_ref, mixed_ref, own_ref, got_ref, gq_ref, *refs):
    micro, member, first_query, prefix_len = where_ref[0], where_ref[1], where_ref[2], where_ref[3]
    grad_ref = refs[-1]
    whole = len(refs) == 5
    keep_ref, give_ref, gk_ref, gv_ref = refs[:4] if whole else (None, None) + refs[:2]
    rows_q, rows_k = grad_ref.shape[0], mixed_ref.shape[0]
    tok = rows_q // 16
    for slot in range(8):
        here = slice(slot * tok, (slot + 1) * tok)
        grad_ref[pl.ds(place(micro, member, 0, slot, tok), tok), :] = own_ref[here, :]
        grad_ref[pl.ds(place(micro, member, 1, slot, tok), tok), :] = got_ref[here, :]
    lanes = lax.broadcasted_iota(jnp.int32, (BLOCK, PAIR_DIM), 1)
    gq_ref[...] = jnp.zeros_like(gq_ref)
    gk_ref[...] = jnp.zeros_like(gk_ref)
    gv_ref[...] = jnp.zeros_like(gv_ref)
    for begin, end, width in spans(rows_q, rows_k):

        @pl.loop(0, 2 * (end - begin) // BLOCK)
        def _(step, begin=begin, width=width):
            start = pl.multiple_of(begin + (step // 2) * BLOCK, BLOCK)
            at = pl.multiple_of(first_query + start, BLOCK)
            mine = (lanes // HEAD_DIM) == step % 2
            query = mixed_ref[pl.ds(at, BLOCK), 0:PAIR_DIM]
            grad = grad_ref[pl.ds(start, BLOCK), :]
            keys = mixed_ref[0:width, PAIR_DIM : 2 * PAIR_DIM]
            values = mixed_ref[0:width, 2 * PAIR_DIM :]
            key_pos = lax.broadcasted_iota(jnp.int32, (width, BLOCK), 0)
            query_pos = at + lax.broadcasted_iota(jnp.int32, (width, BLOCK), 1)
            allowed = (key_pos <= query_pos) | (key_pos < prefix_len)
            own_query = jnp.where(mine, query, jnp.zeros_like(query))
            own_grad = jnp.where(mine, grad, jnp.zeros_like(grad))
            scores = nt(keys, own_query) * HEAD_DIM**-0.5
            scores = jnp.where(allowed, scores, NEG)
            top = jnp.max(scores, axis=0, keepdims=True)
            weights = jnp.exp(scores - top)
            probs = weights / jnp.sum(weights, axis=0, keepdims=True)
            grad_probs = nt(values, own_grad)
            delta = jnp.sum(probs * grad_probs, axis=0, keepdims=True)
            grad_scores = (probs * (grad_probs - delta)).astype(BF16)
            gv_ref[0:width, :] += nn(probs.astype(BF16), own_grad)
            gk_ref[0:width, :] += nn(grad_scores, own_query) * HEAD_DIM**-0.5
            grad_q = (tn(grad_scores, keys) * HEAD_DIM**-0.5).astype(BF16)
            before = gq_ref[pl.ds(start, BLOCK), 0:PAIR_DIM]
            gq_ref[pl.ds(start, BLOCK), 0:PAIR_DIM] = jnp.where(mine, grad_q, before)
    if whole:
        gq_ref[:, PAIR_DIM : 2 * PAIR_DIM] = gk_ref[...].astype(BF16)
        gq_ref[:, 2 * PAIR_DIM :] = gv_ref[...].astype(BF16)
        for slot in range(8):
            here = slice(slot * tok, (slot + 1) * tok)
            keep_ref[here, :] = gq_ref[pl.ds(place(micro, member, 0, slot, tok), tok), :]
            give_ref[here, :] = gq_ref[pl.ds(place(micro, member, 1, slot, tok), tok), :]


def attend_back(where, mixed, own, got):
    rows_q, rows_k = 2 * own.shape[0], mixed.shape[0]
    whole = rows_q == rows_k
    keys = jax.ShapeDtypeStruct((rows_k, PAIR_DIM), F32)
    half = jax.ShapeDtypeStruct((rows_q // 2, 3 * PAIR_DIM), BF16)
    vmem = pl.BlockSpec(memory_space=pltpu.VMEM)
    return pl.pallas_call(
        attend_back_kernel,
        out_shape=(jax.ShapeDtypeStruct((rows_q, (3 if whole else 1) * PAIR_DIM), BF16),)
        + ((half, half) if whole else (keys, keys)),
        in_specs=[pl.BlockSpec(memory_space=pltpu.SMEM)] + [vmem] * 3,
        out_specs=(vmem,) * 3,
        scratch_shapes=[pltpu.VMEM(keys.shape, F32)] * (2 if whole else 0) + [pltpu.VMEM((rows_q, PAIR_DIM), BF16)],
        compiler_params=pltpu.CompilerParams(vmem_limit_bytes=56 << 20),
        cost_estimate=pl.CostEstimate(
            flops=10 * rows_q * rows_k * PAIR_DIM,
            bytes_accessed=8 * rows_k * PAIR_DIM * 4,
            transcendentals=2 * rows_q * rows_k,
        ),
    )(where, mixed, own, got)


def shards(n_dp, n_seq, inputs, teacher, valid_mask, prefix, attn_in, attn_out, mlp_in, mlp_out, norm_gains):
    n_micro, _, tok, width = inputs.shape
    rows = n_micro * tok
    dp = lax.axis_index("dp")
    seq = lax.axis_index("seq")
    me = dp * n_seq + seq
    n_dev = n_dp * n_seq
    n_far = n_seq // 8
    member = seq % 8
    micro = (seq // 8) % 2
    part = seq // 16
    n_parts = n_seq // 16
    rows_q = 16 * tok
    part_groups = [[p * 16 + g for p in range(n_parts)] for g in range(16)]
    gain_one = norm_gains[0:1]
    gain_two = norm_gains[1:2]

    def micro_first(pair):
        return jnp.where(micro == 0, pair, pair[::-1])

    def other_micro(value):
        return swap_seq(value, 8, n_seq)

    own_in = micro_first(inputs[:, 0])

    unit = attn_in.shape[0] // 3
    n_share = PAIR_DIM // unit

    def home(share):
        pair, rest = divmod(share % n_dev, n_share)
        to_dp, to_far = divmod(rest, n_far)
        return to_dp * n_seq + to_far * 8 + pair

    my_share = member * n_share + dp * n_far + seq // 8
    third_inverse = pow(3, -1, n_dev)
    thirds = [(3 * (((my_share - t) * third_inverse) % n_dev) + t) // n_dev for t in range(3)]
    own_units = attn_in.reshape(3, unit, width)
    x_got = other_micro(own_in[1])
    down_rows = lax.ppermute(mlp_out, BOTH, [(b, (b % 2) * n_seq + b // 2) for b in range(n_dev)])
    arrived = [lax.ppermute(own_units[t], BOTH, [(i, home(3 * i + t)) for i in range(n_dev)]) for t in range(3)]
    x_pair = jnp.concatenate([own_in[0], x_got], 0)
    x_pair, arrived, late_in = joint(x_pair, arrived, mlp_in)
    ffn_here = far_spread(late_in, n_seq)
    ffn_there = [swap_dp(late_in)]

    x_blocks = cube_gather(x_pair, n_seq)
    if n_parts > 1:
        whole = lax.all_gather(jnp.stack(x_blocks), "seq", axis=0, axis_index_groups=part_groups, tiled=True)
        x_blocks = [whole[i] for i in range(8 * n_parts)]

    def pick(keys, values, key):
        return jnp.where(keys[0] == key, values[0], jnp.where(keys[1] == key, values[1], values[2]))

    arrived = after(arrived, x_blocks[4])
    my_thirds = jnp.stack([pick(thirds, arrived, third) for third in range(3)])
    here = far_spread(my_thirds, n_seq)
    there = [swap_dp(v) for v in here]

    def by_share(here, there, at):
        order = [jnp.stack([v[j] for j in range(n_far)], at) for v in (here, there)]
        if n_far > 1:
            turn = seq // 8
            for bit in range(n_far.bit_length() - 1):
                index = jnp.arange(n_far) ^ (1 << bit)
                on = (turn // (1 << bit)) % 2
                order = [jnp.where(on == 1, jnp.take(v, index, axis=at), v) for v in order]
        first = jnp.where(dp == 0, order[0], order[1])
        second = jnp.where(dp == 0, order[1], order[0])
        return jnp.stack([first, second], at)

    pair_w = by_share(here, there, 1).reshape(3 * PAIR_DIM, width)

    prefix_len = jnp.where(micro == 0, prefix[0, 0], prefix[1, 0])
    where = jnp.stack([micro, member, part * rows_q, prefix_len]).astype(jnp.int32)
    x_blocks, pair_w, ffn_here, ffn_there, down_rows, late_out = joint(
        x_blocks, pair_w, ffn_here, ffn_there, down_rows, attn_out
    )
    down_here = far_spread(down_rows, n_seq)
    down_there = [swap_dp(down_rows)]
    out_rows = lax.ppermute(late_out, BOTH, [(i, home(i)) for i in range(n_dev)])
    first_in, mixed, att_keep, att_give = attend(where, x_blocks, pair_w, gain_one, rows_q)
    att_give, out_rows = joint(att_give, out_rows)
    out_here = far_spread(out_rows, n_seq)
    out_w = by_share(out_here, [swap_dp(v) for v in out_here], 0).reshape(PAIR_DIM, width)
    att_got = other_micro(att_give)

    ffn_there += [swap_dp(v) for v in after(ffn_here[1:], att_got)]
    down_there += [swap_dp(v) for v in after(down_here[1:], att_got)]
    in_rows = mlp_in.shape[0]

    def by_dp(here, there):
        return jnp.where(dp == 0, jnp.concatenate([here, there], 0), jnp.concatenate([there, here], 0))

    in_w = by_dp(*(jnp.concatenate(blocks, 0) for blocks in (ffn_here, ffn_there)))
    down_w = jnp.concatenate([by_dp(here, there) for here, there in zip(down_here, down_there)], 0)
    n_hidden = n_far * in_rows

    attended = jnp.stack([att_keep.reshape(8, tok, PAIR_DIM), att_got.reshape(8, tok, PAIR_DIM)], 1)
    attended = attended.reshape(8 * rows, PAIR_DIM)
    source = own_in.reshape(rows, width).astype(F32)
    middle = source + cube_reduce(lambda v: nn(v, out_w), attended, n_seq)[0]
    scale_two = rms_scale(middle)
    normed_two = middle * scale_two
    second_in = cube_rows((normed_two * gain_two).astype(BF16), n_seq)

    gate_up = nt(second_in, in_w)
    gate = gate_up[:, :n_hidden]
    up_part = gate_up[:, n_hidden:]
    sigmoid_gate = jax.nn.sigmoid(gate)
    silu_gate = gate * sigmoid_gate
    hidden = (silu_gate * up_part).astype(BF16)
    result = middle + cube_reduce(lambda v: nn(v, down_w), hidden, n_seq)[0]
    late_teacher, late_mask = after((teacher, valid_mask), att_got)
    target = micro_first(late_teacher[:, 0]).reshape(rows, width).astype(F32)
    row_mask = micro_first(late_mask[:, 0]).reshape(rows, 1).astype(F32)
    error = row_mask * (result - target)
    error_low = cube_rows(error.astype(BF16), n_seq)
    grad_hidden = nt(error_low, down_w)
    grad_gate = (grad_hidden * up_part * sigmoid_gate * (1.0 + gate * (1.0 - sigmoid_gate))).astype(BF16)
    grad_up = (grad_hidden * silu_gate).astype(BF16)
    grad_both = jnp.concatenate([grad_gate, grad_up], 1)
    grad_second, begun, _ = cube_reduce(lambda v: nn(v, in_w), grad_both, n_seq)

    hidden_late, both_late = after((hidden, grad_both), begun)
    down_terms = tn(hidden_late, error_low).reshape(n_far, 2, mlp_out.shape[0], width)
    in_terms = tn(both_late, second_in).reshape(n_dp, n_far, in_rows, width)
    down_got = swap_dp(jnp.where(dp == 0, down_terms[:, 1], down_terms[:, 0]).astype(BF16))
    in_got = swap_dp(jnp.where(dp == 0, in_terms[1], in_terms[0]).astype(BF16))
    down_terms = jnp.where(dp == 0, down_terms[:, 0], down_terms[:, 1])
    in_terms = jnp.where(dp == 0, in_terms[0], in_terms[1])

    grad_middle = error + norm_back(grad_second, normed_two, scale_two, gain_two)
    middle_low = cube_rows(grad_middle.astype(BF16), n_seq)
    grad_att = nt(middle_low, out_w).astype(BF16).reshape(8, 2, tok, PAIR_DIM)
    grad_keep = grad_att[:, 0].reshape(8 * tok, PAIR_DIM)
    grad_got = other_micro(grad_att[:, 1].reshape(8 * tok, PAIR_DIM))

    in_terms = in_terms + after(in_got, grad_got).astype(F32)
    in_pairs = in_terms.reshape((n_far // 2, 2) + in_terms.shape[1:])
    in_low = swap_seq(in_pairs[:, 1].astype(BF16), 8, n_seq)
    grads = attend_back(where, mixed, grad_keep, grad_got)
    if n_parts > 1:
        grad_k, grad_v = (
            lax.psum_scatter(v, "seq", scatter_dimension=0, axis_index_groups=part_groups, tiled=True).astype(BF16)
            for v in grads[1:]
        )
        grad_mixed = jnp.concatenate([grads[0], grad_k, grad_v], 1)
        first_part = lax.dynamic_slice_in_dim(first_in, part * rows_q, rows_q, 0)
        places = (member ^ jnp.array(CUBE, jnp.int32)) + 8 * micro
        by_rows = grad_mixed.reshape(16, tok, 3 * PAIR_DIM)
        mixed_keep, mixed_give = (by_rows[p].reshape(8 * tok, 3 * PAIR_DIM) for p in (places, places ^ 8))
    else:
        grad_mixed, mixed_keep, mixed_give = grads
        first_part = first_in
    mixed_give, mixed_keep, grad_mixed, in_low, first_part = joint(
        mixed_give, mixed_keep, grad_mixed, in_low, first_part
    )
    mixed_got = other_micro(mixed_give)

    mixed_rows = jnp.stack([v.reshape(8, tok, 3 * PAIR_DIM) for v in (mixed_keep, mixed_got)], 1)
    grad_first, last, _ = cube_reduce(
        lambda v: nn(v, pair_w), mixed_rows.reshape(8 * rows, 3 * PAIR_DIM), n_seq
    )
    mlp_in_grad = far_reduce(in_pairs[:, 0] + in_low.astype(F32), [grad_first], n_seq, 16)
    down_terms = down_terms + after(down_got, mixed_got).astype(F32)
    down_sum = far_reduce(down_terms, [last], n_seq)
    mlp_out_grad = lax.ppermute(
        down_sum.astype(BF16), BOTH, [((b % 2) * n_seq + b // 2, b) for b in range(n_dev)]
    )

    scale_one = rms_scale(source)
    input_grad = grad_middle + norm_back(grad_first, source * scale_one, scale_one, gain_one)
    mlp_out_grad = after(mlp_out_grad, grad_first).astype(F32)

    def share_reduce(terms, gates):
        give = jnp.where(dp == 0, terms[:, 1], terms[:, 0]).astype(BF16)
        terms = jnp.where(dp == 0, terms[:, 0], terms[:, 1]) + after(swap_dp(give), gates[0]).astype(F32)
        bits = 8
        while bits < n_seq:
            on = (seq // bits) % 2
            pairs = terms.reshape((terms.shape[0], terms.shape[1] // 2, 2) + terms.shape[2:])
            give = jnp.where(on == 0, pairs[:, :, 1], pairs[:, :, 0]).astype(BF16)
            got = after(swap_seq(give, bits, n_seq), gates[1])
            terms = jnp.where(on == 0, pairs[:, :, 0], pairs[:, :, 1]) + got.astype(F32)
            bits *= 2
        return terms[:, 0].astype(BF16)

    pair_terms = tn(grad_mixed, first_part)
    gain_term = jnp.sum(pair_terms * pair_w.astype(F32), axis=0) / gain_one[0]
    terms = jnp.concatenate([pair_terms, tn(attended, middle_low)], 0).reshape(4, n_dp, n_far, unit, width)
    terms = share_reduce(terms, [mixed_got, grad_first])
    attn_out_grad = lax.ppermute(terms[3], BOTH, [(home(i), i) for i in range(n_dev)]).astype(F32)
    returned = [
        lax.ppermute(
            jnp.where(thirds[t] == 0, terms[0], jnp.where(thirds[t] == 1, terms[1], terms[2])),
            BOTH,
            [(home(3 * i + t), i) for i in range(n_dev)],
        )
        for t in range(3)
    ]
    attn_in_grad = jnp.concatenate(returned, 0).astype(F32)

    squares = micro_first(jnp.sum((error * error).reshape(n_micro, tok * width), axis=1))
    scalars = jnp.zeros((width,), F32).at[0:2].set(squares).at[2].set(jnp.sum(row_mask))
    sums = jnp.stack([gain_term, jnp.sum(grad_second * normed_two, axis=0), scalars])
    sums = sums + swap_seq(sums, 1, n_seq)
    sums = sums + swap_dp(sums)
    bits = 2
    while bits < n_seq:
        sums = sums + after(swap_seq(sums, bits, n_seq), mixed_keep if bits < 8 else last)
        bits *= 2
    losses = sums[2, 0:2] / (width * sums[2, 2])

    def by_micro(value):
        return micro_first(value.reshape(n_micro, 1, tok, width))

    return (
        by_micro(result.astype(BF16)),
        losses,
        by_micro(input_grad),
        attn_in_grad,
        attn_out_grad,
        mlp_in_grad,
        mlp_out_grad,
        sums[0:2],
    )


def solution(mesh):
    n_dp, n_seq = mesh.shape["dp"], mesh.shape["seq"]
    placed = (
        P(None, "dp", "seq", None),
        P(None, "dp", "seq", None),
        P(None, "dp", "seq"),
        P(None, "dp"),
        P(BOTH, None),
        P(BOTH, None),
        P(BOTH, None),
        P(BOTH, None),
        P(),
    )
    return jax.shard_map(
        functools.partial(shards, n_dp, n_seq),
        mesh=mesh,
        in_specs=placed,
        out_specs=(
            P(None, "dp", "seq", None),
            P(),
            P(None, "dp", "seq", None),
            P(BOTH, None),
            P(BOTH, None),
            P(BOTH, None),
            P(BOTH, None),
            P(),
        ),
        check_vma=False,
    )
```

time: 446 us -> 353 us (0.79)
  waiting for transfers between devices: 173 us -> 146 us
  starting transfers between devices: 122 us -> 99 us
  between operations: 27 us -> 4.05 us
  local copies, waits for them, and re-layouts: 32.4 us -> 20.9 us
  matrix products: 35.2 us -> 25.9 us
  Pallas kernels: 18.6 us -> 23.2 us
    all_to_all x3 -> x0, waiting for transfers between devices: 15.9 us -> none  [the longest x2 15.9 us: to_rows(): moved = lax.all_to_all(by_device, 'seq', 0, 0, axis_index_groups=in_groups)]
    all_to_all x3 -> x0, starting transfers between devices: 15.9 us -> none  [the longest x2 10.7 us: to_rows(): moved = lax.all_to_all(by_device, 'seq', 0, 0, axis_index_groups=in_groups)]
    ppermute x13 -> x12, waiting for transfers between devices: 27.7 us -> 12.6 us  [swap_dp(): return lax.ppermute(value, 'dp', [(0, 1), (1, 0)])]
    dot_general x5 -> x4, matrix products: 18.3 us -> 6.27 us  [tn(): lax.dot_general(left, right, (((0,), (0,)), ((), ())), preferred_element_...]
    ppermute x8 -> x9, starting transfers between devices: 35.5 us -> 25.6 us  [the longest x3 11.9 us: shards(): lax.ppermute(jnp.where(thirds[t] == 0, terms[0], jnp.where(thirds[t] == 1...]
    ppermute x46 -> x67, waiting for transfers between devices: 120 us -> 128 us  [swap_seq(): return lax.ppermute(value, 'seq', [(i, i ^ bits) for i in range(n_seq)])]
    ppermute x46 -> x67, starting transfers between devices: 50.8 us -> 58.1 us  [swap_seq(): return lax.ppermute(value, 'seq', [(i, i ^ bits) for i in range(n_seq)])]
    unnamed x100 -> x101, local copies, waits for them, and re-layouts: 13.8 us -> 7.52 us
  transfers between devices with their start and end apart: 73 -> 89, of which waited for: 31 -> 47; matrix products, arithmetic and copies ran while one was open for 17% -> 14% of each run, Pallas kernels for 4% -> 7%
where the time goes in v3:
time: 353 us; the launch traced here: 350 us
  waiting for transfers between devices  146 us (41%)
  starting transfers between devices  99 us (28%)
  other arithmetic  30.8 us (9%)
  matrix products  25.9 us (7%)
  Pallas kernels  23.2 us (7%)
  local copies, waits for them, and re-layouts  20.9 us (6%)
  between operations  4.05 us (1%)
    ppermute x67, waiting for transfers between devices, swap_seq(): return lax.ppermute(value, 'seq', [(i, i ^ bits) for i in range(n_seq)])  128 us
    ppermute x67, starting transfers between devices, swap_seq(): return lax.ppermute(value, 'seq', [(i, i ^ bits) for i in range(n_seq)])  58.1 us
    ppermute x12, waiting for transfers between devices, swap_dp(): return lax.ppermute(value, 'dp', [(0, 1), (1, 0)])  12.6 us
    ppermute x3, starting transfers between devices, shards(): lax.ppermute(jnp.where(thirds[t] == 0, terms[0], jnp.where(thirds[t] == 1...  11.9 us
    pallas_call x1, Pallas kernels, attend(): pl.pallas_call(attend_kernel, out_shape=(jax.ShapeDtypeStruct((rows_k, wi...  11.8 us
    pallas_call x1, Pallas kernels, attend_back(): pl.pallas_call(attend_back_kernel, out_shape=(jax.ShapeDtypeStruct((rows_...  11.5 us
    ppermute x12, starting transfers between devices, swap_dp(): return lax.ppermute(value, 'dp', [(0, 1), (1, 0)])  10.8 us
    dot_general x8, matrix products, nn(): return jnp.dot(left, right, preferred_element_type=F32)  10.1 us
  transfers between devices with their start and end apart: 89, of which 47 were waited for; matrix products, arithmetic and copies ran while one was open for 14% of the time, Pallas kernels for 7%

profile of v3, /device:TPU:2, one launch (start us, length us, event | category | flops | bytes accessed | tf_op | source)
XLA Modules:
  0.0 349.6 jit_solution(2726314936365864260)
XLA Ops:
  0.7 1.8 fusion.33
  2.5 2.7 collective-permute-start
  6.0 2.6 collective-permute-start.1
  8.6 3.7 %collective-permute-start.2 = (bf16[32,1024]{1,0:T(8,128)(2,1)S(1)}, bf16[32,1024]{1,0:T(8,128)(2,1)S(1)}, u32[]{:S(2)}, u32[]{:S(2)}) collective-permute-start(bf16[32,1024]{1,0:T(8,128)(2,1)S(1)} %get-tuple-element.208), channel_id=1, source_target_pairs={{0,8},{1,1},{2,25},{3,18},{4,11},{5,4},{6,28},{7,21},{8,14},{9,7},... | collective-permute-start | bytes 196616 | tf_op jit(solution)/shard_map/ppermute | solution.py:315
  13.0 4.5 %collective-permute-start.17 = (bf16[128,1024]{1,0:T(8,128)(2,1)}, bf16[128,1024]{1,0:T(8,128)(2,1)S(1)}, u32[]{:S(2)}, u32[]{:S(2)}) collective-permute-start(bf16[128,1024]{1,0:T(8,128)(2,1)} %param.24), channel_id=1, source_target_pairs={{0,0},{1,16},{2,1},{3,17},{4,2},{5,18},{6,3},{7,19},{8,4},{9,20},{... | collective-permute-start | bytes 786440 | tf_op jit(solution)/shard_map/ppermute | solution.py:314
  18.9 3.5 %collective-permute-start.4 = (bf16[128,1024]{1,0:T(8,128)(2,1)S(1)}, bf16[128,1024]{1,0:T(8,128)(2,1)S(1)}, u32[]{:S(2)}, u32[]{:S(2)}) collective-permute-start(bf16[128,1024]{1,0:T(8,128)(2,1)S(1)} %pad_maximum_fusion.11.refs_0_), channel_id=1, source_target_pairs={{0,2},{1,3},{2,0},{3,1},{4,6},{5,7},{6,4},{7,5},{8,10},{9,11},{10,... | collective-permute-start | bytes 786440 | tf_op jit(solution)/shard_map/ppermute | solution.py:44
  25.6 6.2 %collective-permute-done.5.refs_2_ = bf16[128,1024]{1,0:T(8,128)(2,1)S(1)} collective-permute-done((bf16[128,1024]{1,0:T(8,128)(2,1)S(1)}, bf16[128,1024]{1,0:T(8,128)(2,1)S(1)}, u32[]{:S(2)}, u32[]{:S(2)}) %collective-permute-start.5) | collective-permute-done | bytes 262176 | tf_op jit(solution)/shard_map/ppermute | solution.py:44
  32.3 2.9 collective-permute-start.7
  37.0 2.4 collective-permute-start.15
  42.1 17.3 %collective-permute-done.12 = bf16[3,32,1024]{2,1,0:T(8,128)(2,1)S(1)} collective-permute-done((bf16[3,32,1024]{2,1,0:T(8,128)(2,1)S(1)}, bf16[3,32,1024]{2,1,0:T(8,128)(2,1)S(1)}, u32[]{:S(2)}, u32[]{:S(2)}) %collective-permute-start.12) | collective-permute-done | bytes 196640 | tf_op jit(solution)/shard_map/ppermute | solution.py:44
  62.0 3.3 collective-permute-done.14
  67.8 2.5 collective-permute-done.15
  70.3 2.8 collective-permute-start.18
  73.1 11.8 %shard_map.152 = (bf16[1024,1024]{1,0:T(8,128)(2,1)}, bf16[1024,384]{1,0:T(8,128)(2,1)}, bf16[512,128]{1,0:T(8,128)(2,1)}, bf16[512,128]{1,0:T(8,128)(2,1)}) custom-call(s32[4]{0:T(128)} %pad_add_fusion.where_ref, bf16[128,1024]{1,0:T(8,128)(2,1)} %copy-done.22, bf16[128,1024]{1,0:T(8,128)(2,1)} %copy-done.23, bf16[128,1024]{1,0:T(8,128)(2,1)} %copy-done.24, ...), custom_call_target="tpu_custom_call" | custom-call | flops 1342177280 | bytes 4194304 | tf_op jit(solution)/shard_map/pallas_call | solution.py:181
  84.9 1.4 collective-permute-start.20
  86.3 1.5 collective-permute-start.19
  87.9 5.2 %collective-permute-done.20 = bf16[32,1024]{1,0:T(8,128)(2,1)S(1)} collective-permute-done((bf16[32,1024]{1,0:T(8,128)(2,1)S(1)}, bf16[32,1024]{1,0:T(8,128)(2,1)S(1)}, u32[]{:S(2)}, u32[]{:S(2)}) %collective-permute-start.20) | collective-permute-done | bytes 65568 | tf_op jit(solution)/shard_map/ppermute | solution.py:44
  96.2 1.8 collective-permute-done.22
  99.2 2.6 collective-permute-done.23
  103.0 3.3 collective-permute-start.38
  106.3 3.2 collective-permute-done.24
  110.2 1.6 collective-permute-start.37
  111.8 6.3 %collective-permute-done.38 = bf16[128,1024]{1,0:T(8,128)(2,1)S(1)} collective-permute-done((bf16[128,1024]{1,0:T(8,128)(2,1)S(1)}, bf16[128,1024]{1,0:T(8,128)(2,1)S(1)}, u32[]{:S(2)}, u32[]{:S(2)}) %collective-permute-start.38) | collective-permute-done | bytes 262176 | tf_op jit(solution)/shard_map/ppermute | solution.py:44
  119.0 2.1 collective-permute-done.27
  123.1 4.2 %collective-permute-done.39 = bf16[128,1024]{1,0:T(8,128)(2,1)S(1)} collective-permute-done((bf16[128,1024]{1,0:T(8,128)(2,1)S(1)}, bf16[128,1024]{1,0:T(8,128)(2,1)S(1)}, u32[]{:S(2)}, u32[]{:S(2)}) %collective-permute-start.39) | collective-permute-done | bytes 262176 | tf_op jit(solution)/shard_map/ppermute | solution.py:48
  128.9 1.9 collective-permute-start.31
  130.8 2.7 collective-permute-done.30
  136.6 6.9 %fusion.58 = f32[1024,1024]{0,1:T(8,128)S(1)} fusion(bf16[1024,1024]{1,0:T(8,128)(2,1)S(1)} %constant_dynamic-update-slice_fusion.2, bf16[256,1024]{1,0:T(8,128)(2,1)S(1)} %collective-permute-done.36, bf16[256,1024]{1,0:T(8,128)(2,1)} %collective-permute-done.16, bf16[256,1024]{1,0:T(8,128)(2,1)} %collective-permute-done.15, bf16[256,1024]{1,0:T(8,128)(2,1)} %param.23, ...), kind=kOutput, calls=%fused_computation.209 | convolution fusion | flops 2165309440 | bytes 8388609 | tf_op jit(solution)/shard_map/dot_general | solution.py:27
  146.6 2.5 collective-permute-done.40
  152.5 3.1 collective-permute-done.41
  163.7 2.1 collective-permute-done.44
  167.1 2.0 fusion.56
  172.3 4.1 %collective-permute-done.46 = bf16[128,1024]{1,0:T(8,128)(2,1)S(1)} collective-permute-done((bf16[128,1024]{1,0:T(8,128)(2,1)S(1)}, bf16[128,1024]{1,0:T(8,128)(2,1)S(1)}, u32[]{:S(2)}, u32[]{:S(2)}) %collective-permute-start.46) | collective-permute-done | bytes 262176 | tf_op jit(solution)/shard_map/ppermute | solution.py:44
  179.4 2.0 collective-permute-done.47
  184.3 1.9 multiply_convert_fusion
  186.3 3.3 convolution_convert_fusion.2
  190.7 1.4 copy-done.27
  192.1 2.3 fusion.76
  196.4 3.0 fusion.74
  202.8 2.3 collective-permute-done.54
  210.1 3.3 collective-permute-done.57
  218.1 1.7 slice_select_fusion
  220.1 4.0 %collective-permute-done.59 = bf16[128,1024]{1,0:T(8,128)(2,1)S(1)} collective-permute-done((bf16[128,1024]{1,0:T(8,128)(2,1)}, bf16[128,1024]{1,0:T(8,128)(2,1)S(1)}, u32[]{:S(2)}, u32[]{:S(2)}) %collective-permute-start.59) | collective-permute-done | bytes 262176 | tf_op jit(solution)/shard_map/ppermute | solution.py:44
  226.2 2.9 collective-permute-done.60
  233.3 3.0 collective-permute-start.66
  237.0 6.0 %collective-permute-done.66.got_ref = bf16[512,128]{1,0:T(8,128)(2,1)S(1)} collective-permute-done((bf16[512,128]{1,0:T(8,128)(2,1)S(1)}, bf16[512,128]{1,0:T(8,128)(2,1)S(1)}, u32[]{:S(2)}, u32[]{:S(2)}) %collective-permute-start.66) | collective-permute-done | bytes 131104 | tf_op jit(solution)/shard_map/ppermute | solution.py:44
  243.7 1.7 add_bitcast_fusion
  248.8 11.5 %shard_map.153 = (bf16[1024,384]{1,0:T(8,128)(2,1)}, bf16[512,384]{1,0:T(8,128)(2,1)}, bf16[512,384]{1,0:T(8,128)(2,1)}) custom-call(s32[4]{0:T(128)} %pad_add_fusion.where_ref, bf16[1024,384]{1,0:T(8,128)(2,1)} %get-tuple-element.113.mixed_ref, bf16[512,128]{1,0:T(8,128)(2,1)} %bitcast.253, bf16[512,128]{1,0:T(8,128)(2,1)} %copy-done.37), custom_call_target="tpu_custom_call" | custom-call | flops 1342177280 | bytes 4194304 | tf_op jit(solution)/shard_map/pallas_call | solution.py:260
  260.3 13.0 %collective-permute-done.68 = bf16[1,256,1024]{2,1,0:T(8,128)(2,1)} collective-permute-done((bf16[1,256,1024]{2,1,0:T(8,128)(2,1)}, bf16[1,256,1024]{2,1,0:T(8,128)(2,1)}, u32[]{:S(2)}, u32[]{:S(2)}) %collective-permute-start.68) | collective-permute-done | bytes 524320 | tf_op jit(solution)/shard_map/ppermute | solution.py:44
  273.4 2.2 multiply_reduce_fusion
  277.9 2.8 collective-permute-done.70
  282.6 1.9 collective-permute-done.71
  285.6 9.9 %collective-permute-done.74 = bf16[512,384]{1,0:T(8,128)(2,1)S(1)} collective-permute-done((bf16[512,384]{1,0:T(8,128)(2,1)S(1)}, bf16[512,384]{1,0:T(8,128)(2,1)S(1)}, u32[]{:S(2)}, u32[]{:S(2)}) %collective-permute-start.74) | collective-permute-done | bytes 393248 | tf_op jit(solution)/shard_map/ppermute | solution.py:44
  296.4 2.1 fusion.6
  300.0 3.0 collective-permute-start.87
  305.4 3.0 collective-permute-start.81
  309.5 3.0 collective-permute-done.77
  312.6 2.5 collective-permute-start.79
  316.1 5.3 %collective-permute-done.87 = bf16[1,128,1024]{2,1,0:T(8,128)(2,1)S(1)} collective-permute-done((bf16[1,128,1024]{2,1,0:T(8,128)(2,1)S(1)}, bf16[1,128,1024]{2,1,0:T(8,128)(2,1)S(1)}, u32[]{:S(2)}, u32[]{:S(2)}) %collective-permute-start.87) | collective-permute-done | bytes 262176 | tf_op jit(solution)/shard_map/ppermute | solution.py:44
  322.7 2.0 collective-permute-start.88
  328.2 6.0 %collective-permute-start.83 = (bf16[32,1024]{1,0:T(8,128)(2,1)S(1)}, bf16[32,1024]{1,0:T(8,128)(2,1)S(1)}, u32[]{:S(2)}, u32[]{:S(2)}) collective-permute-start(bf16[32,1024]{1,0:T(8,128)(2,1)S(1)} %get-tuple-element.193), channel_id=1, source_target_pairs={{8,0},{1,1},{25,2},{18,3},{11,4},{4,5},{28,6},{21,7},{14,8},{7,9},... | collective-permute-start | bytes 196616 | tf_op jit(solution)/shard_map/ppermute | solution.py:469
  334.2 5.3 %collective-permute-start.82 = (bf16[32,1024]{1,0:T(8,128)(2,1)S(1)}, bf16[32,1024]{1,0:T(8,128)(2,1)S(1)}, u32[]{:S(2)}, u32[]{:S(2)}) collective-permute-start(bf16[32,1024]{1,0:T(8,128)(2,1)S(1)} %get-tuple-element.192), channel_id=1, source_target_pairs={{0,0},{24,1},{17,2},{10,3},{3,4},{27,5},{20,6},{13,7},{6,8},{30,9}... | collective-permute-start | bytes 196616 | tf_op jit(solution)/shard_map/ppermute | solution.py:469
  339.5 1.9 collective-permute-start.85
  343.1 5.0 %collective-permute-done.85 = bf16[32,1024]{1,0:T(8,128)(2,1)S(1)} collective-permute-done((bf16[32,1024]{1,0:T(8,128)(2,1)S(1)}, bf16[32,1024]{1,0:T(8,128)(2,1)S(1)}, u32[]{:S(2)}, u32[]{:S(2)}) %collective-permute-start.85) | collective-permute-done | bytes 65568 | tf_op jit(solution)/shard_map/ppermute | solution.py:467
  (350 shorter events, 99.6 us)
Async XLA Ops:
  2.5 16.4 %collective-permute-start = (bf16[64,1024]{1,0:T(8,128)(2,1)S(1)}, bf16[64,1024]{1,0:T(8,128)(2,1)S(1)}, u32[]{:S(2)}, u32[]{:S(2)}) collective-permute-start(bf16[64,1024]{1,0:T(8,128)(2,1)S(1)} %get-tuple-element.200), channel_id=1, source_target_pairs={{0,8},{1,9},{2,10},{3,11},{4,12},{5,13},{6,14},{7,15},{8,0},{9,1},... | collective-permute-start | bytes 393224 | tf_op jit(solution)/shard_map/ppermute | solution.py:44
  6.0 12.8 %collective-permute-start.1 = (bf16[32,1024]{1,0:T(8,128)(2,1)S(1)}, bf16[32,1024]{1,0:T(8,128)(2,1)S(1)}, u32[]{:S(2)}, u32[]{:S(2)}) collective-permute-start(bf16[32,1024]{1,0:T(8,128)(2,1)S(1)} %get-tuple-element.207), channel_id=1, source_target_pairs={{0,0},{1,24},{2,17},{3,10},{4,3},{5,27},{6,20},{7,13},{8,6},{9,30}... | collective-permute-start | bytes 196616 | tf_op jit(solution)/shard_map/ppermute | solution.py:315
  8.6 10.3 %collective-permute-start.2 = (bf16[32,1024]{1,0:T(8,128)(2,1)S(1)}, bf16[32,1024]{1,0:T(8,128)(2,1)S(1)}, u32[]{:S(2)}, u32[]{:S(2)}) collective-permute-start(bf16[32,1024]{1,0:T(8,128)(2,1)S(1)} %get-tuple-element.208), channel_id=1, source_target_pairs={{0,8},{1,1},{2,25},{3,18},{4,11},{5,4},{6,28},{7,21},{8,14},{9,7},... | collective-permute-start | bytes 196616 | tf_op jit(solution)/shard_map/ppermute | solution.py:315
  12.3 6.5 %collective-permute-start.3 = (bf16[32,1024]{1,0:T(8,128)(2,1)S(1)}, bf16[32,1024]{1,0:T(8,128)(2,1)S(1)}, u32[]{:S(2)}, u32[]{:S(2)}) collective-permute-start(bf16[32,1024]{1,0:T(8,128)(2,1)S(1)} %get-tuple-element.206), channel_id=1, source_target_pairs={{0,16},{1,9},{2,2},{3,26},{4,19},{5,12},{6,5},{7,29},{8,22},{9,15}... | collective-permute-start | bytes 196616 | tf_op jit(solution)/shard_map/ppermute | solution.py:315
  13.0 52.9 %collective-permute-start.17 = (bf16[128,1024]{1,0:T(8,128)(2,1)}, bf16[128,1024]{1,0:T(8,128)(2,1)S(1)}, u32[]{:S(2)}, u32[]{:S(2)}) collective-permute-start(bf16[128,1024]{1,0:T(8,128)(2,1)} %param.24), channel_id=1, source_target_pairs={{0,0},{1,16},{2,1},{3,17},{4,2},{5,18},{6,3},{7,19},{8,4},{9,20},{... | collective-permute-start | bytes 786440 | tf_op jit(solution)/shard_map/ppermute | solution.py:314
  18.9 13.4 %collective-permute-start.4 = (bf16[128,1024]{1,0:T(8,128)(2,1)S(1)}, bf16[128,1024]{1,0:T(8,128)(2,1)S(1)}, u32[]{:S(2)}, u32[]{:S(2)}) collective-permute-start(bf16[128,1024]{1,0:T(8,128)(2,1)S(1)} %pad_maximum_fusion.11.refs_0_), channel_id=1, source_target_pairs={{0,2},{1,3},{2,0},{3,1},{4,6},{5,7},{6,4},{7,5},{8,10},{9,11},{10,... | collective-permute-start | bytes 786440 | tf_op jit(solution)/shard_map/ppermute | solution.py:44
  22.5 9.3 %collective-permute-start.5 = (bf16[128,1024]{1,0:T(8,128)(2,1)S(1)}, bf16[128,1024]{1,0:T(8,128)(2,1)S(1)}, u32[]{:S(2)}, u32[]{:S(2)}) collective-permute-start(bf16[128,1024]{1,0:T(8,128)(2,1)S(1)} %pad_maximum_fusion.11.refs_0_), channel_id=1, source_target_pairs={{0,4},{1,5},{2,6},{3,7},{4,0},{5,1},{6,2},{7,3},{8,12},{9,13},{10,... | collective-permute-start | bytes 786440 | tf_op jit(solution)/shard_map/ppermute | solution.py:44
  22.5 12.7 %collective-permute-start.8 = (bf16[128,1024]{1,0:T(8,128)(2,1)S(1)}, bf16[128,1024]{1,0:T(8,128)(2,1)S(1)}, u32[]{:S(2)}, u32[]{:S(2)}) collective-permute-start(bf16[128,1024]{1,0:T(8,128)(2,1)S(1)} %pad_maximum_fusion.11.refs_0_), channel_id=1, source_target_pairs={{0,1},{1,0},{2,3},{3,2},{4,5},{5,4},{6,7},{7,6},{8,9},{9,8},{10,11... | collective-permute-start | bytes 786440 | tf_op jit(solution)/shard_map/ppermute | solution.py:44
  31.8 7.7 %collective-permute-start.6 = (bf16[64,1024]{1,0:T(8,128)(2,1)S(1)}, bf16[64,1024]{1,0:T(8,128)(2,1)S(1)}, u32[]{:S(2)}, u32[]{:S(2)}) collective-permute-start(bf16[64,1024]{1,0:T(8,128)(2,1)S(1)} %slice.420), channel_id=1, source_target_pairs={{0,2},{1,3},{2,0},{3,1},{4,6},{5,7},{6,4},{7,5},{8,10},{9,11},{10,... | collective-permute-start | bytes 393224 | tf_op jit(solution)/shard_map/ppermute | solution.py:44
  32.3 8.8 %collective-permute-start.7 = (bf16[64,1024]{1,0:T(8,128)(2,1)S(1)}, bf16[64,1024]{1,0:T(8,128)(2,1)S(1)}, u32[]{:S(2)}, u32[]{:S(2)}) collective-permute-start(bf16[64,1024]{1,0:T(8,128)(2,1)S(1)} %slice.421), channel_id=1, source_target_pairs={{0,4},{1,5},{2,6},{3,7},{4,0},{5,1},{6,2},{7,3},{8,12},{9,13},{10,... | collective-permute-start | bytes 393224 | tf_op jit(solution)/shard_map/ppermute | solution.py:44
  35.9 23.5 %collective-permute-start.12 = (bf16[3,32,1024]{2,1,0:T(8,128)(2,1)S(1)}, bf16[3,32,1024]{2,1,0:T(8,128)(2,1)S(1)}, u32[]{:S(2)}, u32[]{:S(2)}) collective-permute-start(bf16[3,32,1024]{2,1,0:T(8,128)(2,1)S(1)} %get-tuple-element.202), channel_id=1, source_target_pairs={{0,8},{1,9},{2,10},{3,11},{4,12},{5,13},{6,14},{7,15},{8,0},{9,1},... | collective-permute-start | bytes 589832 | tf_op jit(solution)/shard_map/ppermute | solution.py:44
  37.0 33.2 %collective-permute-start.15 = (bf16[256,1024]{1,0:T(8,128)(2,1)}, bf16[256,1024]{1,0:T(8,128)(2,1)}, u32[]{:S(2)}, u32[]{:S(2)}) collective-permute-start(bf16[256,1024]{1,0:T(8,128)(2,1)} %param.23), channel_id=1, source_target_pairs={{0,8},{1,9},{2,10},{3,11},{4,12},{5,13},{6,14},{7,15},{8,0},{9,1},... | collective-permute-start | bytes 1572872 | tf_op jit(solution)/shard_map/ppermute | solution.py:44
  39.4 30.8 %collective-permute-start.16 = (bf16[256,1024]{1,0:T(8,128)(2,1)}, bf16[256,1024]{1,0:T(8,128)(2,1)}, u32[]{:S(2)}, u32[]{:S(2)}) collective-permute-start(bf16[256,1024]{1,0:T(8,128)(2,1)} %param.23), channel_id=1, source_target_pairs={{0,16},{16,0},{1,17},{17,1},{2,18},{18,2},{3,19},{19,3},{4,20},{20... | collective-permute-start | bytes 1572872 | tf_op jit(solution)/shard_map/ppermute | solution.py:48
  41.0 20.9 %collective-permute-start.13 = (bf16[3,32,1024]{2,1,0:T(8,128)(2,1)S(1)}, bf16[3,32,1024]{2,1,0:T(8,128)(2,1)S(1)}, u32[]{:S(2)}, u32[]{:S(2)}) collective-permute-start(bf16[3,32,1024]{2,1,0:T(8,128)(2,1)S(1)} %get-tuple-element.202), channel_id=1, source_target_pairs={{0,16},{16,0},{1,17},{17,1},{2,18},{18,2},{3,19},{19,3},{4,20},{20... | collective-permute-start | bytes 589832 | tf_op jit(solution)/shard_map/ppermute | solution.py:48
  59.4 5.8 %collective-permute-start.14 = (bf16[3,32,1024]{2,1,0:T(8,128)(2,1)S(1)}, bf16[3,32,1024]{2,1,0:T(8,128)(2,1)S(1)}, u32[]{:S(2)}, u32[]{:S(2)}) collective-permute-start(bf16[3,32,1024]{2,1,0:T(8,128)(2,1)S(1)} %collective-permute-done.12), channel_id=1, source_target_pairs={{0,16},{16,0},{1,17},{17,1},{2,18},{18,2},{3,19},{19,3},{4,20},{20... | collective-permute-start | bytes 589832 | tf_op jit(solution)/shard_map/ppermute | solution.py:48
  61.9 5.8 %collective-permute-start.9 = (bf16[128,1024]{1,0:T(8,128)(2,1)S(1)}, bf16[128,1024]{1,0:T(8,128)(2,1)}, u32[]{:S(2)}, u32[]{:S(2)}) collective-permute-start(bf16[128,1024]{1,0:T(8,128)(2,1)S(1)} %collective-permute-done.4.refs_1_), channel_id=1, source_target_pairs={{0,1},{1,0},{2,3},{3,2},{4,5},{5,4},{6,7},{7,6},{8,9},{9,8},{10,11... | collective-permute-start | bytes 786440 | tf_op jit(solution)/shard_map/ppermute | solution.py:44
  70.3 14.6 %collective-permute-start.18 = (bf16[32,1024]{1,0:T(8,128)(2,1)S(1)}, bf16[32,1024]{1,0:T(8,128)(2,1)S(1)}, u32[]{:S(2)}, u32[]{:S(2)}) collective-permute-start(bf16[32,1024]{1,0:T(8,128)(2,1)S(1)} %copy-done.38), channel_id=1, source_target_pairs={{0,0},{1,8},{2,16},{3,24},{4,1},{5,9},{6,17},{7,25},{8,2},{9,10},{... | collective-permute-start | bytes 196616 | tf_op jit(solution)/shard_map/ppermute | solution.py:355
  84.9 8.2 %collective-permute-start.20 = (bf16[32,1024]{1,0:T(8,128)(2,1)S(1)}, bf16[32,1024]{1,0:T(8,128)(2,1)S(1)}, u32[]{:S(2)}, u32[]{:S(2)}) collective-permute-start(bf16[32,1024]{1,0:T(8,128)(2,1)S(1)} %collective-permute-done.18), channel_id=1, source_target_pairs={{0,8},{1,9},{2,10},{3,11},{4,12},{5,13},{6,14},{7,15},{8,0},{9,1},... | collective-permute-start | bytes 196616 | tf_op jit(solution)/shard_map/ppermute | solution.py:44
  86.3 8.9 %collective-permute-start.19 = (bf16[512,128]{1,0:T(8,128)(2,1)}, bf16[512,128]{1,0:T(8,128)(2,1)S(1)}, u32[]{:S(2)}, u32[]{:S(2)}) collective-permute-start(bf16[512,128]{1,0:T(8,128)(2,1)} %get-tuple-element.105), channel_id=1, source_target_pairs={{0,8},{1,9},{2,10},{3,11},{4,12},{5,13},{6,14},{7,15},{8,0},{9,1},... | collective-permute-start | bytes 393224 | tf_op jit(solution)/shard_map/ppermute | solution.py:44
  87.9 8.3 %collective-permute-start.21 = (bf16[32,1024]{1,0:T(8,128)(2,1)S(1)}, bf16[32,1024]{1,0:T(8,128)(2,1)S(1)}, u32[]{:S(2)}, u32[]{:S(2)}) collective-permute-start(bf16[32,1024]{1,0:T(8,128)(2,1)S(1)} %collective-permute-done.18), channel_id=1, source_target_pairs={{0,16},{16,0},{1,17},{17,1},{2,18},{18,2},{3,19},{19,3},{4,20},{20... | collective-permute-start | bytes 196616 | tf_op jit(solution)/shard_map/ppermute | solution.py:48
  102.4 7.2 %collective-permute-start.24 = (bf16[64,1024]{1,0:T(8,128)(2,1)S(1)}, bf16[64,1024]{1,0:T(8,128)(2,1)S(1)}, u32[]{:S(2)}, u32[]{:S(2)}) collective-permute-start(bf16[64,1024]{1,0:T(8,128)(2,1)S(1)} %get-tuple-element.183), channel_id=1, source_target_pairs={{0,4},{1,5},{2,6},{3,7},{4,0},{5,1},{6,2},{7,3},{8,12},{9,13},{10,... | collective-permute-start | bytes 393224 | tf_op jit(solution)/shard_map/ppermute | solution.py:44
  102.4 7.1 %collective-permute-start.26 = (bf16[64,1024]{1,0:T(8,128)(2,1)S(1)}, bf16[64,1024]{1,0:T(8,128)(2,1)S(1)}, u32[]{:S(2)}, u32[]{:S(2)}) collective-permute-start(bf16[64,1024]{1,0:T(8,128)(2,1)S(1)} %get-tuple-element.182), channel_id=1, source_target_pairs={{0,2},{1,3},{2,0},{3,1},{4,6},{5,7},{6,4},{7,5},{8,10},{9,11},{10,... | collective-permute-start | bytes 393224 | tf_op jit(solution)/shard_map/ppermute | solution.py:44
  103.0 15.2 %collective-permute-start.38 = (bf16[128,1024]{1,0:T(8,128)(2,1)S(1)}, bf16[128,1024]{1,0:T(8,128)(2,1)S(1)}, u32[]{:S(2)}, u32[]{:S(2)}) collective-permute-start(bf16[128,1024]{1,0:T(8,128)(2,1)S(1)} %collective-permute-done.17), channel_id=1, source_target_pairs={{0,8},{1,9},{2,10},{3,11},{4,12},{5,13},{6,14},{7,15},{8,0},{9,1},... | collective-permute-start | bytes 786440 | tf_op jit(solution)/shard_map/ppermute | solution.py:44
  109.6 11.4 %collective-permute-start.27 = (bf16[128,1024]{1,0:T(8,128)(2,1)S(1)}, bf16[128,1024]{1,0:T(8,128)(2,1)S(1)}, u32[]{:S(2)}, u32[]{:S(2)}) collective-permute-start(bf16[128,1024]{1,0:T(8,128)(2,1)S(1)} %pad_maximum_fusion.14), channel_id=1, source_target_pairs={{0,4},{1,5},{2,6},{3,7},{4,0},{5,1},{6,2},{7,3},{8,12},{9,13},{10,... | collective-permute-start | bytes 786440 | tf_op jit(solution)/shard_map/ppermute | solution.py:44
  109.9 11.2 %collective-permute-start.25 = (bf16[128,1024]{1,0:T(8,128)(2,1)S(1)}, bf16[128,1024]{1,0:T(8,128)(2,1)S(1)}, u32[]{:S(2)}, u32[]{:S(2)}) collective-permute-start(bf16[128,1024]{1,0:T(8,128)(2,1)S(1)} %pad_maximum_fusion.13), channel_id=1, source_target_pairs={{0,2},{1,3},{2,0},{3,1},{4,6},{5,7},{6,4},{7,5},{8,10},{9,11},{10,... | collective-permute-start | bytes 786440 | tf_op jit(solution)/shard_map/ppermute | solution.py:44
  110.2 12.7 %collective-permute-start.37 = (bf16[128,1024]{1,0:T(8,128)(2,1)S(1)}, bf16[128,1024]{1,0:T(8,128)(2,1)S(1)}, u32[]{:S(2)}, u32[]{:S(2)}) collective-permute-start(bf16[128,1024]{1,0:T(8,128)(2,1)S(1)} %collective-permute-done.17), channel_id=1, source_target_pairs={{0,16},{16,0},{1,17},{17,1},{2,18},{18,2},{3,19},{19,3},{4,20},{20... | collective-permute-start | bytes 786440 | tf_op jit(solution)/shard_map/ppermute | solution.py:48
  118.1 9.2 %collective-permute-start.39 = (bf16[128,1024]{1,0:T(8,128)(2,1)S(1)}, bf16[128,1024]{1,0:T(8,128)(2,1)S(1)}, u32[]{:S(2)}, u32[]{:S(2)}) collective-permute-start(bf16[128,1024]{1,0:T(8,128)(2,1)S(1)} %collective-permute-done.38), channel_id=1, source_target_pairs={{0,16},{16,0},{1,17},{17,1},{2,18},{18,2},{3,19},{19,3},{4,20},{20... | collective-permute-start | bytes 786440 | tf_op jit(solution)/shard_map/ppermute | solution.py:48
  121.4 6.4 %collective-permute-start.29 = (bf16[128,1024]{1,0:T(8,128)(2,1)S(1)}, bf16[128,1024]{1,0:T(8,128)(2,1)S(1)}, u32[]{:S(2)}, u32[]{:S(2)}) collective-permute-start(bf16[128,1024]{1,0:T(8,128)(2,1)S(1)} %get-tuple-element.149), channel_id=1, source_target_pairs={{0,4},{1,5},{2,6},{3,7},{4,0},{5,1},{6,2},{7,3},{8,12},{9,13},{10,... | collective-permute-start | bytes 786440 | tf_op jit(solution)/shard_map/ppermute | solution.py:44
  121.5 7.3 %collective-permute-start.28 = (bf16[128,1024]{1,0:T(8,128)(2,1)S(1)}, bf16[128,1024]{1,0:T(8,128)(2,1)S(1)}, u32[]{:S(2)}, u32[]{:S(2)}) collective-permute-start(bf16[128,1024]{1,0:T(8,128)(2,1)S(1)} %get-tuple-element.149), channel_id=1, source_target_pairs={{0,2},{1,3},{2,0},{3,1},{4,6},{5,7},{6,4},{7,5},{8,10},{9,11},{10,... | collective-permute-start | bytes 786440 | tf_op jit(solution)/shard_map/ppermute | solution.py:44
  121.6 15.0 %collective-permute-start.36 = (bf16[256,1024]{1,0:T(8,128)(2,1)}, bf16[256,1024]{1,0:T(8,128)(2,1)S(1)}, u32[]{:S(2)}, u32[]{:S(2)}) collective-permute-start(bf16[256,1024]{1,0:T(8,128)(2,1)} %collective-permute-done.15), channel_id=1, source_target_pairs={{0,16},{16,0},{1,17},{17,1},{2,18},{18,2},{3,19},{19,3},{4,20},{20... | collective-permute-start | bytes 1572872 | tf_op jit(solution)/shard_map/ppermute | solution.py:48
  127.5 7.1 %collective-permute-start.32 = (bf16[128,1024]{1,0:T(8,128)(2,1)S(1)}, bf16[128,1024]{1,0:T(8,128)(2,1)S(1)}, u32[]{:S(2)}, u32[]{:S(2)}) collective-permute-start(bf16[128,1024]{1,0:T(8,128)(2,1)S(1)} %get-tuple-element.149), channel_id=1, source_target_pairs={{0,1},{1,0},{2,3},{3,2},{4,5},{5,4},{6,7},{7,6},{8,9},{9,8},{10,11... | collective-permute-start | bytes 786440 | tf_op jit(solution)/shard_map/ppermute | solution.py:44
  127.9 5.7 %collective-permute-start.30 = (bf16[64,1024]{1,0:T(8,128)(2,1)S(1)}, bf16[64,1024]{1,0:T(8,128)(2,1)S(1)}, u32[]{:S(2)}, u32[]{:S(2)}) collective-permute-start(bf16[64,1024]{1,0:T(8,128)(2,1)S(1)} %slice.432), channel_id=1, source_target_pairs={{0,2},{1,3},{2,0},{3,1},{4,6},{5,7},{6,4},{7,5},{8,10},{9,11},{10,... | collective-permute-start | bytes 393224 | tf_op jit(solution)/shard_map/ppermute | solution.py:44
  128.9 5.7 %collective-permute-start.31 = (bf16[64,1024]{1,0:T(8,128)(2,1)S(1)}, bf16[64,1024]{1,0:T(8,128)(2,1)S(1)}, u32[]{:S(2)}, u32[]{:S(2)}) collective-permute-start(bf16[64,1024]{1,0:T(8,128)(2,1)S(1)} %slice.433), channel_id=1, source_target_pairs={{0,4},{1,5},{2,6},{3,7},{4,0},{5,1},{6,2},{7,3},{8,12},{9,13},{10,... | collective-permute-start | bytes 393224 | tf_op jit(solution)/shard_map/ppermute | solution.py:44
  149.9 5.7 %collective-permute-start.41 = (bf16[64,1024]{1,0:T(8,128)(2,1)S(1)}, bf16[64,1024]{1,0:T(8,128)(2,1)}, u32[]{:S(2)}, u32[]{:S(2)}) collective-permute-start(bf16[64,1024]{1,0:T(8,128)(2,1)S(1)} %get-tuple-element.179), channel_id=1, source_target_pairs={{0,4},{1,5},{2,6},{3,7},{4,0},{5,1},{6,2},{7,3},{8,12},{9,13},{10,... | collective-permute-start | bytes 393224 | tf_op jit(solution)/shard_map/ppermute | solution.py:44
  158.3 7.5 %collective-permute-start.44 = (bf16[128,1024]{1,0:T(8,128)(2,1)}, bf16[128,1024]{1,0:T(8,128)(2,1)}, u32[]{:S(2)}, u32[]{:S(2)}) collective-permute-start(bf16[128,1024]{1,0:T(8,128)(2,1)} %pad_maximum_fusion.17), channel_id=1, source_target_pairs={{0,4},{1,5},{2,6},{3,7},{4,0},{5,1},{6,2},{7,3},{8,12},{9,13},{10,... | collective-permute-start | bytes 786440 | tf_op jit(solution)/shard_map/ppermute | solution.py:44
  159.8 7.3 %collective-permute-start.42 = (bf16[128,1024]{1,0:T(8,128)(2,1)}, bf16[128,1024]{1,0:T(8,128)(2,1)}, u32[]{:S(2)}, u32[]{:S(2)}) collective-permute-start(bf16[128,1024]{1,0:T(8,128)(2,1)} %pad_maximum_fusion.16), channel_id=1, source_target_pairs={{0,2},{1,3},{2,0},{3,1},{4,6},{5,7},{6,4},{7,5},{8,10},{9,11},{10,... | collective-permute-start | bytes 786440 | tf_op jit(solution)/shard_map/ppermute | solution.py:44
  169.1 8.5 %collective-permute-start.45 = (bf16[128,1024]{1,0:T(8,128)(2,1)S(1)}, bf16[128,1024]{1,0:T(8,128)(2,1)S(1)}, u32[]{:S(2)}, u32[]{:S(2)}) collective-permute-start(bf16[128,1024]{1,0:T(8,128)(2,1)S(1)} %get-tuple-element.144), channel_id=1, source_target_pairs={{0,2},{1,3},{2,0},{3,1},{4,6},{5,7},{6,4},{7,5},{8,10},{9,11},{10,... | collective-permute-start | bytes 786440 | tf_op jit(solution)/shard_map/ppermute | solution.py:44
  170.0 6.4 %collective-permute-start.46 = (bf16[128,1024]{1,0:T(8,128)(2,1)S(1)}, bf16[128,1024]{1,0:T(8,128)(2,1)S(1)}, u32[]{:S(2)}, u32[]{:S(2)}) collective-permute-start(bf16[128,1024]{1,0:T(8,128)(2,1)S(1)} %get-tuple-element.144), channel_id=1, source_target_pairs={{0,4},{1,5},{2,6},{3,7},{4,0},{5,1},{6,2},{7,3},{8,12},{9,13},{10,... | collective-permute-start | bytes 786440 | tf_op jit(solution)/shard_map/ppermute | solution.py:44
  172.2 10.5 %collective-permute-start.49 = (bf16[128,1024]{1,0:T(8,128)(2,1)S(1)}, bf16[128,1024]{1,0:T(8,128)(2,1)S(1)}, u32[]{:S(2)}, u32[]{:S(2)}) collective-permute-start(bf16[128,1024]{1,0:T(8,128)(2,1)S(1)} %get-tuple-element.144), channel_id=1, source_target_pairs={{0,1},{1,0},{2,3},{3,2},{4,5},{5,4},{6,7},{7,6},{8,9},{9,8},{10,11... | collective-permute-start | bytes 786440 | tf_op jit(solution)/shard_map/ppermute | solution.py:44
  189.6 6.8 %collective-permute-start.53 = (bf16[512,1024]{1,0:T(8,128)(2,1)S(1)}, bf16[512,1024]{1,0:T(8,128)(2,1)S(1)}, u32[]{:S(2)}, u32[]{:S(2)}) collective-permute-start(bf16[512,1024]{1,0:T(8,128)(2,1)S(1)} %convolution_convert_fusion.2), channel_id=1, source_target_pairs={{0,1},{1,0},{2,3},{3,2},{4,5},{5,4},{6,7},{7,6},{8,9},{9,8},{10,11... | collective-permute-start | bytes 3145736 | tf_op jit(solution)/shard_map/ppermute | solution.py:44
  195.6 41.4 %collective-permute-start.67 = (bf16[2,256,1024]{2,1,0:T(8,128)(2,1)}, bf16[2,256,1024]{2,1,0:T(8,128)(2,1)}, u32[]{:S(2)}, u32[]{:S(2)}) collective-permute-start(bf16[2,256,1024]{2,1,0:T(8,128)(2,1)} %bitcast.46), channel_id=1, source_target_pairs={{0,16},{16,0},{1,17},{17,1},{2,18},{18,2},{3,19},{19,3},{4,20},{20... | collective-permute-start | bytes 3145736 | tf_op jit(solution)/shard_map/ppermute | solution.py:48
  206.1 7.3 %collective-permute-start.57 = (bf16[128,1024]{1,0:T(8,128)(2,1)S(1)}, bf16[128,1024]{1,0:T(8,128)(2,1)S(1)}, u32[]{:S(2)}, u32[]{:S(2)}) collective-permute-start(bf16[128,1024]{1,0:T(8,128)(2,1)S(1)} %pad_maximum_fusion.20), channel_id=1, source_target_pairs={{0,4},{1,5},{2,6},{3,7},{4,0},{5,1},{6,2},{7,3},{8,12},{9,13},{10,... | collective-permute-start | bytes 786440 | tf_op jit(solution)/shard_map/ppermute | solution.py:44
  207.0 7.0 %collective-permute-start.55 = (bf16[128,1024]{1,0:T(8,128)(2,1)S(1)}, bf16[128,1024]{1,0:T(8,128)(2,1)S(1)}, u32[]{:S(2)}, u32[]{:S(2)}) collective-permute-start(bf16[128,1024]{1,0:T(8,128)(2,1)S(1)} %pad_maximum_fusion.19), channel_id=1, source_target_pairs={{0,2},{1,3},{2,0},{3,1},{4,6},{5,7},{6,4},{7,5},{8,10},{9,11},{10,... | collective-permute-start | bytes 786440 | tf_op jit(solution)/shard_map/ppermute | solution.py:44
  209.2 89.4 %collective-permute-start.86 = (bf16[2,128,1024]{2,1,0:T(8,128)(2,1)}, bf16[2,128,1024]{2,1,0:T(8,128)(2,1)}, u32[]{:S(2)}, u32[]{:S(2)}) collective-permute-start(bf16[2,128,1024]{2,1,0:T(8,128)(2,1)} %fusion.10), channel_id=1, source_target_pairs={{0,16},{16,0},{1,17},{17,1},{2,18},{18,2},{3,19},{19,3},{4,20},{20... | collective-permute-start | bytes 1572872 | tf_op jit(solution)/shard_map/ppermute | solution.py:48
  216.2 8.7 %collective-permute-start.58 = (bf16[128,1024]{1,0:T(8,128)(2,1)}, bf16[128,1024]{1,0:T(8,128)(2,1)S(1)}, u32[]{:S(2)}, u32[]{:S(2)}) collective-permute-start(bf16[128,1024]{1,0:T(8,128)(2,1)} %get-tuple-element.143), channel_id=1, source_target_pairs={{0,2},{1,3},{2,0},{3,1},{4,6},{5,7},{6,4},{7,5},{8,10},{9,11},{10,... | collective-permute-start | bytes 786440 | tf_op jit(solution)/shard_map/ppermute | solution.py:44
  217.5 6.6 %collective-permute-start.59 = (bf16[128,1024]{1,0:T(8,128)(2,1)}, bf16[128,1024]{1,0:T(8,128)(2,1)S(1)}, u32[]{:S(2)}, u32[]{:S(2)}) collective-permute-start(bf16[128,1024]{1,0:T(8,128)(2,1)} %get-tuple-element.143), channel_id=1, source_target_pairs={{0,4},{1,5},{2,6},{3,7},{4,0},{5,1},{6,2},{7,3},{8,12},{9,13},{10,... | collective-permute-start | bytes 786440 | tf_op jit(solution)/shard_map/ppermute | solution.py:44
  219.8 10.2 %collective-permute-start.62 = (bf16[128,1024]{1,0:T(8,128)(2,1)}, bf16[128,1024]{1,0:T(8,128)(2,1)}, u32[]{:S(2)}, u32[]{:S(2)}) collective-permute-start(bf16[128,1024]{1,0:T(8,128)(2,1)} %get-tuple-element.143), channel_id=1, source_target_pairs={{0,1},{1,0},{2,3},{3,2},{4,5},{5,4},{6,7},{7,6},{8,9},{9,8},{10,11... | collective-permute-start | bytes 786440 | tf_op jit(solution)/shard_map/ppermute | solution.py:44
  233.3 9.7 %collective-permute-start.66 = (bf16[512,128]{1,0:T(8,128)(2,1)S(1)}, bf16[512,128]{1,0:T(8,128)(2,1)S(1)}, u32[]{:S(2)}, u32[]{:S(2)}) collective-permute-start(bf16[512,128]{1,0:T(8,128)(2,1)S(1)} %bitcast.254), channel_id=1, source_target_pairs={{0,8},{1,9},{2,10},{3,11},{4,12},{5,13},{6,14},{7,15},{8,0},{9,1},... | collective-permute-start | bytes 393224 | tf_op jit(solution)/shard_map/ppermute | solution.py:44
  247.6 25.8 %collective-permute-start.68 = (bf16[1,256,1024]{2,1,0:T(8,128)(2,1)}, bf16[1,256,1024]{2,1,0:T(8,128)(2,1)}, u32[]{:S(2)}, u32[]{:S(2)}) collective-permute-start(bf16[1,256,1024]{2,1,0:T(8,128)(2,1)} %fusion.11), channel_id=1, source_target_pairs={{0,8},{1,9},{2,10},{3,11},{4,12},{5,13},{6,14},{7,15},{8,0},{9,1},... | collective-permute-start | bytes 1572872 | tf_op jit(solution)/shard_map/ppermute | solution.py:44
  275.7 19.8 %collective-permute-start.74 = (bf16[512,384]{1,0:T(8,128)(2,1)S(1)}, bf16[512,384]{1,0:T(8,128)(2,1)S(1)}, u32[]{:S(2)}, u32[]{:S(2)}) collective-permute-start(bf16[512,384]{1,0:T(8,128)(2,1)S(1)} %copy-done.34), channel_id=1, source_target_pairs={{0,8},{1,9},{2,10},{3,11},{4,12},{5,13},{6,14},{7,15},{8,0},{9,1},... | collective-permute-start | bytes 1179656 | tf_op jit(solution)/shard_map/ppermute | solution.py:44
  282.1 20.9 %collective-permute-start.80 = (bf16[4,2,32,1024]{3,2,0,1:T(8,128)(2,1)S(1)}, bf16[4,2,32,1024]{3,2,0,1:T(8,128)(2,1)S(1)}, u32[]{:S(2)}, u32[]{:S(2)}) collective-permute-start(bf16[4,2,32,1024]{3,2,0,1:T(8,128)(2,1)S(1)} %fusion.9), channel_id=1, source_target_pairs={{0,16},{16,0},{1,17},{17,1},{2,18},{18,2},{3,19},{19,3},{4,20},{20... | collective-permute-start | bytes 1572872 | tf_op jit(solution)/shard_map/ppermute | solution.py:48
  284.5 14.0 %collective-permute-start.72 = (f32[3,1024]{1,0:T(4,128)S(1)}, f32[3,1024]{1,0:T(4,128)S(1)}, u32[]{:S(2)}, u32[]{:S(2)}) collective-permute-start(f32[3,1024]{1,0:T(4,128)S(1)} %add.210), channel_id=1, source_target_pairs={{0,4},{1,5},{2,6},{3,7},{4,0},{5,1},{6,2},{7,3},{8,12},{9,13},{10,... | collective-permute-start | bytes 36872 | tf_op jit(solution)/shard_map/ppermute | solution.py:44
  296.3 7.0 %collective-permute-start.75 = (bf16[512,1024]{1,0:T(8,128)(2,1)S(1)}, bf16[512,1024]{1,0:T(8,128)(2,1)S(1)}, u32[]{:S(2)}, u32[]{:S(2)}) collective-permute-start(bf16[512,1024]{1,0:T(8,128)(2,1)S(1)} %convolution_convert_fusion.1), channel_id=1, source_target_pairs={{0,1},{1,0},{2,3},{3,2},{4,5},{5,4},{6,7},{7,6},{8,9},{9,8},{10,11... | collective-permute-start | bytes 3145736 | tf_op jit(solution)/shard_map/ppermute | solution.py:44
  298.6 22.9 %collective-permute-start.73 = (f32[3,1024]{1,0:T(4,128)S(1)}, f32[3,1024]{1,0:T(4,128)S(1)}, u32[]{:S(2)}, u32[]{:S(2)}) collective-permute-start(f32[3,1024]{1,0:T(4,128)S(1)} %add.211), channel_id=1, source_target_pairs={{0,8},{1,9},{2,10},{3,11},{4,12},{5,13},{6,14},{7,15},{8,0},{9,1},... | collective-permute-start | bytes 36872 | tf_op jit(solution)/shard_map/ppermute | solution.py:44
  300.0 21.4 %collective-permute-start.87 = (bf16[1,128,1024]{2,1,0:T(8,128)(2,1)S(1)}, bf16[1,128,1024]{2,1,0:T(8,128)(2,1)S(1)}, u32[]{:S(2)}, u32[]{:S(2)}) collective-permute-start(bf16[1,128,1024]{2,1,0:T(8,128)(2,1)S(1)} %fusion.38), channel_id=1, source_target_pairs={{0,8},{1,9},{2,10},{3,11},{4,12},{5,13},{6,14},{7,15},{8,0},{9,1},... | collective-permute-start | bytes 786440 | tf_op jit(solution)/shard_map/ppermute | solution.py:44
  305.0 7.4 %collective-permute-start.77 = (bf16[64,1024]{1,0:T(8,128)(2,1)S(1)}, bf16[64,1024]{1,0:T(8,128)(2,1)S(1)}, u32[]{:S(2)}, u32[]{:S(2)}) collective-permute-start(bf16[64,1024]{1,0:T(8,128)(2,1)S(1)} %get-tuple-element.170), channel_id=1, source_target_pairs={{0,4},{1,5},{2,6},{3,7},{4,0},{5,1},{6,2},{7,3},{8,12},{9,13},{10,... | collective-permute-start | bytes 393224 | tf_op jit(solution)/shard_map/ppermute | solution.py:44
  305.4 22.0 %collective-permute-start.81 = (bf16[4,1,32,1024]{3,2,1,0:T(8,128)(2,1)S(1)}, bf16[4,1,32,1024]{3,2,1,0:T(8,128)(2,1)S(1)}, u32[]{:S(2)}, u32[]{:S(2)}) collective-permute-start(bf16[4,1,32,1024]{3,2,1,0:T(8,128)(2,1)S(1)} %fusion.36), channel_id=1, source_target_pairs={{0,8},{1,9},{2,10},{3,11},{4,12},{5,13},{6,14},{7,15},{8,0},{9,1},... | collective-permute-start | bytes 786440 | tf_op jit(solution)/shard_map/ppermute | solution.py:44
  312.6 14.4 %collective-permute-start.79 = (bf16[128,1024]{1,0:T(8,128)(2,1)S(1)}, bf16[128,1024]{1,0:T(8,128)(2,1)S(1)}, u32[]{:S(2)}, u32[]{:S(2)}) collective-permute-start(bf16[128,1024]{1,0:T(8,128)(2,1)S(1)} %pad_maximum_fusion.23), channel_id=1, source_target_pairs={{0,4},{1,5},{2,6},{3,7},{4,0},{5,1},{6,2},{7,3},{8,12},{9,13},{10,... | collective-permute-start | bytes 786440 | tf_op jit(solution)/shard_map/ppermute | solution.py:44
  315.1 11.8 %collective-permute-start.78 = (bf16[128,1024]{1,0:T(8,128)(2,1)S(1)}, bf16[128,1024]{1,0:T(8,128)(2,1)S(1)}, u32[]{:S(2)}, u32[]{:S(2)}) collective-permute-start(bf16[128,1024]{1,0:T(8,128)(2,1)S(1)} %pad_maximum_fusion.22), channel_id=1, source_target_pairs={{0,2},{1,3},{2,0},{3,1},{4,6},{5,7},{6,4},{7,5},{8,10},{9,11},{10,... | collective-permute-start | bytes 786440 | tf_op jit(solution)/shard_map/ppermute | solution.py:44
  322.7 19.6 %collective-permute-start.88 = (bf16[128,1024]{1,0:T(8,128)(2,1)S(1)}, bf16[128,1024]{1,0:T(8,128)(2,1)S(1)}, u32[]{:S(2)}, u32[]{:S(2)}) collective-permute-start(bf16[128,1024]{1,0:T(8,128)(2,1)S(1)} %fusion.37), channel_id=1, source_target_pairs={{0,0},{16,1},{1,2},{17,3},{2,4},{18,5},{3,6},{19,7},{4,8},{20,9},{... | collective-permute-start | bytes 786440 | tf_op jit(solution)/shard_map/ppermute | solution.py:442
  327.6 21.3 %collective-permute-start.84 = (bf16[32,1024]{1,0:T(8,128)(2,1)S(1)}, bf16[32,1024]{1,0:T(8,128)(2,1)S(1)}, u32[]{:S(2)}, u32[]{:S(2)}) collective-permute-start(bf16[32,1024]{1,0:T(8,128)(2,1)S(1)} %get-tuple-element.194), channel_id=1, source_target_pairs={{16,0},{9,1},{2,2},{26,3},{19,4},{12,5},{5,6},{29,7},{22,8},{15,9}... | collective-permute-start | bytes 196616 | tf_op jit(solution)/shard_map/ppermute | solution.py:469
  328.2 20.6 %collective-permute-start.83 = (bf16[32,1024]{1,0:T(8,128)(2,1)S(1)}, bf16[32,1024]{1,0:T(8,128)(2,1)S(1)}, u32[]{:S(2)}, u32[]{:S(2)}) collective-permute-start(bf16[32,1024]{1,0:T(8,128)(2,1)S(1)} %get-tuple-element.193), channel_id=1, source_target_pairs={{8,0},{1,1},{25,2},{18,3},{11,4},{4,5},{28,6},{21,7},{14,8},{7,9},... | collective-permute-start | bytes 196616 | tf_op jit(solution)/shard_map/ppermute | solution.py:469
  334.2 14.6 %collective-permute-start.82 = (bf16[32,1024]{1,0:T(8,128)(2,1)S(1)}, bf16[32,1024]{1,0:T(8,128)(2,1)S(1)}, u32[]{:S(2)}, u32[]{:S(2)}) collective-permute-start(bf16[32,1024]{1,0:T(8,128)(2,1)S(1)} %get-tuple-element.192), channel_id=1, source_target_pairs={{0,0},{24,1},{17,2},{10,3},{3,4},{27,5},{20,6},{13,7},{6,8},{30,9}... | collective-permute-start | bytes 196616 | tf_op jit(solution)/shard_map/ppermute | solution.py:469
  339.5 8.6 %collective-permute-start.85 = (bf16[32,1024]{1,0:T(8,128)(2,1)S(1)}, bf16[32,1024]{1,0:T(8,128)(2,1)S(1)}, u32[]{:S(2)}, u32[]{:S(2)}) collective-permute-start(bf16[32,1024]{1,0:T(8,128)(2,1)S(1)} %get-tuple-element.191), channel_id=1, source_target_pairs={{0,0},{8,1},{16,2},{24,3},{1,4},{9,5},{17,6},{25,7},{2,8},{10,9},{... | collective-permute-start | bytes 196616 | tf_op jit(solution)/shard_map/ppermute | solution.py:467
  (64 other events, 548.3 us)

commit v4 on v3

--- a/solution.py
+++ b/solution.py
@@ -313,10 +313,9 @@
     x_got = other_micro(own_in[1])
     down_rows = lax.ppermute(mlp_out, BOTH, [(b, (b % 2) * n_seq + b // 2) for b in range(n_dev)])
     arrived = [lax.ppermute(own_units[t], BOTH, [(i, home(3 * i + t)) for i in range(n_dev)]) for t in range(3)]
+    arrived.append(lax.ppermute(attn_out, BOTH, [(i, home(i)) for i in range(n_dev)]))
     x_pair = jnp.concatenate([own_in[0], x_got], 0)
-    x_pair, arrived, late_in = joint(x_pair, arrived, mlp_in)
-    ffn_here = far_spread(late_in, n_seq)
-    ffn_there = [swap_dp(late_in)]
+    x_pair, arrived = joint(x_pair, arrived)
 
     x_blocks = cube_gather(x_pair, n_seq)
     if n_parts > 1:
@@ -327,8 +326,8 @@
         return jnp.where(keys[0] == key, values[0], jnp.where(keys[1] == key, values[1], values[2]))
 
     arrived = after(arrived, x_blocks[4])
-    my_thirds = jnp.stack([pick(thirds, arrived, third) for third in range(3)])
-    here = far_spread(my_thirds, n_seq)
+    my_blocks = jnp.stack([pick(thirds, arrived, third) for third in range(3)] + [arrived[3]])
+    here = far_spread(my_blocks, n_seq)
     there = [swap_dp(v) for v in here]
 
     def by_share(here, there, at):
@@ -343,20 +342,18 @@
         second = jnp.where(dp == 0, order[1], order[0])
         return jnp.stack([first, second], at)
 
-    pair_w = by_share(here, there, 1).reshape(3 * PAIR_DIM, width)
+    head_w = by_share(here, there, 1).reshape(4 * PAIR_DIM, width)
+    pair_w, out_w = head_w[: 3 * PAIR_DIM], head_w[3 * PAIR_DIM :]
 
     prefix_len = jnp.where(micro == 0, prefix[0, 0], prefix[1, 0])
     where = jnp.stack([micro, member, part * rows_q, prefix_len]).astype(jnp.int32)
-    x_blocks, pair_w, ffn_here, ffn_there, down_rows, late_out = joint(
-        x_blocks, pair_w, ffn_here, ffn_there, down_rows, attn_out
-    )
+    x_blocks, pair_w, out_w, late_in = joint(x_blocks, pair_w, out_w, mlp_in)
+    ffn_here = far_spread(late_in, n_seq)
+    ffn_there = [swap_dp(late_in)]
+    first_in, mixed, att_keep, att_give = attend(where, x_blocks, pair_w, gain_one, rows_q)
+    att_give, att_keep, ffn_here, ffn_there, down_rows = joint(att_give, att_keep, ffn_here, ffn_there, down_rows)
     down_here = far_spread(down_rows, n_seq)
     down_there = [swap_dp(down_rows)]
-    out_rows = lax.ppermute(late_out, BOTH, [(i, home(i)) for i in range(n_dev)])
-    first_in, mixed, att_keep, att_give = attend(where, x_blocks, pair_w, gain_one, rows_q)
-    att_give, out_rows = joint(att_give, out_rows)
-    out_here = far_spread(out_rows, n_seq)
-    out_w = by_share(out_here, [swap_dp(v) for v in out_here], 0).reshape(PAIR_DIM, width)
     att_got = other_micro(att_give)
 
     ffn_there += [swap_dp(v) for v in after(ffn_here[1:], att_got)]
@@ -412,7 +409,8 @@
 
     in_terms = in_terms + after(in_got, grad_got).astype(F32)
     in_pairs = in_terms.reshape((n_far // 2, 2) + in_terms.shape[1:])
-    in_low = swap_seq(in_pairs[:, 1].astype(BF16), 8, n_seq)
+    half_rows = in_rows // 2
+    in_low = swap_seq(in_pairs[:, 1, :half_rows].astype(BF16), 8, n_seq)
     grads = attend_back(where, mixed, grad_keep, grad_got)
     if n_parts > 1:
         grad_k, grad_v = (
@@ -432,10 +430,19 @@
     )
     mixed_got = other_micro(mixed_give)
 
+    pair_terms = tn(grad_mixed, first_part)
+    gain_term = jnp.sum(pair_terms * pair_w.astype(F32), axis=0) / gain_one[0]
+    terms = jnp.concatenate([pair_terms, tn(attended, middle_low)], 0).reshape(4, n_dp, n_far, unit, width)
+    terms_got = swap_dp(jnp.where(dp == 0, terms[:, 1], terms[:, 0]).astype(BF16))
+    mixed_got, terms_got = joint(mixed_got, terms_got)
+    terms = jnp.where(dp == 0, terms[:, 0], terms[:, 1]) + terms_got.astype(F32)
+
     mixed_rows = jnp.stack([v.reshape(8, tok, 3 * PAIR_DIM) for v in (mixed_keep, mixed_got)], 1)
-    grad_first, last, _ = cube_reduce(
-        lambda v: nn(v, pair_w), mixed_rows.reshape(8 * rows, 3 * PAIR_DIM), n_seq
+    in_rest = swap_seq(after(in_pairs, mixed_got)[:, 1, half_rows:].astype(BF16), 8, n_seq)
+    grad_first, last, in_rest = cube_reduce(
+        lambda v: nn(v, pair_w), mixed_rows.reshape(8 * rows, 3 * PAIR_DIM), n_seq, in_rest
     )
+    in_low = after(jnp.concatenate([in_low, in_rest], 1), grad_first)
     mlp_in_grad = far_reduce(in_pairs[:, 0] + in_low.astype(F32), [grad_first], n_seq, 16)
     down_terms = down_terms + after(down_got, mixed_got).astype(F32)
     down_sum = far_reduce(down_terms, [last], n_seq)
@@ -447,23 +454,15 @@
     input_grad = grad_middle + norm_back(grad_first, source * scale_one, scale_one, gain_one)
     mlp_out_grad = after(mlp_out_grad, grad_first).astype(F32)
 
-    def share_reduce(terms, gates):
-        give = jnp.where(dp == 0, terms[:, 1], terms[:, 0]).astype(BF16)
-        terms = jnp.where(dp == 0, terms[:, 0], terms[:, 1]) + after(swap_dp(give), gates[0]).astype(F32)
-        bits = 8
-        while bits < n_seq:
-            on = (seq // bits) % 2
-            pairs = terms.reshape((terms.shape[0], terms.shape[1] // 2, 2) + terms.shape[2:])
-            give = jnp.where(on == 0, pairs[:, :, 1], pairs[:, :, 0]).astype(BF16)
-            got = after(swap_seq(give, bits, n_seq), gates[1])
-            terms = jnp.where(on == 0, pairs[:, :, 0], pairs[:, :, 1]) + got.astype(F32)
-            bits *= 2
-        return terms[:, 0].astype(BF16)
-
-    pair_terms = tn(grad_mixed, first_part)
-    gain_term = jnp.sum(pair_terms * pair_w.astype(F32), axis=0) / gain_one[0]
-    terms = jnp.concatenate([pair_terms, tn(attended, middle_low)], 0).reshape(4, n_dp, n_far, unit, width)
-    terms = share_reduce(terms, [mixed_got, grad_first])
+    bits = 8
+    while bits < n_seq:
+        on = (seq // bits) % 2
+        pairs = terms.reshape((terms.shape[0], terms.shape[1] // 2, 2) + terms.shape[2:])
+        give = jnp.where(on == 0, pairs[:, :, 1], pairs[:, :, 0]).astype(BF16)
+        got = after(swap_seq(give, bits, n_seq), grad_first)
+        terms = jnp.where(on == 0, pairs[:, :, 0], pairs[:, :, 1]) + got.astype(F32)
+        bits *= 2
+    terms = terms[:, 0].astype(BF16)
     attn_out_grad = lax.ppermute(terms[3], BOTH, [(home(i), i) for i in range(n_dev)]).astype(F32)
     returned = [
         lax.ppermute(

time: 353 us -> 343 us (0.972)
  starting transfers between devices: 99 us -> 92.3 us
  waiting for transfers between devices: 146 us -> 152 us
  matrix products: 25.9 us -> 21.2 us
    ppermute x67, starting transfers between devices: 58.1 us -> 48.1 us  [swap_seq(): return lax.ppermute(value, 'seq', [(i, i ^ bits) for i in range(n_seq)])]
    ppermute x1, waiting for transfers between devices: 0.01 us -> 6.15 us  [shards(): lax.ppermute(attn_out, BOTH, [(i, home(i)) for i in range(n_dev)])]
    dot_general x3, matrix products: 9.54 us -> 4.98 us  [nt(): lax.dot_general(left, right, (((1,), (1,)), ((), ())), preferred_element_...]
    ppermute x12 -> x10, starting transfers between devices: 10.8 us -> 13.8 us  [swap_dp(): return lax.ppermute(value, 'dp', [(0, 1), (1, 0)])]
    unnamed x101 -> x133, local copies, waits for them, and re-layouts: 7.52 us -> 5.39 us
    ppermute x12 -> x10, waiting for transfers between devices: 12.6 us -> 12.8 us  [swap_dp(): return lax.ppermute(value, 'dp', [(0, 1), (1, 0)])]
  transfers between devices with their start and end apart: 89 -> 87, of which waited for: 47 -> 50; matrix products, arithmetic and copies ran while one was open for 14% -> 12% of each run, Pallas kernels for 7% -> 7%
where the time goes in v4:
time: 343 us; the launch traced here: 341 us
  waiting for transfers between devices  152 us (44%)
  starting transfers between devices  92.3 us (27%)
  other arithmetic  29.9 us (9%)
  Pallas kernels  23.4 us (7%)
  matrix products  21.2 us (6%)
  local copies, waits for them, and re-layouts  17.9 us (5%)
  between operations  4.3 us (1%)
    ppermute x67, waiting for transfers between devices, swap_seq(): return lax.ppermute(value, 'seq', [(i, i ^ bits) for i in range(n_seq)])  130 us
    ppermute x67, starting transfers between devices, swap_seq(): return lax.ppermute(value, 'seq', [(i, i ^ bits) for i in range(n_seq)])  48.1 us
    ppermute x10, starting transfers between devices, swap_dp(): return lax.ppermute(value, 'dp', [(0, 1), (1, 0)])  13.8 us
    ppermute x10, waiting for transfers between devices, swap_dp(): return lax.ppermute(value, 'dp', [(0, 1), (1, 0)])  12.8 us
    ppermute x3, starting transfers between devices, shards(): lax.ppermute(jnp.where(thirds[t] == 0, terms[0], jnp.where(thirds[t] == 1...  12.6 us
    pallas_call x1, Pallas kernels, attend(): pl.pallas_call(attend_kernel, out_shape=(jax.ShapeDtypeStruct((rows_k, wi...  11.9 us
    pallas_call x1, Pallas kernels, attend_back(): pl.pallas_call(attend_back_kernel, out_shape=(jax.ShapeDtypeStruct((rows_...  11.5 us
    dot_general x8, matrix products, nn(): return jnp.dot(left, right, preferred_element_type=F32)  8.66 us
  transfers between devices with their start and end apart: 87, of which 50 were waited for; matrix products, arithmetic and copies ran while one was open for 12% of the time, Pallas kernels for 7%

profile of v4, /device:TPU:2, one launch (start us, length us, event | category | flops | bytes accessed | tf_op | source)
XLA Modules:
  0.0 341.2 jit_solution(8102508824719448445)
XLA Ops:
  0.7 1.8 fusion.33
  2.5 2.7 collective-permute-start
  6.0 2.6 collective-permute-start.1
  8.6 3.7 %collective-permute-start.2 = (bf16[32,1024]{1,0:T(8,128)(2,1)S(1)}, bf16[32,1024]{1,0:T(8,128)(2,1)S(1)}, u32[]{:S(2)}, u32[]{:S(2)}) collective-permute-start(bf16[32,1024]{1,0:T(8,128)(2,1)S(1)} %get-tuple-element.217), channel_id=1, source_target_pairs={{0,8},{1,1},{2,25},{3,18},{4,11},{5,4},{6,28},{7,21},{8,14},{9,7},... | collective-permute-start | bytes 196616 | tf_op jit(solution)/shard_map/ppermute | solution.py:315
  13.0 5.1 %collective-permute-start.4 = (bf16[32,1024]{1,0:T(8,128)(2,1)}, bf16[32,1024]{1,0:T(8,128)(2,1)S(1)}, u32[]{:S(2)}, u32[]{:S(2)}) collective-permute-start(bf16[32,1024]{1,0:T(8,128)(2,1)} %param.20), channel_id=1, source_target_pairs={{0,0},{1,8},{2,16},{3,24},{4,1},{5,9},{6,17},{7,25},{8,2},{9,10},{... | collective-permute-start | bytes 196616 | tf_op jit(solution)/shard_map/ppermute | solution.py:316
  18.2 6.2 %collective-permute-done.4 = bf16[32,1024]{1,0:T(8,128)(2,1)S(1)} collective-permute-done((bf16[32,1024]{1,0:T(8,128)(2,1)}, bf16[32,1024]{1,0:T(8,128)(2,1)S(1)}, u32[]{:S(2)}, u32[]{:S(2)}) %collective-permute-start.4) | collective-permute-done | bytes 65568 | tf_op jit(solution)/shard_map/ppermute | solution.py:316
  24.4 1.9 collective-permute-start.18
  26.5 3.6 %collective-permute-start.6 = (bf16[128,1024]{1,0:T(8,128)(2,1)S(1)}, bf16[128,1024]{1,0:T(8,128)(2,1)}, u32[]{:S(2)}, u32[]{:S(2)}) collective-permute-start(bf16[128,1024]{1,0:T(8,128)(2,1)S(1)} %pad_maximum_fusion.12.refs_0_), channel_id=1, source_target_pairs={{0,4},{1,5},{2,6},{3,7},{4,0},{5,1},{6,2},{7,3},{8,12},{9,13},{10,... | collective-permute-start | bytes 786440 | tf_op jit(solution)/shard_map/ppermute | solution.py:44
  30.2 4.4 %collective-permute-start.13 = (bf16[4,32,1024]{2,1,0:T(8,128)(2,1)S(1)}, bf16[4,32,1024]{2,1,0:T(8,128)(2,1)S(1)}, u32[]{:S(2)}, u32[]{:S(2)}) collective-permute-start(bf16[4,32,1024]{2,1,0:T(8,128)(2,1)S(1)} %get-tuple-element.209), channel_id=1, source_target_pairs={{0,8},{1,9},{2,10},{3,11},{4,12},{5,13},{6,14},{7,15},{8,0},{9,1},... | collective-permute-start | bytes 786440 | tf_op jit(solution)/shard_map/ppermute | solution.py:44
  34.5 7.7 %collective-permute-done.6.refs_2_ = bf16[128,1024]{1,0:T(8,128)(2,1)} collective-permute-done((bf16[128,1024]{1,0:T(8,128)(2,1)S(1)}, bf16[128,1024]{1,0:T(8,128)(2,1)}, u32[]{:S(2)}, u32[]{:S(2)}) %collective-permute-start.6) | collective-permute-done | bytes 262176 | tf_op jit(solution)/shard_map/ppermute | solution.py:44
  44.4 2.8 collective-permute-start.14
  48.2 3.9 %collective-permute-done.13 = bf16[4,32,1024]{2,1,0:T(8,128)(2,1)S(1)} collective-permute-done((bf16[4,32,1024]{2,1,0:T(8,128)(2,1)S(1)}, bf16[4,32,1024]{2,1,0:T(8,128)(2,1)S(1)}, u32[]{:S(2)}, u32[]{:S(2)}) %collective-permute-start.13) | collective-permute-done | bytes 262176 | tf_op jit(solution)/shard_map/ppermute | solution.py:44
  52.1 1.7 collective-permute-done.8
  55.8 4.3 %collective-permute-done.15 = bf16[4,32,1024]{2,1,0:T(8,128)(2,1)S(1)} collective-permute-done((bf16[4,32,1024]{2,1,0:T(8,128)(2,1)S(1)}, bf16[4,32,1024]{2,1,0:T(8,128)(2,1)S(1)}, u32[]{:S(2)}, u32[]{:S(2)}) %collective-permute-start.15) | collective-permute-done | bytes 262176 | tf_op jit(solution)/shard_map/ppermute | solution.py:48
  67.5 11.9 %shard_map.152 = (bf16[1024,1024]{1,0:T(8,128)(2,1)}, bf16[1024,384]{1,0:T(8,128)(2,1)}, bf16[512,128]{1,0:T(8,128)(2,1)}, bf16[512,128]{1,0:T(8,128)(2,1)}) custom-call(s32[4]{0:T(128)} %pad_add_fusion.where_ref, bf16[128,1024]{1,0:T(8,128)(2,1)} %copy-done.22, bf16[128,1024]{1,0:T(8,128)(2,1)} %collective-permute-done.5.refs_1_, ...), custom_call_target="tpu_custom_call" | custom-call | flops 1342177280 | bytes 4194304 | tf_op jit(solution)/shard_map/pallas_call | solution.py:181
  79.4 6.9 %collective-permute-done.16 = bf16[256,1024]{1,0:T(8,128)(2,1)S(1)} collective-permute-done((bf16[256,1024]{1,0:T(8,128)(2,1)S(1)}, bf16[256,1024]{1,0:T(8,128)(2,1)S(1)}, u32[]{:S(2)}, u32[]{:S(2)}) %collective-permute-start.16) | collective-permute-done | bytes 524320 | tf_op jit(solution)/shard_map/ppermute | solution.py:44
  86.4 8.8 %collective-permute-done.19 = bf16[512,128]{1,0:T(8,128)(2,1)S(1)} collective-permute-done((bf16[512,128]{1,0:T(8,128)(2,1)}, bf16[512,128]{1,0:T(8,128)(2,1)S(1)}, u32[]{:S(2)}, u32[]{:S(2)}) %collective-permute-start.19) | collective-permute-done | bytes 131104 | tf_op jit(solution)/shard_map/ppermute | solution.py:44
  96.7 2.6 collective-permute-done.20
  100.0 2.1 collective-permute-start.35
  102.1 5.0 %collective-permute-done.21 = bf16[64,1024]{1,0:T(8,128)(2,1)S(1)} collective-permute-done((bf16[64,1024]{1,0:T(8,128)(2,1)S(1)}, bf16[64,1024]{1,0:T(8,128)(2,1)S(1)}, u32[]{:S(2)}, u32[]{:S(2)}) %collective-permute-start.21) | collective-permute-done | bytes 131104 | tf_op jit(solution)/shard_map/ppermute | solution.py:44
  109.3 5.8 %collective-permute-done.35 = bf16[128,1024]{1,0:T(8,128)(2,1)S(1)} collective-permute-done((bf16[128,1024]{1,0:T(8,128)(2,1)S(1)}, bf16[128,1024]{1,0:T(8,128)(2,1)S(1)}, u32[]{:S(2)}, u32[]{:S(2)}) %collective-permute-start.35) | collective-permute-done | bytes 262176 | tf_op jit(solution)/shard_map/ppermute | solution.py:44
  116.5 2.2 collective-permute-done.24
  119.3 1.8 collective-permute-start.33
  121.2 3.1 collective-permute-done.36
  126.0 2.5 collective-permute-start.28
  128.6 2.3 collective-permute-done.27
  133.8 2.4 fusion.60
  139.1 2.6 collective-permute-done.37
  145.9 3.0 collective-permute-done.38
  157.4 1.9 collective-permute-done.41
  159.3 1.9 collective-permute-done.39
  161.2 2.0 fusion.58
  165.0 4.5 %collective-permute-done.43 = bf16[128,1024]{1,0:T(8,128)(2,1)S(1)} collective-permute-done((bf16[128,1024]{1,0:T(8,128)(2,1)S(1)}, bf16[128,1024]{1,0:T(8,128)(2,1)S(1)}, u32[]{:S(2)}, u32[]{:S(2)}) %collective-permute-start.43) | collective-permute-done | bytes 262176 | tf_op jit(solution)/shard_map/ppermute | solution.py:44
  170.9 2.2 collective-permute-start.45
  177.7 1.9 multiply_convert_fusion
  179.9 2.3 convolution_convert_fusion.2
  183.8 2.1 pad_maximum_fusion
  186.0 2.4 fusion.78
  188.4 2.6 fusion.76
  191.1 2.1 collective-permute-start.51
  194.3 1.8 collective-permute-start.64
  200.8 2.6 fusion.80
  203.3 2.9 collective-permute-done.54
  212.9 3.8 %collective-permute-done.56 = bf16[128,1024]{1,0:T(8,128)(2,1)S(1)} collective-permute-done((bf16[128,1024]{1,0:T(8,128)(2,1)}, bf16[128,1024]{1,0:T(8,128)(2,1)S(1)}, u32[]{:S(2)}, u32[]{:S(2)}) %collective-permute-start.56) | collective-permute-done | bytes 262176 | tf_op jit(solution)/shard_map/ppermute | solution.py:44
  219.1 2.6 collective-permute-done.57
  227.6 7.3 %collective-permute-done.63.got_ref = bf16[512,128]{1,0:T(8,128)(2,1)S(1)} collective-permute-done((bf16[512,128]{1,0:T(8,128)(2,1)S(1)}, bf16[512,128]{1,0:T(8,128)(2,1)S(1)}, u32[]{:S(2)}, u32[]{:S(2)}) %collective-permute-start.63) | collective-permute-done | bytes 131104 | tf_op jit(solution)/shard_map/ppermute | solution.py:44
  235.6 2.3 add_bitcast_fusion
  238.6 11.5 %shard_map.153 = (bf16[1024,384]{1,0:T(8,128)(2,1)}, bf16[512,384]{1,0:T(8,128)(2,1)}, bf16[512,384]{1,0:T(8,128)(2,1)}) custom-call(s32[4]{0:T(128)} %pad_add_fusion.where_ref, bf16[1024,384]{1,0:T(8,128)(2,1)} %get-tuple-element.121.mixed_ref, bf16[512,128]{1,0:T(8,128)(2,1)} %bitcast.240, bf16[512,128]{1,0:T(8,128)(2,1)} %copy-done.54), custom_call_target="tpu_custom_call" | custom-call | flops 1342177280 | bytes 4194304 | tf_op jit(solution)/shard_map/pallas_call | solution.py:260
  251.4 2.2 multiply_reduce_fusion
  253.7 2.4 collective-permute-start.71
  262.2 2.0 collective-permute-done.68
  265.7 5.0 %collective-permute-done.69 = f32[3,1024]{1,0:T(4,128)S(1)} collective-permute-done((f32[3,1024]{1,0:T(4,128)S(1)}, f32[3,1024]{1,0:T(4,128)S(1)}, u32[]{:S(2)}, u32[]{:S(2)}) %collective-permute-start.69) | collective-permute-done | bytes 12320 | tf_op jit(solution)/shard_map/ppermute | solution.py:44
  270.8 4.4 %collective-permute-done.71 = bf16[512,384]{1,0:T(8,128)(2,1)S(1)} collective-permute-done((bf16[512,384]{1,0:T(8,128)(2,1)S(1)}, bf16[512,384]{1,0:T(8,128)(2,1)S(1)}, u32[]{:S(2)}, u32[]{:S(2)}) %collective-permute-start.71) | collective-permute-done | bytes 393248 | tf_op jit(solution)/shard_map/ppermute | solution.py:44
  276.5 3.0 collective-permute-start.79
  279.4 3.2 collective-permute-done.84
  282.9 14.1 %collective-permute-done.74 = bf16[1,128,1024]{2,1,0:T(8,128)(2,1)S(1)} collective-permute-done((bf16[1,128,1024]{2,1,0:T(8,128)(2,1)S(1)}, bf16[1,128,1024]{2,1,0:T(8,128)(2,1)S(1)}, u32[]{:S(2)}, u32[]{:S(2)}) %collective-permute-start.74) | collective-permute-done | bytes 262176 | tf_op jit(solution)/shard_map/ppermute | solution.py:44
  299.5 2.3 collective-permute-start.85
  303.2 3.9 %collective-permute-done.76 = bf16[64,1024]{1,0:T(8,128)(2,1)S(1)} collective-permute-done((bf16[64,1024]{1,0:T(8,128)(2,1)S(1)}, bf16[64,1024]{1,0:T(8,128)(2,1)S(1)}, u32[]{:S(2)}, u32[]{:S(2)}) %collective-permute-start.76) | collective-permute-done | bytes 131104 | tf_op jit(solution)/shard_map/ppermute | solution.py:44
  308.0 6.1 %collective-permute-done.85 = bf16[1,128,1024]{2,1,0:T(8,128)(2,1)S(1)} collective-permute-done((bf16[1,128,1024]{2,1,0:T(8,128)(2,1)S(1)}, bf16[1,128,1024]{2,1,0:T(8,128)(2,1)S(1)}, u32[]{:S(2)}, u32[]{:S(2)}) %collective-permute-start.85) | collective-permute-done | bytes 262176 | tf_op jit(solution)/shard_map/ppermute | solution.py:44
  315.4 1.9 collective-permute-start.86
  320.1 6.9 %collective-permute-start.81 = (bf16[32,1024]{1,0:T(8,128)(2,1)S(1)}, bf16[32,1024]{1,0:T(8,128)(2,1)S(1)}, u32[]{:S(2)}, u32[]{:S(2)}) collective-permute-start(bf16[32,1024]{1,0:T(8,128)(2,1)S(1)} %get-tuple-element.202), channel_id=1, source_target_pairs={{8,0},{1,1},{25,2},{18,3},{11,4},{4,5},{28,6},{21,7},{14,8},{7,9},... | collective-permute-start | bytes 196616 | tf_op jit(solution)/shard_map/ppermute | solution.py:468
  326.9 5.0 %collective-permute-start.80 = (bf16[32,1024]{1,0:T(8,128)(2,1)S(1)}, bf16[32,1024]{1,0:T(8,128)(2,1)S(1)}, u32[]{:S(2)}, u32[]{:S(2)}) collective-permute-start(bf16[32,1024]{1,0:T(8,128)(2,1)S(1)} %get-tuple-element.201), channel_id=1, source_target_pairs={{0,0},{24,1},{17,2},{10,3},{3,4},{27,5},{20,6},{13,7},{6,8},{30,9}... | collective-permute-start | bytes 196616 | tf_op jit(solution)/shard_map/ppermute | solution.py:468
  332.0 1.9 collective-permute-start.83
  337.0 2.8 collective-permute-done.83
  (375 shorter events, 93.6 us)
Async XLA Ops:
  2.5 15.7 %collective-permute-start = (bf16[64,1024]{1,0:T(8,128)(2,1)S(1)}, bf16[64,1024]{1,0:T(8,128)(2,1)S(1)}, u32[]{:S(2)}, u32[]{:S(2)}) collective-permute-start(bf16[64,1024]{1,0:T(8,128)(2,1)S(1)} %get-tuple-element.211), channel_id=1, source_target_pairs={{0,8},{1,9},{2,10},{3,11},{4,12},{5,13},{6,14},{7,15},{8,0},{9,1},... | collective-permute-start | bytes 393224 | tf_op jit(solution)/shard_map/ppermute | solution.py:44
  6.0 12.1 %collective-permute-start.1 = (bf16[32,1024]{1,0:T(8,128)(2,1)S(1)}, bf16[32,1024]{1,0:T(8,128)(2,1)S(1)}, u32[]{:S(2)}, u32[]{:S(2)}) collective-permute-start(bf16[32,1024]{1,0:T(8,128)(2,1)S(1)} %get-tuple-element.216), channel_id=1, source_target_pairs={{0,0},{1,24},{2,17},{3,10},{4,3},{5,27},{6,20},{7,13},{8,6},{9,30}... | collective-permute-start | bytes 196616 | tf_op jit(solution)/shard_map/ppermute | solution.py:315
  8.6 9.6 %collective-permute-start.2 = (bf16[32,1024]{1,0:T(8,128)(2,1)S(1)}, bf16[32,1024]{1,0:T(8,128)(2,1)S(1)}, u32[]{:S(2)}, u32[]{:S(2)}) collective-permute-start(bf16[32,1024]{1,0:T(8,128)(2,1)S(1)} %get-tuple-element.217), channel_id=1, source_target_pairs={{0,8},{1,1},{2,25},{3,18},{4,11},{5,4},{6,28},{7,21},{8,14},{9,7},... | collective-permute-start | bytes 196616 | tf_op jit(solution)/shard_map/ppermute | solution.py:315
  12.3 5.9 %collective-permute-start.3 = (bf16[32,1024]{1,0:T(8,128)(2,1)S(1)}, bf16[32,1024]{1,0:T(8,128)(2,1)S(1)}, u32[]{:S(2)}, u32[]{:S(2)}) collective-permute-start(bf16[32,1024]{1,0:T(8,128)(2,1)S(1)} %get-tuple-element.215), channel_id=1, source_target_pairs={{0,16},{1,9},{2,2},{3,26},{4,19},{5,12},{6,5},{7,29},{8,22},{9,15}... | collective-permute-start | bytes 196616 | tf_op jit(solution)/shard_map/ppermute | solution.py:315
  13.0 11.4 %collective-permute-start.4 = (bf16[32,1024]{1,0:T(8,128)(2,1)}, bf16[32,1024]{1,0:T(8,128)(2,1)S(1)}, u32[]{:S(2)}, u32[]{:S(2)}) collective-permute-start(bf16[32,1024]{1,0:T(8,128)(2,1)} %param.20), channel_id=1, source_target_pairs={{0,0},{1,8},{2,16},{3,24},{4,1},{5,9},{6,17},{7,25},{8,2},{9,10},{... | collective-permute-start | bytes 196616 | tf_op jit(solution)/shard_map/ppermute | solution.py:316
  24.4 5.7 %collective-permute-start.9 = (bf16[128,1024]{1,0:T(8,128)(2,1)S(1)}, bf16[128,1024]{1,0:T(8,128)(2,1)}, u32[]{:S(2)}, u32[]{:S(2)}) collective-permute-start(bf16[128,1024]{1,0:T(8,128)(2,1)S(1)} %pad_maximum_fusion.12.refs_0_), channel_id=1, source_target_pairs={{0,1},{1,0},{2,3},{3,2},{4,5},{5,4},{6,7},{7,6},{8,9},{9,8},{10,11... | collective-permute-start | bytes 786440 | tf_op jit(solution)/shard_map/ppermute | solution.py:44
  24.4 55.1 %collective-permute-start.18 = (bf16[128,1024]{1,0:T(8,128)(2,1)}, bf16[128,1024]{1,0:T(8,128)(2,1)S(1)}, u32[]{:S(2)}, u32[]{:S(2)}) collective-permute-start(bf16[128,1024]{1,0:T(8,128)(2,1)} %param.22), channel_id=1, source_target_pairs={{0,0},{1,16},{2,1},{3,17},{4,2},{5,18},{6,3},{7,19},{8,4},{9,20},{... | collective-permute-start | bytes 786440 | tf_op jit(solution)/shard_map/ppermute | solution.py:314
  26.4 17.0 %collective-permute-start.5 = (bf16[128,1024]{1,0:T(8,128)(2,1)S(1)}, bf16[128,1024]{1,0:T(8,128)(2,1)}, u32[]{:S(2)}, u32[]{:S(2)}) collective-permute-start(bf16[128,1024]{1,0:T(8,128)(2,1)S(1)} %pad_maximum_fusion.12.refs_0_), channel_id=1, source_target_pairs={{0,2},{1,3},{2,0},{3,1},{4,6},{5,7},{6,4},{7,5},{8,10},{9,11},{10,... | collective-permute-start | bytes 786440 | tf_op jit(solution)/shard_map/ppermute | solution.py:44
  26.5 15.7 %collective-permute-start.6 = (bf16[128,1024]{1,0:T(8,128)(2,1)S(1)}, bf16[128,1024]{1,0:T(8,128)(2,1)}, u32[]{:S(2)}, u32[]{:S(2)}) collective-permute-start(bf16[128,1024]{1,0:T(8,128)(2,1)S(1)} %pad_maximum_fusion.12.refs_0_), channel_id=1, source_target_pairs={{0,4},{1,5},{2,6},{3,7},{4,0},{5,1},{6,2},{7,3},{8,12},{9,13},{10,... | collective-permute-start | bytes 786440 | tf_op jit(solution)/shard_map/ppermute | solution.py:44
  30.2 21.9 %collective-permute-start.13 = (bf16[4,32,1024]{2,1,0:T(8,128)(2,1)S(1)}, bf16[4,32,1024]{2,1,0:T(8,128)(2,1)S(1)}, u32[]{:S(2)}, u32[]{:S(2)}) collective-permute-start(bf16[4,32,1024]{2,1,0:T(8,128)(2,1)S(1)} %get-tuple-element.209), channel_id=1, source_target_pairs={{0,8},{1,9},{2,10},{3,11},{4,12},{5,13},{6,14},{7,15},{8,0},{9,1},... | collective-permute-start | bytes 786440 | tf_op jit(solution)/shard_map/ppermute | solution.py:44
  44.3 9.6 %collective-permute-start.8 = (bf16[64,1024]{1,0:T(8,128)(2,1)S(1)}, bf16[64,1024]{1,0:T(8,128)(2,1)S(1)}, u32[]{:S(2)}, u32[]{:S(2)}) collective-permute-start(bf16[64,1024]{1,0:T(8,128)(2,1)S(1)} %slice.438), channel_id=1, source_target_pairs={{0,4},{1,5},{2,6},{3,7},{4,0},{5,1},{6,2},{7,3},{8,12},{9,13},{10,... | collective-permute-start | bytes 393224 | tf_op jit(solution)/shard_map/ppermute | solution.py:44
  44.4 10.8 %collective-permute-start.14 = (bf16[4,32,1024]{2,1,0:T(8,128)(2,1)S(1)}, bf16[4,32,1024]{2,1,0:T(8,128)(2,1)S(1)}, u32[]{:S(2)}, u32[]{:S(2)}) collective-permute-start(bf16[4,32,1024]{2,1,0:T(8,128)(2,1)S(1)} %get-tuple-element.209), channel_id=1, source_target_pairs={{0,16},{16,0},{1,17},{17,1},{2,18},{18,2},{3,19},{19,3},{4,20},{20... | collective-permute-start | bytes 786440 | tf_op jit(solution)/shard_map/ppermute | solution.py:48
  48.2 14.0 %collective-permute-start.10 = (bf16[128,1024]{1,0:T(8,128)(2,1)}, bf16[128,1024]{1,0:T(8,128)(2,1)}, u32[]{:S(2)}, u32[]{:S(2)}) collective-permute-start(bf16[128,1024]{1,0:T(8,128)(2,1)} %collective-permute-done.5.refs_1_), channel_id=1, source_target_pairs={{0,1},{1,0},{2,3},{3,2},{4,5},{5,4},{6,7},{7,6},{8,9},{9,8},{10,11... | collective-permute-start | bytes 786440 | tf_op jit(solution)/shard_map/ppermute | solution.py:44
  52.1 8.0 %collective-permute-start.15 = (bf16[4,32,1024]{2,1,0:T(8,128)(2,1)S(1)}, bf16[4,32,1024]{2,1,0:T(8,128)(2,1)S(1)}, u32[]{:S(2)}, u32[]{:S(2)}) collective-permute-start(bf16[4,32,1024]{2,1,0:T(8,128)(2,1)S(1)} %collective-permute-done.13), channel_id=1, source_target_pairs={{0,16},{16,0},{1,17},{17,1},{2,18},{18,2},{3,19},{19,3},{4,20},{20... | collective-permute-start | bytes 786440 | tf_op jit(solution)/shard_map/ppermute | solution.py:48
  53.9 8.3 %collective-permute-start.11 = (bf16[128,1024]{1,0:T(8,128)(2,1)}, bf16[128,1024]{1,0:T(8,128)(2,1)}, u32[]{:S(2)}, u32[]{:S(2)}) collective-permute-start(bf16[128,1024]{1,0:T(8,128)(2,1)} %collective-permute-done.6.refs_2_), channel_id=1, source_target_pairs={{0,1},{1,0},{2,3},{3,2},{4,5},{5,4},{6,7},{7,6},{8,9},{9,8},{10,11... | collective-permute-start | bytes 786440 | tf_op jit(solution)/shard_map/ppermute | solution.py:44
  55.3 6.9 %collective-permute-start.12 = (bf16[128,1024]{1,0:T(8,128)(2,1)}, bf16[128,1024]{1,0:T(8,128)(2,1)S(1)}, u32[]{:S(2)}, u32[]{:S(2)}) collective-permute-start(bf16[128,1024]{1,0:T(8,128)(2,1)} %copy-done.26), channel_id=1, source_target_pairs={{0,1},{1,0},{2,3},{3,2},{4,5},{5,4},{6,7},{7,6},{8,9},{9,8},{10,11... | collective-permute-start | bytes 786440 | tf_op jit(solution)/shard_map/ppermute | solution.py:44
  62.2 24.2 %collective-permute-start.16 = (bf16[256,1024]{1,0:T(8,128)(2,1)S(1)}, bf16[256,1024]{1,0:T(8,128)(2,1)S(1)}, u32[]{:S(2)}, u32[]{:S(2)}) collective-permute-start(bf16[256,1024]{1,0:T(8,128)(2,1)S(1)} %copy-done.38), channel_id=1, source_target_pairs={{0,8},{1,9},{2,10},{3,11},{4,12},{5,13},{6,14},{7,15},{8,0},{9,1},... | collective-permute-start | bytes 1572872 | tf_op jit(solution)/shard_map/ppermute | solution.py:44
  62.6 23.8 %collective-permute-start.17 = (bf16[256,1024]{1,0:T(8,128)(2,1)S(1)}, bf16[256,1024]{1,0:T(8,128)(2,1)S(1)}, u32[]{:S(2)}, u32[]{:S(2)}) collective-permute-start(bf16[256,1024]{1,0:T(8,128)(2,1)S(1)} %copy-done.38), channel_id=1, source_target_pairs={{0,16},{16,0},{1,17},{17,1},{2,18},{18,2},{3,19},{19,3},{4,20},{20... | collective-permute-start | bytes 1572872 | tf_op jit(solution)/shard_map/ppermute | solution.py:48
  86.4 8.9 %collective-permute-start.19 = (bf16[512,128]{1,0:T(8,128)(2,1)}, bf16[512,128]{1,0:T(8,128)(2,1)S(1)}, u32[]{:S(2)}, u32[]{:S(2)}) collective-permute-start(bf16[512,128]{1,0:T(8,128)(2,1)} %get-tuple-element.113), channel_id=1, source_target_pairs={{0,8},{1,9},{2,10},{3,11},{4,12},{5,13},{6,14},{7,15},{8,0},{9,1},... | collective-permute-start | bytes 393224 | tf_op jit(solution)/shard_map/ppermute | solution.py:44
  99.8 7.3 %collective-permute-start.21 = (bf16[64,1024]{1,0:T(8,128)(2,1)S(1)}, bf16[64,1024]{1,0:T(8,128)(2,1)S(1)}, u32[]{:S(2)}, u32[]{:S(2)}) collective-permute-start(bf16[64,1024]{1,0:T(8,128)(2,1)S(1)} %get-tuple-element.194), channel_id=1, source_target_pairs={{0,4},{1,5},{2,6},{3,7},{4,0},{5,1},{6,2},{7,3},{8,12},{9,13},{10,... | collective-permute-start | bytes 393224 | tf_op jit(solution)/shard_map/ppermute | solution.py:44
  99.9 7.3 %collective-permute-start.23 = (bf16[64,1024]{1,0:T(8,128)(2,1)S(1)}, bf16[64,1024]{1,0:T(8,128)(2,1)S(1)}, u32[]{:S(2)}, u32[]{:S(2)}) collective-permute-start(bf16[64,1024]{1,0:T(8,128)(2,1)S(1)} %get-tuple-element.193), channel_id=1, source_target_pairs={{0,2},{1,3},{2,0},{3,1},{4,6},{5,7},{6,4},{7,5},{8,10},{9,11},{10,... | collective-permute-start | bytes 393224 | tf_op jit(solution)/shard_map/ppermute | solution.py:44
  100.0 15.1 %collective-permute-start.35 = (bf16[128,1024]{1,0:T(8,128)(2,1)S(1)}, bf16[128,1024]{1,0:T(8,128)(2,1)S(1)}, u32[]{:S(2)}, u32[]{:S(2)}) collective-permute-start(bf16[128,1024]{1,0:T(8,128)(2,1)S(1)} %collective-permute-done.18), channel_id=1, source_target_pairs={{0,8},{1,9},{2,10},{3,11},{4,12},{5,13},{6,14},{7,15},{8,0},{9,1},... | collective-permute-start | bytes 786440 | tf_op jit(solution)/shard_map/ppermute | solution.py:44
  107.3 11.5 %collective-permute-start.24 = (bf16[128,1024]{1,0:T(8,128)(2,1)S(1)}, bf16[128,1024]{1,0:T(8,128)(2,1)S(1)}, u32[]{:S(2)}, u32[]{:S(2)}) collective-permute-start(bf16[128,1024]{1,0:T(8,128)(2,1)S(1)} %pad_maximum_fusion.15), channel_id=1, source_target_pairs={{0,4},{1,5},{2,6},{3,7},{4,0},{5,1},{6,2},{7,3},{8,12},{9,13},{10,... | collective-permute-start | bytes 786440 | tf_op jit(solution)/shard_map/ppermute | solution.py:44
  107.4 11.4 %collective-permute-start.22 = (bf16[128,1024]{1,0:T(8,128)(2,1)S(1)}, bf16[128,1024]{1,0:T(8,128)(2,1)S(1)}, u32[]{:S(2)}, u32[]{:S(2)}) collective-permute-start(bf16[128,1024]{1,0:T(8,128)(2,1)S(1)} %pad_maximum_fusion.14), channel_id=1, source_target_pairs={{0,2},{1,3},{2,0},{3,1},{4,6},{5,7},{6,4},{7,5},{8,10},{9,11},{10,... | collective-permute-start | bytes 786440 | tf_op jit(solution)/shard_map/ppermute | solution.py:44
  107.7 13.4 %collective-permute-start.34 = (bf16[128,1024]{1,0:T(8,128)(2,1)S(1)}, bf16[128,1024]{1,0:T(8,128)(2,1)S(1)}, u32[]{:S(2)}, u32[]{:S(2)}) collective-permute-start(bf16[128,1024]{1,0:T(8,128)(2,1)S(1)} %collective-permute-done.18), channel_id=1, source_target_pairs={{0,16},{16,0},{1,17},{17,1},{2,18},{18,2},{3,19},{19,3},{4,20},{20... | collective-permute-start | bytes 786440 | tf_op jit(solution)/shard_map/ppermute | solution.py:48
  115.1 9.2 %collective-permute-start.36 = (bf16[128,1024]{1,0:T(8,128)(2,1)S(1)}, bf16[128,1024]{1,0:T(8,128)(2,1)S(1)}, u32[]{:S(2)}, u32[]{:S(2)}) collective-permute-start(bf16[128,1024]{1,0:T(8,128)(2,1)S(1)} %collective-permute-done.35), channel_id=1, source_target_pairs={{0,16},{16,0},{1,17},{17,1},{2,18},{18,2},{3,19},{19,3},{4,20},{20... | collective-permute-start | bytes 786440 | tf_op jit(solution)/shard_map/ppermute | solution.py:48
  119.1 6.8 %collective-permute-start.26 = (bf16[128,1024]{1,0:T(8,128)(2,1)S(1)}, bf16[128,1024]{1,0:T(8,128)(2,1)S(1)}, u32[]{:S(2)}, u32[]{:S(2)}) collective-permute-start(bf16[128,1024]{1,0:T(8,128)(2,1)S(1)} %get-tuple-element.162), channel_id=1, source_target_pairs={{0,4},{1,5},{2,6},{3,7},{4,0},{5,1},{6,2},{7,3},{8,12},{9,13},{10,... | collective-permute-start | bytes 786440 | tf_op jit(solution)/shard_map/ppermute | solution.py:44
  119.2 6.8 %collective-permute-start.25 = (bf16[128,1024]{1,0:T(8,128)(2,1)S(1)}, bf16[128,1024]{1,0:T(8,128)(2,1)S(1)}, u32[]{:S(2)}, u32[]{:S(2)}) collective-permute-start(bf16[128,1024]{1,0:T(8,128)(2,1)S(1)} %get-tuple-element.162), channel_id=1, source_target_pairs={{0,2},{1,3},{2,0},{3,1},{4,6},{5,7},{6,4},{7,5},{8,10},{9,11},{10,... | collective-permute-start | bytes 786440 | tf_op jit(solution)/shard_map/ppermute | solution.py:44
  119.3 14.5 %collective-permute-start.33 = (bf16[256,1024]{1,0:T(8,128)(2,1)S(1)}, bf16[256,1024]{1,0:T(8,128)(2,1)S(1)}, u32[]{:S(2)}, u32[]{:S(2)}) collective-permute-start(bf16[256,1024]{1,0:T(8,128)(2,1)S(1)} %copy-done.42), channel_id=1, source_target_pairs={{0,16},{16,0},{1,17},{17,1},{2,18},{18,2},{3,19},{19,3},{4,20},{20... | collective-permute-start | bytes 1572872 | tf_op jit(solution)/shard_map/ppermute | solution.py:48
  124.5 7.2 %collective-permute-start.29 = (bf16[128,1024]{1,0:T(8,128)(2,1)S(1)}, bf16[128,1024]{1,0:T(8,128)(2,1)S(1)}, u32[]{:S(2)}, u32[]{:S(2)}) collective-permute-start(bf16[128,1024]{1,0:T(8,128)(2,1)S(1)} %get-tuple-element.162), channel_id=1, source_target_pairs={{0,1},{1,0},{2,3},{3,2},{4,5},{5,4},{6,7},{7,6},{8,9},{9,8},{10,11... | collective-permute-start | bytes 786440 | tf_op jit(solution)/shard_map/ppermute | solution.py:44
  143.2 5.8 %collective-permute-start.38 = (bf16[64,1024]{1,0:T(8,128)(2,1)}, bf16[64,1024]{1,0:T(8,128)(2,1)S(1)}, u32[]{:S(2)}, u32[]{:S(2)}) collective-permute-start(bf16[64,1024]{1,0:T(8,128)(2,1)} %get-tuple-element.190), channel_id=1, source_target_pairs={{0,4},{1,5},{2,6},{3,7},{4,0},{5,1},{6,2},{7,3},{8,12},{9,13},{10,... | collective-permute-start | bytes 393224 | tf_op jit(solution)/shard_map/ppermute | solution.py:44
  151.8 7.5 %collective-permute-start.41 = (bf16[128,1024]{1,0:T(8,128)(2,1)}, bf16[128,1024]{1,0:T(8,128)(2,1)}, u32[]{:S(2)}, u32[]{:S(2)}) collective-permute-start(bf16[128,1024]{1,0:T(8,128)(2,1)} %pad_maximum_fusion.18), channel_id=1, source_target_pairs={{0,4},{1,5},{2,6},{3,7},{4,0},{5,1},{6,2},{7,3},{8,12},{9,13},{10,... | collective-permute-start | bytes 786440 | tf_op jit(solution)/shard_map/ppermute | solution.py:44
  153.5 7.7 %collective-permute-start.39 = (bf16[128,1024]{1,0:T(8,128)(2,1)}, bf16[128,1024]{1,0:T(8,128)(2,1)}, u32[]{:S(2)}, u32[]{:S(2)}) collective-permute-start(bf16[128,1024]{1,0:T(8,128)(2,1)} %pad_maximum_fusion.17), channel_id=1, source_target_pairs={{0,2},{1,3},{2,0},{3,1},{4,6},{5,7},{6,4},{7,5},{8,10},{9,11},{10,... | collective-permute-start | bytes 786440 | tf_op jit(solution)/shard_map/ppermute | solution.py:44
  163.1 6.4 %collective-permute-start.43 = (bf16[128,1024]{1,0:T(8,128)(2,1)S(1)}, bf16[128,1024]{1,0:T(8,128)(2,1)S(1)}, u32[]{:S(2)}, u32[]{:S(2)}) collective-permute-start(bf16[128,1024]{1,0:T(8,128)(2,1)S(1)} %get-tuple-element.157), channel_id=1, source_target_pairs={{0,4},{1,5},{2,6},{3,7},{4,0},{5,1},{6,2},{7,3},{8,12},{9,13},{10,... | collective-permute-start | bytes 786440 | tf_op jit(solution)/shard_map/ppermute | solution.py:44
  163.7 7.1 %collective-permute-start.42 = (bf16[128,1024]{1,0:T(8,128)(2,1)S(1)}, bf16[128,1024]{1,0:T(8,128)(2,1)S(1)}, u32[]{:S(2)}, u32[]{:S(2)}) collective-permute-start(bf16[128,1024]{1,0:T(8,128)(2,1)S(1)} %get-tuple-element.157), channel_id=1, source_target_pairs={{0,2},{1,3},{2,0},{3,1},{4,6},{5,7},{6,4},{7,5},{8,10},{9,11},{10,... | collective-permute-start | bytes 786440 | tf_op jit(solution)/shard_map/ppermute | solution.py:44
  165.0 11.1 %collective-permute-start.46 = (bf16[128,1024]{1,0:T(8,128)(2,1)S(1)}, bf16[128,1024]{1,0:T(8,128)(2,1)S(1)}, u32[]{:S(2)}, u32[]{:S(2)}) collective-permute-start(bf16[128,1024]{1,0:T(8,128)(2,1)S(1)} %get-tuple-element.157), channel_id=1, source_target_pairs={{0,1},{1,0},{2,3},{3,2},{4,5},{5,4},{6,7},{7,6},{8,9},{9,8},{10,11... | collective-permute-start | bytes 786440 | tf_op jit(solution)/shard_map/ppermute | solution.py:44
  182.3 6.1 %collective-permute-start.50 = (bf16[512,1024]{1,0:T(8,128)(2,1)}, bf16[512,1024]{1,0:T(8,128)(2,1)}, u32[]{:S(2)}, u32[]{:S(2)}) collective-permute-start(bf16[512,1024]{1,0:T(8,128)(2,1)} %convolution_convert_fusion.2), channel_id=1, source_target_pairs={{0,1},{1,0},{2,3},{3,2},{4,5},{5,4},{6,7},{7,6},{8,9},{9,8},{10,11... | collective-permute-start | bytes 3145736 | tf_op jit(solution)/shard_map/ppermute | solution.py:44
  191.1 6.1 %collective-permute-start.51 = (bf16[64,1024]{1,0:T(8,128)(2,1)S(1)}, bf16[64,1024]{1,0:T(8,128)(2,1)S(1)}, u32[]{:S(2)}, u32[]{:S(2)}) collective-permute-start(bf16[64,1024]{1,0:T(8,128)(2,1)S(1)} %get-tuple-element.186), channel_id=1, source_target_pairs={{0,4},{1,5},{2,6},{3,7},{4,0},{5,1},{6,2},{7,3},{8,12},{9,13},{10,... | collective-permute-start | bytes 393224 | tf_op jit(solution)/shard_map/ppermute | solution.py:44
  194.3 33.3 %collective-permute-start.64 = (bf16[2,256,1024]{2,1,0:T(8,128)(2,1)}, bf16[2,256,1024]{2,1,0:T(8,128)(2,1)}, u32[]{:S(2)}, u32[]{:S(2)}) collective-permute-start(bf16[2,256,1024]{2,1,0:T(8,128)(2,1)} %bitcast.41), channel_id=1, source_target_pairs={{0,16},{16,0},{1,17},{17,1},{2,18},{18,2},{3,19},{19,3},{4,20},{20... | collective-permute-start | bytes 3145736 | tf_op jit(solution)/shard_map/ppermute | solution.py:48
  198.7 7.5 %collective-permute-start.54 = (bf16[128,1024]{1,0:T(8,128)(2,1)S(1)}, bf16[128,1024]{1,0:T(8,128)(2,1)S(1)}, u32[]{:S(2)}, u32[]{:S(2)}) collective-permute-start(bf16[128,1024]{1,0:T(8,128)(2,1)S(1)} %pad_maximum_fusion.21), channel_id=1, source_target_pairs={{0,4},{1,5},{2,6},{3,7},{4,0},{5,1},{6,2},{7,3},{8,12},{9,13},{10,... | collective-permute-start | bytes 786440 | tf_op jit(solution)/shard_map/ppermute | solution.py:44
  199.2 7.6 %collective-permute-start.52 = (bf16[128,1024]{1,0:T(8,128)(2,1)S(1)}, bf16[128,1024]{1,0:T(8,128)(2,1)S(1)}, u32[]{:S(2)}, u32[]{:S(2)}) collective-permute-start(bf16[128,1024]{1,0:T(8,128)(2,1)S(1)} %pad_maximum_fusion.20), channel_id=1, source_target_pairs={{0,2},{1,3},{2,0},{3,1},{4,6},{5,7},{6,4},{7,5},{8,10},{9,11},{10,... | collective-permute-start | bytes 786440 | tf_op jit(solution)/shard_map/ppermute | solution.py:44
  208.9 8.7 %collective-permute-start.55 = (bf16[128,1024]{1,0:T(8,128)(2,1)}, bf16[128,1024]{1,0:T(8,128)(2,1)S(1)}, u32[]{:S(2)}, u32[]{:S(2)}) collective-permute-start(bf16[128,1024]{1,0:T(8,128)(2,1)} %get-tuple-element.156), channel_id=1, source_target_pairs={{0,2},{1,3},{2,0},{3,1},{4,6},{5,7},{6,4},{7,5},{8,10},{9,11},{10,... | collective-permute-start | bytes 786440 | tf_op jit(solution)/shard_map/ppermute | solution.py:44
  210.1 6.6 %collective-permute-start.56 = (bf16[128,1024]{1,0:T(8,128)(2,1)}, bf16[128,1024]{1,0:T(8,128)(2,1)S(1)}, u32[]{:S(2)}, u32[]{:S(2)}) collective-permute-start(bf16[128,1024]{1,0:T(8,128)(2,1)} %get-tuple-element.156), channel_id=1, source_target_pairs={{0,4},{1,5},{2,6},{3,7},{4,0},{5,1},{6,2},{7,3},{8,12},{9,13},{10,... | collective-permute-start | bytes 786440 | tf_op jit(solution)/shard_map/ppermute | solution.py:44
  212.6 10.2 %collective-permute-start.59 = (bf16[128,1024]{1,0:T(8,128)(2,1)}, bf16[128,1024]{1,0:T(8,128)(2,1)}, u32[]{:S(2)}, u32[]{:S(2)}) collective-permute-start(bf16[128,1024]{1,0:T(8,128)(2,1)} %get-tuple-element.156), channel_id=1, source_target_pairs={{0,1},{1,0},{2,3},{3,2},{4,5},{5,4},{6,7},{7,6},{8,9},{9,8},{10,11... | collective-permute-start | bytes 786440 | tf_op jit(solution)/shard_map/ppermute | solution.py:44
  225.7 9.2 %collective-permute-start.63 = (bf16[512,128]{1,0:T(8,128)(2,1)S(1)}, bf16[512,128]{1,0:T(8,128)(2,1)S(1)}, u32[]{:S(2)}, u32[]{:S(2)}) collective-permute-start(bf16[512,128]{1,0:T(8,128)(2,1)S(1)} %bitcast.241), channel_id=1, source_target_pairs={{0,8},{1,9},{2,10},{3,11},{4,12},{5,13},{6,14},{7,15},{8,0},{9,1},... | collective-permute-start | bytes 393224 | tf_op jit(solution)/shard_map/ppermute | solution.py:44
  238.0 12.6 %collective-permute-start.65 = (bf16[1,128,1024]{2,1,0:T(8,128)(2,1)S(1)}, bf16[1,128,1024]{2,1,0:T(8,128)(2,1)S(1)}, u32[]{:S(2)}, u32[]{:S(2)}) collective-permute-start(bf16[1,128,1024]{2,1,0:T(8,128)(2,1)S(1)} %fusion.37), channel_id=1, source_target_pairs={{0,8},{1,9},{2,10},{3,11},{4,12},{5,13},{6,14},{7,15},{8,0},{9,1},... | collective-permute-start | bytes 786440 | tf_op jit(solution)/shard_map/ppermute | solution.py:44
  253.7 21.4 %collective-permute-start.71 = (bf16[512,384]{1,0:T(8,128)(2,1)S(1)}, bf16[512,384]{1,0:T(8,128)(2,1)S(1)}, u32[]{:S(2)}, u32[]{:S(2)}) collective-permute-start(bf16[512,384]{1,0:T(8,128)(2,1)S(1)} %copy-done.52), channel_id=1, source_target_pairs={{0,8},{1,9},{2,10},{3,11},{4,12},{5,13},{6,14},{7,15},{8,0},{9,1},... | collective-permute-start | bytes 1179656 | tf_op jit(solution)/shard_map/ppermute | solution.py:44
  257.4 17.7 %collective-permute-start.72 = (bf16[4,2,32,1024]{3,2,0,1:T(8,128)(2,1)S(1)}, bf16[4,2,32,1024]{3,2,0,1:T(8,128)(2,1)S(1)}, u32[]{:S(2)}, u32[]{:S(2)}) collective-permute-start(bf16[4,2,32,1024]{3,2,0,1:T(8,128)(2,1)S(1)} %fusion.10), channel_id=1, source_target_pairs={{0,16},{16,0},{1,17},{17,1},{2,18},{18,2},{3,19},{19,3},{4,20},{20... | collective-permute-start | bytes 1572872 | tf_op jit(solution)/shard_map/ppermute | solution.py:48
  261.6 21.0 %collective-permute-start.84 = (bf16[2,128,1024]{2,1,0:T(8,128)(2,1)S(1)}, bf16[2,128,1024]{2,1,0:T(8,128)(2,1)S(1)}, u32[]{:S(2)}, u32[]{:S(2)}) collective-permute-start(bf16[2,128,1024]{2,1,0:T(8,128)(2,1)S(1)} %fusion.11), channel_id=1, source_target_pairs={{0,16},{16,0},{1,17},{17,1},{2,18},{18,2},{3,19},{19,3},{4,20},{20... | collective-permute-start | bytes 1572872 | tf_op jit(solution)/shard_map/ppermute | solution.py:48
  264.2 6.5 %collective-permute-start.69 = (f32[3,1024]{1,0:T(4,128)S(1)}, f32[3,1024]{1,0:T(4,128)S(1)}, u32[]{:S(2)}, u32[]{:S(2)}) collective-permute-start(f32[3,1024]{1,0:T(4,128)S(1)} %add.206), channel_id=1, source_target_pairs={{0,4},{1,5},{2,6},{3,7},{4,0},{5,1},{6,2},{7,3},{8,12},{9,13},{10,... | collective-permute-start | bytes 36872 | tf_op jit(solution)/shard_map/ppermute | solution.py:44
  270.7 43.5 %collective-permute-start.70 = (f32[3,1024]{1,0:T(4,128)S(1)}, f32[3,1024]{1,0:T(4,128)S(1)}, u32[]{:S(2)}, u32[]{:S(2)}) collective-permute-start(f32[3,1024]{1,0:T(4,128)S(1)} %add.207), channel_id=1, source_target_pairs={{0,8},{1,9},{2,10},{3,11},{4,12},{5,13},{6,14},{7,15},{8,0},{9,1},... | collective-permute-start | bytes 36872 | tf_op jit(solution)/shard_map/ppermute | solution.py:44
  275.9 21.0 %collective-permute-start.73 = (bf16[512,1024]{1,0:T(8,128)(2,1)S(1)}, bf16[512,1024]{1,0:T(8,128)(2,1)S(1)}, u32[]{:S(2)}, u32[]{:S(2)}) collective-permute-start(bf16[512,1024]{1,0:T(8,128)(2,1)S(1)} %convolution_convert_fusion.1), channel_id=1, source_target_pairs={{0,1},{1,0},{2,3},{3,2},{4,5},{5,4},{6,7},{7,6},{8,9},{9,8},{10,11... | collective-permute-start | bytes 3145736 | tf_op jit(solution)/shard_map/ppermute | solution.py:44
  276.1 20.9 %collective-permute-start.74 = (bf16[1,128,1024]{2,1,0:T(8,128)(2,1)S(1)}, bf16[1,128,1024]{2,1,0:T(8,128)(2,1)S(1)}, u32[]{:S(2)}, u32[]{:S(2)}) collective-permute-start(bf16[1,128,1024]{2,1,0:T(8,128)(2,1)S(1)} %fusion.38), channel_id=1, source_target_pairs={{0,8},{1,9},{2,10},{3,11},{4,12},{5,13},{6,14},{7,15},{8,0},{9,1},... | collective-permute-start | bytes 786440 | tf_op jit(solution)/shard_map/ppermute | solution.py:44
  276.5 42.8 %collective-permute-start.79 = (bf16[4,1,32,1024]{3,2,1,0:T(8,128)(2,1)S(1)}, bf16[4,1,32,1024]{3,2,1,0:T(8,128)(2,1)S(1)}, u32[]{:S(2)}, u32[]{:S(2)}) collective-permute-start(bf16[4,1,32,1024]{3,2,1,0:T(8,128)(2,1)S(1)} %fusion.36), channel_id=1, source_target_pairs={{0,8},{1,9},{2,10},{3,11},{4,12},{5,13},{6,14},{7,15},{8,0},{9,1},... | collective-permute-start | bytes 786440 | tf_op jit(solution)/shard_map/ppermute | solution.py:44
  297.7 5.5 %collective-permute-start.75 = (bf16[64,1024]{1,0:T(8,128)(2,1)S(1)}, bf16[64,1024]{1,0:T(8,128)(2,1)S(1)}, u32[]{:S(2)}, u32[]{:S(2)}) collective-permute-start(bf16[64,1024]{1,0:T(8,128)(2,1)S(1)} %get-tuple-element.182), channel_id=1, source_target_pairs={{0,2},{1,3},{2,0},{3,1},{4,6},{5,7},{6,4},{7,5},{8,10},{9,11},{10,... | collective-permute-start | bytes 393224 | tf_op jit(solution)/shard_map/ppermute | solution.py:44
  299.4 7.7 %collective-permute-start.76 = (bf16[64,1024]{1,0:T(8,128)(2,1)S(1)}, bf16[64,1024]{1,0:T(8,128)(2,1)S(1)}, u32[]{:S(2)}, u32[]{:S(2)}) collective-permute-start(bf16[64,1024]{1,0:T(8,128)(2,1)S(1)} %get-tuple-element.181), channel_id=1, source_target_pairs={{0,4},{1,5},{2,6},{3,7},{4,0},{5,1},{6,2},{7,3},{8,12},{9,13},{10,... | collective-permute-start | bytes 393224 | tf_op jit(solution)/shard_map/ppermute | solution.py:44
  299.5 14.7 %collective-permute-start.85 = (bf16[1,128,1024]{2,1,0:T(8,128)(2,1)S(1)}, bf16[1,128,1024]{2,1,0:T(8,128)(2,1)S(1)}, u32[]{:S(2)}, u32[]{:S(2)}) collective-permute-start(bf16[1,128,1024]{2,1,0:T(8,128)(2,1)S(1)} %fusion.40), channel_id=1, source_target_pairs={{0,8},{1,9},{2,10},{3,11},{4,12},{5,13},{6,14},{7,15},{8,0},{9,1},... | collective-permute-start | bytes 786440 | tf_op jit(solution)/shard_map/ppermute | solution.py:44
  307.2 11.7 %collective-permute-start.78 = (bf16[128,1024]{1,0:T(8,128)(2,1)S(1)}, bf16[128,1024]{1,0:T(8,128)(2,1)S(1)}, u32[]{:S(2)}, u32[]{:S(2)}) collective-permute-start(bf16[128,1024]{1,0:T(8,128)(2,1)S(1)} %pad_maximum_fusion.24), channel_id=1, source_target_pairs={{0,4},{1,5},{2,6},{3,7},{4,0},{5,1},{6,2},{7,3},{8,12},{9,13},{10,... | collective-permute-start | bytes 786440 | tf_op jit(solution)/shard_map/ppermute | solution.py:44
  307.3 11.6 %collective-permute-start.77 = (bf16[128,1024]{1,0:T(8,128)(2,1)S(1)}, bf16[128,1024]{1,0:T(8,128)(2,1)S(1)}, u32[]{:S(2)}, u32[]{:S(2)}) collective-permute-start(bf16[128,1024]{1,0:T(8,128)(2,1)S(1)} %pad_maximum_fusion.23), channel_id=1, source_target_pairs={{0,2},{1,3},{2,0},{3,1},{4,6},{5,7},{6,4},{7,5},{8,10},{9,11},{10,... | collective-permute-start | bytes 786440 | tf_op jit(solution)/shard_map/ppermute | solution.py:44
  315.4 20.7 %collective-permute-start.86 = (bf16[128,1024]{1,0:T(8,128)(2,1)S(1)}, bf16[128,1024]{1,0:T(8,128)(2,1)S(1)}, u32[]{:S(2)}, u32[]{:S(2)}) collective-permute-start(bf16[128,1024]{1,0:T(8,128)(2,1)S(1)} %fusion.39), channel_id=1, source_target_pairs={{0,0},{16,1},{1,2},{17,3},{2,4},{18,5},{3,6},{19,7},{4,8},{20,9},{... | collective-permute-start | bytes 786440 | tf_op jit(solution)/shard_map/ppermute | solution.py:449
  319.4 21.0 %collective-permute-start.82 = (bf16[32,1024]{1,0:T(8,128)(2,1)S(1)}, bf16[32,1024]{1,0:T(8,128)(2,1)S(1)}, u32[]{:S(2)}, u32[]{:S(2)}) collective-permute-start(bf16[32,1024]{1,0:T(8,128)(2,1)S(1)} %get-tuple-element.203), channel_id=1, source_target_pairs={{16,0},{9,1},{2,2},{26,3},{19,4},{12,5},{5,6},{29,7},{22,8},{15,9}... | collective-permute-start | bytes 196616 | tf_op jit(solution)/shard_map/ppermute | solution.py:468
  320.1 20.4 %collective-permute-start.81 = (bf16[32,1024]{1,0:T(8,128)(2,1)S(1)}, bf16[32,1024]{1,0:T(8,128)(2,1)S(1)}, u32[]{:S(2)}, u32[]{:S(2)}) collective-permute-start(bf16[32,1024]{1,0:T(8,128)(2,1)S(1)} %get-tuple-element.202), channel_id=1, source_target_pairs={{8,0},{1,1},{25,2},{18,3},{11,4},{4,5},{28,6},{21,7},{14,8},{7,9},... | collective-permute-start | bytes 196616 | tf_op jit(solution)/shard_map/ppermute | solution.py:468
  326.9 13.5 %collective-permute-start.80 = (bf16[32,1024]{1,0:T(8,128)(2,1)S(1)}, bf16[32,1024]{1,0:T(8,128)(2,1)S(1)}, u32[]{:S(2)}, u32[]{:S(2)}) collective-permute-start(bf16[32,1024]{1,0:T(8,128)(2,1)S(1)} %get-tuple-element.201), channel_id=1, source_target_pairs={{0,0},{24,1},{17,2},{10,3},{3,4},{27,5},{20,6},{13,7},{6,8},{30,9}... | collective-permute-start | bytes 196616 | tf_op jit(solution)/shard_map/ppermute | solution.py:468
  332.0 7.8 %collective-permute-start.83 = (bf16[32,1024]{1,0:T(8,128)(2,1)S(1)}, bf16[32,1024]{1,0:T(8,128)(2,1)S(1)}, u32[]{:S(2)}, u32[]{:S(2)}) collective-permute-start(bf16[32,1024]{1,0:T(8,128)(2,1)S(1)} %get-tuple-element.200), channel_id=1, source_target_pairs={{0,0},{8,1},{16,2},{24,3},{1,4},{9,5},{17,6},{25,7},{2,8},{10,9},{... | collective-permute-start | bytes 196616 | tf_op jit(solution)/shard_map/ppermute | solution.py:466
  (78 other events, 484.8 us)

commit v5 on v4

--- a/solution.py
+++ b/solution.py
@@ -10,6 +10,7 @@
 HEADS = 16
 HEAD_DIM = 64
 PAIR_DIM = 2 * HEAD_DIM
+SCALE = HEAD_DIM**-0.5
 EPS = 1e-05
 NEG = -1e30
 F32 = jnp.float32
@@ -158,15 +159,17 @@
             query = mixed_ref[pl.ds(at, BLOCK), 0:PAIR_DIM]
             keys = mixed_ref[0:width, PAIR_DIM : 2 * PAIR_DIM]
             values = mixed_ref[0:width, 2 * PAIR_DIM :]
-            key_pos = lax.broadcasted_iota(jnp.int32, (BLOCK, width), 1)
-            query_pos = at + lax.broadcasted_iota(jnp.int32, (BLOCK, width), 0)
+            free = begin if rows_q == rows_k else 0
+            key_pos = free + lax.broadcasted_iota(jnp.int32, (BLOCK, width - free), 1)
+            query_pos = at + lax.broadcasted_iota(jnp.int32, (BLOCK, width - free), 0)
             allowed = (key_pos <= query_pos) | (key_pos < prefix_len)
-            scores = nt(jnp.where(mine, query, jnp.zeros_like(query)), keys) * HEAD_DIM**-0.5
-            scores = jnp.where(allowed, scores, NEG)
+            scores = nt(jnp.where(mine, query * SCALE, jnp.zeros_like(query)), keys)
+            masked = jnp.where(allowed, scores[:, free:], NEG)
+            scores = jnp.concatenate([scores[:, :free], masked], 1) if free else masked
             top = jnp.max(scores, axis=-1, keepdims=True)
             weights = jnp.exp(scores - top)
             total = jnp.sum(weights, axis=-1, keepdims=True)
-            probs = (weights / total).astype(BF16)
+            probs = (weights * (1.0 / total)).astype(BF16)
             before = att_ref[pl.ds(start, BLOCK), :]
             att_ref[pl.ds(start, BLOCK), :] = jnp.where(mine, nn(probs, values).astype(BF16), before)
     for slot in range(8):
@@ -224,22 +227,24 @@
             grad = grad_ref[pl.ds(start, BLOCK), :]
             keys = mixed_ref[0:width, PAIR_DIM : 2 * PAIR_DIM]
             values = mixed_ref[0:width, 2 * PAIR_DIM :]
-            key_pos = lax.broadcasted_iota(jnp.int32, (width, BLOCK), 0)
-            query_pos = at + lax.broadcasted_iota(jnp.int32, (width, BLOCK), 1)
+            free = begin if rows_q == rows_k else 0
+            key_pos = free + lax.broadcasted_iota(jnp.int32, (width - free, BLOCK), 0)
+            query_pos = at + lax.broadcasted_iota(jnp.int32, (width - free, BLOCK), 1)
             allowed = (key_pos <= query_pos) | (key_pos < prefix_len)
-            own_query = jnp.where(mine, query, jnp.zeros_like(query))
+            own_query = jnp.where(mine, query * SCALE, jnp.zeros_like(query))
             own_grad = jnp.where(mine, grad, jnp.zeros_like(grad))
-            scores = nt(keys, own_query) * HEAD_DIM**-0.5
-            scores = jnp.where(allowed, scores, NEG)
+            scores = nt(keys, own_query)
+            masked = jnp.where(allowed, scores[free:], NEG)
+            scores = jnp.concatenate([scores[:free], masked], 0) if free else masked
             top = jnp.max(scores, axis=0, keepdims=True)
             weights = jnp.exp(scores - top)
-            probs = weights / jnp.sum(weights, axis=0, keepdims=True)
+            probs = weights * (1.0 / jnp.sum(weights, axis=0, keepdims=True))
             grad_probs = nt(values, own_grad)
             delta = jnp.sum(probs * grad_probs, axis=0, keepdims=True)
             grad_scores = (probs * (grad_probs - delta)).astype(BF16)
             gv_ref[0:width, :] += nn(probs.astype(BF16), own_grad)
-            gk_ref[0:width, :] += nn(grad_scores, own_query) * HEAD_DIM**-0.5
-            grad_q = (tn(grad_scores, keys) * HEAD_DIM**-0.5).astype(BF16)
+            gk_ref[0:width, :] += nn(grad_scores, own_query)
+            grad_q = (tn(grad_scores, keys) * SCALE).astype(BF16)
             before = gq_ref[pl.ds(start, BLOCK), 0:PAIR_DIM]
             gq_ref[pl.ds(start, BLOCK), 0:PAIR_DIM] = jnp.where(mine, grad_q, before)
     if whole:
@@ -351,7 +356,7 @@
     ffn_here = far_spread(late_in, n_seq)
     ffn_there = [swap_dp(late_in)]
     first_in, mixed, att_keep, att_give = attend(where, x_blocks, pair_w, gain_one, rows_q)
-    att_give, att_keep, ffn_here, ffn_there, down_rows = joint(att_give, att_keep, ffn_here, ffn_there, down_rows)
+    att_keep, ffn_here, ffn_there, down_rows = joint(att_keep, ffn_here, ffn_there, down_rows)
     down_here = far_spread(down_rows, n_seq)
     down_there = [swap_dp(down_rows)]
     att_got = other_micro(att_give)
@@ -409,7 +414,7 @@
 
     in_terms = in_terms + after(in_got, grad_got).astype(F32)
     in_pairs = in_terms.reshape((n_far // 2, 2) + in_terms.shape[1:])
-    half_rows = in_rows // 2
+    half_rows = 3 * in_rows // 4
     in_low = swap_seq(in_pairs[:, 1, :half_rows].astype(BF16), 8, n_seq)
     grads = attend_back(where, mixed, grad_keep, grad_got)
     if n_parts > 1:
@@ -425,8 +430,8 @@
     else:
         grad_mixed, mixed_keep, mixed_give = grads
         first_part = first_in
-    mixed_give, mixed_keep, grad_mixed, in_low, first_part = joint(
-        mixed_give, mixed_keep, grad_mixed, in_low, first_part
+    mixed_give, mixed_keep, grad_mixed, in_low, first_part, down_got = joint(
+        mixed_give, mixed_keep, grad_mixed, in_low, first_part, down_got
     )
     mixed_got = other_micro(mixed_give)
 

time: 343 us -> 339 us (0.988)
  waiting for transfers between devices: 152 us -> 147 us
  other arithmetic: 29.9 us -> 33.5 us
    ppermute x10, starting transfers between devices: 13.8 us -> 9.81 us  [swap_dp(): return lax.ppermute(value, 'dp', [(0, 1), (1, 0)])]
    ppermute x67, starting transfers between devices: 48.1 us -> 51.8 us  [swap_seq(): return lax.ppermute(value, 'seq', [(i, i ^ bits) for i in range(n_seq)])]
    ppermute x10, waiting for transfers between devices: 12.8 us -> 9.32 us  [swap_dp(): return lax.ppermute(value, 'dp', [(0, 1), (1, 0)])]
  transfers between devices with their start and end apart: 87 -> 87, of which waited for: 50 -> 49; matrix products, arithmetic and copies ran while one was open for 12% -> 15% of each run, Pallas kernels for 7% -> 7%
where the time goes in v5:
time: 339 us; the launch traced here: 338 us
  waiting for transfers between devices  147 us (43%)
  starting transfers between devices  91.2 us (27%)
  other arithmetic  33.5 us (10%)
  Pallas kernels  22.9 us (7%)
  local copies, waits for them, and re-layouts  20.9 us (6%)
  matrix products  17.9 us (5%)
  between operations  4.22 us (1%)
    ppermute x67, waiting for transfers between devices, swap_seq(): return lax.ppermute(value, 'seq', [(i, i ^ bits) for i in range(n_seq)])  128 us
    ppermute x67, starting transfers between devices, swap_seq(): return lax.ppermute(value, 'seq', [(i, i ^ bits) for i in range(n_seq)])  51.8 us
    ppermute x3, starting transfers between devices, shards(): lax.ppermute(jnp.where(thirds[t] == 0, terms[0], jnp.where(thirds[t] == 1...  11.8 us
    pallas_call x1, Pallas kernels, attend(): pl.pallas_call(attend_kernel, out_shape=(jax.ShapeDtypeStruct((rows_k, wi...  11.5 us
    pallas_call x1, Pallas kernels, attend_back(): pl.pallas_call(attend_back_kernel, out_shape=(jax.ShapeDtypeStruct((rows_...  11.4 us
    ppermute x10, starting transfers between devices, swap_dp(): return lax.ppermute(value, 'dp', [(0, 1), (1, 0)])  9.81 us
    ppermute x10, waiting for transfers between devices, swap_dp(): return lax.ppermute(value, 'dp', [(0, 1), (1, 0)])  9.32 us
    ppermute x3, starting transfers between devices, shards(): lax.ppermute(own_units[t], BOTH, [(i, home(3 * i + t)) for i in range(n_d...  6.96 us
  transfers between devices with their start and end apart: 87, of which 49 were waited for; matrix products, arithmetic and copies ran while one was open for 15% of the time, Pallas kernels for 7%

profile of v5, /device:TPU:2, one launch (start us, length us, event | category | flops | bytes accessed | tf_op | source)
XLA Modules:
  0.0 337.6 jit_solution(9873976810740665801)
XLA Ops:
  0.7 1.8 fusion.33
  2.5 2.7 collective-permute-start
  6.1 2.6 collective-permute-start.1
  8.6 3.7 %collective-permute-start.2 = (bf16[32,1024]{1,0:T(8,128)(2,1)S(1)}, bf16[32,1024]{1,0:T(8,128)(2,1)S(1)}, u32[]{:S(2)}, u32[]{:S(2)}) collective-permute-start(bf16[32,1024]{1,0:T(8,128)(2,1)S(1)} %get-tuple-element.217), channel_id=1, source_target_pairs={{0,8},{1,1},{2,25},{3,18},{4,11},{5,4},{6,28},{7,21},{8,14},{9,7},... | collective-permute-start | bytes 196616 | tf_op jit(solution)/shard_map/ppermute | solution.py:320
  13.1 5.1 %collective-permute-start.4 = (bf16[32,1024]{1,0:T(8,128)(2,1)}, bf16[32,1024]{1,0:T(8,128)(2,1)S(1)}, u32[]{:S(2)}, u32[]{:S(2)}) collective-permute-start(bf16[32,1024]{1,0:T(8,128)(2,1)} %param.20), channel_id=1, source_target_pairs={{0,0},{1,8},{2,16},{3,24},{4,1},{5,9},{6,17},{7,25},{8,2},{9,10},{... | collective-permute-start | bytes 196616 | tf_op jit(solution)/shard_map/ppermute | solution.py:321
  18.3 6.2 %collective-permute-done.4 = bf16[32,1024]{1,0:T(8,128)(2,1)S(1)} collective-permute-done((bf16[32,1024]{1,0:T(8,128)(2,1)}, bf16[32,1024]{1,0:T(8,128)(2,1)S(1)}, u32[]{:S(2)}, u32[]{:S(2)}) %collective-permute-start.4) | collective-permute-done | bytes 65568 | tf_op jit(solution)/shard_map/ppermute | solution.py:321
  24.4 1.9 collective-permute-start.18
  27.9 2.7 collective-permute-start.6
  30.7 4.4 %collective-permute-start.13 = (bf16[4,32,1024]{2,1,0:T(8,128)(2,1)S(1)}, bf16[4,32,1024]{2,1,0:T(8,128)(2,1)S(1)}, u32[]{:S(2)}, u32[]{:S(2)}) collective-permute-start(bf16[4,32,1024]{2,1,0:T(8,128)(2,1)S(1)} %get-tuple-element.209), channel_id=1, source_target_pairs={{0,8},{1,9},{2,10},{3,11},{4,12},{5,13},{6,14},{7,15},{8,0},{9,1},... | collective-permute-start | bytes 786440 | tf_op jit(solution)/shard_map/ppermute | solution.py:45
  35.1 7.1 %collective-permute-done.6.refs_2_ = bf16[128,1024]{1,0:T(8,128)(2,1)} collective-permute-done((bf16[128,1024]{1,0:T(8,128)(2,1)S(1)}, bf16[128,1024]{1,0:T(8,128)(2,1)}, u32[]{:S(2)}, u32[]{:S(2)}) %collective-permute-start.6) | collective-permute-done | bytes 262176 | tf_op jit(solution)/shard_map/ppermute | solution.py:45
  45.8 2.8 collective-permute-start.14
  48.6 3.6 %collective-permute-done.13 = bf16[4,32,1024]{2,1,0:T(8,128)(2,1)S(1)} collective-permute-done((bf16[4,32,1024]{2,1,0:T(8,128)(2,1)S(1)}, bf16[4,32,1024]{2,1,0:T(8,128)(2,1)S(1)}, u32[]{:S(2)}, u32[]{:S(2)}) %collective-permute-start.13) | collective-permute-done | bytes 262176 | tf_op jit(solution)/shard_map/ppermute | solution.py:45
  56.0 4.1 %collective-permute-done.15 = bf16[4,32,1024]{2,1,0:T(8,128)(2,1)S(1)} collective-permute-done((bf16[4,32,1024]{2,1,0:T(8,128)(2,1)S(1)}, bf16[4,32,1024]{2,1,0:T(8,128)(2,1)S(1)}, u32[]{:S(2)}, u32[]{:S(2)}) %collective-permute-start.15) | collective-permute-done | bytes 262176 | tf_op jit(solution)/shard_map/ppermute | solution.py:49
  62.2 1.8 collective-permute-start.16
  64.0 1.7 collective-permute-start.17
  67.0 11.5 %shard_map.152 = (bf16[1024,1024]{1,0:T(8,128)(2,1)}, bf16[1024,384]{1,0:T(8,128)(2,1)}, bf16[512,128]{1,0:T(8,128)(2,1)}, bf16[512,128]{1,0:T(8,128)(2,1)}) custom-call(s32[4]{0:T(128)} %pad_add_fusion.where_ref, bf16[128,1024]{1,0:T(8,128)(2,1)} %copy-done.20, bf16[128,1024]{1,0:T(8,128)(2,1)} %collective-permute-done.5.refs_1_, ...), custom_call_target="tpu_custom_call" | custom-call | flops 1342177280 | bytes 4194304 | tf_op jit(solution)/shard_map/pallas_call | solution.py:184
  78.6 11.4 %collective-permute-done.16 = bf16[256,1024]{1,0:T(8,128)(2,1)S(1)} collective-permute-done((bf16[256,1024]{1,0:T(8,128)(2,1)S(1)}, bf16[256,1024]{1,0:T(8,128)(2,1)S(1)}, u32[]{:S(2)}, u32[]{:S(2)}) %collective-permute-start.16) | collective-permute-done | bytes 524320 | tf_op jit(solution)/shard_map/ppermute | solution.py:45
  90.1 2.7 collective-permute-done.19
  94.1 2.6 collective-permute-done.20
  98.2 2.5 collective-permute-start.35
  100.7 3.4 %collective-permute-done.21 = bf16[64,1024]{1,0:T(8,128)(2,1)S(1)} collective-permute-done((bf16[64,1024]{1,0:T(8,128)(2,1)S(1)}, bf16[64,1024]{1,0:T(8,128)(2,1)S(1)}, u32[]{:S(2)}, u32[]{:S(2)}) %collective-permute-start.21) | collective-permute-done | bytes 131104 | tf_op jit(solution)/shard_map/ppermute | solution.py:45
  106.2 6.8 %collective-permute-done.35 = bf16[128,1024]{1,0:T(8,128)(2,1)S(1)} collective-permute-done((bf16[128,1024]{1,0:T(8,128)(2,1)}, bf16[128,1024]{1,0:T(8,128)(2,1)S(1)}, u32[]{:S(2)}, u32[]{:S(2)}) %collective-permute-start.35) | collective-permute-done | bytes 262176 | tf_op jit(solution)/shard_map/ppermute | solution.py:45
  113.7 2.4 collective-permute-done.24
  118.5 3.9 %collective-permute-done.36 = bf16[128,1024]{1,0:T(8,128)(2,1)S(1)} collective-permute-done((bf16[128,1024]{1,0:T(8,128)(2,1)S(1)}, bf16[128,1024]{1,0:T(8,128)(2,1)S(1)}, u32[]{:S(2)}, u32[]{:S(2)}) %collective-permute-start.36) | collective-permute-done | bytes 262176 | tf_op jit(solution)/shard_map/ppermute | solution.py:49
  123.7 2.3 collective-permute-start.28
  126.1 2.5 collective-permute-done.27
  131.5 2.5 fusion.60
  136.9 2.6 collective-permute-done.37
  142.9 4.0 %collective-permute-done.38 = bf16[64,1024]{1,0:T(8,128)(2,1)} collective-permute-done((bf16[64,1024]{1,0:T(8,128)(2,1)}, bf16[64,1024]{1,0:T(8,128)(2,1)}, u32[]{:S(2)}, u32[]{:S(2)}) %collective-permute-start.38) | collective-permute-done | bytes 131104 | tf_op jit(solution)/shard_map/ppermute | solution.py:45
  155.4 1.6 collective-permute-done.41
  161.4 4.5 %collective-permute-done.43 = bf16[128,1024]{1,0:T(8,128)(2,1)S(1)} collective-permute-done((bf16[128,1024]{1,0:T(8,128)(2,1)S(1)}, bf16[128,1024]{1,0:T(8,128)(2,1)S(1)}, u32[]{:S(2)}, u32[]{:S(2)}) %collective-permute-start.43) | collective-permute-done | bytes 262176 | tf_op jit(solution)/shard_map/ppermute | solution.py:45
  170.9 2.6 collective-permute-done.45
  175.2 1.9 multiply_convert_fusion
  181.0 2.3 fusion.78
  185.9 1.6 collective-permute-start.51
  190.2 1.6 collective-permute-done.51
  196.9 3.2 collective-permute-done.54
  203.9 1.4 collective-permute-start.56
  205.4 1.7 slice_select_fusion
  207.9 2.7 collective-permute-done.56
  216.7 2.0 collective-permute-done.58
  222.1 1.7 collective-permute-start.63
  224.6 6.8 %collective-permute-done.63.got_ref = bf16[512,128]{1,0:T(8,128)(2,1)S(1)} collective-permute-done((bf16[512,128]{1,0:T(8,128)(2,1)S(1)}, bf16[512,128]{1,0:T(8,128)(2,1)S(1)}, u32[]{:S(2)}, u32[]{:S(2)}) %collective-permute-start.63) | collective-permute-done | bytes 131104 | tf_op jit(solution)/shard_map/ppermute | solution.py:45
  231.5 2.4 add_bitcast_fusion
  235.2 11.4 %shard_map.153 = (bf16[1024,384]{1,0:T(8,128)(2,1)}, bf16[512,384]{1,0:T(8,128)(2,1)}, bf16[512,384]{1,0:T(8,128)(2,1)}) custom-call(s32[4]{0:T(128)} %pad_add_fusion.where_ref, bf16[1024,384]{1,0:T(8,128)(2,1)} %get-tuple-element.120.mixed_ref, bf16[512,128]{1,0:T(8,128)(2,1)} %bitcast.239, bf16[512,128]{1,0:T(8,128)(2,1)} %copy-done.46), custom_call_target="tpu_custom_call" | custom-call | flops 1342177280 | bytes 4194304 | tf_op jit(solution)/shard_map/pallas_call | solution.py:265
  246.6 6.8 %collective-permute-done.65 = bf16[1,192,1024]{2,1,0:T(8,128)(2,1)S(1)} collective-permute-done((bf16[1,192,1024]{2,1,0:T(8,128)(2,1)S(1)}, bf16[1,192,1024]{2,1,0:T(8,128)(2,1)S(1)}, u32[]{:S(2)}, u32[]{:S(2)}) %collective-permute-start.65) | collective-permute-done | bytes 393248 | tf_op jit(solution)/shard_map/ppermute | solution.py:45
  253.5 2.3 multiply_reduce_fusion
  258.6 1.5 collective-permute-start.73
  262.0 2.8 collective-permute-done.69
  264.7 1.8 collective-permute-start.70
  267.2 4.3 %collective-permute-done.70 = f32[3,1024]{1,0:T(4,128)S(1)} collective-permute-done((f32[3,1024]{1,0:T(4,128)S(1)}, f32[3,1024]{1,0:T(4,128)S(1)}, u32[]{:S(2)}, u32[]{:S(2)}) %collective-permute-start.70) | collective-permute-done | bytes 12320 | tf_op jit(solution)/shard_map/ppermute | solution.py:45
  271.5 5.1 %collective-permute-done.72 = bf16[512,384]{1,0:T(8,128)(2,1)} collective-permute-done((bf16[512,384]{1,0:T(8,128)(2,1)}, bf16[512,384]{1,0:T(8,128)(2,1)}, u32[]{:S(2)}, u32[]{:S(2)}) %collective-permute-start.72) | collective-permute-done | bytes 393248 | tf_op jit(solution)/shard_map/ppermute | solution.py:45
  280.3 2.8 collective-permute-start.80
  284.6 9.0 %collective-permute-done.75 = bf16[1,64,1024]{2,1,0:T(8,128)(2,1)S(1)} collective-permute-done((bf16[1,64,1024]{2,1,0:T(8,128)(2,1)S(1)}, bf16[1,64,1024]{2,1,0:T(8,128)(2,1)S(1)}, u32[]{:S(2)}, u32[]{:S(2)}) %collective-permute-start.75) | collective-permute-done | bytes 131104 | tf_op jit(solution)/shard_map/ppermute | solution.py:45
  295.3 2.1 collective-permute-start.85
  297.4 2.4 collective-permute-done.76
  299.8 3.2 collective-permute-done.77
  303.2 1.5 collective-permute-start.78
  304.7 5.8 %collective-permute-done.85 = bf16[1,128,1024]{2,1,0:T(8,128)(2,1)S(1)} collective-permute-done((bf16[1,128,1024]{2,1,0:T(8,128)(2,1)S(1)}, bf16[1,128,1024]{2,1,0:T(8,128)(2,1)S(1)}, u32[]{:S(2)}, u32[]{:S(2)}) %collective-permute-start.85) | collective-permute-done | bytes 262176 | tf_op jit(solution)/shard_map/ppermute | solution.py:45
  311.8 1.9 collective-permute-start.86
  317.1 6.6 %collective-permute-start.82 = (bf16[32,1024]{1,0:T(8,128)(2,1)S(1)}, bf16[32,1024]{1,0:T(8,128)(2,1)S(1)}, u32[]{:S(2)}, u32[]{:S(2)}) collective-permute-start(bf16[32,1024]{1,0:T(8,128)(2,1)S(1)} %get-tuple-element.202), channel_id=1, source_target_pairs={{8,0},{1,1},{25,2},{18,3},{11,4},{4,5},{28,6},{21,7},{14,8},{7,9},... | collective-permute-start | bytes 196616 | tf_op jit(solution)/shard_map/ppermute | solution.py:473
  323.8 4.4 %collective-permute-start.81 = (bf16[32,1024]{1,0:T(8,128)(2,1)S(1)}, bf16[32,1024]{1,0:T(8,128)(2,1)S(1)}, u32[]{:S(2)}, u32[]{:S(2)}) collective-permute-start(bf16[32,1024]{1,0:T(8,128)(2,1)S(1)} %get-tuple-element.201), channel_id=1, source_target_pairs={{0,0},{24,1},{17,2},{10,3},{3,4},{27,5},{20,6},{13,7},{6,8},{30,9}... | collective-permute-start | bytes 196616 | tf_op jit(solution)/shard_map/ppermute | solution.py:473
  328.1 1.9 collective-permute-start.84
  333.1 3.0 collective-permute-done.84
  (359 shorter events, 101.4 us)
Async XLA Ops:
  2.5 15.7 %collective-permute-start = (bf16[64,1024]{1,0:T(8,128)(2,1)S(1)}, bf16[64,1024]{1,0:T(8,128)(2,1)S(1)}, u32[]{:S(2)}, u32[]{:S(2)}) collective-permute-start(bf16[64,1024]{1,0:T(8,128)(2,1)S(1)} %get-tuple-element.211), channel_id=1, source_target_pairs={{0,8},{1,9},{2,10},{3,11},{4,12},{5,13},{6,14},{7,15},{8,0},{9,1},... | collective-permute-start | bytes 393224 | tf_op jit(solution)/shard_map/ppermute | solution.py:45
  6.1 12.1 %collective-permute-start.1 = (bf16[32,1024]{1,0:T(8,128)(2,1)S(1)}, bf16[32,1024]{1,0:T(8,128)(2,1)S(1)}, u32[]{:S(2)}, u32[]{:S(2)}) collective-permute-start(bf16[32,1024]{1,0:T(8,128)(2,1)S(1)} %get-tuple-element.216), channel_id=1, source_target_pairs={{0,0},{1,24},{2,17},{3,10},{4,3},{5,27},{6,20},{7,13},{8,6},{9,30}... | collective-permute-start | bytes 196616 | tf_op jit(solution)/shard_map/ppermute | solution.py:320
  8.6 9.6 %collective-permute-start.2 = (bf16[32,1024]{1,0:T(8,128)(2,1)S(1)}, bf16[32,1024]{1,0:T(8,128)(2,1)S(1)}, u32[]{:S(2)}, u32[]{:S(2)}) collective-permute-start(bf16[32,1024]{1,0:T(8,128)(2,1)S(1)} %get-tuple-element.217), channel_id=1, source_target_pairs={{0,8},{1,1},{2,25},{3,18},{4,11},{5,4},{6,28},{7,21},{8,14},{9,7},... | collective-permute-start | bytes 196616 | tf_op jit(solution)/shard_map/ppermute | solution.py:320
  12.4 5.9 %collective-permute-start.3 = (bf16[32,1024]{1,0:T(8,128)(2,1)S(1)}, bf16[32,1024]{1,0:T(8,128)(2,1)S(1)}, u32[]{:S(2)}, u32[]{:S(2)}) collective-permute-start(bf16[32,1024]{1,0:T(8,128)(2,1)S(1)} %get-tuple-element.215), channel_id=1, source_target_pairs={{0,16},{1,9},{2,2},{3,26},{4,19},{5,12},{6,5},{7,29},{8,22},{9,15}... | collective-permute-start | bytes 196616 | tf_op jit(solution)/shard_map/ppermute | solution.py:320
  13.1 11.4 %collective-permute-start.4 = (bf16[32,1024]{1,0:T(8,128)(2,1)}, bf16[32,1024]{1,0:T(8,128)(2,1)S(1)}, u32[]{:S(2)}, u32[]{:S(2)}) collective-permute-start(bf16[32,1024]{1,0:T(8,128)(2,1)} %param.20), channel_id=1, source_target_pairs={{0,0},{1,8},{2,16},{3,24},{4,1},{5,9},{6,17},{7,25},{8,2},{9,10},{... | collective-permute-start | bytes 196616 | tf_op jit(solution)/shard_map/ppermute | solution.py:321
  24.4 6.2 %collective-permute-start.9 = (bf16[128,1024]{1,0:T(8,128)(2,1)S(1)}, bf16[128,1024]{1,0:T(8,128)(2,1)}, u32[]{:S(2)}, u32[]{:S(2)}) collective-permute-start(bf16[128,1024]{1,0:T(8,128)(2,1)S(1)} %pad_maximum_fusion.12.refs_0_), channel_id=1, source_target_pairs={{0,1},{1,0},{2,3},{3,2},{4,5},{5,4},{6,7},{7,6},{8,9},{9,8},{10,11... | collective-permute-start | bytes 786440 | tf_op jit(solution)/shard_map/ppermute | solution.py:45
  24.4 54.2 %collective-permute-start.18 = (bf16[128,1024]{1,0:T(8,128)(2,1)}, bf16[128,1024]{1,0:T(8,128)(2,1)}, u32[]{:S(2)}, u32[]{:S(2)}) collective-permute-start(bf16[128,1024]{1,0:T(8,128)(2,1)} %param.22), channel_id=1, source_target_pairs={{0,0},{1,16},{2,1},{3,17},{4,2},{5,18},{6,3},{7,19},{8,4},{9,20},{... | collective-permute-start | bytes 786440 | tf_op jit(solution)/shard_map/ppermute | solution.py:319
  27.0 16.4 %collective-permute-start.5 = (bf16[128,1024]{1,0:T(8,128)(2,1)S(1)}, bf16[128,1024]{1,0:T(8,128)(2,1)}, u32[]{:S(2)}, u32[]{:S(2)}) collective-permute-start(bf16[128,1024]{1,0:T(8,128)(2,1)S(1)} %pad_maximum_fusion.12.refs_0_), channel_id=1, source_target_pairs={{0,2},{1,3},{2,0},{3,1},{4,6},{5,7},{6,4},{7,5},{8,10},{9,11},{10,... | collective-permute-start | bytes 786440 | tf_op jit(solution)/shard_map/ppermute | solution.py:45
  27.9 14.4 %collective-permute-start.6 = (bf16[128,1024]{1,0:T(8,128)(2,1)S(1)}, bf16[128,1024]{1,0:T(8,128)(2,1)}, u32[]{:S(2)}, u32[]{:S(2)}) collective-permute-start(bf16[128,1024]{1,0:T(8,128)(2,1)S(1)} %pad_maximum_fusion.12.refs_0_), channel_id=1, source_target_pairs={{0,4},{1,5},{2,6},{3,7},{4,0},{5,1},{6,2},{7,3},{8,12},{9,13},{10,... | collective-permute-start | bytes 786440 | tf_op jit(solution)/shard_map/ppermute | solution.py:45
  30.7 21.5 %collective-permute-start.13 = (bf16[4,32,1024]{2,1,0:T(8,128)(2,1)S(1)}, bf16[4,32,1024]{2,1,0:T(8,128)(2,1)S(1)}, u32[]{:S(2)}, u32[]{:S(2)}) collective-permute-start(bf16[4,32,1024]{2,1,0:T(8,128)(2,1)S(1)} %get-tuple-element.209), channel_id=1, source_target_pairs={{0,8},{1,9},{2,10},{3,11},{4,12},{5,13},{6,14},{7,15},{8,0},{9,1},... | collective-permute-start | bytes 786440 | tf_op jit(solution)/shard_map/ppermute | solution.py:45
  44.3 9.8 %collective-permute-start.8 = (bf16[64,1024]{1,0:T(8,128)(2,1)S(1)}, bf16[64,1024]{1,0:T(8,128)(2,1)S(1)}, u32[]{:S(2)}, u32[]{:S(2)}) collective-permute-start(bf16[64,1024]{1,0:T(8,128)(2,1)S(1)} %slice.438), channel_id=1, source_target_pairs={{0,4},{1,5},{2,6},{3,7},{4,0},{5,1},{6,2},{7,3},{8,12},{9,13},{10,... | collective-permute-start | bytes 393224 | tf_op jit(solution)/shard_map/ppermute | solution.py:45
  45.8 9.7 %collective-permute-start.14 = (bf16[4,32,1024]{2,1,0:T(8,128)(2,1)S(1)}, bf16[4,32,1024]{2,1,0:T(8,128)(2,1)S(1)}, u32[]{:S(2)}, u32[]{:S(2)}) collective-permute-start(bf16[4,32,1024]{2,1,0:T(8,128)(2,1)S(1)} %get-tuple-element.209), channel_id=1, source_target_pairs={{0,16},{16,0},{1,17},{17,1},{2,18},{18,2},{3,19},{19,3},{4,20},{20... | collective-permute-start | bytes 786440 | tf_op jit(solution)/shard_map/ppermute | solution.py:49
  48.6 13.5 %collective-permute-start.10 = (bf16[128,1024]{1,0:T(8,128)(2,1)}, bf16[128,1024]{1,0:T(8,128)(2,1)}, u32[]{:S(2)}, u32[]{:S(2)}) collective-permute-start(bf16[128,1024]{1,0:T(8,128)(2,1)} %collective-permute-done.5.refs_1_), channel_id=1, source_target_pairs={{0,1},{1,0},{2,3},{3,2},{4,5},{5,4},{6,7},{7,6},{8,9},{9,8},{10,11... | collective-permute-start | bytes 786440 | tf_op jit(solution)/shard_map/ppermute | solution.py:45
  52.2 8.0 %collective-permute-start.15 = (bf16[4,32,1024]{2,1,0:T(8,128)(2,1)S(1)}, bf16[4,32,1024]{2,1,0:T(8,128)(2,1)S(1)}, u32[]{:S(2)}, u32[]{:S(2)}) collective-permute-start(bf16[4,32,1024]{2,1,0:T(8,128)(2,1)S(1)} %collective-permute-done.13), channel_id=1, source_target_pairs={{0,16},{16,0},{1,17},{17,1},{2,18},{18,2},{3,19},{19,3},{4,20},{20... | collective-permute-start | bytes 786440 | tf_op jit(solution)/shard_map/ppermute | solution.py:49
  54.1 8.0 %collective-permute-start.11 = (bf16[128,1024]{1,0:T(8,128)(2,1)}, bf16[128,1024]{1,0:T(8,128)(2,1)}, u32[]{:S(2)}, u32[]{:S(2)}) collective-permute-start(bf16[128,1024]{1,0:T(8,128)(2,1)} %collective-permute-done.6.refs_2_), channel_id=1, source_target_pairs={{0,1},{1,0},{2,3},{3,2},{4,5},{5,4},{6,7},{7,6},{8,9},{9,8},{10,11... | collective-permute-start | bytes 786440 | tf_op jit(solution)/shard_map/ppermute | solution.py:45
  55.5 6.7 %collective-permute-start.12 = (bf16[128,1024]{1,0:T(8,128)(2,1)}, bf16[128,1024]{1,0:T(8,128)(2,1)S(1)}, u32[]{:S(2)}, u32[]{:S(2)}) collective-permute-start(bf16[128,1024]{1,0:T(8,128)(2,1)} %constant_dynamic-update-slice_fusion.refs_3_), channel_id=1, source_target_pairs={{0,1},{1,0},{2,3},{3,2},{4,5},{5,4},{6,7},{7,6},{8,9},{9,8},{10,11... | collective-permute-start | bytes 786440 | tf_op jit(solution)/shard_map/ppermute | solution.py:45
  62.2 27.9 %collective-permute-start.16 = (bf16[256,1024]{1,0:T(8,128)(2,1)S(1)}, bf16[256,1024]{1,0:T(8,128)(2,1)S(1)}, u32[]{:S(2)}, u32[]{:S(2)}) collective-permute-start(bf16[256,1024]{1,0:T(8,128)(2,1)S(1)} %copy-done.37), channel_id=1, source_target_pairs={{0,8},{1,9},{2,10},{3,11},{4,12},{5,13},{6,14},{7,15},{8,0},{9,1},... | collective-permute-start | bytes 1572872 | tf_op jit(solution)/shard_map/ppermute | solution.py:45
  64.0 26.1 %collective-permute-start.17 = (bf16[256,1024]{1,0:T(8,128)(2,1)S(1)}, bf16[256,1024]{1,0:T(8,128)(2,1)S(1)}, u32[]{:S(2)}, u32[]{:S(2)}) collective-permute-start(bf16[256,1024]{1,0:T(8,128)(2,1)S(1)} %copy-done.37), channel_id=1, source_target_pairs={{0,16},{16,0},{1,17},{17,1},{2,18},{18,2},{3,19},{19,3},{4,20},{20... | collective-permute-start | bytes 1572872 | tf_op jit(solution)/shard_map/ppermute | solution.py:49
  78.5 14.3 %collective-permute-start.19 = (bf16[512,128]{1,0:T(8,128)(2,1)}, bf16[512,128]{1,0:T(8,128)(2,1)S(1)}, u32[]{:S(2)}, u32[]{:S(2)}) collective-permute-start(bf16[512,128]{1,0:T(8,128)(2,1)} %get-tuple-element.112), channel_id=1, source_target_pairs={{0,8},{1,9},{2,10},{3,11},{4,12},{5,13},{6,14},{7,15},{8,0},{9,1},... | collective-permute-start | bytes 393224 | tf_op jit(solution)/shard_map/ppermute | solution.py:45
  97.3 6.8 %collective-permute-start.21 = (bf16[64,1024]{1,0:T(8,128)(2,1)S(1)}, bf16[64,1024]{1,0:T(8,128)(2,1)S(1)}, u32[]{:S(2)}, u32[]{:S(2)}) collective-permute-start(bf16[64,1024]{1,0:T(8,128)(2,1)S(1)} %get-tuple-element.194), channel_id=1, source_target_pairs={{0,4},{1,5},{2,6},{3,7},{4,0},{5,1},{6,2},{7,3},{8,12},{9,13},{10,... | collective-permute-start | bytes 393224 | tf_op jit(solution)/shard_map/ppermute | solution.py:45
  97.3 6.7 %collective-permute-start.23 = (bf16[64,1024]{1,0:T(8,128)(2,1)S(1)}, bf16[64,1024]{1,0:T(8,128)(2,1)S(1)}, u32[]{:S(2)}, u32[]{:S(2)}) collective-permute-start(bf16[64,1024]{1,0:T(8,128)(2,1)S(1)} %get-tuple-element.193), channel_id=1, source_target_pairs={{0,2},{1,3},{2,0},{3,1},{4,6},{5,7},{6,4},{7,5},{8,10},{9,11},{10,... | collective-permute-start | bytes 393224 | tf_op jit(solution)/shard_map/ppermute | solution.py:45
  98.2 14.9 %collective-permute-start.35 = (bf16[128,1024]{1,0:T(8,128)(2,1)}, bf16[128,1024]{1,0:T(8,128)(2,1)S(1)}, u32[]{:S(2)}, u32[]{:S(2)}) collective-permute-start(bf16[128,1024]{1,0:T(8,128)(2,1)} %collective-permute-done.18), channel_id=1, source_target_pairs={{0,8},{1,9},{2,10},{3,11},{4,12},{5,13},{6,14},{7,15},{8,0},{9,1},... | collective-permute-start | bytes 786440 | tf_op jit(solution)/shard_map/ppermute | solution.py:45
  104.1 12.0 %collective-permute-start.24 = (bf16[128,1024]{1,0:T(8,128)(2,1)S(1)}, bf16[128,1024]{1,0:T(8,128)(2,1)S(1)}, u32[]{:S(2)}, u32[]{:S(2)}) collective-permute-start(bf16[128,1024]{1,0:T(8,128)(2,1)S(1)} %pad_maximum_fusion.15), channel_id=1, source_target_pairs={{0,4},{1,5},{2,6},{3,7},{4,0},{5,1},{6,2},{7,3},{8,12},{9,13},{10,... | collective-permute-start | bytes 786440 | tf_op jit(solution)/shard_map/ppermute | solution.py:45
  104.8 11.4 %collective-permute-start.22 = (bf16[128,1024]{1,0:T(8,128)(2,1)S(1)}, bf16[128,1024]{1,0:T(8,128)(2,1)S(1)}, u32[]{:S(2)}, u32[]{:S(2)}) collective-permute-start(bf16[128,1024]{1,0:T(8,128)(2,1)S(1)} %pad_maximum_fusion.14), channel_id=1, source_target_pairs={{0,2},{1,3},{2,0},{3,1},{4,6},{5,7},{6,4},{7,5},{8,10},{9,11},{10,... | collective-permute-start | bytes 786440 | tf_op jit(solution)/shard_map/ppermute | solution.py:45
  105.6 11.6 %collective-permute-start.34 = (bf16[128,1024]{1,0:T(8,128)(2,1)}, bf16[128,1024]{1,0:T(8,128)(2,1)S(1)}, u32[]{:S(2)}, u32[]{:S(2)}) collective-permute-start(bf16[128,1024]{1,0:T(8,128)(2,1)} %collective-permute-done.18), channel_id=1, source_target_pairs={{0,16},{16,0},{1,17},{17,1},{2,18},{18,2},{3,19},{19,3},{4,20},{20... | collective-permute-start | bytes 786440 | tf_op jit(solution)/shard_map/ppermute | solution.py:49
  113.1 9.2 %collective-permute-start.36 = (bf16[128,1024]{1,0:T(8,128)(2,1)S(1)}, bf16[128,1024]{1,0:T(8,128)(2,1)S(1)}, u32[]{:S(2)}, u32[]{:S(2)}) collective-permute-start(bf16[128,1024]{1,0:T(8,128)(2,1)S(1)} %collective-permute-done.35), channel_id=1, source_target_pairs={{0,16},{16,0},{1,17},{17,1},{2,18},{18,2},{3,19},{19,3},{4,20},{20... | collective-permute-start | bytes 786440 | tf_op jit(solution)/shard_map/ppermute | solution.py:49
  116.5 6.9 %collective-permute-start.26 = (bf16[128,1024]{1,0:T(8,128)(2,1)S(1)}, bf16[128,1024]{1,0:T(8,128)(2,1)S(1)}, u32[]{:S(2)}, u32[]{:S(2)}) collective-permute-start(bf16[128,1024]{1,0:T(8,128)(2,1)S(1)} %get-tuple-element.162), channel_id=1, source_target_pairs={{0,4},{1,5},{2,6},{3,7},{4,0},{5,1},{6,2},{7,3},{8,12},{9,13},{10,... | collective-permute-start | bytes 786440 | tf_op jit(solution)/shard_map/ppermute | solution.py:45
  116.6 7.1 %collective-permute-start.25 = (bf16[128,1024]{1,0:T(8,128)(2,1)S(1)}, bf16[128,1024]{1,0:T(8,128)(2,1)S(1)}, u32[]{:S(2)}, u32[]{:S(2)}) collective-permute-start(bf16[128,1024]{1,0:T(8,128)(2,1)S(1)} %get-tuple-element.162), channel_id=1, source_target_pairs={{0,2},{1,3},{2,0},{3,1},{4,6},{5,7},{6,4},{7,5},{8,10},{9,11},{10,... | collective-permute-start | bytes 786440 | tf_op jit(solution)/shard_map/ppermute | solution.py:45
  116.7 14.8 %collective-permute-start.33 = (bf16[256,1024]{1,0:T(8,128)(2,1)S(1)}, bf16[256,1024]{1,0:T(8,128)(2,1)S(1)}, u32[]{:S(2)}, u32[]{:S(2)}) collective-permute-start(bf16[256,1024]{1,0:T(8,128)(2,1)S(1)} %collective-permute-done.16), channel_id=1, source_target_pairs={{0,16},{16,0},{1,17},{17,1},{2,18},{18,2},{3,19},{19,3},{4,20},{20... | collective-permute-start | bytes 1572872 | tf_op jit(solution)/shard_map/ppermute | solution.py:49
  122.5 7.0 %collective-permute-start.29 = (bf16[128,1024]{1,0:T(8,128)(2,1)S(1)}, bf16[128,1024]{1,0:T(8,128)(2,1)S(1)}, u32[]{:S(2)}, u32[]{:S(2)}) collective-permute-start(bf16[128,1024]{1,0:T(8,128)(2,1)S(1)} %get-tuple-element.162), channel_id=1, source_target_pairs={{0,1},{1,0},{2,3},{3,2},{4,5},{5,4},{6,7},{7,6},{8,9},{9,8},{10,11... | collective-permute-start | bytes 786440 | tf_op jit(solution)/shard_map/ppermute | solution.py:45
  123.7 5.7 %collective-permute-start.28 = (bf16[64,1024]{1,0:T(8,128)(2,1)S(1)}, bf16[64,1024]{1,0:T(8,128)(2,1)S(1)}, u32[]{:S(2)}, u32[]{:S(2)}) collective-permute-start(bf16[64,1024]{1,0:T(8,128)(2,1)S(1)} %slice.452), channel_id=1, source_target_pairs={{0,4},{1,5},{2,6},{3,7},{4,0},{5,1},{6,2},{7,3},{8,12},{9,13},{10,... | collective-permute-start | bytes 393224 | tf_op jit(solution)/shard_map/ppermute | solution.py:45
  141.1 5.9 %collective-permute-start.38 = (bf16[64,1024]{1,0:T(8,128)(2,1)}, bf16[64,1024]{1,0:T(8,128)(2,1)}, u32[]{:S(2)}, u32[]{:S(2)}) collective-permute-start(bf16[64,1024]{1,0:T(8,128)(2,1)} %get-tuple-element.190), channel_id=1, source_target_pairs={{0,4},{1,5},{2,6},{3,7},{4,0},{5,1},{6,2},{7,3},{8,12},{9,13},{10,... | collective-permute-start | bytes 393224 | tf_op jit(solution)/shard_map/ppermute | solution.py:45
  149.6 7.5 %collective-permute-start.41 = (bf16[128,1024]{1,0:T(8,128)(2,1)}, bf16[128,1024]{1,0:T(8,128)(2,1)}, u32[]{:S(2)}, u32[]{:S(2)}) collective-permute-start(bf16[128,1024]{1,0:T(8,128)(2,1)} %pad_maximum_fusion.18), channel_id=1, source_target_pairs={{0,4},{1,5},{2,6},{3,7},{4,0},{5,1},{6,2},{7,3},{8,12},{9,13},{10,... | collective-permute-start | bytes 786440 | tf_op jit(solution)/shard_map/ppermute | solution.py:45
  151.2 7.1 %collective-permute-start.39 = (bf16[128,1024]{1,0:T(8,128)(2,1)}, bf16[128,1024]{1,0:T(8,128)(2,1)S(1)}, u32[]{:S(2)}, u32[]{:S(2)}) collective-permute-start(bf16[128,1024]{1,0:T(8,128)(2,1)} %pad_maximum_fusion.17), channel_id=1, source_target_pairs={{0,2},{1,3},{2,0},{3,1},{4,6},{5,7},{6,4},{7,5},{8,10},{9,11},{10,... | collective-permute-start | bytes 786440 | tf_op jit(solution)/shard_map/ppermute | solution.py:45
  159.4 6.4 %collective-permute-start.43 = (bf16[128,1024]{1,0:T(8,128)(2,1)S(1)}, bf16[128,1024]{1,0:T(8,128)(2,1)S(1)}, u32[]{:S(2)}, u32[]{:S(2)}) collective-permute-start(bf16[128,1024]{1,0:T(8,128)(2,1)S(1)} %get-tuple-element.157), channel_id=1, source_target_pairs={{0,4},{1,5},{2,6},{3,7},{4,0},{5,1},{6,2},{7,3},{8,12},{9,13},{10,... | collective-permute-start | bytes 786440 | tf_op jit(solution)/shard_map/ppermute | solution.py:45
  160.7 7.8 %collective-permute-start.42 = (bf16[128,1024]{1,0:T(8,128)(2,1)S(1)}, bf16[128,1024]{1,0:T(8,128)(2,1)S(1)}, u32[]{:S(2)}, u32[]{:S(2)}) collective-permute-start(bf16[128,1024]{1,0:T(8,128)(2,1)S(1)} %get-tuple-element.157), channel_id=1, source_target_pairs={{0,2},{1,3},{2,0},{3,1},{4,6},{5,7},{6,4},{7,5},{8,10},{9,11},{10,... | collective-permute-start | bytes 786440 | tf_op jit(solution)/shard_map/ppermute | solution.py:45
  161.4 12.2 %collective-permute-start.46 = (bf16[128,1024]{1,0:T(8,128)(2,1)S(1)}, bf16[128,1024]{1,0:T(8,128)(2,1)S(1)}, u32[]{:S(2)}, u32[]{:S(2)}) collective-permute-start(bf16[128,1024]{1,0:T(8,128)(2,1)S(1)} %get-tuple-element.157), channel_id=1, source_target_pairs={{0,1},{1,0},{2,3},{3,2},{4,5},{5,4},{6,7},{7,6},{8,9},{9,8},{10,11... | collective-permute-start | bytes 786440 | tf_op jit(solution)/shard_map/ppermute | solution.py:45
  178.5 6.0 %collective-permute-start.50 = (bf16[512,1024]{1,0:T(8,128)(2,1)S(1)}, bf16[512,1024]{1,0:T(8,128)(2,1)S(1)}, u32[]{:S(2)}, u32[]{:S(2)}) collective-permute-start(bf16[512,1024]{1,0:T(8,128)(2,1)S(1)} %convolution_convert_fusion.2), channel_id=1, source_target_pairs={{0,1},{1,0},{2,3},{3,2},{4,5},{5,4},{6,7},{7,6},{8,9},{9,8},{10,11... | collective-permute-start | bytes 3145736 | tf_op jit(solution)/shard_map/ppermute | solution.py:45
  184.5 40.1 %collective-permute-start.64 = (bf16[2,256,1024]{2,1,0:T(8,128)(2,1)}, bf16[2,256,1024]{2,1,0:T(8,128)(2,1)}, u32[]{:S(2)}, u32[]{:S(2)}) collective-permute-start(bf16[2,256,1024]{2,1,0:T(8,128)(2,1)} %bitcast.41), channel_id=1, source_target_pairs={{0,16},{16,0},{1,17},{17,1},{2,18},{18,2},{3,19},{19,3},{4,20},{20... | collective-permute-start | bytes 3145736 | tf_op jit(solution)/shard_map/ppermute | solution.py:49
  185.9 5.8 %collective-permute-start.51 = (bf16[64,1024]{1,0:T(8,128)(2,1)S(1)}, bf16[64,1024]{1,0:T(8,128)(2,1)S(1)}, u32[]{:S(2)}, u32[]{:S(2)}) collective-permute-start(bf16[64,1024]{1,0:T(8,128)(2,1)S(1)} %get-tuple-element.186), channel_id=1, source_target_pairs={{0,4},{1,5},{2,6},{3,7},{4,0},{5,1},{6,2},{7,3},{8,12},{9,13},{10,... | collective-permute-start | bytes 393224 | tf_op jit(solution)/shard_map/ppermute | solution.py:45
  192.8 7.3 %collective-permute-start.54 = (bf16[128,1024]{1,0:T(8,128)(2,1)S(1)}, bf16[128,1024]{1,0:T(8,128)(2,1)S(1)}, u32[]{:S(2)}, u32[]{:S(2)}) collective-permute-start(bf16[128,1024]{1,0:T(8,128)(2,1)S(1)} %pad_maximum_fusion.21), channel_id=1, source_target_pairs={{0,4},{1,5},{2,6},{3,7},{4,0},{5,1},{6,2},{7,3},{8,12},{9,13},{10,... | collective-permute-start | bytes 786440 | tf_op jit(solution)/shard_map/ppermute | solution.py:45
  193.7 7.3 %collective-permute-start.52 = (bf16[128,1024]{1,0:T(8,128)(2,1)S(1)}, bf16[128,1024]{1,0:T(8,128)(2,1)S(1)}, u32[]{:S(2)}, u32[]{:S(2)}) collective-permute-start(bf16[128,1024]{1,0:T(8,128)(2,1)S(1)} %pad_maximum_fusion.20), channel_id=1, source_target_pairs={{0,2},{1,3},{2,0},{3,1},{4,6},{5,7},{6,4},{7,5},{8,10},{9,11},{10,... | collective-permute-start | bytes 786440 | tf_op jit(solution)/shard_map/ppermute | solution.py:45
  195.6 51.1 %collective-permute-start.66 = (bf16[2,128,1024]{2,1,0:T(8,128)(2,1)}, bf16[2,128,1024]{2,1,0:T(8,128)(2,1)}, u32[]{:S(2)}, u32[]{:S(2)}) collective-permute-start(bf16[2,128,1024]{2,1,0:T(8,128)(2,1)} %fusion.10), channel_id=1, source_target_pairs={{0,16},{16,0},{1,17},{17,1},{2,18},{18,2},{3,19},{19,3},{4,20},{20... | collective-permute-start | bytes 1572872 | tf_op jit(solution)/shard_map/ppermute | solution.py:49
  203.1 9.7 %collective-permute-start.55 = (bf16[128,1024]{1,0:T(8,128)(2,1)}, bf16[128,1024]{1,0:T(8,128)(2,1)}, u32[]{:S(2)}, u32[]{:S(2)}) collective-permute-start(bf16[128,1024]{1,0:T(8,128)(2,1)} %get-tuple-element.156), channel_id=1, source_target_pairs={{0,2},{1,3},{2,0},{3,1},{4,6},{5,7},{6,4},{7,5},{8,10},{9,11},{10,... | collective-permute-start | bytes 786440 | tf_op jit(solution)/shard_map/ppermute | solution.py:45
  203.9 6.7 %collective-permute-start.56 = (bf16[128,1024]{1,0:T(8,128)(2,1)}, bf16[128,1024]{1,0:T(8,128)(2,1)}, u32[]{:S(2)}, u32[]{:S(2)}) collective-permute-start(bf16[128,1024]{1,0:T(8,128)(2,1)} %get-tuple-element.156), channel_id=1, source_target_pairs={{0,4},{1,5},{2,6},{3,7},{4,0},{5,1},{6,2},{7,3},{8,12},{9,13},{10,... | collective-permute-start | bytes 786440 | tf_op jit(solution)/shard_map/ppermute | solution.py:45
  207.1 11.7 %collective-permute-start.59 = (bf16[128,1024]{1,0:T(8,128)(2,1)}, bf16[128,1024]{1,0:T(8,128)(2,1)S(1)}, u32[]{:S(2)}, u32[]{:S(2)}) collective-permute-start(bf16[128,1024]{1,0:T(8,128)(2,1)} %get-tuple-element.156), channel_id=1, source_target_pairs={{0,1},{1,0},{2,3},{3,2},{4,5},{5,4},{6,7},{7,6},{8,9},{9,8},{10,11... | collective-permute-start | bytes 786440 | tf_op jit(solution)/shard_map/ppermute | solution.py:45
  222.1 9.4 %collective-permute-start.63 = (bf16[512,128]{1,0:T(8,128)(2,1)S(1)}, bf16[512,128]{1,0:T(8,128)(2,1)S(1)}, u32[]{:S(2)}, u32[]{:S(2)}) collective-permute-start(bf16[512,128]{1,0:T(8,128)(2,1)S(1)} %bitcast.240), channel_id=1, source_target_pairs={{0,8},{1,9},{2,10},{3,11},{4,12},{5,13},{6,14},{7,15},{8,0},{9,1},... | collective-permute-start | bytes 393224 | tf_op jit(solution)/shard_map/ppermute | solution.py:45
  233.9 19.5 %collective-permute-start.65 = (bf16[1,192,1024]{2,1,0:T(8,128)(2,1)S(1)}, bf16[1,192,1024]{2,1,0:T(8,128)(2,1)S(1)}, u32[]{:S(2)}, u32[]{:S(2)}) collective-permute-start(bf16[1,192,1024]{2,1,0:T(8,128)(2,1)S(1)} %fusion.35), channel_id=1, source_target_pairs={{0,8},{1,9},{2,10},{3,11},{4,12},{5,13},{6,14},{7,15},{8,0},{9,1},... | collective-permute-start | bytes 1179656 | tf_op jit(solution)/shard_map/ppermute | solution.py:45
  255.9 20.7 %collective-permute-start.72 = (bf16[512,384]{1,0:T(8,128)(2,1)}, bf16[512,384]{1,0:T(8,128)(2,1)}, u32[]{:S(2)}, u32[]{:S(2)}) collective-permute-start(bf16[512,384]{1,0:T(8,128)(2,1)} %get-tuple-element.135), channel_id=1, source_target_pairs={{0,8},{1,9},{2,10},{3,11},{4,12},{5,13},{6,14},{7,15},{8,0},{9,1},... | collective-permute-start | bytes 1179656 | tf_op jit(solution)/shard_map/ppermute | solution.py:45
  258.6 18.0 %collective-permute-start.73 = (bf16[4,2,32,1024]{3,2,0,1:T(8,128)(2,1)}, bf16[4,2,32,1024]{3,2,0,1:T(8,128)(2,1)}, u32[]{:S(2)}, u32[]{:S(2)}) collective-permute-start(bf16[4,2,32,1024]{3,2,0,1:T(8,128)(2,1)} %fusion.11), channel_id=1, source_target_pairs={{0,16},{16,0},{1,17},{17,1},{2,18},{18,2},{3,19},{19,3},{4,20},{20... | collective-permute-start | bytes 1572872 | tf_op jit(solution)/shard_map/ppermute | solution.py:49
  264.7 6.8 %collective-permute-start.70 = (f32[3,1024]{1,0:T(4,128)S(1)}, f32[3,1024]{1,0:T(4,128)S(1)}, u32[]{:S(2)}, u32[]{:S(2)}) collective-permute-start(f32[3,1024]{1,0:T(4,128)S(1)} %add.206), channel_id=1, source_target_pairs={{0,4},{1,5},{2,6},{3,7},{4,0},{5,1},{6,2},{7,3},{8,12},{9,13},{10,... | collective-permute-start | bytes 36872 | tf_op jit(solution)/shard_map/ppermute | solution.py:45
  271.5 39.0 %collective-permute-start.71 = (f32[3,1024]{1,0:T(4,128)S(1)}, f32[3,1024]{1,0:T(4,128)S(1)}, u32[]{:S(2)}, u32[]{:S(2)}) collective-permute-start(f32[3,1024]{1,0:T(4,128)S(1)} %add.207), channel_id=1, source_target_pairs={{0,8},{1,9},{2,10},{3,11},{4,12},{5,13},{6,14},{7,15},{8,0},{9,1},... | collective-permute-start | bytes 36872 | tf_op jit(solution)/shard_map/ppermute | solution.py:45
  278.7 14.9 %collective-permute-start.74 = (bf16[512,1024]{1,0:T(8,128)(2,1)S(1)}, bf16[512,1024]{1,0:T(8,128)(2,1)S(1)}, u32[]{:S(2)}, u32[]{:S(2)}) collective-permute-start(bf16[512,1024]{1,0:T(8,128)(2,1)S(1)} %convolution_convert_fusion.1), channel_id=1, source_target_pairs={{0,1},{1,0},{2,3},{3,2},{4,5},{5,4},{6,7},{7,6},{8,9},{9,8},{10,11... | collective-permute-start | bytes 3145736 | tf_op jit(solution)/shard_map/ppermute | solution.py:45
  278.8 14.7 %collective-permute-start.75 = (bf16[1,64,1024]{2,1,0:T(8,128)(2,1)S(1)}, bf16[1,64,1024]{2,1,0:T(8,128)(2,1)S(1)}, u32[]{:S(2)}, u32[]{:S(2)}) collective-permute-start(bf16[1,64,1024]{2,1,0:T(8,128)(2,1)S(1)} %fusion.48), channel_id=1, source_target_pairs={{0,8},{1,9},{2,10},{3,11},{4,12},{5,13},{6,14},{7,15},{8,0},{9,1},... | collective-permute-start | bytes 393224 | tf_op jit(solution)/shard_map/ppermute | solution.py:45
  280.3 35.8 %collective-permute-start.80 = (bf16[4,1,32,1024]{3,2,1,0:T(8,128)(2,1)S(1)}, bf16[4,1,32,1024]{3,2,1,0:T(8,128)(2,1)S(1)}, u32[]{:S(2)}, u32[]{:S(2)}) collective-permute-start(bf16[4,1,32,1024]{3,2,1,0:T(8,128)(2,1)S(1)} %fusion.37), channel_id=1, source_target_pairs={{0,8},{1,9},{2,10},{3,11},{4,12},{5,13},{6,14},{7,15},{8,0},{9,1},... | collective-permute-start | bytes 786440 | tf_op jit(solution)/shard_map/ppermute | solution.py:45
  295.2 7.7 %collective-permute-start.77 = (bf16[64,1024]{1,0:T(8,128)(2,1)S(1)}, bf16[64,1024]{1,0:T(8,128)(2,1)S(1)}, u32[]{:S(2)}, u32[]{:S(2)}) collective-permute-start(bf16[64,1024]{1,0:T(8,128)(2,1)S(1)} %get-tuple-element.181), channel_id=1, source_target_pairs={{0,4},{1,5},{2,6},{3,7},{4,0},{5,1},{6,2},{7,3},{8,12},{9,13},{10,... | collective-permute-start | bytes 393224 | tf_op jit(solution)/shard_map/ppermute | solution.py:45
  295.3 15.2 %collective-permute-start.85 = (bf16[1,128,1024]{2,1,0:T(8,128)(2,1)S(1)}, bf16[1,128,1024]{2,1,0:T(8,128)(2,1)S(1)}, u32[]{:S(2)}, u32[]{:S(2)}) collective-permute-start(bf16[1,128,1024]{2,1,0:T(8,128)(2,1)S(1)} %fusion.39), channel_id=1, source_target_pairs={{0,8},{1,9},{2,10},{3,11},{4,12},{5,13},{6,14},{7,15},{8,0},{9,1},... | collective-permute-start | bytes 786440 | tf_op jit(solution)/shard_map/ppermute | solution.py:45
  303.1 12.8 %collective-permute-start.79 = (bf16[128,1024]{1,0:T(8,128)(2,1)S(1)}, bf16[128,1024]{1,0:T(8,128)(2,1)S(1)}, u32[]{:S(2)}, u32[]{:S(2)}) collective-permute-start(bf16[128,1024]{1,0:T(8,128)(2,1)S(1)} %pad_maximum_fusion.24), channel_id=1, source_target_pairs={{0,4},{1,5},{2,6},{3,7},{4,0},{5,1},{6,2},{7,3},{8,12},{9,13},{10,... | collective-permute-start | bytes 786440 | tf_op jit(solution)/shard_map/ppermute | solution.py:45
  303.2 12.7 %collective-permute-start.78 = (bf16[128,1024]{1,0:T(8,128)(2,1)S(1)}, bf16[128,1024]{1,0:T(8,128)(2,1)S(1)}, u32[]{:S(2)}, u32[]{:S(2)}) collective-permute-start(bf16[128,1024]{1,0:T(8,128)(2,1)S(1)} %pad_maximum_fusion.23), channel_id=1, source_target_pairs={{0,2},{1,3},{2,0},{3,1},{4,6},{5,7},{6,4},{7,5},{8,10},{9,11},{10,... | collective-permute-start | bytes 786440 | tf_op jit(solution)/shard_map/ppermute | solution.py:45
  311.8 20.5 %collective-permute-start.86 = (bf16[128,1024]{1,0:T(8,128)(2,1)S(1)}, bf16[128,1024]{1,0:T(8,128)(2,1)S(1)}, u32[]{:S(2)}, u32[]{:S(2)}) collective-permute-start(bf16[128,1024]{1,0:T(8,128)(2,1)S(1)} %fusion.38), channel_id=1, source_target_pairs={{0,0},{16,1},{1,2},{17,3},{2,4},{18,5},{3,6},{19,7},{4,8},{20,9},{... | collective-permute-start | bytes 786440 | tf_op jit(solution)/shard_map/ppermute | solution.py:454
  316.3 20.5 %collective-permute-start.83 = (bf16[32,1024]{1,0:T(8,128)(2,1)S(1)}, bf16[32,1024]{1,0:T(8,128)(2,1)S(1)}, u32[]{:S(2)}, u32[]{:S(2)}) collective-permute-start(bf16[32,1024]{1,0:T(8,128)(2,1)S(1)} %get-tuple-element.203), channel_id=1, source_target_pairs={{16,0},{9,1},{2,2},{26,3},{19,4},{12,5},{5,6},{29,7},{22,8},{15,9}... | collective-permute-start | bytes 196616 | tf_op jit(solution)/shard_map/ppermute | solution.py:473
  317.1 19.7 %collective-permute-start.82 = (bf16[32,1024]{1,0:T(8,128)(2,1)S(1)}, bf16[32,1024]{1,0:T(8,128)(2,1)S(1)}, u32[]{:S(2)}, u32[]{:S(2)}) collective-permute-start(bf16[32,1024]{1,0:T(8,128)(2,1)S(1)} %get-tuple-element.202), channel_id=1, source_target_pairs={{8,0},{1,1},{25,2},{18,3},{11,4},{4,5},{28,6},{21,7},{14,8},{7,9},... | collective-permute-start | bytes 196616 | tf_op jit(solution)/shard_map/ppermute | solution.py:473
  323.8 13.1 %collective-permute-start.81 = (bf16[32,1024]{1,0:T(8,128)(2,1)S(1)}, bf16[32,1024]{1,0:T(8,128)(2,1)S(1)}, u32[]{:S(2)}, u32[]{:S(2)}) collective-permute-start(bf16[32,1024]{1,0:T(8,128)(2,1)S(1)} %get-tuple-element.201), channel_id=1, source_target_pairs={{0,0},{24,1},{17,2},{10,3},{3,4},{27,5},{20,6},{13,7},{6,8},{30,9}... | collective-permute-start | bytes 196616 | tf_op jit(solution)/shard_map/ppermute | solution.py:473
  328.1 8.0 %collective-permute-start.84 = (bf16[32,1024]{1,0:T(8,128)(2,1)S(1)}, bf16[32,1024]{1,0:T(8,128)(2,1)S(1)}, u32[]{:S(2)}, u32[]{:S(2)}) collective-permute-start(bf16[32,1024]{1,0:T(8,128)(2,1)S(1)} %get-tuple-element.200), channel_id=1, source_target_pairs={{0,0},{8,1},{16,2},{24,3},{1,4},{9,5},{17,6},{25,7},{2,8},{10,9},{... | collective-permute-start | bytes 196616 | tf_op jit(solution)/shard_map/ppermute | solution.py:471
  (70 other events, 548.4 us)

commit v6 on v5

--- a/solution.py
+++ b/solution.py
@@ -414,7 +414,7 @@
 
     in_terms = in_terms + after(in_got, grad_got).astype(F32)
     in_pairs = in_terms.reshape((n_far // 2, 2) + in_terms.shape[1:])
-    half_rows = 3 * in_rows // 4
+    half_rows = 7 * in_rows // 8
     in_low = swap_seq(in_pairs[:, 1, :half_rows].astype(BF16), 8, n_seq)
     grads = attend_back(where, mixed, grad_keep, grad_got)
     if n_parts > 1:

time: 339 us -> 337 us (level)
  waiting for transfers between devices: 147 us -> 143 us
  starting transfers between devices: 91.2 us -> 94.8 us
    ppermute x67, waiting for transfers between devices: 128 us -> 125 us  [swap_seq(): return lax.ppermute(value, 'seq', [(i, i ^ bits) for i in range(n_seq)])]
  transfers between devices with their start and end apart: 87 -> 87, of which waited for: 49 -> 49; matrix products, arithmetic and copies ran while one was open for 15% -> 14% of each run, Pallas kernels for 7% -> 7%
where the time goes in v6:
time: 337 us; the launch traced here: 336 us
  waiting for transfers between devices  143 us (42%)
  starting transfers between devices  94.8 us (28%)
  other arithmetic  33.4 us (10%)
  Pallas kernels  22.9 us (7%)
  local copies, waits for them, and re-layouts  19.2 us (6%)
  matrix products  17.7 us (5%)
  between operations  4.16 us (1%)
    ppermute x67, waiting for transfers between devices, swap_seq(): return lax.ppermute(value, 'seq', [(i, i ^ bits) for i in range(n_seq)])  125 us
    ppermute x67, starting transfers between devices, swap_seq(): return lax.ppermute(value, 'seq', [(i, i ^ bits) for i in range(n_seq)])  52.8 us
    ppermute x3, starting transfers between devices, shards(): lax.ppermute(jnp.where(thirds[t] == 0, terms[0], jnp.where(thirds[t] == 1...  13.6 us
    pallas_call x1, Pallas kernels, attend(): pl.pallas_call(attend_kernel, out_shape=(jax.ShapeDtypeStruct((rows_k, wi...  11.5 us
    pallas_call x1, Pallas kernels, attend_back(): pl.pallas_call(attend_back_kernel, out_shape=(jax.ShapeDtypeStruct((rows_...  11.4 us
    ppermute x10, starting transfers between devices, swap_dp(): return lax.ppermute(value, 'dp', [(0, 1), (1, 0)])  10.6 us
    ppermute x10, waiting for transfers between devices, swap_dp(): return lax.ppermute(value, 'dp', [(0, 1), (1, 0)])  9.48 us
    ppermute x3, starting transfers between devices, shards(): lax.ppermute(own_units[t], BOTH, [(i, home(3 * i + t)) for i in range(n_d...  6.96 us
  transfers between devices with their start and end apart: 87, of which 49 were waited for; matrix products, arithmetic and copies ran while one was open for 14% of the time, Pallas kernels for 7%

profile of v6, /device:TPU:2, one launch (start us, length us, event | category | flops | bytes accessed | tf_op | source)
XLA Modules:
  0.0 335.5 jit_solution(987904046013591151)
XLA Ops:
  0.7 1.8 fusion.33
  2.5 2.7 collective-permute-start
  6.1 2.6 collective-permute-start.1
  8.6 3.7 %collective-permute-start.2 = (bf16[32,1024]{1,0:T(8,128)(2,1)S(1)}, bf16[32,1024]{1,0:T(8,128)(2,1)S(1)}, u32[]{:S(2)}, u32[]{:S(2)}) collective-permute-start(bf16[32,1024]{1,0:T(8,128)(2,1)S(1)} %get-tuple-element.217), channel_id=1, source_target_pairs={{0,8},{1,1},{2,25},{3,18},{4,11},{5,4},{6,28},{7,21},{8,14},{9,7},... | collective-permute-start | bytes 196616 | tf_op jit(solution)/shard_map/ppermute | solution.py:320
  13.1 5.1 %collective-permute-start.4 = (bf16[32,1024]{1,0:T(8,128)(2,1)}, bf16[32,1024]{1,0:T(8,128)(2,1)S(1)}, u32[]{:S(2)}, u32[]{:S(2)}) collective-permute-start(bf16[32,1024]{1,0:T(8,128)(2,1)} %param.20), channel_id=1, source_target_pairs={{0,0},{1,8},{2,16},{3,24},{4,1},{5,9},{6,17},{7,25},{8,2},{9,10},{... | collective-permute-start | bytes 196616 | tf_op jit(solution)/shard_map/ppermute | solution.py:321
  18.3 6.2 %collective-permute-done.4 = bf16[32,1024]{1,0:T(8,128)(2,1)S(1)} collective-permute-done((bf16[32,1024]{1,0:T(8,128)(2,1)}, bf16[32,1024]{1,0:T(8,128)(2,1)S(1)}, u32[]{:S(2)}, u32[]{:S(2)}) %collective-permute-start.4) | collective-permute-done | bytes 65568 | tf_op jit(solution)/shard_map/ppermute | solution.py:321
  24.4 1.9 collective-permute-start.18
  27.9 2.7 collective-permute-start.6
  31.3 4.4 %collective-permute-start.13 = (bf16[4,32,1024]{2,1,0:T(8,128)(2,1)S(1)}, bf16[4,32,1024]{2,1,0:T(8,128)(2,1)S(1)}, u32[]{:S(2)}, u32[]{:S(2)}) collective-permute-start(bf16[4,32,1024]{2,1,0:T(8,128)(2,1)S(1)} %get-tuple-element.209), channel_id=1, source_target_pairs={{0,8},{1,9},{2,10},{3,11},{4,12},{5,13},{6,14},{7,15},{8,0},{9,1},... | collective-permute-start | bytes 786440 | tf_op jit(solution)/shard_map/ppermute | solution.py:45
  35.8 6.5 %collective-permute-done.6.refs_2_ = bf16[128,1024]{1,0:T(8,128)(2,1)} collective-permute-done((bf16[128,1024]{1,0:T(8,128)(2,1)S(1)}, bf16[128,1024]{1,0:T(8,128)(2,1)}, u32[]{:S(2)}, u32[]{:S(2)}) %collective-permute-start.6) | collective-permute-done | bytes 262176 | tf_op jit(solution)/shard_map/ppermute | solution.py:45
  45.8 2.8 collective-permute-start.14
  48.6 3.6 %collective-permute-done.13 = bf16[4,32,1024]{2,1,0:T(8,128)(2,1)S(1)} collective-permute-done((bf16[4,32,1024]{2,1,0:T(8,128)(2,1)S(1)}, bf16[4,32,1024]{2,1,0:T(8,128)(2,1)S(1)}, u32[]{:S(2)}, u32[]{:S(2)}) %collective-permute-start.13) | collective-permute-done | bytes 262176 | tf_op jit(solution)/shard_map/ppermute | solution.py:45
  55.6 4.6 %collective-permute-done.15 = bf16[4,32,1024]{2,1,0:T(8,128)(2,1)S(1)} collective-permute-done((bf16[4,32,1024]{2,1,0:T(8,128)(2,1)S(1)}, bf16[4,32,1024]{2,1,0:T(8,128)(2,1)S(1)}, u32[]{:S(2)}, u32[]{:S(2)}) %collective-permute-start.15) | collective-permute-done | bytes 262176 | tf_op jit(solution)/shard_map/ppermute | solution.py:49
  62.2 2.5 collective-permute-start.16
  66.9 11.5 %shard_map.152 = (bf16[1024,1024]{1,0:T(8,128)(2,1)}, bf16[1024,384]{1,0:T(8,128)(2,1)}, bf16[512,128]{1,0:T(8,128)(2,1)}, bf16[512,128]{1,0:T(8,128)(2,1)}) custom-call(s32[4]{0:T(128)} %pad_add_fusion.where_ref, bf16[128,1024]{1,0:T(8,128)(2,1)} %copy-done.18, bf16[128,1024]{1,0:T(8,128)(2,1)} %collective-permute-done.5.refs_1_, ...), custom_call_target="tpu_custom_call" | custom-call | flops 1342177280 | bytes 4194304 | tf_op jit(solution)/shard_map/pallas_call | solution.py:184
  78.5 11.9 %collective-permute-done.16 = bf16[256,1024]{1,0:T(8,128)(2,1)S(1)} collective-permute-done((bf16[256,1024]{1,0:T(8,128)(2,1)S(1)}, bf16[256,1024]{1,0:T(8,128)(2,1)S(1)}, u32[]{:S(2)}, u32[]{:S(2)}) %collective-permute-start.16) | collective-permute-done | bytes 524320 | tf_op jit(solution)/shard_map/ppermute | solution.py:45
  90.4 2.4 collective-permute-done.19
  94.1 2.6 collective-permute-done.20
  98.1 2.6 collective-permute-start.35
  100.7 3.7 %collective-permute-done.21 = bf16[64,1024]{1,0:T(8,128)(2,1)S(1)} collective-permute-done((bf16[64,1024]{1,0:T(8,128)(2,1)S(1)}, bf16[64,1024]{1,0:T(8,128)(2,1)S(1)}, u32[]{:S(2)}, u32[]{:S(2)}) %collective-permute-start.21) | collective-permute-done | bytes 131104 | tf_op jit(solution)/shard_map/ppermute | solution.py:45
  106.4 6.7 %collective-permute-done.35 = bf16[128,1024]{1,0:T(8,128)(2,1)S(1)} collective-permute-done((bf16[128,1024]{1,0:T(8,128)(2,1)}, bf16[128,1024]{1,0:T(8,128)(2,1)S(1)}, u32[]{:S(2)}, u32[]{:S(2)}) %collective-permute-start.35) | collective-permute-done | bytes 262176 | tf_op jit(solution)/shard_map/ppermute | solution.py:45
  114.1 2.0 collective-permute-done.24
  118.5 3.8 %collective-permute-done.36 = bf16[128,1024]{1,0:T(8,128)(2,1)S(1)} collective-permute-done((bf16[128,1024]{1,0:T(8,128)(2,1)S(1)}, bf16[128,1024]{1,0:T(8,128)(2,1)S(1)}, u32[]{:S(2)}, u32[]{:S(2)}) %collective-permute-start.36) | collective-permute-done | bytes 262176 | tf_op jit(solution)/shard_map/ppermute | solution.py:49
  123.9 1.8 collective-permute-start.28
  125.8 2.7 collective-permute-done.27
  131.5 2.4 fusion.60
  134.6 1.4 copy-done.7
  136.8 2.6 collective-permute-done.37
  142.8 4.0 %collective-permute-done.38 = bf16[64,1024]{1,0:T(8,128)(2,1)} collective-permute-done((bf16[64,1024]{1,0:T(8,128)(2,1)}, bf16[64,1024]{1,0:T(8,128)(2,1)}, u32[]{:S(2)}, u32[]{:S(2)}) %collective-permute-start.38) | collective-permute-done | bytes 131104 | tf_op jit(solution)/shard_map/ppermute | solution.py:45
  155.3 1.4 collective-permute-done.41
  156.7 1.5 collective-permute-done.39
  161.3 4.4 %collective-permute-done.43 = bf16[128,1024]{1,0:T(8,128)(2,1)S(1)} collective-permute-done((bf16[128,1024]{1,0:T(8,128)(2,1)S(1)}, bf16[128,1024]{1,0:T(8,128)(2,1)S(1)}, u32[]{:S(2)}, u32[]{:S(2)}) %collective-permute-start.43) | collective-permute-done | bytes 262176 | tf_op jit(solution)/shard_map/ppermute | solution.py:45
  165.7 1.4 collective-permute-start.44
  170.8 2.3 collective-permute-done.45
  173.3 1.4 collective-permute-done.49
  174.8 1.9 multiply_convert_fusion
  180.6 2.3 fusion.78
  194.3 4.4 %collective-permute-done.54 = bf16[128,1024]{1,0:T(8,128)(2,1)S(1)} collective-permute-done((bf16[128,1024]{1,0:T(8,128)(2,1)S(1)}, bf16[128,1024]{1,0:T(8,128)(2,1)S(1)}, u32[]{:S(2)}, u32[]{:S(2)}) %collective-permute-start.54) | collective-permute-done | bytes 262176 | tf_op jit(solution)/shard_map/ppermute | solution.py:45
  201.7 1.4 collective-permute-start.56
  203.1 1.7 slice_select_fusion
  204.9 3.2 collective-permute-done.56
  210.4 2.7 collective-permute-done.57
  217.3 1.7 collective-permute-start.63
  219.9 1.4 collective-permute-start.66
  221.6 5.0 %collective-permute-done.63.got_ref = bf16[512,128]{1,0:T(8,128)(2,1)S(1)} collective-permute-done((bf16[512,128]{1,0:T(8,128)(2,1)S(1)}, bf16[512,128]{1,0:T(8,128)(2,1)S(1)}, u32[]{:S(2)}, u32[]{:S(2)}) %collective-permute-start.63) | collective-permute-done | bytes 131104 | tf_op jit(solution)/shard_map/ppermute | solution.py:45
  227.2 2.2 add_bitcast_fusion
  232.8 11.4 %shard_map.153 = (bf16[1024,384]{1,0:T(8,128)(2,1)}, bf16[512,384]{1,0:T(8,128)(2,1)}, bf16[512,384]{1,0:T(8,128)(2,1)}) custom-call(s32[4]{0:T(128)} %pad_add_fusion.where_ref, bf16[1024,384]{1,0:T(8,128)(2,1)} %get-tuple-element.120.mixed_ref, bf16[512,128]{1,0:T(8,128)(2,1)} %bitcast.239, bf16[512,128]{1,0:T(8,128)(2,1)} %copy-done.42), custom_call_target="tpu_custom_call" | custom-call | flops 1342177280 | bytes 4194304 | tf_op jit(solution)/shard_map/pallas_call | solution.py:265
  244.2 9.7 %collective-permute-done.65 = bf16[1,224,1024]{2,1,0:T(8,128)(2,1)} collective-permute-done((bf16[1,224,1024]{2,1,0:T(8,128)(2,1)}, bf16[1,224,1024]{2,1,0:T(8,128)(2,1)}, u32[]{:S(2)}, u32[]{:S(2)}) %collective-permute-start.65) | collective-permute-done | bytes 458784 | tf_op jit(solution)/shard_map/ppermute | solution.py:45
  253.9 2.1 multiply_reduce_fusion
  262.2 2.7 collective-permute-done.69
  265.0 1.7 collective-permute-start.70
  267.4 4.3 %collective-permute-done.70 = f32[3,1024]{1,0:T(4,128)S(1)} collective-permute-done((f32[3,1024]{1,0:T(4,128)S(1)}, f32[3,1024]{1,0:T(4,128)S(1)}, u32[]{:S(2)}, u32[]{:S(2)}) %collective-permute-start.70) | collective-permute-done | bytes 12320 | tf_op jit(solution)/shard_map/ppermute | solution.py:45
  271.8 5.2 %collective-permute-done.72 = bf16[512,384]{1,0:T(8,128)(2,1)} collective-permute-done((bf16[512,384]{1,0:T(8,128)(2,1)}, bf16[512,384]{1,0:T(8,128)(2,1)}, u32[]{:S(2)}, u32[]{:S(2)}) %collective-permute-start.72) | collective-permute-done | bytes 393248 | tf_op jit(solution)/shard_map/ppermute | solution.py:45
  279.2 1.4 fusion.8
  280.7 2.8 collective-permute-start.80
  283.5 1.4 fusion.7
  287.1 2.4 collective-permute-start.85
  291.6 2.9 collective-permute-done.77
  296.6 11.3 %collective-permute-done.85 = bf16[1,128,1024]{2,1,0:T(8,128)(2,1)S(1)} collective-permute-done((bf16[1,128,1024]{2,1,0:T(8,128)(2,1)S(1)}, bf16[1,128,1024]{2,1,0:T(8,128)(2,1)S(1)}, u32[]{:S(2)}, u32[]{:S(2)}) %collective-permute-start.85) | collective-permute-done | bytes 262176 | tf_op jit(solution)/shard_map/ppermute | solution.py:45
  309.2 1.9 collective-permute-start.86
  313.5 8.4 %collective-permute-start.82 = (bf16[32,1024]{1,0:T(8,128)(2,1)S(1)}, bf16[32,1024]{1,0:T(8,128)(2,1)S(1)}, u32[]{:S(2)}, u32[]{:S(2)}) collective-permute-start(bf16[32,1024]{1,0:T(8,128)(2,1)S(1)} %get-tuple-element.202), channel_id=1, source_target_pairs={{8,0},{1,1},{25,2},{18,3},{11,4},{4,5},{28,6},{21,7},{14,8},{7,9},... | collective-permute-start | bytes 196616 | tf_op jit(solution)/shard_map/ppermute | solution.py:473
  321.9 4.4 %collective-permute-start.81 = (bf16[32,1024]{1,0:T(8,128)(2,1)S(1)}, bf16[32,1024]{1,0:T(8,128)(2,1)S(1)}, u32[]{:S(2)}, u32[]{:S(2)}) collective-permute-start(bf16[32,1024]{1,0:T(8,128)(2,1)S(1)} %get-tuple-element.201), channel_id=1, source_target_pairs={{0,0},{24,1},{17,2},{10,3},{3,4},{27,5},{20,6},{13,7},{6,8},{30,9}... | collective-permute-start | bytes 196616 | tf_op jit(solution)/shard_map/ppermute | solution.py:473
  326.3 1.9 collective-permute-start.84
  331.3 2.7 collective-permute-done.84
  (351 shorter events, 99.4 us)
Async XLA Ops:
  2.5 15.7 %collective-permute-start = (bf16[64,1024]{1,0:T(8,128)(2,1)S(1)}, bf16[64,1024]{1,0:T(8,128)(2,1)S(1)}, u32[]{:S(2)}, u32[]{:S(2)}) collective-permute-start(bf16[64,1024]{1,0:T(8,128)(2,1)S(1)} %get-tuple-element.211), channel_id=1, source_target_pairs={{0,8},{1,9},{2,10},{3,11},{4,12},{5,13},{6,14},{7,15},{8,0},{9,1},... | collective-permute-start | bytes 393224 | tf_op jit(solution)/shard_map/ppermute | solution.py:45
  6.1 12.1 %collective-permute-start.1 = (bf16[32,1024]{1,0:T(8,128)(2,1)S(1)}, bf16[32,1024]{1,0:T(8,128)(2,1)S(1)}, u32[]{:S(2)}, u32[]{:S(2)}) collective-permute-start(bf16[32,1024]{1,0:T(8,128)(2,1)S(1)} %get-tuple-element.216), channel_id=1, source_target_pairs={{0,0},{1,24},{2,17},{3,10},{4,3},{5,27},{6,20},{7,13},{8,6},{9,30}... | collective-permute-start | bytes 196616 | tf_op jit(solution)/shard_map/ppermute | solution.py:320
  8.6 9.6 %collective-permute-start.2 = (bf16[32,1024]{1,0:T(8,128)(2,1)S(1)}, bf16[32,1024]{1,0:T(8,128)(2,1)S(1)}, u32[]{:S(2)}, u32[]{:S(2)}) collective-permute-start(bf16[32,1024]{1,0:T(8,128)(2,1)S(1)} %get-tuple-element.217), channel_id=1, source_target_pairs={{0,8},{1,1},{2,25},{3,18},{4,11},{5,4},{6,28},{7,21},{8,14},{9,7},... | collective-permute-start | bytes 196616 | tf_op jit(solution)/shard_map/ppermute | solution.py:320
  12.4 5.9 %collective-permute-start.3 = (bf16[32,1024]{1,0:T(8,128)(2,1)S(1)}, bf16[32,1024]{1,0:T(8,128)(2,1)S(1)}, u32[]{:S(2)}, u32[]{:S(2)}) collective-permute-start(bf16[32,1024]{1,0:T(8,128)(2,1)S(1)} %get-tuple-element.215), channel_id=1, source_target_pairs={{0,16},{1,9},{2,2},{3,26},{4,19},{5,12},{6,5},{7,29},{8,22},{9,15}... | collective-permute-start | bytes 196616 | tf_op jit(solution)/shard_map/ppermute | solution.py:320
  13.1 11.4 %collective-permute-start.4 = (bf16[32,1024]{1,0:T(8,128)(2,1)}, bf16[32,1024]{1,0:T(8,128)(2,1)S(1)}, u32[]{:S(2)}, u32[]{:S(2)}) collective-permute-start(bf16[32,1024]{1,0:T(8,128)(2,1)} %param.20), channel_id=1, source_target_pairs={{0,0},{1,8},{2,16},{3,24},{4,1},{5,9},{6,17},{7,25},{8,2},{9,10},{... | collective-permute-start | bytes 196616 | tf_op jit(solution)/shard_map/ppermute | solution.py:321
  24.4 6.2 %collective-permute-start.9 = (bf16[128,1024]{1,0:T(8,128)(2,1)S(1)}, bf16[128,1024]{1,0:T(8,128)(2,1)S(1)}, u32[]{:S(2)}, u32[]{:S(2)}) collective-permute-start(bf16[128,1024]{1,0:T(8,128)(2,1)S(1)} %pad_maximum_fusion.12.refs_0_), channel_id=1, source_target_pairs={{0,1},{1,0},{2,3},{3,2},{4,5},{5,4},{6,7},{7,6},{8,9},{9,8},{10,11... | collective-permute-start | bytes 786440 | tf_op jit(solution)/shard_map/ppermute | solution.py:45
  24.4 54.1 %collective-permute-start.18 = (bf16[128,1024]{1,0:T(8,128)(2,1)}, bf16[128,1024]{1,0:T(8,128)(2,1)}, u32[]{:S(2)}, u32[]{:S(2)}) collective-permute-start(bf16[128,1024]{1,0:T(8,128)(2,1)} %param.22), channel_id=1, source_target_pairs={{0,0},{1,16},{2,1},{3,17},{4,2},{5,18},{6,3},{7,19},{8,4},{9,20},{... | collective-permute-start | bytes 786440 | tf_op jit(solution)/shard_map/ppermute | solution.py:319
  27.0 16.4 %collective-permute-start.5 = (bf16[128,1024]{1,0:T(8,128)(2,1)S(1)}, bf16[128,1024]{1,0:T(8,128)(2,1)}, u32[]{:S(2)}, u32[]{:S(2)}) collective-permute-start(bf16[128,1024]{1,0:T(8,128)(2,1)S(1)} %pad_maximum_fusion.12.refs_0_), channel_id=1, source_target_pairs={{0,2},{1,3},{2,0},{3,1},{4,6},{5,7},{6,4},{7,5},{8,10},{9,11},{10,... | collective-permute-start | bytes 786440 | tf_op jit(solution)/shard_map/ppermute | solution.py:45
  27.9 14.4 %collective-permute-start.6 = (bf16[128,1024]{1,0:T(8,128)(2,1)S(1)}, bf16[128,1024]{1,0:T(8,128)(2,1)}, u32[]{:S(2)}, u32[]{:S(2)}) collective-permute-start(bf16[128,1024]{1,0:T(8,128)(2,1)S(1)} %pad_maximum_fusion.12.refs_0_), channel_id=1, source_target_pairs={{0,4},{1,5},{2,6},{3,7},{4,0},{5,1},{6,2},{7,3},{8,12},{9,13},{10,... | collective-permute-start | bytes 786440 | tf_op jit(solution)/shard_map/ppermute | solution.py:45
  31.3 20.8 %collective-permute-start.13 = (bf16[4,32,1024]{2,1,0:T(8,128)(2,1)S(1)}, bf16[4,32,1024]{2,1,0:T(8,128)(2,1)S(1)}, u32[]{:S(2)}, u32[]{:S(2)}) collective-permute-start(bf16[4,32,1024]{2,1,0:T(8,128)(2,1)S(1)} %get-tuple-element.209), channel_id=1, source_target_pairs={{0,8},{1,9},{2,10},{3,11},{4,12},{5,13},{6,14},{7,15},{8,0},{9,1},... | collective-permute-start | bytes 786440 | tf_op jit(solution)/shard_map/ppermute | solution.py:45
  44.3 9.3 %collective-permute-start.8 = (bf16[64,1024]{1,0:T(8,128)(2,1)S(1)}, bf16[64,1024]{1,0:T(8,128)(2,1)S(1)}, u32[]{:S(2)}, u32[]{:S(2)}) collective-permute-start(bf16[64,1024]{1,0:T(8,128)(2,1)S(1)} %slice.438), channel_id=1, source_target_pairs={{0,4},{1,5},{2,6},{3,7},{4,0},{5,1},{6,2},{7,3},{8,12},{9,13},{10,... | collective-permute-start | bytes 393224 | tf_op jit(solution)/shard_map/ppermute | solution.py:45
  45.8 9.3 %collective-permute-start.14 = (bf16[4,32,1024]{2,1,0:T(8,128)(2,1)S(1)}, bf16[4,32,1024]{2,1,0:T(8,128)(2,1)S(1)}, u32[]{:S(2)}, u32[]{:S(2)}) collective-permute-start(bf16[4,32,1024]{2,1,0:T(8,128)(2,1)S(1)} %get-tuple-element.209), channel_id=1, source_target_pairs={{0,16},{16,0},{1,17},{17,1},{2,18},{18,2},{3,19},{19,3},{4,20},{20... | collective-permute-start | bytes 786440 | tf_op jit(solution)/shard_map/ppermute | solution.py:49
  48.6 13.5 %collective-permute-start.10 = (bf16[128,1024]{1,0:T(8,128)(2,1)}, bf16[128,1024]{1,0:T(8,128)(2,1)}, u32[]{:S(2)}, u32[]{:S(2)}) collective-permute-start(bf16[128,1024]{1,0:T(8,128)(2,1)} %collective-permute-done.5.refs_1_), channel_id=1, source_target_pairs={{0,1},{1,0},{2,3},{3,2},{4,5},{5,4},{6,7},{7,6},{8,9},{9,8},{10,11... | collective-permute-start | bytes 786440 | tf_op jit(solution)/shard_map/ppermute | solution.py:45
  52.2 8.0 %collective-permute-start.15 = (bf16[4,32,1024]{2,1,0:T(8,128)(2,1)S(1)}, bf16[4,32,1024]{2,1,0:T(8,128)(2,1)S(1)}, u32[]{:S(2)}, u32[]{:S(2)}) collective-permute-start(bf16[4,32,1024]{2,1,0:T(8,128)(2,1)S(1)} %collective-permute-done.13), channel_id=1, source_target_pairs={{0,16},{16,0},{1,17},{17,1},{2,18},{18,2},{3,19},{19,3},{4,20},{20... | collective-permute-start | bytes 786440 | tf_op jit(solution)/shard_map/ppermute | solution.py:49
  53.7 8.4 %collective-permute-start.11 = (bf16[128,1024]{1,0:T(8,128)(2,1)}, bf16[128,1024]{1,0:T(8,128)(2,1)}, u32[]{:S(2)}, u32[]{:S(2)}) collective-permute-start(bf16[128,1024]{1,0:T(8,128)(2,1)} %collective-permute-done.6.refs_2_), channel_id=1, source_target_pairs={{0,1},{1,0},{2,3},{3,2},{4,5},{5,4},{6,7},{7,6},{8,9},{9,8},{10,11... | collective-permute-start | bytes 786440 | tf_op jit(solution)/shard_map/ppermute | solution.py:45
  55.0 7.1 %collective-permute-start.12 = (bf16[128,1024]{1,0:T(8,128)(2,1)}, bf16[128,1024]{1,0:T(8,128)(2,1)S(1)}, u32[]{:S(2)}, u32[]{:S(2)}) collective-permute-start(bf16[128,1024]{1,0:T(8,128)(2,1)} %constant_dynamic-update-slice_fusion.refs_3_), channel_id=1, source_target_pairs={{0,1},{1,0},{2,3},{3,2},{4,5},{5,4},{6,7},{7,6},{8,9},{9,8},{10,11... | collective-permute-start | bytes 786440 | tf_op jit(solution)/shard_map/ppermute | solution.py:45
  62.2 28.2 %collective-permute-start.16 = (bf16[256,1024]{1,0:T(8,128)(2,1)S(1)}, bf16[256,1024]{1,0:T(8,128)(2,1)S(1)}, u32[]{:S(2)}, u32[]{:S(2)}) collective-permute-start(bf16[256,1024]{1,0:T(8,128)(2,1)S(1)} %copy-done.32), channel_id=1, source_target_pairs={{0,8},{1,9},{2,10},{3,11},{4,12},{5,13},{6,14},{7,15},{8,0},{9,1},... | collective-permute-start | bytes 1572872 | tf_op jit(solution)/shard_map/ppermute | solution.py:45
  64.7 25.7 %collective-permute-start.17 = (bf16[256,1024]{1,0:T(8,128)(2,1)S(1)}, bf16[256,1024]{1,0:T(8,128)(2,1)S(1)}, u32[]{:S(2)}, u32[]{:S(2)}) collective-permute-start(bf16[256,1024]{1,0:T(8,128)(2,1)S(1)} %copy-done.32), channel_id=1, source_target_pairs={{0,16},{16,0},{1,17},{17,1},{2,18},{18,2},{3,19},{19,3},{4,20},{20... | collective-permute-start | bytes 1572872 | tf_op jit(solution)/shard_map/ppermute | solution.py:49
  78.4 14.3 %collective-permute-start.19 = (bf16[512,128]{1,0:T(8,128)(2,1)}, bf16[512,128]{1,0:T(8,128)(2,1)S(1)}, u32[]{:S(2)}, u32[]{:S(2)}) collective-permute-start(bf16[512,128]{1,0:T(8,128)(2,1)} %get-tuple-element.112), channel_id=1, source_target_pairs={{0,8},{1,9},{2,10},{3,11},{4,12},{5,13},{6,14},{7,15},{8,0},{9,1},... | collective-permute-start | bytes 393224 | tf_op jit(solution)/shard_map/ppermute | solution.py:45
  97.2 7.2 %collective-permute-start.21 = (bf16[64,1024]{1,0:T(8,128)(2,1)S(1)}, bf16[64,1024]{1,0:T(8,128)(2,1)S(1)}, u32[]{:S(2)}, u32[]{:S(2)}) collective-permute-start(bf16[64,1024]{1,0:T(8,128)(2,1)S(1)} %get-tuple-element.194), channel_id=1, source_target_pairs={{0,4},{1,5},{2,6},{3,7},{4,0},{5,1},{6,2},{7,3},{8,12},{9,13},{10,... | collective-permute-start | bytes 393224 | tf_op jit(solution)/shard_map/ppermute | solution.py:45
  97.3 7.1 %collective-permute-start.23 = (bf16[64,1024]{1,0:T(8,128)(2,1)S(1)}, bf16[64,1024]{1,0:T(8,128)(2,1)S(1)}, u32[]{:S(2)}, u32[]{:S(2)}) collective-permute-start(bf16[64,1024]{1,0:T(8,128)(2,1)S(1)} %get-tuple-element.193), channel_id=1, source_target_pairs={{0,2},{1,3},{2,0},{3,1},{4,6},{5,7},{6,4},{7,5},{8,10},{9,11},{10,... | collective-permute-start | bytes 393224 | tf_op jit(solution)/shard_map/ppermute | solution.py:45
  98.1 14.9 %collective-permute-start.35 = (bf16[128,1024]{1,0:T(8,128)(2,1)}, bf16[128,1024]{1,0:T(8,128)(2,1)S(1)}, u32[]{:S(2)}, u32[]{:S(2)}) collective-permute-start(bf16[128,1024]{1,0:T(8,128)(2,1)} %collective-permute-done.18), channel_id=1, source_target_pairs={{0,8},{1,9},{2,10},{3,11},{4,12},{5,13},{6,14},{7,15},{8,0},{9,1},... | collective-permute-start | bytes 786440 | tf_op jit(solution)/shard_map/ppermute | solution.py:45
  104.5 11.5 %collective-permute-start.24 = (bf16[128,1024]{1,0:T(8,128)(2,1)S(1)}, bf16[128,1024]{1,0:T(8,128)(2,1)S(1)}, u32[]{:S(2)}, u32[]{:S(2)}) collective-permute-start(bf16[128,1024]{1,0:T(8,128)(2,1)S(1)} %pad_maximum_fusion.15), channel_id=1, source_target_pairs={{0,4},{1,5},{2,6},{3,7},{4,0},{5,1},{6,2},{7,3},{8,12},{9,13},{10,... | collective-permute-start | bytes 786440 | tf_op jit(solution)/shard_map/ppermute | solution.py:45
  104.8 11.3 %collective-permute-start.22 = (bf16[128,1024]{1,0:T(8,128)(2,1)S(1)}, bf16[128,1024]{1,0:T(8,128)(2,1)S(1)}, u32[]{:S(2)}, u32[]{:S(2)}) collective-permute-start(bf16[128,1024]{1,0:T(8,128)(2,1)S(1)} %pad_maximum_fusion.14), channel_id=1, source_target_pairs={{0,2},{1,3},{2,0},{3,1},{4,6},{5,7},{6,4},{7,5},{8,10},{9,11},{10,... | collective-permute-start | bytes 786440 | tf_op jit(solution)/shard_map/ppermute | solution.py:45
  105.6 11.7 %collective-permute-start.34 = (bf16[128,1024]{1,0:T(8,128)(2,1)}, bf16[128,1024]{1,0:T(8,128)(2,1)S(1)}, u32[]{:S(2)}, u32[]{:S(2)}) collective-permute-start(bf16[128,1024]{1,0:T(8,128)(2,1)} %collective-permute-done.18), channel_id=1, source_target_pairs={{0,16},{16,0},{1,17},{17,1},{2,18},{18,2},{3,19},{19,3},{4,20},{20... | collective-permute-start | bytes 786440 | tf_op jit(solution)/shard_map/ppermute | solution.py:49
  113.1 9.2 %collective-permute-start.36 = (bf16[128,1024]{1,0:T(8,128)(2,1)S(1)}, bf16[128,1024]{1,0:T(8,128)(2,1)S(1)}, u32[]{:S(2)}, u32[]{:S(2)}) collective-permute-start(bf16[128,1024]{1,0:T(8,128)(2,1)S(1)} %collective-permute-done.35), channel_id=1, source_target_pairs={{0,16},{16,0},{1,17},{17,1},{2,18},{18,2},{3,19},{19,3},{4,20},{20... | collective-permute-start | bytes 786440 | tf_op jit(solution)/shard_map/ppermute | solution.py:49
  116.4 6.6 %collective-permute-start.26 = (bf16[128,1024]{1,0:T(8,128)(2,1)S(1)}, bf16[128,1024]{1,0:T(8,128)(2,1)S(1)}, u32[]{:S(2)}, u32[]{:S(2)}) collective-permute-start(bf16[128,1024]{1,0:T(8,128)(2,1)S(1)} %get-tuple-element.162), channel_id=1, source_target_pairs={{0,4},{1,5},{2,6},{3,7},{4,0},{5,1},{6,2},{7,3},{8,12},{9,13},{10,... | collective-permute-start | bytes 786440 | tf_op jit(solution)/shard_map/ppermute | solution.py:45
  116.5 7.5 %collective-permute-start.25 = (bf16[128,1024]{1,0:T(8,128)(2,1)S(1)}, bf16[128,1024]{1,0:T(8,128)(2,1)S(1)}, u32[]{:S(2)}, u32[]{:S(2)}) collective-permute-start(bf16[128,1024]{1,0:T(8,128)(2,1)S(1)} %get-tuple-element.162), channel_id=1, source_target_pairs={{0,2},{1,3},{2,0},{3,1},{4,6},{5,7},{6,4},{7,5},{8,10},{9,11},{10,... | collective-permute-start | bytes 786440 | tf_op jit(solution)/shard_map/ppermute | solution.py:45
  116.6 14.9 %collective-permute-start.33 = (bf16[256,1024]{1,0:T(8,128)(2,1)S(1)}, bf16[256,1024]{1,0:T(8,128)(2,1)S(1)}, u32[]{:S(2)}, u32[]{:S(2)}) collective-permute-start(bf16[256,1024]{1,0:T(8,128)(2,1)S(1)} %collective-permute-done.16), channel_id=1, source_target_pairs={{0,16},{16,0},{1,17},{17,1},{2,18},{18,2},{3,19},{19,3},{4,20},{20... | collective-permute-start | bytes 1572872 | tf_op jit(solution)/shard_map/ppermute | solution.py:49
  122.5 7.3 %collective-permute-start.29 = (bf16[128,1024]{1,0:T(8,128)(2,1)S(1)}, bf16[128,1024]{1,0:T(8,128)(2,1)S(1)}, u32[]{:S(2)}, u32[]{:S(2)}) collective-permute-start(bf16[128,1024]{1,0:T(8,128)(2,1)S(1)} %get-tuple-element.162), channel_id=1, source_target_pairs={{0,1},{1,0},{2,3},{3,2},{4,5},{5,4},{6,7},{7,6},{8,9},{9,8},{10,11... | collective-permute-start | bytes 786440 | tf_op jit(solution)/shard_map/ppermute | solution.py:45
  123.9 5.7 %collective-permute-start.28 = (bf16[64,1024]{1,0:T(8,128)(2,1)S(1)}, bf16[64,1024]{1,0:T(8,128)(2,1)S(1)}, u32[]{:S(2)}, u32[]{:S(2)}) collective-permute-start(bf16[64,1024]{1,0:T(8,128)(2,1)S(1)} %slice.452), channel_id=1, source_target_pairs={{0,4},{1,5},{2,6},{3,7},{4,0},{5,1},{6,2},{7,3},{8,12},{9,13},{10,... | collective-permute-start | bytes 393224 | tf_op jit(solution)/shard_map/ppermute | solution.py:45
  140.9 5.9 %collective-permute-start.38 = (bf16[64,1024]{1,0:T(8,128)(2,1)}, bf16[64,1024]{1,0:T(8,128)(2,1)}, u32[]{:S(2)}, u32[]{:S(2)}) collective-permute-start(bf16[64,1024]{1,0:T(8,128)(2,1)} %get-tuple-element.190), channel_id=1, source_target_pairs={{0,4},{1,5},{2,6},{3,7},{4,0},{5,1},{6,2},{7,3},{8,12},{9,13},{10,... | collective-permute-start | bytes 393224 | tf_op jit(solution)/shard_map/ppermute | solution.py:45
  141.8 5.6 %collective-permute-start.40 = (bf16[64,1024]{1,0:T(8,128)(2,1)}, bf16[64,1024]{1,0:T(8,128)(2,1)}, u32[]{:S(2)}, u32[]{:S(2)}) collective-permute-start(bf16[64,1024]{1,0:T(8,128)(2,1)} %get-tuple-element.189), channel_id=1, source_target_pairs={{0,2},{1,3},{2,0},{3,1},{4,6},{5,7},{6,4},{7,5},{8,10},{9,11},{10,... | collective-permute-start | bytes 393224 | tf_op jit(solution)/shard_map/ppermute | solution.py:45
  149.2 7.5 %collective-permute-start.41 = (bf16[128,1024]{1,0:T(8,128)(2,1)}, bf16[128,1024]{1,0:T(8,128)(2,1)}, u32[]{:S(2)}, u32[]{:S(2)}) collective-permute-start(bf16[128,1024]{1,0:T(8,128)(2,1)} %pad_maximum_fusion.18), channel_id=1, source_target_pairs={{0,4},{1,5},{2,6},{3,7},{4,0},{5,1},{6,2},{7,3},{8,12},{9,13},{10,... | collective-permute-start | bytes 786440 | tf_op jit(solution)/shard_map/ppermute | solution.py:45
  151.0 7.1 %collective-permute-start.39 = (bf16[128,1024]{1,0:T(8,128)(2,1)}, bf16[128,1024]{1,0:T(8,128)(2,1)S(1)}, u32[]{:S(2)}, u32[]{:S(2)}) collective-permute-start(bf16[128,1024]{1,0:T(8,128)(2,1)} %pad_maximum_fusion.17), channel_id=1, source_target_pairs={{0,2},{1,3},{2,0},{3,1},{4,6},{5,7},{6,4},{7,5},{8,10},{9,11},{10,... | collective-permute-start | bytes 786440 | tf_op jit(solution)/shard_map/ppermute | solution.py:45
  159.3 6.4 %collective-permute-start.43 = (bf16[128,1024]{1,0:T(8,128)(2,1)S(1)}, bf16[128,1024]{1,0:T(8,128)(2,1)S(1)}, u32[]{:S(2)}, u32[]{:S(2)}) collective-permute-start(bf16[128,1024]{1,0:T(8,128)(2,1)S(1)} %get-tuple-element.157), channel_id=1, source_target_pairs={{0,4},{1,5},{2,6},{3,7},{4,0},{5,1},{6,2},{7,3},{8,12},{9,13},{10,... | collective-permute-start | bytes 786440 | tf_op jit(solution)/shard_map/ppermute | solution.py:45
  160.2 7.8 %collective-permute-start.42 = (bf16[128,1024]{1,0:T(8,128)(2,1)S(1)}, bf16[128,1024]{1,0:T(8,128)(2,1)S(1)}, u32[]{:S(2)}, u32[]{:S(2)}) collective-permute-start(bf16[128,1024]{1,0:T(8,128)(2,1)S(1)} %get-tuple-element.157), channel_id=1, source_target_pairs={{0,2},{1,3},{2,0},{3,1},{4,6},{5,7},{6,4},{7,5},{8,10},{9,11},{10,... | collective-permute-start | bytes 786440 | tf_op jit(solution)/shard_map/ppermute | solution.py:45
  161.2 12.0 %collective-permute-start.46 = (bf16[128,1024]{1,0:T(8,128)(2,1)S(1)}, bf16[128,1024]{1,0:T(8,128)(2,1)S(1)}, u32[]{:S(2)}, u32[]{:S(2)}) collective-permute-start(bf16[128,1024]{1,0:T(8,128)(2,1)S(1)} %get-tuple-element.157), channel_id=1, source_target_pairs={{0,1},{1,0},{2,3},{3,2},{4,5},{5,4},{6,7},{7,6},{8,9},{9,8},{10,11... | collective-permute-start | bytes 786440 | tf_op jit(solution)/shard_map/ppermute | solution.py:45
  184.4 5.8 %collective-permute-start.51 = (bf16[64,1024]{1,0:T(8,128)(2,1)S(1)}, bf16[64,1024]{1,0:T(8,128)(2,1)S(1)}, u32[]{:S(2)}, u32[]{:S(2)}) collective-permute-start(bf16[64,1024]{1,0:T(8,128)(2,1)S(1)} %get-tuple-element.186), channel_id=1, source_target_pairs={{0,4},{1,5},{2,6},{3,7},{4,0},{5,1},{6,2},{7,3},{8,12},{9,13},{10,... | collective-permute-start | bytes 393224 | tf_op jit(solution)/shard_map/ppermute | solution.py:45
  188.0 33.5 %collective-permute-start.64 = (bf16[2,256,1024]{2,1,0:T(8,128)(2,1)}, bf16[2,256,1024]{2,1,0:T(8,128)(2,1)}, u32[]{:S(2)}, u32[]{:S(2)}) collective-permute-start(bf16[2,256,1024]{2,1,0:T(8,128)(2,1)} %bitcast.41), channel_id=1, source_target_pairs={{0,16},{16,0},{1,17},{17,1},{2,18},{18,2},{3,19},{19,3},{4,20},{20... | collective-permute-start | bytes 3145736 | tf_op jit(solution)/shard_map/ppermute | solution.py:49
  191.2 7.5 %collective-permute-start.54 = (bf16[128,1024]{1,0:T(8,128)(2,1)S(1)}, bf16[128,1024]{1,0:T(8,128)(2,1)S(1)}, u32[]{:S(2)}, u32[]{:S(2)}) collective-permute-start(bf16[128,1024]{1,0:T(8,128)(2,1)S(1)} %pad_maximum_fusion.21), channel_id=1, source_target_pairs={{0,4},{1,5},{2,6},{3,7},{4,0},{5,1},{6,2},{7,3},{8,12},{9,13},{10,... | collective-permute-start | bytes 786440 | tf_op jit(solution)/shard_map/ppermute | solution.py:45
  192.2 7.2 %collective-permute-start.52 = (bf16[128,1024]{1,0:T(8,128)(2,1)S(1)}, bf16[128,1024]{1,0:T(8,128)(2,1)S(1)}, u32[]{:S(2)}, u32[]{:S(2)}) collective-permute-start(bf16[128,1024]{1,0:T(8,128)(2,1)S(1)} %pad_maximum_fusion.20), channel_id=1, source_target_pairs={{0,2},{1,3},{2,0},{3,1},{4,6},{5,7},{6,4},{7,5},{8,10},{9,11},{10,... | collective-permute-start | bytes 786440 | tf_op jit(solution)/shard_map/ppermute | solution.py:45
  200.6 8.5 %collective-permute-start.55 = (bf16[128,1024]{1,0:T(8,128)(2,1)S(1)}, bf16[128,1024]{1,0:T(8,128)(2,1)S(1)}, u32[]{:S(2)}, u32[]{:S(2)}) collective-permute-start(bf16[128,1024]{1,0:T(8,128)(2,1)S(1)} %get-tuple-element.156), channel_id=1, source_target_pairs={{0,2},{1,3},{2,0},{3,1},{4,6},{5,7},{6,4},{7,5},{8,10},{9,11},{10,... | collective-permute-start | bytes 786440 | tf_op jit(solution)/shard_map/ppermute | solution.py:45
  201.7 6.4 %collective-permute-start.56 = (bf16[128,1024]{1,0:T(8,128)(2,1)S(1)}, bf16[128,1024]{1,0:T(8,128)(2,1)S(1)}, u32[]{:S(2)}, u32[]{:S(2)}) collective-permute-start(bf16[128,1024]{1,0:T(8,128)(2,1)S(1)} %get-tuple-element.156), channel_id=1, source_target_pairs={{0,4},{1,5},{2,6},{3,7},{4,0},{5,1},{6,2},{7,3},{8,12},{9,13},{10,... | collective-permute-start | bytes 786440 | tf_op jit(solution)/shard_map/ppermute | solution.py:45
  204.8 9.5 %collective-permute-start.59 = (bf16[128,1024]{1,0:T(8,128)(2,1)S(1)}, bf16[128,1024]{1,0:T(8,128)(2,1)S(1)}, u32[]{:S(2)}, u32[]{:S(2)}) collective-permute-start(bf16[128,1024]{1,0:T(8,128)(2,1)S(1)} %get-tuple-element.156), channel_id=1, source_target_pairs={{0,1},{1,0},{2,3},{3,2},{4,5},{5,4},{6,7},{7,6},{8,9},{9,8},{10,11... | collective-permute-start | bytes 786440 | tf_op jit(solution)/shard_map/ppermute | solution.py:45
  217.3 9.2 %collective-permute-start.63 = (bf16[512,128]{1,0:T(8,128)(2,1)S(1)}, bf16[512,128]{1,0:T(8,128)(2,1)S(1)}, u32[]{:S(2)}, u32[]{:S(2)}) collective-permute-start(bf16[512,128]{1,0:T(8,128)(2,1)S(1)} %bitcast.240), channel_id=1, source_target_pairs={{0,8},{1,9},{2,10},{3,11},{4,12},{5,13},{6,14},{7,15},{8,0},{9,1},... | collective-permute-start | bytes 393224 | tf_op jit(solution)/shard_map/ppermute | solution.py:45
  219.9 24.3 %collective-permute-start.66 = (bf16[2,128,1024]{2,1,0:T(8,128)(2,1)}, bf16[2,128,1024]{2,1,0:T(8,128)(2,1)}, u32[]{:S(2)}, u32[]{:S(2)}) collective-permute-start(bf16[2,128,1024]{2,1,0:T(8,128)(2,1)} %fusion.10), channel_id=1, source_target_pairs={{0,16},{16,0},{1,17},{17,1},{2,18},{18,2},{3,19},{19,3},{4,20},{20... | collective-permute-start | bytes 1572872 | tf_op jit(solution)/shard_map/ppermute | solution.py:49
  231.6 22.3 %collective-permute-start.65 = (bf16[1,224,1024]{2,1,0:T(8,128)(2,1)}, bf16[1,224,1024]{2,1,0:T(8,128)(2,1)}, u32[]{:S(2)}, u32[]{:S(2)}) collective-permute-start(bf16[1,224,1024]{2,1,0:T(8,128)(2,1)} %fusion.34), channel_id=1, source_target_pairs={{0,8},{1,9},{2,10},{3,11},{4,12},{5,13},{6,14},{7,15},{8,0},{9,1},... | collective-permute-start | bytes 1376264 | tf_op jit(solution)/shard_map/ppermute | solution.py:45
  256.1 20.8 %collective-permute-start.72 = (bf16[512,384]{1,0:T(8,128)(2,1)}, bf16[512,384]{1,0:T(8,128)(2,1)}, u32[]{:S(2)}, u32[]{:S(2)}) collective-permute-start(bf16[512,384]{1,0:T(8,128)(2,1)} %get-tuple-element.135), channel_id=1, source_target_pairs={{0,8},{1,9},{2,10},{3,11},{4,12},{5,13},{6,14},{7,15},{8,0},{9,1},... | collective-permute-start | bytes 1179656 | tf_op jit(solution)/shard_map/ppermute | solution.py:45
  259.4 17.5 %collective-permute-start.73 = (bf16[4,2,32,1024]{3,2,0,1:T(8,128)(2,1)}, bf16[4,2,32,1024]{3,2,0,1:T(8,128)(2,1)}, u32[]{:S(2)}, u32[]{:S(2)}) collective-permute-start(bf16[4,2,32,1024]{3,2,0,1:T(8,128)(2,1)} %fusion.11), channel_id=1, source_target_pairs={{0,16},{16,0},{1,17},{17,1},{2,18},{18,2},{3,19},{19,3},{4,20},{20... | collective-permute-start | bytes 1572872 | tf_op jit(solution)/shard_map/ppermute | solution.py:49
  265.0 6.8 %collective-permute-start.70 = (f32[3,1024]{1,0:T(4,128)S(1)}, f32[3,1024]{1,0:T(4,128)S(1)}, u32[]{:S(2)}, u32[]{:S(2)}) collective-permute-start(f32[3,1024]{1,0:T(4,128)S(1)} %add.206), channel_id=1, source_target_pairs={{0,4},{1,5},{2,6},{3,7},{4,0},{5,1},{6,2},{7,3},{8,12},{9,13},{10,... | collective-permute-start | bytes 36872 | tf_op jit(solution)/shard_map/ppermute | solution.py:45
  271.8 36.2 %collective-permute-start.71 = (f32[3,1024]{1,0:T(4,128)S(1)}, f32[3,1024]{1,0:T(4,128)S(1)}, u32[]{:S(2)}, u32[]{:S(2)}) collective-permute-start(f32[3,1024]{1,0:T(4,128)S(1)} %add.207), channel_id=1, source_target_pairs={{0,8},{1,9},{2,10},{3,11},{4,12},{5,13},{6,14},{7,15},{8,0},{9,1},... | collective-permute-start | bytes 36872 | tf_op jit(solution)/shard_map/ppermute | solution.py:45
  279.0 6.3 %collective-permute-start.74 = (bf16[512,1024]{1,0:T(8,128)(2,1)S(1)}, bf16[512,1024]{1,0:T(8,128)(2,1)S(1)}, u32[]{:S(2)}, u32[]{:S(2)}) collective-permute-start(bf16[512,1024]{1,0:T(8,128)(2,1)S(1)} %convolution_convert_fusion.1), channel_id=1, source_target_pairs={{0,1},{1,0},{2,3},{3,2},{4,5},{5,4},{6,7},{7,6},{8,9},{9,8},{10,11... | collective-permute-start | bytes 3145736 | tf_op jit(solution)/shard_map/ppermute | solution.py:45
  279.1 6.2 %collective-permute-start.75 = (bf16[1,32,1024]{2,1,0:T(8,128)(2,1)S(1)}, bf16[1,32,1024]{2,1,0:T(8,128)(2,1)S(1)}, u32[]{:S(2)}, u32[]{:S(2)}) collective-permute-start(bf16[1,32,1024]{2,1,0:T(8,128)(2,1)S(1)} %fusion.50), channel_id=1, source_target_pairs={{0,8},{1,9},{2,10},{3,11},{4,12},{5,13},{6,14},{7,15},{8,0},{9,1},... | collective-permute-start | bytes 196616 | tf_op jit(solution)/shard_map/ppermute | solution.py:45
  280.7 31.9 %collective-permute-start.80 = (bf16[4,1,32,1024]{3,2,1,0:T(8,128)(2,1)S(1)}, bf16[4,1,32,1024]{3,2,1,0:T(8,128)(2,1)S(1)}, u32[]{:S(2)}, u32[]{:S(2)}) collective-permute-start(bf16[4,1,32,1024]{3,2,1,0:T(8,128)(2,1)S(1)} %fusion.37), channel_id=1, source_target_pairs={{0,8},{1,9},{2,10},{3,11},{4,12},{5,13},{6,14},{7,15},{8,0},{9,1},... | collective-permute-start | bytes 786440 | tf_op jit(solution)/shard_map/ppermute | solution.py:45
  287.1 7.4 %collective-permute-start.77 = (bf16[64,1024]{1,0:T(8,128)(2,1)S(1)}, bf16[64,1024]{1,0:T(8,128)(2,1)S(1)}, u32[]{:S(2)}, u32[]{:S(2)}) collective-permute-start(bf16[64,1024]{1,0:T(8,128)(2,1)S(1)} %get-tuple-element.181), channel_id=1, source_target_pairs={{0,4},{1,5},{2,6},{3,7},{4,0},{5,1},{6,2},{7,3},{8,12},{9,13},{10,... | collective-permute-start | bytes 393224 | tf_op jit(solution)/shard_map/ppermute | solution.py:45
  287.1 20.8 %collective-permute-start.85 = (bf16[1,128,1024]{2,1,0:T(8,128)(2,1)S(1)}, bf16[1,128,1024]{2,1,0:T(8,128)(2,1)S(1)}, u32[]{:S(2)}, u32[]{:S(2)}) collective-permute-start(bf16[1,128,1024]{2,1,0:T(8,128)(2,1)S(1)} %fusion.39), channel_id=1, source_target_pairs={{0,8},{1,9},{2,10},{3,11},{4,12},{5,13},{6,14},{7,15},{8,0},{9,1},... | collective-permute-start | bytes 786440 | tf_op jit(solution)/shard_map/ppermute | solution.py:45
  294.6 17.7 %collective-permute-start.79 = (bf16[128,1024]{1,0:T(8,128)(2,1)S(1)}, bf16[128,1024]{1,0:T(8,128)(2,1)S(1)}, u32[]{:S(2)}, u32[]{:S(2)}) collective-permute-start(bf16[128,1024]{1,0:T(8,128)(2,1)S(1)} %pad_maximum_fusion.24), channel_id=1, source_target_pairs={{0,4},{1,5},{2,6},{3,7},{4,0},{5,1},{6,2},{7,3},{8,12},{9,13},{10,... | collective-permute-start | bytes 786440 | tf_op jit(solution)/shard_map/ppermute | solution.py:45
  295.7 16.6 %collective-permute-start.78 = (bf16[128,1024]{1,0:T(8,128)(2,1)S(1)}, bf16[128,1024]{1,0:T(8,128)(2,1)S(1)}, u32[]{:S(2)}, u32[]{:S(2)}) collective-permute-start(bf16[128,1024]{1,0:T(8,128)(2,1)S(1)} %pad_maximum_fusion.23), channel_id=1, source_target_pairs={{0,2},{1,3},{2,0},{3,1},{4,6},{5,7},{6,4},{7,5},{8,10},{9,11},{10,... | collective-permute-start | bytes 786440 | tf_op jit(solution)/shard_map/ppermute | solution.py:45
  309.2 21.3 %collective-permute-start.86 = (bf16[128,1024]{1,0:T(8,128)(2,1)S(1)}, bf16[128,1024]{1,0:T(8,128)(2,1)S(1)}, u32[]{:S(2)}, u32[]{:S(2)}) collective-permute-start(bf16[128,1024]{1,0:T(8,128)(2,1)S(1)} %fusion.38), channel_id=1, source_target_pairs={{0,0},{16,1},{1,2},{17,3},{2,4},{18,5},{3,6},{19,7},{4,8},{20,9},{... | collective-permute-start | bytes 786440 | tf_op jit(solution)/shard_map/ppermute | solution.py:454
  312.7 22.0 %collective-permute-start.83 = (bf16[32,1024]{1,0:T(8,128)(2,1)S(1)}, bf16[32,1024]{1,0:T(8,128)(2,1)S(1)}, u32[]{:S(2)}, u32[]{:S(2)}) collective-permute-start(bf16[32,1024]{1,0:T(8,128)(2,1)S(1)} %get-tuple-element.203), channel_id=1, source_target_pairs={{16,0},{9,1},{2,2},{26,3},{19,4},{12,5},{5,6},{29,7},{22,8},{15,9}... | collective-permute-start | bytes 196616 | tf_op jit(solution)/shard_map/ppermute | solution.py:473
  313.5 21.2 %collective-permute-start.82 = (bf16[32,1024]{1,0:T(8,128)(2,1)S(1)}, bf16[32,1024]{1,0:T(8,128)(2,1)S(1)}, u32[]{:S(2)}, u32[]{:S(2)}) collective-permute-start(bf16[32,1024]{1,0:T(8,128)(2,1)S(1)} %get-tuple-element.202), channel_id=1, source_target_pairs={{8,0},{1,1},{25,2},{18,3},{11,4},{4,5},{28,6},{21,7},{14,8},{7,9},... | collective-permute-start | bytes 196616 | tf_op jit(solution)/shard_map/ppermute | solution.py:473
  321.9 12.8 %collective-permute-start.81 = (bf16[32,1024]{1,0:T(8,128)(2,1)S(1)}, bf16[32,1024]{1,0:T(8,128)(2,1)S(1)}, u32[]{:S(2)}, u32[]{:S(2)}) collective-permute-start(bf16[32,1024]{1,0:T(8,128)(2,1)S(1)} %get-tuple-element.201), channel_id=1, source_target_pairs={{0,0},{24,1},{17,2},{10,3},{3,4},{27,5},{20,6},{13,7},{6,8},{30,9}... | collective-permute-start | bytes 196616 | tf_op jit(solution)/shard_map/ppermute | solution.py:473
  326.3 7.8 %collective-permute-start.84 = (bf16[32,1024]{1,0:T(8,128)(2,1)S(1)}, bf16[32,1024]{1,0:T(8,128)(2,1)S(1)}, u32[]{:S(2)}, u32[]{:S(2)}) collective-permute-start(bf16[32,1024]{1,0:T(8,128)(2,1)S(1)} %get-tuple-element.200), channel_id=1, source_target_pairs={{0,0},{8,1},{16,2},{24,3},{1,4},{9,5},{17,6},{25,7},{2,8},{10,9},{... | collective-permute-start | bytes 196616 | tf_op jit(solution)/shard_map/ppermute | solution.py:471
  (66 other events, 545.9 us)

commit v7 on v6

--- a/solution.py
+++ b/solution.py
@@ -464,7 +464,7 @@
         on = (seq // bits) % 2
         pairs = terms.reshape((terms.shape[0], terms.shape[1] // 2, 2) + terms.shape[2:])
         give = jnp.where(on == 0, pairs[:, :, 1], pairs[:, :, 0]).astype(BF16)
-        got = after(swap_seq(give, bits, n_seq), grad_first)
+        got = after(swap_seq(give, bits, n_seq), last)
         terms = jnp.where(on == 0, pairs[:, :, 0], pairs[:, :, 1]) + got.astype(F32)
         bits *= 2
     terms = terms[:, 0].astype(BF16)

time: 337 us -> 336 us (level)
  starting transfers between devices: 94.8 us -> 91 us
    ppermute x3, starting transfers between devices: 13.6 us -> 9.73 us  [shards(): lax.ppermute(jnp.where(thirds[t] == 0, terms[0], jnp.where(thirds[t] == 1...]
  transfers between devices with their start and end apart: 87 -> 87, of which waited for: 49 -> 51; matrix products, arithmetic and copies ran while one was open for 14% -> 14% of each run, Pallas kernels for 7% -> 7%
where the time goes in v7:
time: 336 us; the launch traced here: 332 us
  waiting for transfers between devices  143 us (43%)
  starting transfers between devices  91 us (27%)
  other arithmetic  33.4 us (10%)
  Pallas kernels  22.9 us (7%)
  local copies, waits for them, and re-layouts  19.2 us (6%)
  matrix products  17.7 us (5%)
  between operations  4.16 us (1%)
    ppermute x67, waiting for transfers between devices, swap_seq(): return lax.ppermute(value, 'seq', [(i, i ^ bits) for i in range(n_seq)])  124 us
    ppermute x67, starting transfers between devices, swap_seq(): return lax.ppermute(value, 'seq', [(i, i ^ bits) for i in range(n_seq)])  52.8 us
    pallas_call x1, Pallas kernels, attend(): pl.pallas_call(attend_kernel, out_shape=(jax.ShapeDtypeStruct((rows_k, wi...  11.5 us
    pallas_call x1, Pallas kernels, attend_back(): pl.pallas_call(attend_back_kernel, out_shape=(jax.ShapeDtypeStruct((rows_...  11.4 us
    ppermute x10, starting transfers between devices, swap_dp(): return lax.ppermute(value, 'dp', [(0, 1), (1, 0)])  10.6 us
    ppermute x3, starting transfers between devices, shards(): lax.ppermute(jnp.where(thirds[t] == 0, terms[0], jnp.where(thirds[t] == 1...  9.73 us
    ppermute x10, waiting for transfers between devices, swap_dp(): return lax.ppermute(value, 'dp', [(0, 1), (1, 0)])  9.48 us
    ppermute x3, starting transfers between devices, shards(): lax.ppermute(own_units[t], BOTH, [(i, home(3 * i + t)) for i in range(n_d...  6.96 us
  transfers between devices with their start and end apart: 87, of which 51 were waited for; matrix products, arithmetic and copies ran while one was open for 14% of the time, Pallas kernels for 7%

profile of v7, /device:TPU:2, one launch (start us, length us, event | category | flops | bytes accessed | tf_op | source)
XLA Modules:
  0.0 331.6 jit_solution(13656840155331965888)
XLA Ops:
  0.7 1.8 fusion.33
  2.5 2.7 collective-permute-start
  6.1 2.6 collective-permute-start.1
  8.6 3.7 %collective-permute-start.2 = (bf16[32,1024]{1,0:T(8,128)(2,1)S(1)}, bf16[32,1024]{1,0:T(8,128)(2,1)S(1)}, u32[]{:S(2)}, u32[]{:S(2)}) collective-permute-start(bf16[32,1024]{1,0:T(8,128)(2,1)S(1)} %get-tuple-element.217), channel_id=1, source_target_pairs={{0,8},{1,1},{2,25},{3,18},{4,11},{5,4},{6,28},{7,21},{8,14},{9,7},... | collective-permute-start | bytes 196616 | tf_op jit(solution)/shard_map/ppermute | solution.py:320
  13.1 5.1 %collective-permute-start.4 = (bf16[32,1024]{1,0:T(8,128)(2,1)}, bf16[32,1024]{1,0:T(8,128)(2,1)S(1)}, u32[]{:S(2)}, u32[]{:S(2)}) collective-permute-start(bf16[32,1024]{1,0:T(8,128)(2,1)} %param.20), channel_id=1, source_target_pairs={{0,0},{1,8},{2,16},{3,24},{4,1},{5,9},{6,17},{7,25},{8,2},{9,10},{... | collective-permute-start | bytes 196616 | tf_op jit(solution)/shard_map/ppermute | solution.py:321
  18.3 6.2 %collective-permute-done.4 = bf16[32,1024]{1,0:T(8,128)(2,1)S(1)} collective-permute-done((bf16[32,1024]{1,0:T(8,128)(2,1)}, bf16[32,1024]{1,0:T(8,128)(2,1)S(1)}, u32[]{:S(2)}, u32[]{:S(2)}) %collective-permute-start.4) | collective-permute-done | bytes 65568 | tf_op jit(solution)/shard_map/ppermute | solution.py:321
  24.4 1.9 collective-permute-start.18
  27.9 2.7 collective-permute-start.6
  31.3 4.4 %collective-permute-start.13 = (bf16[4,32,1024]{2,1,0:T(8,128)(2,1)S(1)}, bf16[4,32,1024]{2,1,0:T(8,128)(2,1)S(1)}, u32[]{:S(2)}, u32[]{:S(2)}) collective-permute-start(bf16[4,32,1024]{2,1,0:T(8,128)(2,1)S(1)} %get-tuple-element.209), channel_id=1, source_target_pairs={{0,8},{1,9},{2,10},{3,11},{4,12},{5,13},{6,14},{7,15},{8,0},{9,1},... | collective-permute-start | bytes 786440 | tf_op jit(solution)/shard_map/ppermute | solution.py:45
  35.8 6.5 %collective-permute-done.6.refs_2_ = bf16[128,1024]{1,0:T(8,128)(2,1)} collective-permute-done((bf16[128,1024]{1,0:T(8,128)(2,1)S(1)}, bf16[128,1024]{1,0:T(8,128)(2,1)}, u32[]{:S(2)}, u32[]{:S(2)}) %collective-permute-start.6) | collective-permute-done | bytes 262176 | tf_op jit(solution)/shard_map/ppermute | solution.py:45
  45.8 2.8 collective-permute-start.14
  48.6 3.6 %collective-permute-done.13 = bf16[4,32,1024]{2,1,0:T(8,128)(2,1)S(1)} collective-permute-done((bf16[4,32,1024]{2,1,0:T(8,128)(2,1)S(1)}, bf16[4,32,1024]{2,1,0:T(8,128)(2,1)S(1)}, u32[]{:S(2)}, u32[]{:S(2)}) %collective-permute-start.13) | collective-permute-done | bytes 262176 | tf_op jit(solution)/shard_map/ppermute | solution.py:45
  55.6 4.6 %collective-permute-done.15 = bf16[4,32,1024]{2,1,0:T(8,128)(2,1)S(1)} collective-permute-done((bf16[4,32,1024]{2,1,0:T(8,128)(2,1)S(1)}, bf16[4,32,1024]{2,1,0:T(8,128)(2,1)S(1)}, u32[]{:S(2)}, u32[]{:S(2)}) %collective-permute-start.15) | collective-permute-done | bytes 262176 | tf_op jit(solution)/shard_map/ppermute | solution.py:49
  62.2 2.5 collective-permute-start.16
  66.9 11.5 %shard_map.152 = (bf16[1024,1024]{1,0:T(8,128)(2,1)}, bf16[1024,384]{1,0:T(8,128)(2,1)}, bf16[512,128]{1,0:T(8,128)(2,1)}, bf16[512,128]{1,0:T(8,128)(2,1)}) custom-call(s32[4]{0:T(128)} %pad_add_fusion.where_ref, bf16[128,1024]{1,0:T(8,128)(2,1)} %copy-done.18, bf16[128,1024]{1,0:T(8,128)(2,1)} %collective-permute-done.5.refs_1_, ...), custom_call_target="tpu_custom_call" | custom-call | flops 1342177280 | bytes 4194304 | tf_op jit(solution)/shard_map/pallas_call | solution.py:184
  78.5 11.9 %collective-permute-done.16 = bf16[256,1024]{1,0:T(8,128)(2,1)S(1)} collective-permute-done((bf16[256,1024]{1,0:T(8,128)(2,1)S(1)}, bf16[256,1024]{1,0:T(8,128)(2,1)S(1)}, u32[]{:S(2)}, u32[]{:S(2)}) %collective-permute-start.16) | collective-permute-done | bytes 524320 | tf_op jit(solution)/shard_map/ppermute | solution.py:45
  90.4 2.4 collective-permute-done.19
  94.1 2.6 collective-permute-done.20
  98.1 2.6 collective-permute-start.35
  100.7 3.7 %collective-permute-done.21 = bf16[64,1024]{1,0:T(8,128)(2,1)S(1)} collective-permute-done((bf16[64,1024]{1,0:T(8,128)(2,1)S(1)}, bf16[64,1024]{1,0:T(8,128)(2,1)S(1)}, u32[]{:S(2)}, u32[]{:S(2)}) %collective-permute-start.21) | collective-permute-done | bytes 131104 | tf_op jit(solution)/shard_map/ppermute | solution.py:45
  106.4 6.7 %collective-permute-done.35 = bf16[128,1024]{1,0:T(8,128)(2,1)S(1)} collective-permute-done((bf16[128,1024]{1,0:T(8,128)(2,1)}, bf16[128,1024]{1,0:T(8,128)(2,1)S(1)}, u32[]{:S(2)}, u32[]{:S(2)}) %collective-permute-start.35) | collective-permute-done | bytes 262176 | tf_op jit(solution)/shard_map/ppermute | solution.py:45
  114.1 2.0 collective-permute-done.24
  118.5 3.8 %collective-permute-done.36 = bf16[128,1024]{1,0:T(8,128)(2,1)S(1)} collective-permute-done((bf16[128,1024]{1,0:T(8,128)(2,1)S(1)}, bf16[128,1024]{1,0:T(8,128)(2,1)S(1)}, u32[]{:S(2)}, u32[]{:S(2)}) %collective-permute-start.36) | collective-permute-done | bytes 262176 | tf_op jit(solution)/shard_map/ppermute | solution.py:49
  123.9 1.8 collective-permute-start.28
  125.8 2.7 collective-permute-done.27
  131.5 2.4 fusion.60
  134.6 1.4 copy-done.7
  136.8 2.6 collective-permute-done.37
  142.8 4.0 %collective-permute-done.38 = bf16[64,1024]{1,0:T(8,128)(2,1)} collective-permute-done((bf16[64,1024]{1,0:T(8,128)(2,1)}, bf16[64,1024]{1,0:T(8,128)(2,1)}, u32[]{:S(2)}, u32[]{:S(2)}) %collective-permute-start.38) | collective-permute-done | bytes 131104 | tf_op jit(solution)/shard_map/ppermute | solution.py:45
  155.3 1.4 collective-permute-done.41
  156.7 1.5 collective-permute-done.39
  161.3 4.4 %collective-permute-done.43 = bf16[128,1024]{1,0:T(8,128)(2,1)S(1)} collective-permute-done((bf16[128,1024]{1,0:T(8,128)(2,1)S(1)}, bf16[128,1024]{1,0:T(8,128)(2,1)S(1)}, u32[]{:S(2)}, u32[]{:S(2)}) %collective-permute-start.43) | collective-permute-done | bytes 262176 | tf_op jit(solution)/shard_map/ppermute | solution.py:45
  165.7 1.4 collective-permute-start.44
  170.8 2.3 collective-permute-done.45
  173.3 1.4 collective-permute-done.49
  174.8 1.9 multiply_convert_fusion
  180.6 2.3 fusion.78
  194.3 4.4 %collective-permute-done.54 = bf16[128,1024]{1,0:T(8,128)(2,1)S(1)} collective-permute-done((bf16[128,1024]{1,0:T(8,128)(2,1)S(1)}, bf16[128,1024]{1,0:T(8,128)(2,1)S(1)}, u32[]{:S(2)}, u32[]{:S(2)}) %collective-permute-start.54) | collective-permute-done | bytes 262176 | tf_op jit(solution)/shard_map/ppermute | solution.py:45
  201.7 1.4 collective-permute-start.56
  203.1 1.7 slice_select_fusion
  204.9 3.2 collective-permute-done.56
  210.4 2.7 collective-permute-done.57
  217.3 1.7 collective-permute-start.63
  221.6 5.0 %collective-permute-done.63.got_ref = bf16[512,128]{1,0:T(8,128)(2,1)S(1)} collective-permute-done((bf16[512,128]{1,0:T(8,128)(2,1)S(1)}, bf16[512,128]{1,0:T(8,128)(2,1)S(1)}, u32[]{:S(2)}, u32[]{:S(2)}) %collective-permute-start.63) | collective-permute-done | bytes 131104 | tf_op jit(solution)/shard_map/ppermute | solution.py:45
  227.2 2.2 add_bitcast_fusion
  232.8 11.4 %shard_map.153 = (bf16[1024,384]{1,0:T(8,128)(2,1)}, bf16[512,384]{1,0:T(8,128)(2,1)}, bf16[512,384]{1,0:T(8,128)(2,1)}) custom-call(s32[4]{0:T(128)} %pad_add_fusion.where_ref, bf16[1024,384]{1,0:T(8,128)(2,1)} %get-tuple-element.120.mixed_ref, bf16[512,128]{1,0:T(8,128)(2,1)} %bitcast.239, bf16[512,128]{1,0:T(8,128)(2,1)} %copy-done.42), custom_call_target="tpu_custom_call" | custom-call | flops 1342177280 | bytes 4194304 | tf_op jit(solution)/shard_map/pallas_call | solution.py:265
  244.2 9.7 %collective-permute-done.65 = bf16[1,224,1024]{2,1,0:T(8,128)(2,1)} collective-permute-done((bf16[1,224,1024]{2,1,0:T(8,128)(2,1)}, bf16[1,224,1024]{2,1,0:T(8,128)(2,1)}, u32[]{:S(2)}, u32[]{:S(2)}) %collective-permute-start.65) | collective-permute-done | bytes 458784 | tf_op jit(solution)/shard_map/ppermute | solution.py:45
  253.9 2.1 multiply_reduce_fusion
  262.2 2.7 collective-permute-done.69
  265.0 1.7 collective-permute-start.70
  267.4 4.3 %collective-permute-done.70 = f32[3,1024]{1,0:T(4,128)S(1)} collective-permute-done((f32[3,1024]{1,0:T(4,128)S(1)}, f32[3,1024]{1,0:T(4,128)S(1)}, u32[]{:S(2)}, u32[]{:S(2)}) %collective-permute-start.70) | collective-permute-done | bytes 12320 | tf_op jit(solution)/shard_map/ppermute | solution.py:45
  271.8 5.2 %collective-permute-done.72 = bf16[512,384]{1,0:T(8,128)(2,1)} collective-permute-done((bf16[512,384]{1,0:T(8,128)(2,1)}, bf16[512,384]{1,0:T(8,128)(2,1)}, u32[]{:S(2)}, u32[]{:S(2)}) %collective-permute-start.72) | collective-permute-done | bytes 393248 | tf_op jit(solution)/shard_map/ppermute | solution.py:45
  279.2 1.4 fusion.8
  280.7 2.8 collective-permute-start.80
  283.5 1.4 fusion.7
  287.1 2.4 collective-permute-start.85
  291.6 2.9 collective-permute-done.77
  296.6 5.8 %collective-permute-done.80 = bf16[4,1,32,1024]{3,2,1,0:T(8,128)(2,1)S(1)} collective-permute-done((bf16[4,1,32,1024]{3,2,1,0:T(8,128)(2,1)S(1)}, bf16[4,1,32,1024]{3,2,1,0:T(8,128)(2,1)S(1)}, u32[]{:S(2)}, u32[]{:S(2)}) %collective-permute-start.80) | collective-permute-done | bytes 262176 | tf_op jit(solution)/shard_map/ppermute | solution.py:45
  303.1 4.8 %collective-permute-done.85 = bf16[1,128,1024]{2,1,0:T(8,128)(2,1)S(1)} collective-permute-done((bf16[1,128,1024]{2,1,0:T(8,128)(2,1)S(1)}, bf16[1,128,1024]{2,1,0:T(8,128)(2,1)S(1)}, u32[]{:S(2)}, u32[]{:S(2)}) %collective-permute-start.85) | collective-permute-done | bytes 262176 | tf_op jit(solution)/shard_map/ppermute | solution.py:45
  307.9 1.9 collective-permute-start.84
  309.9 3.5 %collective-permute-start.82 = (bf16[32,1024]{1,0:T(8,128)(2,1)S(1)}, bf16[32,1024]{1,0:T(8,128)(2,1)S(1)}, u32[]{:S(2)}, u32[]{:S(2)}) collective-permute-start(bf16[32,1024]{1,0:T(8,128)(2,1)S(1)} %get-tuple-element.202), channel_id=1, source_target_pairs={{8,0},{1,1},{25,2},{18,3},{11,4},{4,5},{28,6},{21,7},{14,8},{7,9},... | collective-permute-start | bytes 196616 | tf_op jit(solution)/shard_map/ppermute | solution.py:473
  315.0 5.6 %collective-permute-start.81 = (bf16[32,1024]{1,0:T(8,128)(2,1)S(1)}, bf16[32,1024]{1,0:T(8,128)(2,1)S(1)}, u32[]{:S(2)}, u32[]{:S(2)}) collective-permute-start(bf16[32,1024]{1,0:T(8,128)(2,1)S(1)} %get-tuple-element.201), channel_id=1, source_target_pairs={{0,0},{24,1},{17,2},{10,3},{3,4},{27,5},{20,6},{13,7},{6,8},{30,9}... | collective-permute-start | bytes 196616 | tf_op jit(solution)/shard_map/ppermute | solution.py:473
  322.4 2.0 collective-permute-start.86
  327.7 3.1 collective-permute-done.86
  (351 shorter events, 101.0 us)
Async XLA Ops:
  2.5 15.7 %collective-permute-start = (bf16[64,1024]{1,0:T(8,128)(2,1)S(1)}, bf16[64,1024]{1,0:T(8,128)(2,1)S(1)}, u32[]{:S(2)}, u32[]{:S(2)}) collective-permute-start(bf16[64,1024]{1,0:T(8,128)(2,1)S(1)} %get-tuple-element.211), channel_id=1, source_target_pairs={{0,8},{1,9},{2,10},{3,11},{4,12},{5,13},{6,14},{7,15},{8,0},{9,1},... | collective-permute-start | bytes 393224 | tf_op jit(solution)/shard_map/ppermute | solution.py:45
  6.1 12.1 %collective-permute-start.1 = (bf16[32,1024]{1,0:T(8,128)(2,1)S(1)}, bf16[32,1024]{1,0:T(8,128)(2,1)S(1)}, u32[]{:S(2)}, u32[]{:S(2)}) collective-permute-start(bf16[32,1024]{1,0:T(8,128)(2,1)S(1)} %get-tuple-element.216), channel_id=1, source_target_pairs={{0,0},{1,24},{2,17},{3,10},{4,3},{5,27},{6,20},{7,13},{8,6},{9,30}... | collective-permute-start | bytes 196616 | tf_op jit(solution)/shard_map/ppermute | solution.py:320
  8.6 9.6 %collective-permute-start.2 = (bf16[32,1024]{1,0:T(8,128)(2,1)S(1)}, bf16[32,1024]{1,0:T(8,128)(2,1)S(1)}, u32[]{:S(2)}, u32[]{:S(2)}) collective-permute-start(bf16[32,1024]{1,0:T(8,128)(2,1)S(1)} %get-tuple-element.217), channel_id=1, source_target_pairs={{0,8},{1,1},{2,25},{3,18},{4,11},{5,4},{6,28},{7,21},{8,14},{9,7},... | collective-permute-start | bytes 196616 | tf_op jit(solution)/shard_map/ppermute | solution.py:320
  12.4 5.9 %collective-permute-start.3 = (bf16[32,1024]{1,0:T(8,128)(2,1)S(1)}, bf16[32,1024]{1,0:T(8,128)(2,1)S(1)}, u32[]{:S(2)}, u32[]{:S(2)}) collective-permute-start(bf16[32,1024]{1,0:T(8,128)(2,1)S(1)} %get-tuple-element.215), channel_id=1, source_target_pairs={{0,16},{1,9},{2,2},{3,26},{4,19},{5,12},{6,5},{7,29},{8,22},{9,15}... | collective-permute-start | bytes 196616 | tf_op jit(solution)/shard_map/ppermute | solution.py:320
  13.1 11.4 %collective-permute-start.4 = (bf16[32,1024]{1,0:T(8,128)(2,1)}, bf16[32,1024]{1,0:T(8,128)(2,1)S(1)}, u32[]{:S(2)}, u32[]{:S(2)}) collective-permute-start(bf16[32,1024]{1,0:T(8,128)(2,1)} %param.20), channel_id=1, source_target_pairs={{0,0},{1,8},{2,16},{3,24},{4,1},{5,9},{6,17},{7,25},{8,2},{9,10},{... | collective-permute-start | bytes 196616 | tf_op jit(solution)/shard_map/ppermute | solution.py:321
  24.4 6.2 %collective-permute-start.9 = (bf16[128,1024]{1,0:T(8,128)(2,1)S(1)}, bf16[128,1024]{1,0:T(8,128)(2,1)S(1)}, u32[]{:S(2)}, u32[]{:S(2)}) collective-permute-start(bf16[128,1024]{1,0:T(8,128)(2,1)S(1)} %pad_maximum_fusion.12.refs_0_), channel_id=1, source_target_pairs={{0,1},{1,0},{2,3},{3,2},{4,5},{5,4},{6,7},{7,6},{8,9},{9,8},{10,11... | collective-permute-start | bytes 786440 | tf_op jit(solution)/shard_map/ppermute | solution.py:45
  24.4 54.1 %collective-permute-start.18 = (bf16[128,1024]{1,0:T(8,128)(2,1)}, bf16[128,1024]{1,0:T(8,128)(2,1)}, u32[]{:S(2)}, u32[]{:S(2)}) collective-permute-start(bf16[128,1024]{1,0:T(8,128)(2,1)} %param.22), channel_id=1, source_target_pairs={{0,0},{1,16},{2,1},{3,17},{4,2},{5,18},{6,3},{7,19},{8,4},{9,20},{... | collective-permute-start | bytes 786440 | tf_op jit(solution)/shard_map/ppermute | solution.py:319
  27.0 16.4 %collective-permute-start.5 = (bf16[128,1024]{1,0:T(8,128)(2,1)S(1)}, bf16[128,1024]{1,0:T(8,128)(2,1)}, u32[]{:S(2)}, u32[]{:S(2)}) collective-permute-start(bf16[128,1024]{1,0:T(8,128)(2,1)S(1)} %pad_maximum_fusion.12.refs_0_), channel_id=1, source_target_pairs={{0,2},{1,3},{2,0},{3,1},{4,6},{5,7},{6,4},{7,5},{8,10},{9,11},{10,... | collective-permute-start | bytes 786440 | tf_op jit(solution)/shard_map/ppermute | solution.py:45
  27.9 14.4 %collective-permute-start.6 = (bf16[128,1024]{1,0:T(8,128)(2,1)S(1)}, bf16[128,1024]{1,0:T(8,128)(2,1)}, u32[]{:S(2)}, u32[]{:S(2)}) collective-permute-start(bf16[128,1024]{1,0:T(8,128)(2,1)S(1)} %pad_maximum_fusion.12.refs_0_), channel_id=1, source_target_pairs={{0,4},{1,5},{2,6},{3,7},{4,0},{5,1},{6,2},{7,3},{8,12},{9,13},{10,... | collective-permute-start | bytes 786440 | tf_op jit(solution)/shard_map/ppermute | solution.py:45
  31.3 20.8 %collective-permute-start.13 = (bf16[4,32,1024]{2,1,0:T(8,128)(2,1)S(1)}, bf16[4,32,1024]{2,1,0:T(8,128)(2,1)S(1)}, u32[]{:S(2)}, u32[]{:S(2)}) collective-permute-start(bf16[4,32,1024]{2,1,0:T(8,128)(2,1)S(1)} %get-tuple-element.209), channel_id=1, source_target_pairs={{0,8},{1,9},{2,10},{3,11},{4,12},{5,13},{6,14},{7,15},{8,0},{9,1},... | collective-permute-start | bytes 786440 | tf_op jit(solution)/shard_map/ppermute | solution.py:45
  44.3 9.3 %collective-permute-start.8 = (bf16[64,1024]{1,0:T(8,128)(2,1)S(1)}, bf16[64,1024]{1,0:T(8,128)(2,1)S(1)}, u32[]{:S(2)}, u32[]{:S(2)}) collective-permute-start(bf16[64,1024]{1,0:T(8,128)(2,1)S(1)} %slice.438), channel_id=1, source_target_pairs={{0,4},{1,5},{2,6},{3,7},{4,0},{5,1},{6,2},{7,3},{8,12},{9,13},{10,... | collective-permute-start | bytes 393224 | tf_op jit(solution)/shard_map/ppermute | solution.py:45
  45.8 9.3 %collective-permute-start.14 = (bf16[4,32,1024]{2,1,0:T(8,128)(2,1)S(1)}, bf16[4,32,1024]{2,1,0:T(8,128)(2,1)S(1)}, u32[]{:S(2)}, u32[]{:S(2)}) collective-permute-start(bf16[4,32,1024]{2,1,0:T(8,128)(2,1)S(1)} %get-tuple-element.209), channel_id=1, source_target_pairs={{0,16},{16,0},{1,17},{17,1},{2,18},{18,2},{3,19},{19,3},{4,20},{20... | collective-permute-start | bytes 786440 | tf_op jit(solution)/shard_map/ppermute | solution.py:49
  48.6 13.5 %collective-permute-start.10 = (bf16[128,1024]{1,0:T(8,128)(2,1)}, bf16[128,1024]{1,0:T(8,128)(2,1)}, u32[]{:S(2)}, u32[]{:S(2)}) collective-permute-start(bf16[128,1024]{1,0:T(8,128)(2,1)} %collective-permute-done.5.refs_1_), channel_id=1, source_target_pairs={{0,1},{1,0},{2,3},{3,2},{4,5},{5,4},{6,7},{7,6},{8,9},{9,8},{10,11... | collective-permute-start | bytes 786440 | tf_op jit(solution)/shard_map/ppermute | solution.py:45
  52.2 8.0 %collective-permute-start.15 = (bf16[4,32,1024]{2,1,0:T(8,128)(2,1)S(1)}, bf16[4,32,1024]{2,1,0:T(8,128)(2,1)S(1)}, u32[]{:S(2)}, u32[]{:S(2)}) collective-permute-start(bf16[4,32,1024]{2,1,0:T(8,128)(2,1)S(1)} %collective-permute-done.13), channel_id=1, source_target_pairs={{0,16},{16,0},{1,17},{17,1},{2,18},{18,2},{3,19},{19,3},{4,20},{20... | collective-permute-start | bytes 786440 | tf_op jit(solution)/shard_map/ppermute | solution.py:49
  53.7 8.4 %collective-permute-start.11 = (bf16[128,1024]{1,0:T(8,128)(2,1)}, bf16[128,1024]{1,0:T(8,128)(2,1)}, u32[]{:S(2)}, u32[]{:S(2)}) collective-permute-start(bf16[128,1024]{1,0:T(8,128)(2,1)} %collective-permute-done.6.refs_2_), channel_id=1, source_target_pairs={{0,1},{1,0},{2,3},{3,2},{4,5},{5,4},{6,7},{7,6},{8,9},{9,8},{10,11... | collective-permute-start | bytes 786440 | tf_op jit(solution)/shard_map/ppermute | solution.py:45
  55.0 7.1 %collective-permute-start.12 = (bf16[128,1024]{1,0:T(8,128)(2,1)}, bf16[128,1024]{1,0:T(8,128)(2,1)S(1)}, u32[]{:S(2)}, u32[]{:S(2)}) collective-permute-start(bf16[128,1024]{1,0:T(8,128)(2,1)} %constant_dynamic-update-slice_fusion.refs_3_), channel_id=1, source_target_pairs={{0,1},{1,0},{2,3},{3,2},{4,5},{5,4},{6,7},{7,6},{8,9},{9,8},{10,11... | collective-permute-start | bytes 786440 | tf_op jit(solution)/shard_map/ppermute | solution.py:45
  62.2 28.2 %collective-permute-start.16 = (bf16[256,1024]{1,0:T(8,128)(2,1)S(1)}, bf16[256,1024]{1,0:T(8,128)(2,1)S(1)}, u32[]{:S(2)}, u32[]{:S(2)}) collective-permute-start(bf16[256,1024]{1,0:T(8,128)(2,1)S(1)} %copy-done.32), channel_id=1, source_target_pairs={{0,8},{1,9},{2,10},{3,11},{4,12},{5,13},{6,14},{7,15},{8,0},{9,1},... | collective-permute-start | bytes 1572872 | tf_op jit(solution)/shard_map/ppermute | solution.py:45
  64.7 25.7 %collective-permute-start.17 = (bf16[256,1024]{1,0:T(8,128)(2,1)S(1)}, bf16[256,1024]{1,0:T(8,128)(2,1)S(1)}, u32[]{:S(2)}, u32[]{:S(2)}) collective-permute-start(bf16[256,1024]{1,0:T(8,128)(2,1)S(1)} %copy-done.32), channel_id=1, source_target_pairs={{0,16},{16,0},{1,17},{17,1},{2,18},{18,2},{3,19},{19,3},{4,20},{20... | collective-permute-start | bytes 1572872 | tf_op jit(solution)/shard_map/ppermute | solution.py:49
  78.4 14.3 %collective-permute-start.19 = (bf16[512,128]{1,0:T(8,128)(2,1)}, bf16[512,128]{1,0:T(8,128)(2,1)S(1)}, u32[]{:S(2)}, u32[]{:S(2)}) collective-permute-start(bf16[512,128]{1,0:T(8,128)(2,1)} %get-tuple-element.112), channel_id=1, source_target_pairs={{0,8},{1,9},{2,10},{3,11},{4,12},{5,13},{6,14},{7,15},{8,0},{9,1},... | collective-permute-start | bytes 393224 | tf_op jit(solution)/shard_map/ppermute | solution.py:45
  97.2 7.2 %collective-permute-start.21 = (bf16[64,1024]{1,0:T(8,128)(2,1)S(1)}, bf16[64,1024]{1,0:T(8,128)(2,1)S(1)}, u32[]{:S(2)}, u32[]{:S(2)}) collective-permute-start(bf16[64,1024]{1,0:T(8,128)(2,1)S(1)} %get-tuple-element.194), channel_id=1, source_target_pairs={{0,4},{1,5},{2,6},{3,7},{4,0},{5,1},{6,2},{7,3},{8,12},{9,13},{10,... | collective-permute-start | bytes 393224 | tf_op jit(solution)/shard_map/ppermute | solution.py:45
  97.3 7.1 %collective-permute-start.23 = (bf16[64,1024]{1,0:T(8,128)(2,1)S(1)}, bf16[64,1024]{1,0:T(8,128)(2,1)S(1)}, u32[]{:S(2)}, u32[]{:S(2)}) collective-permute-start(bf16[64,1024]{1,0:T(8,128)(2,1)S(1)} %get-tuple-element.193), channel_id=1, source_target_pairs={{0,2},{1,3},{2,0},{3,1},{4,6},{5,7},{6,4},{7,5},{8,10},{9,11},{10,... | collective-permute-start | bytes 393224 | tf_op jit(solution)/shard_map/ppermute | solution.py:45
  98.1 14.9 %collective-permute-start.35 = (bf16[128,1024]{1,0:T(8,128)(2,1)}, bf16[128,1024]{1,0:T(8,128)(2,1)S(1)}, u32[]{:S(2)}, u32[]{:S(2)}) collective-permute-start(bf16[128,1024]{1,0:T(8,128)(2,1)} %collective-permute-done.18), channel_id=1, source_target_pairs={{0,8},{1,9},{2,10},{3,11},{4,12},{5,13},{6,14},{7,15},{8,0},{9,1},... | collective-permute-start | bytes 786440 | tf_op jit(solution)/shard_map/ppermute | solution.py:45
  104.5 11.5 %collective-permute-start.24 = (bf16[128,1024]{1,0:T(8,128)(2,1)S(1)}, bf16[128,1024]{1,0:T(8,128)(2,1)S(1)}, u32[]{:S(2)}, u32[]{:S(2)}) collective-permute-start(bf16[128,1024]{1,0:T(8,128)(2,1)S(1)} %pad_maximum_fusion.15), channel_id=1, source_target_pairs={{0,4},{1,5},{2,6},{3,7},{4,0},{5,1},{6,2},{7,3},{8,12},{9,13},{10,... | collective-permute-start | bytes 786440 | tf_op jit(solution)/shard_map/ppermute | solution.py:45
  104.8 11.3 %collective-permute-start.22 = (bf16[128,1024]{1,0:T(8,128)(2,1)S(1)}, bf16[128,1024]{1,0:T(8,128)(2,1)S(1)}, u32[]{:S(2)}, u32[]{:S(2)}) collective-permute-start(bf16[128,1024]{1,0:T(8,128)(2,1)S(1)} %pad_maximum_fusion.14), channel_id=1, source_target_pairs={{0,2},{1,3},{2,0},{3,1},{4,6},{5,7},{6,4},{7,5},{8,10},{9,11},{10,... | collective-permute-start | bytes 786440 | tf_op jit(solution)/shard_map/ppermute | solution.py:45
  105.6 11.7 %collective-permute-start.34 = (bf16[128,1024]{1,0:T(8,128)(2,1)}, bf16[128,1024]{1,0:T(8,128)(2,1)S(1)}, u32[]{:S(2)}, u32[]{:S(2)}) collective-permute-start(bf16[128,1024]{1,0:T(8,128)(2,1)} %collective-permute-done.18), channel_id=1, source_target_pairs={{0,16},{16,0},{1,17},{17,1},{2,18},{18,2},{3,19},{19,3},{4,20},{20... | collective-permute-start | bytes 786440 | tf_op jit(solution)/shard_map/ppermute | solution.py:49
  113.1 9.2 %collective-permute-start.36 = (bf16[128,1024]{1,0:T(8,128)(2,1)S(1)}, bf16[128,1024]{1,0:T(8,128)(2,1)S(1)}, u32[]{:S(2)}, u32[]{:S(2)}) collective-permute-start(bf16[128,1024]{1,0:T(8,128)(2,1)S(1)} %collective-permute-done.35), channel_id=1, source_target_pairs={{0,16},{16,0},{1,17},{17,1},{2,18},{18,2},{3,19},{19,3},{4,20},{20... | collective-permute-start | bytes 786440 | tf_op jit(solution)/shard_map/ppermute | solution.py:49
  116.4 6.6 %collective-permute-start.26 = (bf16[128,1024]{1,0:T(8,128)(2,1)S(1)}, bf16[128,1024]{1,0:T(8,128)(2,1)S(1)}, u32[]{:S(2)}, u32[]{:S(2)}) collective-permute-start(bf16[128,1024]{1,0:T(8,128)(2,1)S(1)} %get-tuple-element.162), channel_id=1, source_target_pairs={{0,4},{1,5},{2,6},{3,7},{4,0},{5,1},{6,2},{7,3},{8,12},{9,13},{10,... | collective-permute-start | bytes 786440 | tf_op jit(solution)/shard_map/ppermute | solution.py:45
  116.5 7.5 %collective-permute-start.25 = (bf16[128,1024]{1,0:T(8,128)(2,1)S(1)}, bf16[128,1024]{1,0:T(8,128)(2,1)S(1)}, u32[]{:S(2)}, u32[]{:S(2)}) collective-permute-start(bf16[128,1024]{1,0:T(8,128)(2,1)S(1)} %get-tuple-element.162), channel_id=1, source_target_pairs={{0,2},{1,3},{2,0},{3,1},{4,6},{5,7},{6,4},{7,5},{8,10},{9,11},{10,... | collective-permute-start | bytes 786440 | tf_op jit(solution)/shard_map/ppermute | solution.py:45
  116.6 14.9 %collective-permute-start.33 = (bf16[256,1024]{1,0:T(8,128)(2,1)S(1)}, bf16[256,1024]{1,0:T(8,128)(2,1)S(1)}, u32[]{:S(2)}, u32[]{:S(2)}) collective-permute-start(bf16[256,1024]{1,0:T(8,128)(2,1)S(1)} %collective-permute-done.16), channel_id=1, source_target_pairs={{0,16},{16,0},{1,17},{17,1},{2,18},{18,2},{3,19},{19,3},{4,20},{20... | collective-permute-start | bytes 1572872 | tf_op jit(solution)/shard_map/ppermute | solution.py:49
  122.5 7.3 %collective-permute-start.29 = (bf16[128,1024]{1,0:T(8,128)(2,1)S(1)}, bf16[128,1024]{1,0:T(8,128)(2,1)S(1)}, u32[]{:S(2)}, u32[]{:S(2)}) collective-permute-start(bf16[128,1024]{1,0:T(8,128)(2,1)S(1)} %get-tuple-element.162), channel_id=1, source_target_pairs={{0,1},{1,0},{2,3},{3,2},{4,5},{5,4},{6,7},{7,6},{8,9},{9,8},{10,11... | collective-permute-start | bytes 786440 | tf_op jit(solution)/shard_map/ppermute | solution.py:45
  123.9 5.7 %collective-permute-start.28 = (bf16[64,1024]{1,0:T(8,128)(2,1)S(1)}, bf16[64,1024]{1,0:T(8,128)(2,1)S(1)}, u32[]{:S(2)}, u32[]{:S(2)}) collective-permute-start(bf16[64,1024]{1,0:T(8,128)(2,1)S(1)} %slice.452), channel_id=1, source_target_pairs={{0,4},{1,5},{2,6},{3,7},{4,0},{5,1},{6,2},{7,3},{8,12},{9,13},{10,... | collective-permute-start | bytes 393224 | tf_op jit(solution)/shard_map/ppermute | solution.py:45
  140.9 5.9 %collective-permute-start.38 = (bf16[64,1024]{1,0:T(8,128)(2,1)}, bf16[64,1024]{1,0:T(8,128)(2,1)}, u32[]{:S(2)}, u32[]{:S(2)}) collective-permute-start(bf16[64,1024]{1,0:T(8,128)(2,1)} %get-tuple-element.190), channel_id=1, source_target_pairs={{0,4},{1,5},{2,6},{3,7},{4,0},{5,1},{6,2},{7,3},{8,12},{9,13},{10,... | collective-permute-start | bytes 393224 | tf_op jit(solution)/shard_map/ppermute | solution.py:45
  141.8 5.6 %collective-permute-start.40 = (bf16[64,1024]{1,0:T(8,128)(2,1)}, bf16[64,1024]{1,0:T(8,128)(2,1)}, u32[]{:S(2)}, u32[]{:S(2)}) collective-permute-start(bf16[64,1024]{1,0:T(8,128)(2,1)} %get-tuple-element.189), channel_id=1, source_target_pairs={{0,2},{1,3},{2,0},{3,1},{4,6},{5,7},{6,4},{7,5},{8,10},{9,11},{10,... | collective-permute-start | bytes 393224 | tf_op jit(solution)/shard_map/ppermute | solution.py:45
  149.2 7.5 %collective-permute-start.41 = (bf16[128,1024]{1,0:T(8,128)(2,1)}, bf16[128,1024]{1,0:T(8,128)(2,1)}, u32[]{:S(2)}, u32[]{:S(2)}) collective-permute-start(bf16[128,1024]{1,0:T(8,128)(2,1)} %pad_maximum_fusion.18), channel_id=1, source_target_pairs={{0,4},{1,5},{2,6},{3,7},{4,0},{5,1},{6,2},{7,3},{8,12},{9,13},{10,... | collective-permute-start | bytes 786440 | tf_op jit(solution)/shard_map/ppermute | solution.py:45
  151.0 7.1 %collective-permute-start.39 = (bf16[128,1024]{1,0:T(8,128)(2,1)}, bf16[128,1024]{1,0:T(8,128)(2,1)S(1)}, u32[]{:S(2)}, u32[]{:S(2)}) collective-permute-start(bf16[128,1024]{1,0:T(8,128)(2,1)} %pad_maximum_fusion.17), channel_id=1, source_target_pairs={{0,2},{1,3},{2,0},{3,1},{4,6},{5,7},{6,4},{7,5},{8,10},{9,11},{10,... | collective-permute-start | bytes 786440 | tf_op jit(solution)/shard_map/ppermute | solution.py:45
  159.3 6.4 %collective-permute-start.43 = (bf16[128,1024]{1,0:T(8,128)(2,1)S(1)}, bf16[128,1024]{1,0:T(8,128)(2,1)S(1)}, u32[]{:S(2)}, u32[]{:S(2)}) collective-permute-start(bf16[128,1024]{1,0:T(8,128)(2,1)S(1)} %get-tuple-element.157), channel_id=1, source_target_pairs={{0,4},{1,5},{2,6},{3,7},{4,0},{5,1},{6,2},{7,3},{8,12},{9,13},{10,... | collective-permute-start | bytes 786440 | tf_op jit(solution)/shard_map/ppermute | solution.py:45
  160.2 7.8 %collective-permute-start.42 = (bf16[128,1024]{1,0:T(8,128)(2,1)S(1)}, bf16[128,1024]{1,0:T(8,128)(2,1)S(1)}, u32[]{:S(2)}, u32[]{:S(2)}) collective-permute-start(bf16[128,1024]{1,0:T(8,128)(2,1)S(1)} %get-tuple-element.157), channel_id=1, source_target_pairs={{0,2},{1,3},{2,0},{3,1},{4,6},{5,7},{6,4},{7,5},{8,10},{9,11},{10,... | collective-permute-start | bytes 786440 | tf_op jit(solution)/shard_map/ppermute | solution.py:45
  161.2 12.0 %collective-permute-start.46 = (bf16[128,1024]{1,0:T(8,128)(2,1)S(1)}, bf16[128,1024]{1,0:T(8,128)(2,1)S(1)}, u32[]{:S(2)}, u32[]{:S(2)}) collective-permute-start(bf16[128,1024]{1,0:T(8,128)(2,1)S(1)} %get-tuple-element.157), channel_id=1, source_target_pairs={{0,1},{1,0},{2,3},{3,2},{4,5},{5,4},{6,7},{7,6},{8,9},{9,8},{10,11... | collective-permute-start | bytes 786440 | tf_op jit(solution)/shard_map/ppermute | solution.py:45
  184.4 5.8 %collective-permute-start.51 = (bf16[64,1024]{1,0:T(8,128)(2,1)S(1)}, bf16[64,1024]{1,0:T(8,128)(2,1)S(1)}, u32[]{:S(2)}, u32[]{:S(2)}) collective-permute-start(bf16[64,1024]{1,0:T(8,128)(2,1)S(1)} %get-tuple-element.186), channel_id=1, source_target_pairs={{0,4},{1,5},{2,6},{3,7},{4,0},{5,1},{6,2},{7,3},{8,12},{9,13},{10,... | collective-permute-start | bytes 393224 | tf_op jit(solution)/shard_map/ppermute | solution.py:45
  188.0 33.5 %collective-permute-start.64 = (bf16[2,256,1024]{2,1,0:T(8,128)(2,1)}, bf16[2,256,1024]{2,1,0:T(8,128)(2,1)}, u32[]{:S(2)}, u32[]{:S(2)}) collective-permute-start(bf16[2,256,1024]{2,1,0:T(8,128)(2,1)} %bitcast.41), channel_id=1, source_target_pairs={{0,16},{16,0},{1,17},{17,1},{2,18},{18,2},{3,19},{19,3},{4,20},{20... | collective-permute-start | bytes 3145736 | tf_op jit(solution)/shard_map/ppermute | solution.py:49
  191.2 7.5 %collective-permute-start.54 = (bf16[128,1024]{1,0:T(8,128)(2,1)S(1)}, bf16[128,1024]{1,0:T(8,128)(2,1)S(1)}, u32[]{:S(2)}, u32[]{:S(2)}) collective-permute-start(bf16[128,1024]{1,0:T(8,128)(2,1)S(1)} %pad_maximum_fusion.21), channel_id=1, source_target_pairs={{0,4},{1,5},{2,6},{3,7},{4,0},{5,1},{6,2},{7,3},{8,12},{9,13},{10,... | collective-permute-start | bytes 786440 | tf_op jit(solution)/shard_map/ppermute | solution.py:45
  192.2 7.2 %collective-permute-start.52 = (bf16[128,1024]{1,0:T(8,128)(2,1)S(1)}, bf16[128,1024]{1,0:T(8,128)(2,1)S(1)}, u32[]{:S(2)}, u32[]{:S(2)}) collective-permute-start(bf16[128,1024]{1,0:T(8,128)(2,1)S(1)} %pad_maximum_fusion.20), channel_id=1, source_target_pairs={{0,2},{1,3},{2,0},{3,1},{4,6},{5,7},{6,4},{7,5},{8,10},{9,11},{10,... | collective-permute-start | bytes 786440 | tf_op jit(solution)/shard_map/ppermute | solution.py:45
  200.6 8.5 %collective-permute-start.55 = (bf16[128,1024]{1,0:T(8,128)(2,1)S(1)}, bf16[128,1024]{1,0:T(8,128)(2,1)S(1)}, u32[]{:S(2)}, u32[]{:S(2)}) collective-permute-start(bf16[128,1024]{1,0:T(8,128)(2,1)S(1)} %get-tuple-element.156), channel_id=1, source_target_pairs={{0,2},{1,3},{2,0},{3,1},{4,6},{5,7},{6,4},{7,5},{8,10},{9,11},{10,... | collective-permute-start | bytes 786440 | tf_op jit(solution)/shard_map/ppermute | solution.py:45
  201.7 6.4 %collective-permute-start.56 = (bf16[128,1024]{1,0:T(8,128)(2,1)S(1)}, bf16[128,1024]{1,0:T(8,128)(2,1)S(1)}, u32[]{:S(2)}, u32[]{:S(2)}) collective-permute-start(bf16[128,1024]{1,0:T(8,128)(2,1)S(1)} %get-tuple-element.156), channel_id=1, source_target_pairs={{0,4},{1,5},{2,6},{3,7},{4,0},{5,1},{6,2},{7,3},{8,12},{9,13},{10,... | collective-permute-start | bytes 786440 | tf_op jit(solution)/shard_map/ppermute | solution.py:45
  204.8 9.5 %collective-permute-start.59 = (bf16[128,1024]{1,0:T(8,128)(2,1)S(1)}, bf16[128,1024]{1,0:T(8,128)(2,1)S(1)}, u32[]{:S(2)}, u32[]{:S(2)}) collective-permute-start(bf16[128,1024]{1,0:T(8,128)(2,1)S(1)} %get-tuple-element.156), channel_id=1, source_target_pairs={{0,1},{1,0},{2,3},{3,2},{4,5},{5,4},{6,7},{7,6},{8,9},{9,8},{10,11... | collective-permute-start | bytes 786440 | tf_op jit(solution)/shard_map/ppermute | solution.py:45
  217.3 9.2 %collective-permute-start.63 = (bf16[512,128]{1,0:T(8,128)(2,1)S(1)}, bf16[512,128]{1,0:T(8,128)(2,1)S(1)}, u32[]{:S(2)}, u32[]{:S(2)}) collective-permute-start(bf16[512,128]{1,0:T(8,128)(2,1)S(1)} %bitcast.240), channel_id=1, source_target_pairs={{0,8},{1,9},{2,10},{3,11},{4,12},{5,13},{6,14},{7,15},{8,0},{9,1},... | collective-permute-start | bytes 393224 | tf_op jit(solution)/shard_map/ppermute | solution.py:45
  219.9 24.3 %collective-permute-start.66 = (bf16[2,128,1024]{2,1,0:T(8,128)(2,1)}, bf16[2,128,1024]{2,1,0:T(8,128)(2,1)}, u32[]{:S(2)}, u32[]{:S(2)}) collective-permute-start(bf16[2,128,1024]{2,1,0:T(8,128)(2,1)} %fusion.10), channel_id=1, source_target_pairs={{0,16},{16,0},{1,17},{17,1},{2,18},{18,2},{3,19},{19,3},{4,20},{20... | collective-permute-start | bytes 1572872 | tf_op jit(solution)/shard_map/ppermute | solution.py:49
  231.6 22.3 %collective-permute-start.65 = (bf16[1,224,1024]{2,1,0:T(8,128)(2,1)}, bf16[1,224,1024]{2,1,0:T(8,128)(2,1)}, u32[]{:S(2)}, u32[]{:S(2)}) collective-permute-start(bf16[1,224,1024]{2,1,0:T(8,128)(2,1)} %fusion.34), channel_id=1, source_target_pairs={{0,8},{1,9},{2,10},{3,11},{4,12},{5,13},{6,14},{7,15},{8,0},{9,1},... | collective-permute-start | bytes 1376264 | tf_op jit(solution)/shard_map/ppermute | solution.py:45
  256.1 20.8 %collective-permute-start.72 = (bf16[512,384]{1,0:T(8,128)(2,1)}, bf16[512,384]{1,0:T(8,128)(2,1)}, u32[]{:S(2)}, u32[]{:S(2)}) collective-permute-start(bf16[512,384]{1,0:T(8,128)(2,1)} %get-tuple-element.135), channel_id=1, source_target_pairs={{0,8},{1,9},{2,10},{3,11},{4,12},{5,13},{6,14},{7,15},{8,0},{9,1},... | collective-permute-start | bytes 1179656 | tf_op jit(solution)/shard_map/ppermute | solution.py:45
  259.4 17.5 %collective-permute-start.73 = (bf16[4,2,32,1024]{3,2,0,1:T(8,128)(2,1)}, bf16[4,2,32,1024]{3,2,0,1:T(8,128)(2,1)}, u32[]{:S(2)}, u32[]{:S(2)}) collective-permute-start(bf16[4,2,32,1024]{3,2,0,1:T(8,128)(2,1)} %fusion.11), channel_id=1, source_target_pairs={{0,16},{16,0},{1,17},{17,1},{2,18},{18,2},{3,19},{19,3},{4,20},{20... | collective-permute-start | bytes 1572872 | tf_op jit(solution)/shard_map/ppermute | solution.py:49
  265.0 6.8 %collective-permute-start.70 = (f32[3,1024]{1,0:T(4,128)S(1)}, f32[3,1024]{1,0:T(4,128)S(1)}, u32[]{:S(2)}, u32[]{:S(2)}) collective-permute-start(f32[3,1024]{1,0:T(4,128)S(1)} %add.206), channel_id=1, source_target_pairs={{0,4},{1,5},{2,6},{3,7},{4,0},{5,1},{6,2},{7,3},{8,12},{9,13},{10,... | collective-permute-start | bytes 36872 | tf_op jit(solution)/shard_map/ppermute | solution.py:45
  271.8 38.1 %collective-permute-start.71 = (f32[3,1024]{1,0:T(4,128)S(1)}, f32[3,1024]{1,0:T(4,128)S(1)}, u32[]{:S(2)}, u32[]{:S(2)}) collective-permute-start(f32[3,1024]{1,0:T(4,128)S(1)} %add.207), channel_id=1, source_target_pairs={{0,8},{1,9},{2,10},{3,11},{4,12},{5,13},{6,14},{7,15},{8,0},{9,1},... | collective-permute-start | bytes 36872 | tf_op jit(solution)/shard_map/ppermute | solution.py:45
  279.0 6.3 %collective-permute-start.74 = (bf16[512,1024]{1,0:T(8,128)(2,1)S(1)}, bf16[512,1024]{1,0:T(8,128)(2,1)S(1)}, u32[]{:S(2)}, u32[]{:S(2)}) collective-permute-start(bf16[512,1024]{1,0:T(8,128)(2,1)S(1)} %convolution_convert_fusion.1), channel_id=1, source_target_pairs={{0,1},{1,0},{2,3},{3,2},{4,5},{5,4},{6,7},{7,6},{8,9},{9,8},{10,11... | collective-permute-start | bytes 3145736 | tf_op jit(solution)/shard_map/ppermute | solution.py:45
  279.1 6.2 %collective-permute-start.75 = (bf16[1,32,1024]{2,1,0:T(8,128)(2,1)S(1)}, bf16[1,32,1024]{2,1,0:T(8,128)(2,1)S(1)}, u32[]{:S(2)}, u32[]{:S(2)}) collective-permute-start(bf16[1,32,1024]{2,1,0:T(8,128)(2,1)S(1)} %fusion.50), channel_id=1, source_target_pairs={{0,8},{1,9},{2,10},{3,11},{4,12},{5,13},{6,14},{7,15},{8,0},{9,1},... | collective-permute-start | bytes 196616 | tf_op jit(solution)/shard_map/ppermute | solution.py:45
  280.7 21.7 %collective-permute-start.80 = (bf16[4,1,32,1024]{3,2,1,0:T(8,128)(2,1)S(1)}, bf16[4,1,32,1024]{3,2,1,0:T(8,128)(2,1)S(1)}, u32[]{:S(2)}, u32[]{:S(2)}) collective-permute-start(bf16[4,1,32,1024]{3,2,1,0:T(8,128)(2,1)S(1)} %fusion.37), channel_id=1, source_target_pairs={{0,8},{1,9},{2,10},{3,11},{4,12},{5,13},{6,14},{7,15},{8,0},{9,1},... | collective-permute-start | bytes 786440 | tf_op jit(solution)/shard_map/ppermute | solution.py:45
  287.1 7.4 %collective-permute-start.77 = (bf16[64,1024]{1,0:T(8,128)(2,1)S(1)}, bf16[64,1024]{1,0:T(8,128)(2,1)S(1)}, u32[]{:S(2)}, u32[]{:S(2)}) collective-permute-start(bf16[64,1024]{1,0:T(8,128)(2,1)S(1)} %get-tuple-element.181), channel_id=1, source_target_pairs={{0,4},{1,5},{2,6},{3,7},{4,0},{5,1},{6,2},{7,3},{8,12},{9,13},{10,... | collective-permute-start | bytes 393224 | tf_op jit(solution)/shard_map/ppermute | solution.py:45
  287.1 20.8 %collective-permute-start.85 = (bf16[1,128,1024]{2,1,0:T(8,128)(2,1)S(1)}, bf16[1,128,1024]{2,1,0:T(8,128)(2,1)S(1)}, u32[]{:S(2)}, u32[]{:S(2)}) collective-permute-start(bf16[1,128,1024]{2,1,0:T(8,128)(2,1)S(1)} %fusion.39), channel_id=1, source_target_pairs={{0,8},{1,9},{2,10},{3,11},{4,12},{5,13},{6,14},{7,15},{8,0},{9,1},... | collective-permute-start | bytes 786440 | tf_op jit(solution)/shard_map/ppermute | solution.py:45
  294.6 30.6 %collective-permute-start.79 = (bf16[128,1024]{1,0:T(8,128)(2,1)S(1)}, bf16[128,1024]{1,0:T(8,128)(2,1)S(1)}, u32[]{:S(2)}, u32[]{:S(2)}) collective-permute-start(bf16[128,1024]{1,0:T(8,128)(2,1)S(1)} %pad_maximum_fusion.24), channel_id=1, source_target_pairs={{0,4},{1,5},{2,6},{3,7},{4,0},{5,1},{6,2},{7,3},{8,12},{9,13},{10,... | collective-permute-start | bytes 786440 | tf_op jit(solution)/shard_map/ppermute | solution.py:45
  295.7 29.5 %collective-permute-start.78 = (bf16[128,1024]{1,0:T(8,128)(2,1)S(1)}, bf16[128,1024]{1,0:T(8,128)(2,1)S(1)}, u32[]{:S(2)}, u32[]{:S(2)}) collective-permute-start(bf16[128,1024]{1,0:T(8,128)(2,1)S(1)} %pad_maximum_fusion.23), channel_id=1, source_target_pairs={{0,2},{1,3},{2,0},{3,1},{4,6},{5,7},{6,4},{7,5},{8,10},{9,11},{10,... | collective-permute-start | bytes 786440 | tf_op jit(solution)/shard_map/ppermute | solution.py:45
  302.4 19.9 %collective-permute-start.83 = (bf16[32,1024]{1,0:T(8,128)(2,1)S(1)}, bf16[32,1024]{1,0:T(8,128)(2,1)S(1)}, u32[]{:S(2)}, u32[]{:S(2)}) collective-permute-start(bf16[32,1024]{1,0:T(8,128)(2,1)S(1)} %get-tuple-element.203), channel_id=1, source_target_pairs={{16,0},{9,1},{2,2},{26,3},{19,4},{12,5},{5,6},{29,7},{22,8},{15,9}... | collective-permute-start | bytes 196616 | tf_op jit(solution)/shard_map/ppermute | solution.py:473
  307.9 7.1 %collective-permute-start.84 = (bf16[32,1024]{1,0:T(8,128)(2,1)S(1)}, bf16[32,1024]{1,0:T(8,128)(2,1)S(1)}, u32[]{:S(2)}, u32[]{:S(2)}) collective-permute-start(bf16[32,1024]{1,0:T(8,128)(2,1)S(1)} %get-tuple-element.200), channel_id=1, source_target_pairs={{0,0},{8,1},{16,2},{24,3},{1,4},{9,5},{17,6},{25,7},{2,8},{10,9},{... | collective-permute-start | bytes 196616 | tf_op jit(solution)/shard_map/ppermute | solution.py:471
  309.9 14.4 %collective-permute-start.82 = (bf16[32,1024]{1,0:T(8,128)(2,1)S(1)}, bf16[32,1024]{1,0:T(8,128)(2,1)S(1)}, u32[]{:S(2)}, u32[]{:S(2)}) collective-permute-start(bf16[32,1024]{1,0:T(8,128)(2,1)S(1)} %get-tuple-element.202), channel_id=1, source_target_pairs={{8,0},{1,1},{25,2},{18,3},{11,4},{4,5},{28,6},{21,7},{14,8},{7,9},... | collective-permute-start | bytes 196616 | tf_op jit(solution)/shard_map/ppermute | solution.py:473
  315.0 9.4 %collective-permute-start.81 = (bf16[32,1024]{1,0:T(8,128)(2,1)S(1)}, bf16[32,1024]{1,0:T(8,128)(2,1)S(1)}, u32[]{:S(2)}, u32[]{:S(2)}) collective-permute-start(bf16[32,1024]{1,0:T(8,128)(2,1)S(1)} %get-tuple-element.201), channel_id=1, source_target_pairs={{0,0},{24,1},{17,2},{10,3},{3,4},{27,5},{20,6},{13,7},{6,8},{30,9}... | collective-permute-start | bytes 196616 | tf_op jit(solution)/shard_map/ppermute | solution.py:473
  322.4 8.4 %collective-permute-start.86 = (bf16[128,1024]{1,0:T(8,128)(2,1)S(1)}, bf16[128,1024]{1,0:T(8,128)(2,1)S(1)}, u32[]{:S(2)}, u32[]{:S(2)}) collective-permute-start(bf16[128,1024]{1,0:T(8,128)(2,1)S(1)} %fusion.38), channel_id=1, source_target_pairs={{0,0},{16,1},{1,2},{17,3},{2,4},{18,5},{3,6},{19,7},{4,8},{20,9},{... | collective-permute-start | bytes 786440 | tf_op jit(solution)/shard_map/ppermute | solution.py:454
  (66 other events, 534.9 us)

commit v8 on v7

--- a/solution.py
+++ b/solution.py
@@ -147,31 +147,30 @@
                 first_ref[pl.ds(at, tok), :] = first[here]
                 mixed_ref[pl.ds(at, tok), :] = mixed[here]
 
-    att_ref[...] = jnp.zeros_like(att_ref)
     lanes = lax.broadcasted_iota(jnp.int32, (BLOCK, PAIR_DIM), 1)
     for begin, end, width in spans(rows_q, rows_k):
 
-        @pl.loop(0, 2 * (end - begin) // BLOCK)
+        @pl.loop(0, (end - begin) // BLOCK)
         def _(step, begin=begin, width=width):
-            start = pl.multiple_of(begin + (step // 2) * BLOCK, BLOCK)
+            start = pl.multiple_of(begin + step * BLOCK, BLOCK)
             at = pl.multiple_of(first_query + start, BLOCK)
-            mine = (lanes // HEAD_DIM) == step % 2
-            query = mixed_ref[pl.ds(at, BLOCK), 0:PAIR_DIM]
+            query = mixed_ref[pl.ds(at, BLOCK), 0:PAIR_DIM] * SCALE
             keys = mixed_ref[0:width, PAIR_DIM : 2 * PAIR_DIM]
             values = mixed_ref[0:width, 2 * PAIR_DIM :]
             free = begin if rows_q == rows_k else 0
             key_pos = free + lax.broadcasted_iota(jnp.int32, (BLOCK, width - free), 1)
             query_pos = at + lax.broadcasted_iota(jnp.int32, (BLOCK, width - free), 0)
             allowed = (key_pos <= query_pos) | (key_pos < prefix_len)
-            scores = nt(jnp.where(mine, query * SCALE, jnp.zeros_like(query)), keys)
-            masked = jnp.where(allowed, scores[:, free:], NEG)
-            scores = jnp.concatenate([scores[:, :free], masked], 1) if free else masked
-            top = jnp.max(scores, axis=-1, keepdims=True)
-            weights = jnp.exp(scores - top)
-            total = jnp.sum(weights, axis=-1, keepdims=True)
-            probs = (weights * (1.0 / total)).astype(BF16)
-            before = att_ref[pl.ds(start, BLOCK), :]
-            att_ref[pl.ds(start, BLOCK), :] = jnp.where(mine, nn(probs, values).astype(BF16), before)
+            outs = []
+            for head in range(2):
+                scores = nt(jnp.where((lanes // HEAD_DIM) == head, query, jnp.zeros_like(query)), keys)
+                masked = jnp.where(allowed, scores[:, free:], NEG)
+                scores = jnp.concatenate([scores[:, :free], masked], 1) if free else masked
+                weights = jnp.exp(scores - jnp.max(scores, axis=-1, keepdims=True))
+                total = jnp.sum(weights, axis=-1, keepdims=True)
+                outs.append(nn((weights * (1.0 / total)).astype(BF16), values))
+            att_ref[pl.ds(start, BLOCK), :] = jnp.where(lanes < HEAD_DIM, outs[0], outs[1]).astype(BF16)
+
     for slot in range(8):
         here = slice(slot * tok, (slot + 1) * tok)
         keep_ref[here, :] = att_ref[pl.ds(place(micro, member, 0, slot, tok), tok), :]

time: 336 us -> 340 us (1.012)
  the two profiles are of different devices: /device:TPU:2 before, /device:TPU:6 now
where the time goes in v8:
time: 340 us; the launch traced here: 335 us
  waiting for transfers between devices  142 us (42%)
  starting transfers between devices  96.9 us (28%)
  other arithmetic  33.2 us (10%)
  Pallas kernels  21.3 us (6%)
  local copies, waits for them, and re-layouts  19.4 us (6%)
  matrix products  17.8 us (5%)
  between operations  4.39 us (1%)
    ppermute x67, waiting for transfers between devices, swap_seq(): return lax.ppermute(value, 'seq', [(i, i ^ bits) for i in range(n_seq)])  122 us
    ppermute x67, starting transfers between devices, swap_seq(): return lax.ppermute(value, 'seq', [(i, i ^ bits) for i in range(n_seq)])  50.6 us
    ppermute x10, starting transfers between devices, swap_dp(): return lax.ppermute(value, 'dp', [(0, 1), (1, 0)])  13.7 us
    pallas_call x1, Pallas kernels, attend_back(): pl.pallas_call(attend_back_kernel, out_shape=(jax.ShapeDtypeStruct((rows_...  11.3 us
    ppermute x3, starting transfers between devices, shards(): lax.ppermute(jnp.where(thirds[t] == 0, terms[0], jnp.where(thirds[t] == 1...  11 us
    ppermute x3, starting transfers between devices, shards(): lax.ppermute(own_units[t], BOTH, [(i, home(3 * i + t)) for i in range(n_d...  10.2 us
    pallas_call x1, Pallas kernels, attend(): pl.pallas_call(attend_kernel, out_shape=(jax.ShapeDtypeStruct((rows_k, wi...  9.96 us
    ppermute x10, waiting for transfers between devices, swap_dp(): return lax.ppermute(value, 'dp', [(0, 1), (1, 0)])  8.44 us
  transfers between devices with their start and end apart: 87, of which 48 were waited for; matrix products, arithmetic and copies ran while one was open for 14% of the time, Pallas kernels for 6%

profile of v8, /device:TPU:6, one launch (start us, length us, event | category | flops | bytes accessed | tf_op | source)
XLA Modules:
  0.0 335.3 jit_solution(7302878626144552508)
XLA Ops:
  0.7 1.8 fusion.33
  2.5 2.7 collective-permute-start
  6.1 2.6 collective-permute-start.1
  8.7 1.9 collective-permute-start.2
  10.6 5.7 %collective-permute-start.3 = (bf16[32,1024]{1,0:T(8,128)(2,1)S(1)}, bf16[32,1024]{1,0:T(8,128)(2,1)S(1)}, u32[]{:S(2)}, u32[]{:S(2)}) collective-permute-start(bf16[32,1024]{1,0:T(8,128)(2,1)S(1)} %get-tuple-element.215), channel_id=1, source_target_pairs={{0,16},{1,9},{2,2},{3,26},{4,19},{5,12},{6,5},{7,29},{8,22},{9,15}... | collective-permute-start | bytes 196616 | tf_op jit(solution)/shard_map/ppermute | solution.py:319
  16.3 1.9 collective-permute-start.4
  19.2 5.3 %collective-permute-done.4 = bf16[32,1024]{1,0:T(8,128)(2,1)S(1)} collective-permute-done((bf16[32,1024]{1,0:T(8,128)(2,1)}, bf16[32,1024]{1,0:T(8,128)(2,1)S(1)}, u32[]{:S(2)}, u32[]{:S(2)}) %collective-permute-start.4) | collective-permute-done | bytes 65568 | tf_op jit(solution)/shard_map/ppermute | solution.py:320
  24.6 3.6 %collective-permute-start.18 = (bf16[128,1024]{1,0:T(8,128)(2,1)}, bf16[128,1024]{1,0:T(8,128)(2,1)}, u32[]{:S(2)}, u32[]{:S(2)}) collective-permute-start(bf16[128,1024]{1,0:T(8,128)(2,1)} %param.22), channel_id=1, source_target_pairs={{0,0},{1,16},{2,1},{3,17},{4,2},{5,18},{6,3},{7,19},{8,4},{9,20},{... | collective-permute-start | bytes 786440 | tf_op jit(solution)/shard_map/ppermute | solution.py:318
  30.5 1.7 collective-permute-start.13
  32.2 9.5 %collective-permute-done.6.refs_2_ = bf16[128,1024]{1,0:T(8,128)(2,1)} collective-permute-done((bf16[128,1024]{1,0:T(8,128)(2,1)S(1)}, bf16[128,1024]{1,0:T(8,128)(2,1)}, u32[]{:S(2)}, u32[]{:S(2)}) %collective-permute-start.6) | collective-permute-done | bytes 262176 | tf_op jit(solution)/shard_map/ppermute | solution.py:45
  42.6 1.6 collective-permute-start.7
  47.6 5.0 %collective-permute-start.15 = (bf16[4,32,1024]{2,1,0:T(8,128)(2,1)S(1)}, bf16[4,32,1024]{2,1,0:T(8,128)(2,1)S(1)}, u32[]{:S(2)}, u32[]{:S(2)}) collective-permute-start(bf16[4,32,1024]{2,1,0:T(8,128)(2,1)S(1)} %collective-permute-done.13), channel_id=1, source_target_pairs={{0,16},{16,0},{1,17},{17,1},{2,18},{18,2},{3,19},{19,3},{4,20},{20... | collective-permute-start | bytes 786440 | tf_op jit(solution)/shard_map/ppermute | solution.py:49
  55.2 3.8 %collective-permute-done.15 = bf16[4,32,1024]{2,1,0:T(8,128)(2,1)S(1)} collective-permute-done((bf16[4,32,1024]{2,1,0:T(8,128)(2,1)S(1)}, bf16[4,32,1024]{2,1,0:T(8,128)(2,1)S(1)}, u32[]{:S(2)}, u32[]{:S(2)}) %collective-permute-start.15) | collective-permute-done | bytes 262176 | tf_op jit(solution)/shard_map/ppermute | solution.py:49
  61.1 3.1 collective-permute-start.16
  66.4 10.0 %shard_map.152 = (bf16[1024,1024]{1,0:T(8,128)(2,1)}, bf16[1024,384]{1,0:T(8,128)(2,1)}, bf16[512,128]{1,0:T(8,128)(2,1)}, bf16[512,128]{1,0:T(8,128)(2,1)}) custom-call(s32[4]{0:T(128)} %pad_add_fusion.where_ref, bf16[128,1024]{1,0:T(8,128)(2,1)} %copy-done.18, bf16[128,1024]{1,0:T(8,128)(2,1)} %collective-permute-done.5.refs_1_, ...), custom_call_target="tpu_custom_call" | custom-call | flops 1342177280 | bytes 4194304 | tf_op jit(solution)/shard_map/pallas_call | solution.py:183
  76.8 13.0 %collective-permute-done.16 = bf16[256,1024]{1,0:T(8,128)(2,1)S(1)} collective-permute-done((bf16[256,1024]{1,0:T(8,128)(2,1)S(1)}, bf16[256,1024]{1,0:T(8,128)(2,1)S(1)}, u32[]{:S(2)}, u32[]{:S(2)}) %collective-permute-start.16) | collective-permute-done | bytes 524320 | tf_op jit(solution)/shard_map/ppermute | solution.py:45
  89.8 2.3 collective-permute-done.19
  93.5 2.6 collective-permute-done.20
  97.4 3.1 collective-permute-start.35
  100.5 3.4 %collective-permute-done.21 = bf16[64,1024]{1,0:T(8,128)(2,1)S(1)} collective-permute-done((bf16[64,1024]{1,0:T(8,128)(2,1)S(1)}, bf16[64,1024]{1,0:T(8,128)(2,1)S(1)}, u32[]{:S(2)}, u32[]{:S(2)}) %collective-permute-start.21) | collective-permute-done | bytes 131104 | tf_op jit(solution)/shard_map/ppermute | solution.py:45
  106.1 6.5 %collective-permute-done.35 = bf16[128,1024]{1,0:T(8,128)(2,1)S(1)} collective-permute-done((bf16[128,1024]{1,0:T(8,128)(2,1)}, bf16[128,1024]{1,0:T(8,128)(2,1)S(1)}, u32[]{:S(2)}, u32[]{:S(2)}) %collective-permute-start.35) | collective-permute-done | bytes 262176 | tf_op jit(solution)/shard_map/ppermute | solution.py:45
  113.6 1.5 collective-permute-done.24
  118.4 3.4 %collective-permute-done.36 = bf16[128,1024]{1,0:T(8,128)(2,1)S(1)} collective-permute-done((bf16[128,1024]{1,0:T(8,128)(2,1)S(1)}, bf16[128,1024]{1,0:T(8,128)(2,1)S(1)}, u32[]{:S(2)}, u32[]{:S(2)}) %collective-permute-start.36) | collective-permute-done | bytes 262176 | tf_op jit(solution)/shard_map/ppermute | solution.py:49
  124.1 3.9 %collective-permute-done.27 = bf16[64,1024]{1,0:T(8,128)(2,1)S(1)} collective-permute-done((bf16[64,1024]{1,0:T(8,128)(2,1)S(1)}, bf16[64,1024]{1,0:T(8,128)(2,1)S(1)}, u32[]{:S(2)}, u32[]{:S(2)}) %collective-permute-start.27) | collective-permute-done | bytes 131104 | tf_op jit(solution)/shard_map/ppermute | solution.py:45
  131.0 2.4 fusion.60
  136.2 2.6 collective-permute-done.37
  142.1 4.1 %collective-permute-done.38 = bf16[64,1024]{1,0:T(8,128)(2,1)} collective-permute-done((bf16[64,1024]{1,0:T(8,128)(2,1)}, bf16[64,1024]{1,0:T(8,128)(2,1)}, u32[]{:S(2)}, u32[]{:S(2)}) %collective-permute-start.38) | collective-permute-done | bytes 131104 | tf_op jit(solution)/shard_map/ppermute | solution.py:45
  148.0 1.7 collective-permute-start.41
  155.8 1.8 collective-permute-done.39
  160.6 4.6 %collective-permute-done.43 = bf16[128,1024]{1,0:T(8,128)(2,1)S(1)} collective-permute-done((bf16[128,1024]{1,0:T(8,128)(2,1)S(1)}, bf16[128,1024]{1,0:T(8,128)(2,1)S(1)}, u32[]{:S(2)}, u32[]{:S(2)}) %collective-permute-start.43) | collective-permute-done | bytes 262176 | tf_op jit(solution)/shard_map/ppermute | solution.py:45
  166.9 1.8 collective-permute-start.45
  170.2 1.7 collective-permute-done.45
  173.7 2.1 multiply_convert_fusion
  178.3 1.4 copy-done.21
  179.7 2.3 fusion.78
  183.4 1.8 collective-permute-start.51
  189.3 1.4 collective-permute-done.53
  193.8 4.5 %collective-permute-done.54 = bf16[128,1024]{1,0:T(8,128)(2,1)S(1)} collective-permute-done((bf16[128,1024]{1,0:T(8,128)(2,1)S(1)}, bf16[128,1024]{1,0:T(8,128)(2,1)S(1)}, u32[]{:S(2)}, u32[]{:S(2)}) %collective-permute-start.54) | collective-permute-done | bytes 262176 | tf_op jit(solution)/shard_map/ppermute | solution.py:45
  201.2 1.4 collective-permute-start.56
  202.6 1.7 slice_select_fusion
  204.4 3.2 collective-permute-done.56
  208.5 1.5 collective-permute-start.58
  210.1 2.5 collective-permute-done.57
  216.6 2.4 collective-permute-start.63
  220.9 5.0 %collective-permute-done.63.got_ref = bf16[512,128]{1,0:T(8,128)(2,1)S(1)} collective-permute-done((bf16[512,128]{1,0:T(8,128)(2,1)S(1)}, bf16[512,128]{1,0:T(8,128)(2,1)S(1)}, u32[]{:S(2)}, u32[]{:S(2)}) %collective-permute-start.63) | collective-permute-done | bytes 131104 | tf_op jit(solution)/shard_map/ppermute | solution.py:45
  226.5 2.2 add_bitcast_fusion
  232.2 11.3 %shard_map.153 = (bf16[1024,384]{1,0:T(8,128)(2,1)}, bf16[512,384]{1,0:T(8,128)(2,1)}, bf16[512,384]{1,0:T(8,128)(2,1)}) custom-call(s32[4]{0:T(128)} %pad_add_fusion.where_ref, bf16[1024,384]{1,0:T(8,128)(2,1)} %get-tuple-element.120.mixed_ref, bf16[512,128]{1,0:T(8,128)(2,1)} %bitcast.239, bf16[512,128]{1,0:T(8,128)(2,1)} %copy-done.42), custom_call_target="tpu_custom_call" | custom-call | flops 1342177280 | bytes 4194304 | tf_op jit(solution)/shard_map/pallas_call | solution.py:264
  243.5 10.2 %collective-permute-done.65 = bf16[1,224,1024]{2,1,0:T(8,128)(2,1)} collective-permute-done((bf16[1,224,1024]{2,1,0:T(8,128)(2,1)}, bf16[1,224,1024]{2,1,0:T(8,128)(2,1)}, u32[]{:S(2)}, u32[]{:S(2)}) %collective-permute-start.65) | collective-permute-done | bytes 458784 | tf_op jit(solution)/shard_map/ppermute | solution.py:45
  253.7 2.1 multiply_reduce_fusion
  262.1 2.7 collective-permute-done.69
  266.6 4.9 %collective-permute-done.70 = f32[3,1024]{1,0:T(4,128)S(1)} collective-permute-done((f32[3,1024]{1,0:T(4,128)S(1)}, f32[3,1024]{1,0:T(4,128)S(1)}, u32[]{:S(2)}, u32[]{:S(2)}) %collective-permute-start.70) | collective-permute-done | bytes 12320 | tf_op jit(solution)/shard_map/ppermute | solution.py:45
  271.5 4.6 %collective-permute-done.72 = bf16[512,384]{1,0:T(8,128)(2,1)} collective-permute-done((bf16[512,384]{1,0:T(8,128)(2,1)}, bf16[512,384]{1,0:T(8,128)(2,1)}, u32[]{:S(2)}, u32[]{:S(2)}) %collective-permute-start.72) | collective-permute-done | bytes 393248 | tf_op jit(solution)/shard_map/ppermute | solution.py:45
  278.3 1.4 fusion.8
  279.8 2.8 collective-permute-start.80
  286.9 2.2 collective-permute-start.85
  291.4 2.9 collective-permute-done.77
  296.1 6.1 %collective-permute-done.80 = bf16[4,1,32,1024]{3,2,1,0:T(8,128)(2,1)S(1)} collective-permute-done((bf16[4,1,32,1024]{3,2,1,0:T(8,128)(2,1)S(1)}, bf16[4,1,32,1024]{3,2,1,0:T(8,128)(2,1)S(1)}, u32[]{:S(2)}, u32[]{:S(2)}) %collective-permute-start.80) | collective-permute-done | bytes 262176 | tf_op jit(solution)/shard_map/ppermute | solution.py:45
  302.3 1.9 collective-permute-start.83
  304.3 3.5 %collective-permute-done.85 = bf16[1,128,1024]{2,1,0:T(8,128)(2,1)S(1)} collective-permute-done((bf16[1,128,1024]{2,1,0:T(8,128)(2,1)S(1)}, bf16[1,128,1024]{2,1,0:T(8,128)(2,1)S(1)}, u32[]{:S(2)}, u32[]{:S(2)}) %collective-permute-start.85) | collective-permute-done | bytes 262176 | tf_op jit(solution)/shard_map/ppermute | solution.py:45
  307.7 1.9 collective-permute-start.84
  309.7 4.6 %collective-permute-start.82 = (bf16[32,1024]{1,0:T(8,128)(2,1)S(1)}, bf16[32,1024]{1,0:T(8,128)(2,1)S(1)}, u32[]{:S(2)}, u32[]{:S(2)}) collective-permute-start(bf16[32,1024]{1,0:T(8,128)(2,1)S(1)} %get-tuple-element.202), channel_id=1, source_target_pairs={{8,0},{1,1},{25,2},{18,3},{11,4},{4,5},{28,6},{21,7},{14,8},{7,9},... | collective-permute-start | bytes 196616 | tf_op jit(solution)/shard_map/ppermute | solution.py:472
  315.6 4.5 %collective-permute-start.81 = (bf16[32,1024]{1,0:T(8,128)(2,1)S(1)}, bf16[32,1024]{1,0:T(8,128)(2,1)S(1)}, u32[]{:S(2)}, u32[]{:S(2)}) collective-permute-start(bf16[32,1024]{1,0:T(8,128)(2,1)S(1)} %get-tuple-element.201), channel_id=1, source_target_pairs={{0,0},{24,1},{17,2},{10,3},{3,4},{27,5},{20,6},{13,7},{6,8},{30,9}... | collective-permute-start | bytes 196616 | tf_op jit(solution)/shard_map/ppermute | solution.py:472
  321.9 3.9 %collective-permute-start.86 = (bf16[128,1024]{1,0:T(8,128)(2,1)S(1)}, bf16[128,1024]{1,0:T(8,128)(2,1)S(1)}, u32[]{:S(2)}, u32[]{:S(2)}) collective-permute-start(bf16[128,1024]{1,0:T(8,128)(2,1)S(1)} %fusion.38), channel_id=1, source_target_pairs={{0,0},{16,1},{1,2},{17,3},{2,4},{18,5},{3,6},{19,7},{4,8},{20,9},{... | collective-permute-start | bytes 786440 | tf_op jit(solution)/shard_map/ppermute | solution.py:453
  329.1 5.2 %collective-permute-done.86 = bf16[128,1024]{1,0:T(8,128)(2,1)S(1)} collective-permute-done((bf16[128,1024]{1,0:T(8,128)(2,1)S(1)}, bf16[128,1024]{1,0:T(8,128)(2,1)S(1)}, u32[]{:S(2)}, u32[]{:S(2)}) %collective-permute-start.86) | collective-permute-done | bytes 262176 | tf_op jit(solution)/shard_map/ppermute | solution.py:453
  (351 shorter events, 99.9 us)
Async XLA Ops:
  2.5 15.7 %collective-permute-start = (bf16[64,1024]{1,0:T(8,128)(2,1)S(1)}, bf16[64,1024]{1,0:T(8,128)(2,1)S(1)}, u32[]{:S(2)}, u32[]{:S(2)}) collective-permute-start(bf16[64,1024]{1,0:T(8,128)(2,1)S(1)} %get-tuple-element.211), channel_id=1, source_target_pairs={{0,8},{1,9},{2,10},{3,11},{4,12},{5,13},{6,14},{7,15},{8,0},{9,1},... | collective-permute-start | bytes 393224 | tf_op jit(solution)/shard_map/ppermute | solution.py:45
  6.1 12.2 %collective-permute-start.1 = (bf16[32,1024]{1,0:T(8,128)(2,1)S(1)}, bf16[32,1024]{1,0:T(8,128)(2,1)S(1)}, u32[]{:S(2)}, u32[]{:S(2)}) collective-permute-start(bf16[32,1024]{1,0:T(8,128)(2,1)S(1)} %get-tuple-element.216), channel_id=1, source_target_pairs={{0,0},{1,24},{2,17},{3,10},{4,3},{5,27},{6,20},{7,13},{8,6},{9,30}... | collective-permute-start | bytes 196616 | tf_op jit(solution)/shard_map/ppermute | solution.py:319
  8.7 9.6 %collective-permute-start.2 = (bf16[32,1024]{1,0:T(8,128)(2,1)S(1)}, bf16[32,1024]{1,0:T(8,128)(2,1)S(1)}, u32[]{:S(2)}, u32[]{:S(2)}) collective-permute-start(bf16[32,1024]{1,0:T(8,128)(2,1)S(1)} %get-tuple-element.217), channel_id=1, source_target_pairs={{0,8},{1,1},{2,25},{3,18},{4,11},{5,4},{6,28},{7,21},{8,14},{9,7},... | collective-permute-start | bytes 196616 | tf_op jit(solution)/shard_map/ppermute | solution.py:319
  10.6 8.6 %collective-permute-start.3 = (bf16[32,1024]{1,0:T(8,128)(2,1)S(1)}, bf16[32,1024]{1,0:T(8,128)(2,1)S(1)}, u32[]{:S(2)}, u32[]{:S(2)}) collective-permute-start(bf16[32,1024]{1,0:T(8,128)(2,1)S(1)} %get-tuple-element.215), channel_id=1, source_target_pairs={{0,16},{1,9},{2,2},{3,26},{4,19},{5,12},{6,5},{7,29},{8,22},{9,15}... | collective-permute-start | bytes 196616 | tf_op jit(solution)/shard_map/ppermute | solution.py:319
  16.3 8.3 %collective-permute-start.4 = (bf16[32,1024]{1,0:T(8,128)(2,1)}, bf16[32,1024]{1,0:T(8,128)(2,1)S(1)}, u32[]{:S(2)}, u32[]{:S(2)}) collective-permute-start(bf16[32,1024]{1,0:T(8,128)(2,1)} %param.20), channel_id=1, source_target_pairs={{0,0},{1,8},{2,16},{3,24},{4,1},{5,9},{6,17},{7,25},{8,2},{9,10},{... | collective-permute-start | bytes 196616 | tf_op jit(solution)/shard_map/ppermute | solution.py:320
  24.6 52.3 %collective-permute-start.18 = (bf16[128,1024]{1,0:T(8,128)(2,1)}, bf16[128,1024]{1,0:T(8,128)(2,1)}, u32[]{:S(2)}, u32[]{:S(2)}) collective-permute-start(bf16[128,1024]{1,0:T(8,128)(2,1)} %param.22), channel_id=1, source_target_pairs={{0,0},{1,16},{2,1},{3,17},{4,2},{5,18},{6,3},{7,19},{8,4},{9,20},{... | collective-permute-start | bytes 786440 | tf_op jit(solution)/shard_map/ppermute | solution.py:318
  28.8 15.4 %collective-permute-start.5 = (bf16[128,1024]{1,0:T(8,128)(2,1)S(1)}, bf16[128,1024]{1,0:T(8,128)(2,1)}, u32[]{:S(2)}, u32[]{:S(2)}) collective-permute-start(bf16[128,1024]{1,0:T(8,128)(2,1)S(1)} %pad_maximum_fusion.12.refs_0_), channel_id=1, source_target_pairs={{0,2},{1,3},{2,0},{3,1},{4,6},{5,7},{6,4},{7,5},{8,10},{9,11},{10,... | collective-permute-start | bytes 786440 | tf_op jit(solution)/shard_map/ppermute | solution.py:45
  29.3 12.4 %collective-permute-start.6 = (bf16[128,1024]{1,0:T(8,128)(2,1)S(1)}, bf16[128,1024]{1,0:T(8,128)(2,1)}, u32[]{:S(2)}, u32[]{:S(2)}) collective-permute-start(bf16[128,1024]{1,0:T(8,128)(2,1)S(1)} %pad_maximum_fusion.12.refs_0_), channel_id=1, source_target_pairs={{0,4},{1,5},{2,6},{3,7},{4,0},{5,1},{6,2},{7,3},{8,12},{9,13},{10,... | collective-permute-start | bytes 786440 | tf_op jit(solution)/shard_map/ppermute | solution.py:45
  30.5 17.2 %collective-permute-start.13 = (bf16[4,32,1024]{2,1,0:T(8,128)(2,1)S(1)}, bf16[4,32,1024]{2,1,0:T(8,128)(2,1)S(1)}, u32[]{:S(2)}, u32[]{:S(2)}) collective-permute-start(bf16[4,32,1024]{2,1,0:T(8,128)(2,1)S(1)} %get-tuple-element.209), channel_id=1, source_target_pairs={{0,8},{1,9},{2,10},{3,11},{4,12},{5,13},{6,14},{7,15},{8,0},{9,1},... | collective-permute-start | bytes 786440 | tf_op jit(solution)/shard_map/ppermute | solution.py:45
  45.1 8.2 %collective-permute-start.8 = (bf16[64,1024]{1,0:T(8,128)(2,1)S(1)}, bf16[64,1024]{1,0:T(8,128)(2,1)S(1)}, u32[]{:S(2)}, u32[]{:S(2)}) collective-permute-start(bf16[64,1024]{1,0:T(8,128)(2,1)S(1)} %slice.438), channel_id=1, source_target_pairs={{0,4},{1,5},{2,6},{3,7},{4,0},{5,1},{6,2},{7,3},{8,12},{9,13},{10,... | collective-permute-start | bytes 393224 | tf_op jit(solution)/shard_map/ppermute | solution.py:45
  47.0 7.7 %collective-permute-start.14 = (bf16[4,32,1024]{2,1,0:T(8,128)(2,1)S(1)}, bf16[4,32,1024]{2,1,0:T(8,128)(2,1)S(1)}, u32[]{:S(2)}, u32[]{:S(2)}) collective-permute-start(bf16[4,32,1024]{2,1,0:T(8,128)(2,1)S(1)} %get-tuple-element.209), channel_id=1, source_target_pairs={{0,16},{16,0},{1,17},{17,1},{2,18},{18,2},{3,19},{19,3},{4,20},{20... | collective-permute-start | bytes 786440 | tf_op jit(solution)/shard_map/ppermute | solution.py:49
  47.6 13.4 %collective-permute-start.10 = (bf16[128,1024]{1,0:T(8,128)(2,1)}, bf16[128,1024]{1,0:T(8,128)(2,1)}, u32[]{:S(2)}, u32[]{:S(2)}) collective-permute-start(bf16[128,1024]{1,0:T(8,128)(2,1)} %collective-permute-done.5.refs_1_), channel_id=1, source_target_pairs={{0,1},{1,0},{2,3},{3,2},{4,5},{5,4},{6,7},{7,6},{8,9},{9,8},{10,11... | collective-permute-start | bytes 786440 | tf_op jit(solution)/shard_map/ppermute | solution.py:45
  47.6 11.4 %collective-permute-start.15 = (bf16[4,32,1024]{2,1,0:T(8,128)(2,1)S(1)}, bf16[4,32,1024]{2,1,0:T(8,128)(2,1)S(1)}, u32[]{:S(2)}, u32[]{:S(2)}) collective-permute-start(bf16[4,32,1024]{2,1,0:T(8,128)(2,1)S(1)} %collective-permute-done.13), channel_id=1, source_target_pairs={{0,16},{16,0},{1,17},{17,1},{2,18},{18,2},{3,19},{19,3},{4,20},{20... | collective-permute-start | bytes 786440 | tf_op jit(solution)/shard_map/ppermute | solution.py:49
  53.3 7.7 %collective-permute-start.11 = (bf16[128,1024]{1,0:T(8,128)(2,1)}, bf16[128,1024]{1,0:T(8,128)(2,1)}, u32[]{:S(2)}, u32[]{:S(2)}) collective-permute-start(bf16[128,1024]{1,0:T(8,128)(2,1)} %collective-permute-done.6.refs_2_), channel_id=1, source_target_pairs={{0,1},{1,0},{2,3},{3,2},{4,5},{5,4},{6,7},{7,6},{8,9},{9,8},{10,11... | collective-permute-start | bytes 786440 | tf_op jit(solution)/shard_map/ppermute | solution.py:45
  54.7 6.4 %collective-permute-start.12 = (bf16[128,1024]{1,0:T(8,128)(2,1)}, bf16[128,1024]{1,0:T(8,128)(2,1)S(1)}, u32[]{:S(2)}, u32[]{:S(2)}) collective-permute-start(bf16[128,1024]{1,0:T(8,128)(2,1)} %constant_dynamic-update-slice_fusion.refs_3_), channel_id=1, source_target_pairs={{0,1},{1,0},{2,3},{3,2},{4,5},{5,4},{6,7},{7,6},{8,9},{9,8},{10,11... | collective-permute-start | bytes 786440 | tf_op jit(solution)/shard_map/ppermute | solution.py:45
  61.1 28.7 %collective-permute-start.16 = (bf16[256,1024]{1,0:T(8,128)(2,1)S(1)}, bf16[256,1024]{1,0:T(8,128)(2,1)S(1)}, u32[]{:S(2)}, u32[]{:S(2)}) collective-permute-start(bf16[256,1024]{1,0:T(8,128)(2,1)S(1)} %copy-done.32), channel_id=1, source_target_pairs={{0,8},{1,9},{2,10},{3,11},{4,12},{5,13},{6,14},{7,15},{8,0},{9,1},... | collective-permute-start | bytes 1572872 | tf_op jit(solution)/shard_map/ppermute | solution.py:45
  64.2 25.6 %collective-permute-start.17 = (bf16[256,1024]{1,0:T(8,128)(2,1)S(1)}, bf16[256,1024]{1,0:T(8,128)(2,1)S(1)}, u32[]{:S(2)}, u32[]{:S(2)}) collective-permute-start(bf16[256,1024]{1,0:T(8,128)(2,1)S(1)} %copy-done.32), channel_id=1, source_target_pairs={{0,16},{16,0},{1,17},{17,1},{2,18},{18,2},{3,19},{19,3},{4,20},{20... | collective-permute-start | bytes 1572872 | tf_op jit(solution)/shard_map/ppermute | solution.py:49
  76.3 15.7 %collective-permute-start.19 = (bf16[512,128]{1,0:T(8,128)(2,1)}, bf16[512,128]{1,0:T(8,128)(2,1)S(1)}, u32[]{:S(2)}, u32[]{:S(2)}) collective-permute-start(bf16[512,128]{1,0:T(8,128)(2,1)} %get-tuple-element.112), channel_id=1, source_target_pairs={{0,8},{1,9},{2,10},{3,11},{4,12},{5,13},{6,14},{7,15},{8,0},{9,1},... | collective-permute-start | bytes 393224 | tf_op jit(solution)/shard_map/ppermute | solution.py:45
  96.6 7.3 %collective-permute-start.21 = (bf16[64,1024]{1,0:T(8,128)(2,1)S(1)}, bf16[64,1024]{1,0:T(8,128)(2,1)S(1)}, u32[]{:S(2)}, u32[]{:S(2)}) collective-permute-start(bf16[64,1024]{1,0:T(8,128)(2,1)S(1)} %get-tuple-element.194), channel_id=1, source_target_pairs={{0,4},{1,5},{2,6},{3,7},{4,0},{5,1},{6,2},{7,3},{8,12},{9,13},{10,... | collective-permute-start | bytes 393224 | tf_op jit(solution)/shard_map/ppermute | solution.py:45
  96.7 7.3 %collective-permute-start.23 = (bf16[64,1024]{1,0:T(8,128)(2,1)S(1)}, bf16[64,1024]{1,0:T(8,128)(2,1)S(1)}, u32[]{:S(2)}, u32[]{:S(2)}) collective-permute-start(bf16[64,1024]{1,0:T(8,128)(2,1)S(1)} %get-tuple-element.193), channel_id=1, source_target_pairs={{0,2},{1,3},{2,0},{3,1},{4,6},{5,7},{6,4},{7,5},{8,10},{9,11},{10,... | collective-permute-start | bytes 393224 | tf_op jit(solution)/shard_map/ppermute | solution.py:45
  97.4 15.1 %collective-permute-start.35 = (bf16[128,1024]{1,0:T(8,128)(2,1)}, bf16[128,1024]{1,0:T(8,128)(2,1)S(1)}, u32[]{:S(2)}, u32[]{:S(2)}) collective-permute-start(bf16[128,1024]{1,0:T(8,128)(2,1)} %collective-permute-done.18), channel_id=1, source_target_pairs={{0,8},{1,9},{2,10},{3,11},{4,12},{5,13},{6,14},{7,15},{8,0},{9,1},... | collective-permute-start | bytes 786440 | tf_op jit(solution)/shard_map/ppermute | solution.py:45
  104.0 11.1 %collective-permute-start.24 = (bf16[128,1024]{1,0:T(8,128)(2,1)S(1)}, bf16[128,1024]{1,0:T(8,128)(2,1)S(1)}, u32[]{:S(2)}, u32[]{:S(2)}) collective-permute-start(bf16[128,1024]{1,0:T(8,128)(2,1)S(1)} %pad_maximum_fusion.15), channel_id=1, source_target_pairs={{0,4},{1,5},{2,6},{3,7},{4,0},{5,1},{6,2},{7,3},{8,12},{9,13},{10,... | collective-permute-start | bytes 786440 | tf_op jit(solution)/shard_map/ppermute | solution.py:45
  104.1 11.0 %collective-permute-start.22 = (bf16[128,1024]{1,0:T(8,128)(2,1)S(1)}, bf16[128,1024]{1,0:T(8,128)(2,1)S(1)}, u32[]{:S(2)}, u32[]{:S(2)}) collective-permute-start(bf16[128,1024]{1,0:T(8,128)(2,1)S(1)} %pad_maximum_fusion.14), channel_id=1, source_target_pairs={{0,2},{1,3},{2,0},{3,1},{4,6},{5,7},{6,4},{7,5},{8,10},{9,11},{10,... | collective-permute-start | bytes 786440 | tf_op jit(solution)/shard_map/ppermute | solution.py:45
  104.9 12.3 %collective-permute-start.34 = (bf16[128,1024]{1,0:T(8,128)(2,1)}, bf16[128,1024]{1,0:T(8,128)(2,1)S(1)}, u32[]{:S(2)}, u32[]{:S(2)}) collective-permute-start(bf16[128,1024]{1,0:T(8,128)(2,1)} %collective-permute-done.18), channel_id=1, source_target_pairs={{0,16},{16,0},{1,17},{17,1},{2,18},{18,2},{3,19},{19,3},{4,20},{20... | collective-permute-start | bytes 786440 | tf_op jit(solution)/shard_map/ppermute | solution.py:49
  112.5 9.2 %collective-permute-start.36 = (bf16[128,1024]{1,0:T(8,128)(2,1)S(1)}, bf16[128,1024]{1,0:T(8,128)(2,1)S(1)}, u32[]{:S(2)}, u32[]{:S(2)}) collective-permute-start(bf16[128,1024]{1,0:T(8,128)(2,1)S(1)} %collective-permute-done.35), channel_id=1, source_target_pairs={{0,16},{16,0},{1,17},{17,1},{2,18},{18,2},{3,19},{19,3},{4,20},{20... | collective-permute-start | bytes 786440 | tf_op jit(solution)/shard_map/ppermute | solution.py:49
  115.5 6.6 %collective-permute-start.26 = (bf16[128,1024]{1,0:T(8,128)(2,1)S(1)}, bf16[128,1024]{1,0:T(8,128)(2,1)S(1)}, u32[]{:S(2)}, u32[]{:S(2)}) collective-permute-start(bf16[128,1024]{1,0:T(8,128)(2,1)S(1)} %get-tuple-element.162), channel_id=1, source_target_pairs={{0,4},{1,5},{2,6},{3,7},{4,0},{5,1},{6,2},{7,3},{8,12},{9,13},{10,... | collective-permute-start | bytes 786440 | tf_op jit(solution)/shard_map/ppermute | solution.py:45
  115.5 7.7 %collective-permute-start.25 = (bf16[128,1024]{1,0:T(8,128)(2,1)S(1)}, bf16[128,1024]{1,0:T(8,128)(2,1)S(1)}, u32[]{:S(2)}, u32[]{:S(2)}) collective-permute-start(bf16[128,1024]{1,0:T(8,128)(2,1)S(1)} %get-tuple-element.162), channel_id=1, source_target_pairs={{0,2},{1,3},{2,0},{3,1},{4,6},{5,7},{6,4},{7,5},{8,10},{9,11},{10,... | collective-permute-start | bytes 786440 | tf_op jit(solution)/shard_map/ppermute | solution.py:45
  115.7 15.2 %collective-permute-start.33 = (bf16[256,1024]{1,0:T(8,128)(2,1)S(1)}, bf16[256,1024]{1,0:T(8,128)(2,1)S(1)}, u32[]{:S(2)}, u32[]{:S(2)}) collective-permute-start(bf16[256,1024]{1,0:T(8,128)(2,1)S(1)} %collective-permute-done.16), channel_id=1, source_target_pairs={{0,16},{16,0},{1,17},{17,1},{2,18},{18,2},{3,19},{19,3},{4,20},{20... | collective-permute-start | bytes 1572872 | tf_op jit(solution)/shard_map/ppermute | solution.py:49
  121.9 7.2 %collective-permute-start.29 = (bf16[128,1024]{1,0:T(8,128)(2,1)S(1)}, bf16[128,1024]{1,0:T(8,128)(2,1)S(1)}, u32[]{:S(2)}, u32[]{:S(2)}) collective-permute-start(bf16[128,1024]{1,0:T(8,128)(2,1)S(1)} %get-tuple-element.162), channel_id=1, source_target_pairs={{0,1},{1,0},{2,3},{3,2},{4,5},{5,4},{6,7},{7,6},{8,9},{9,8},{10,11... | collective-permute-start | bytes 786440 | tf_op jit(solution)/shard_map/ppermute | solution.py:45
  122.0 6.0 %collective-permute-start.27 = (bf16[64,1024]{1,0:T(8,128)(2,1)S(1)}, bf16[64,1024]{1,0:T(8,128)(2,1)S(1)}, u32[]{:S(2)}, u32[]{:S(2)}) collective-permute-start(bf16[64,1024]{1,0:T(8,128)(2,1)S(1)} %slice.451), channel_id=1, source_target_pairs={{0,2},{1,3},{2,0},{3,1},{4,6},{5,7},{6,4},{7,5},{8,10},{9,11},{10,... | collective-permute-start | bytes 393224 | tf_op jit(solution)/shard_map/ppermute | solution.py:45
  123.3 5.7 %collective-permute-start.28 = (bf16[64,1024]{1,0:T(8,128)(2,1)S(1)}, bf16[64,1024]{1,0:T(8,128)(2,1)S(1)}, u32[]{:S(2)}, u32[]{:S(2)}) collective-permute-start(bf16[64,1024]{1,0:T(8,128)(2,1)S(1)} %slice.452), channel_id=1, source_target_pairs={{0,4},{1,5},{2,6},{3,7},{4,0},{5,1},{6,2},{7,3},{8,12},{9,13},{10,... | collective-permute-start | bytes 393224 | tf_op jit(solution)/shard_map/ppermute | solution.py:45
  140.4 5.9 %collective-permute-start.38 = (bf16[64,1024]{1,0:T(8,128)(2,1)}, bf16[64,1024]{1,0:T(8,128)(2,1)}, u32[]{:S(2)}, u32[]{:S(2)}) collective-permute-start(bf16[64,1024]{1,0:T(8,128)(2,1)} %get-tuple-element.190), channel_id=1, source_target_pairs={{0,4},{1,5},{2,6},{3,7},{4,0},{5,1},{6,2},{7,3},{8,12},{9,13},{10,... | collective-permute-start | bytes 393224 | tf_op jit(solution)/shard_map/ppermute | solution.py:45
  140.4 5.9 %collective-permute-start.40 = (bf16[64,1024]{1,0:T(8,128)(2,1)}, bf16[64,1024]{1,0:T(8,128)(2,1)}, u32[]{:S(2)}, u32[]{:S(2)}) collective-permute-start(bf16[64,1024]{1,0:T(8,128)(2,1)} %get-tuple-element.189), channel_id=1, source_target_pairs={{0,2},{1,3},{2,0},{3,1},{4,6},{5,7},{6,4},{7,5},{8,10},{9,11},{10,... | collective-permute-start | bytes 393224 | tf_op jit(solution)/shard_map/ppermute | solution.py:45
  148.0 7.8 %collective-permute-start.41 = (bf16[128,1024]{1,0:T(8,128)(2,1)}, bf16[128,1024]{1,0:T(8,128)(2,1)}, u32[]{:S(2)}, u32[]{:S(2)}) collective-permute-start(bf16[128,1024]{1,0:T(8,128)(2,1)} %pad_maximum_fusion.18), channel_id=1, source_target_pairs={{0,4},{1,5},{2,6},{3,7},{4,0},{5,1},{6,2},{7,3},{8,12},{9,13},{10,... | collective-permute-start | bytes 786440 | tf_op jit(solution)/shard_map/ppermute | solution.py:45
  150.5 7.1 %collective-permute-start.39 = (bf16[128,1024]{1,0:T(8,128)(2,1)}, bf16[128,1024]{1,0:T(8,128)(2,1)S(1)}, u32[]{:S(2)}, u32[]{:S(2)}) collective-permute-start(bf16[128,1024]{1,0:T(8,128)(2,1)} %pad_maximum_fusion.17), channel_id=1, source_target_pairs={{0,2},{1,3},{2,0},{3,1},{4,6},{5,7},{6,4},{7,5},{8,10},{9,11},{10,... | collective-permute-start | bytes 786440 | tf_op jit(solution)/shard_map/ppermute | solution.py:45
  158.7 6.4 %collective-permute-start.43 = (bf16[128,1024]{1,0:T(8,128)(2,1)S(1)}, bf16[128,1024]{1,0:T(8,128)(2,1)S(1)}, u32[]{:S(2)}, u32[]{:S(2)}) collective-permute-start(bf16[128,1024]{1,0:T(8,128)(2,1)S(1)} %get-tuple-element.157), channel_id=1, source_target_pairs={{0,4},{1,5},{2,6},{3,7},{4,0},{5,1},{6,2},{7,3},{8,12},{9,13},{10,... | collective-permute-start | bytes 786440 | tf_op jit(solution)/shard_map/ppermute | solution.py:45
  159.4 7.5 %collective-permute-start.42 = (bf16[128,1024]{1,0:T(8,128)(2,1)S(1)}, bf16[128,1024]{1,0:T(8,128)(2,1)S(1)}, u32[]{:S(2)}, u32[]{:S(2)}) collective-permute-start(bf16[128,1024]{1,0:T(8,128)(2,1)S(1)} %get-tuple-element.157), channel_id=1, source_target_pairs={{0,2},{1,3},{2,0},{3,1},{4,6},{5,7},{6,4},{7,5},{8,10},{9,11},{10,... | collective-permute-start | bytes 786440 | tf_op jit(solution)/shard_map/ppermute | solution.py:45
  160.6 11.5 %collective-permute-start.46 = (bf16[128,1024]{1,0:T(8,128)(2,1)S(1)}, bf16[128,1024]{1,0:T(8,128)(2,1)S(1)}, u32[]{:S(2)}, u32[]{:S(2)}) collective-permute-start(bf16[128,1024]{1,0:T(8,128)(2,1)S(1)} %get-tuple-element.157), channel_id=1, source_target_pairs={{0,1},{1,0},{2,3},{3,2},{4,5},{5,4},{6,7},{7,6},{8,9},{9,8},{10,11... | collective-permute-start | bytes 786440 | tf_op jit(solution)/shard_map/ppermute | solution.py:45
  183.4 5.8 %collective-permute-start.51 = (bf16[64,1024]{1,0:T(8,128)(2,1)S(1)}, bf16[64,1024]{1,0:T(8,128)(2,1)S(1)}, u32[]{:S(2)}, u32[]{:S(2)}) collective-permute-start(bf16[64,1024]{1,0:T(8,128)(2,1)S(1)} %get-tuple-element.186), channel_id=1, source_target_pairs={{0,4},{1,5},{2,6},{3,7},{4,0},{5,1},{6,2},{7,3},{8,12},{9,13},{10,... | collective-permute-start | bytes 393224 | tf_op jit(solution)/shard_map/ppermute | solution.py:45
  187.6 33.4 %collective-permute-start.64 = (bf16[2,256,1024]{2,1,0:T(8,128)(2,1)}, bf16[2,256,1024]{2,1,0:T(8,128)(2,1)}, u32[]{:S(2)}, u32[]{:S(2)}) collective-permute-start(bf16[2,256,1024]{2,1,0:T(8,128)(2,1)} %bitcast.41), channel_id=1, source_target_pairs={{0,16},{16,0},{1,17},{17,1},{2,18},{18,2},{3,19},{19,3},{4,20},{20... | collective-permute-start | bytes 3145736 | tf_op jit(solution)/shard_map/ppermute | solution.py:49
  190.8 7.5 %collective-permute-start.54 = (bf16[128,1024]{1,0:T(8,128)(2,1)S(1)}, bf16[128,1024]{1,0:T(8,128)(2,1)S(1)}, u32[]{:S(2)}, u32[]{:S(2)}) collective-permute-start(bf16[128,1024]{1,0:T(8,128)(2,1)S(1)} %pad_maximum_fusion.21), channel_id=1, source_target_pairs={{0,4},{1,5},{2,6},{3,7},{4,0},{5,1},{6,2},{7,3},{8,12},{9,13},{10,... | collective-permute-start | bytes 786440 | tf_op jit(solution)/shard_map/ppermute | solution.py:45
  191.3 7.5 %collective-permute-start.52 = (bf16[128,1024]{1,0:T(8,128)(2,1)S(1)}, bf16[128,1024]{1,0:T(8,128)(2,1)S(1)}, u32[]{:S(2)}, u32[]{:S(2)}) collective-permute-start(bf16[128,1024]{1,0:T(8,128)(2,1)S(1)} %pad_maximum_fusion.20), channel_id=1, source_target_pairs={{0,2},{1,3},{2,0},{3,1},{4,6},{5,7},{6,4},{7,5},{8,10},{9,11},{10,... | collective-permute-start | bytes 786440 | tf_op jit(solution)/shard_map/ppermute | solution.py:45
  200.0 8.5 %collective-permute-start.55 = (bf16[128,1024]{1,0:T(8,128)(2,1)S(1)}, bf16[128,1024]{1,0:T(8,128)(2,1)S(1)}, u32[]{:S(2)}, u32[]{:S(2)}) collective-permute-start(bf16[128,1024]{1,0:T(8,128)(2,1)S(1)} %get-tuple-element.156), channel_id=1, source_target_pairs={{0,2},{1,3},{2,0},{3,1},{4,6},{5,7},{6,4},{7,5},{8,10},{9,11},{10,... | collective-permute-start | bytes 786440 | tf_op jit(solution)/shard_map/ppermute | solution.py:45
  201.2 6.4 %collective-permute-start.56 = (bf16[128,1024]{1,0:T(8,128)(2,1)S(1)}, bf16[128,1024]{1,0:T(8,128)(2,1)S(1)}, u32[]{:S(2)}, u32[]{:S(2)}) collective-permute-start(bf16[128,1024]{1,0:T(8,128)(2,1)S(1)} %get-tuple-element.156), channel_id=1, source_target_pairs={{0,4},{1,5},{2,6},{3,7},{4,0},{5,1},{6,2},{7,3},{8,12},{9,13},{10,... | collective-permute-start | bytes 786440 | tf_op jit(solution)/shard_map/ppermute | solution.py:45
  204.4 9.4 %collective-permute-start.59 = (bf16[128,1024]{1,0:T(8,128)(2,1)S(1)}, bf16[128,1024]{1,0:T(8,128)(2,1)S(1)}, u32[]{:S(2)}, u32[]{:S(2)}) collective-permute-start(bf16[128,1024]{1,0:T(8,128)(2,1)S(1)} %get-tuple-element.156), channel_id=1, source_target_pairs={{0,1},{1,0},{2,3},{3,2},{4,5},{5,4},{6,7},{7,6},{8,9},{9,8},{10,11... | collective-permute-start | bytes 786440 | tf_op jit(solution)/shard_map/ppermute | solution.py:45
  216.6 9.2 %collective-permute-start.63 = (bf16[512,128]{1,0:T(8,128)(2,1)S(1)}, bf16[512,128]{1,0:T(8,128)(2,1)S(1)}, u32[]{:S(2)}, u32[]{:S(2)}) collective-permute-start(bf16[512,128]{1,0:T(8,128)(2,1)S(1)} %bitcast.240), channel_id=1, source_target_pairs={{0,8},{1,9},{2,10},{3,11},{4,12},{5,13},{6,14},{7,15},{8,0},{9,1},... | collective-permute-start | bytes 393224 | tf_op jit(solution)/shard_map/ppermute | solution.py:45
  219.9 23.6 %collective-permute-start.66 = (bf16[2,128,1024]{2,1,0:T(8,128)(2,1)}, bf16[2,128,1024]{2,1,0:T(8,128)(2,1)}, u32[]{:S(2)}, u32[]{:S(2)}) collective-permute-start(bf16[2,128,1024]{2,1,0:T(8,128)(2,1)} %fusion.10), channel_id=1, source_target_pairs={{0,16},{16,0},{1,17},{17,1},{2,18},{18,2},{3,19},{19,3},{4,20},{20... | collective-permute-start | bytes 1572872 | tf_op jit(solution)/shard_map/ppermute | solution.py:49
  230.9 22.8 %collective-permute-start.65 = (bf16[1,224,1024]{2,1,0:T(8,128)(2,1)}, bf16[1,224,1024]{2,1,0:T(8,128)(2,1)}, u32[]{:S(2)}, u32[]{:S(2)}) collective-permute-start(bf16[1,224,1024]{2,1,0:T(8,128)(2,1)} %fusion.34), channel_id=1, source_target_pairs={{0,8},{1,9},{2,10},{3,11},{4,12},{5,13},{6,14},{7,15},{8,0},{9,1},... | collective-permute-start | bytes 1376264 | tf_op jit(solution)/shard_map/ppermute | solution.py:45
  256.0 20.1 %collective-permute-start.72 = (bf16[512,384]{1,0:T(8,128)(2,1)}, bf16[512,384]{1,0:T(8,128)(2,1)}, u32[]{:S(2)}, u32[]{:S(2)}) collective-permute-start(bf16[512,384]{1,0:T(8,128)(2,1)} %get-tuple-element.135), channel_id=1, source_target_pairs={{0,8},{1,9},{2,10},{3,11},{4,12},{5,13},{6,14},{7,15},{8,0},{9,1},... | collective-permute-start | bytes 1179656 | tf_op jit(solution)/shard_map/ppermute | solution.py:45
  259.0 17.2 %collective-permute-start.73 = (bf16[4,2,32,1024]{3,2,0,1:T(8,128)(2,1)}, bf16[4,2,32,1024]{3,2,0,1:T(8,128)(2,1)}, u32[]{:S(2)}, u32[]{:S(2)}) collective-permute-start(bf16[4,2,32,1024]{3,2,0,1:T(8,128)(2,1)} %fusion.11), channel_id=1, source_target_pairs={{0,16},{16,0},{1,17},{17,1},{2,18},{18,2},{3,19},{19,3},{4,20},{20... | collective-permute-start | bytes 1572872 | tf_op jit(solution)/shard_map/ppermute | solution.py:49
  264.8 6.7 %collective-permute-start.70 = (f32[3,1024]{1,0:T(4,128)S(1)}, f32[3,1024]{1,0:T(4,128)S(1)}, u32[]{:S(2)}, u32[]{:S(2)}) collective-permute-start(f32[3,1024]{1,0:T(4,128)S(1)} %add.206), channel_id=1, source_target_pairs={{0,4},{1,5},{2,6},{3,7},{4,0},{5,1},{6,2},{7,3},{8,12},{9,13},{10,... | collective-permute-start | bytes 36872 | tf_op jit(solution)/shard_map/ppermute | solution.py:45
  271.5 38.2 %collective-permute-start.71 = (f32[3,1024]{1,0:T(4,128)S(1)}, f32[3,1024]{1,0:T(4,128)S(1)}, u32[]{:S(2)}, u32[]{:S(2)}) collective-permute-start(f32[3,1024]{1,0:T(4,128)S(1)} %add.207), channel_id=1, source_target_pairs={{0,8},{1,9},{2,10},{3,11},{4,12},{5,13},{6,14},{7,15},{8,0},{9,1},... | collective-permute-start | bytes 36872 | tf_op jit(solution)/shard_map/ppermute | solution.py:45
  278.1 7.1 %collective-permute-start.74 = (bf16[512,1024]{1,0:T(8,128)(2,1)S(1)}, bf16[512,1024]{1,0:T(8,128)(2,1)S(1)}, u32[]{:S(2)}, u32[]{:S(2)}) collective-permute-start(bf16[512,1024]{1,0:T(8,128)(2,1)S(1)} %convolution_convert_fusion.1), channel_id=1, source_target_pairs={{0,1},{1,0},{2,3},{3,2},{4,5},{5,4},{6,7},{7,6},{8,9},{9,8},{10,11... | collective-permute-start | bytes 3145736 | tf_op jit(solution)/shard_map/ppermute | solution.py:45
  278.3 6.9 %collective-permute-start.75 = (bf16[1,32,1024]{2,1,0:T(8,128)(2,1)S(1)}, bf16[1,32,1024]{2,1,0:T(8,128)(2,1)S(1)}, u32[]{:S(2)}, u32[]{:S(2)}) collective-permute-start(bf16[1,32,1024]{2,1,0:T(8,128)(2,1)S(1)} %fusion.50), channel_id=1, source_target_pairs={{0,8},{1,9},{2,10},{3,11},{4,12},{5,13},{6,14},{7,15},{8,0},{9,1},... | collective-permute-start | bytes 196616 | tf_op jit(solution)/shard_map/ppermute | solution.py:45
  279.8 22.4 %collective-permute-start.80 = (bf16[4,1,32,1024]{3,2,1,0:T(8,128)(2,1)S(1)}, bf16[4,1,32,1024]{3,2,1,0:T(8,128)(2,1)S(1)}, u32[]{:S(2)}, u32[]{:S(2)}) collective-permute-start(bf16[4,1,32,1024]{3,2,1,0:T(8,128)(2,1)S(1)} %fusion.37), channel_id=1, source_target_pairs={{0,8},{1,9},{2,10},{3,11},{4,12},{5,13},{6,14},{7,15},{8,0},{9,1},... | collective-permute-start | bytes 786440 | tf_op jit(solution)/shard_map/ppermute | solution.py:45
  286.9 7.4 %collective-permute-start.77 = (bf16[64,1024]{1,0:T(8,128)(2,1)S(1)}, bf16[64,1024]{1,0:T(8,128)(2,1)S(1)}, u32[]{:S(2)}, u32[]{:S(2)}) collective-permute-start(bf16[64,1024]{1,0:T(8,128)(2,1)S(1)} %get-tuple-element.181), channel_id=1, source_target_pairs={{0,4},{1,5},{2,6},{3,7},{4,0},{5,1},{6,2},{7,3},{8,12},{9,13},{10,... | collective-permute-start | bytes 393224 | tf_op jit(solution)/shard_map/ppermute | solution.py:45
  286.9 20.8 %collective-permute-start.85 = (bf16[1,128,1024]{2,1,0:T(8,128)(2,1)S(1)}, bf16[1,128,1024]{2,1,0:T(8,128)(2,1)S(1)}, u32[]{:S(2)}, u32[]{:S(2)}) collective-permute-start(bf16[1,128,1024]{2,1,0:T(8,128)(2,1)S(1)} %fusion.39), channel_id=1, source_target_pairs={{0,8},{1,9},{2,10},{3,11},{4,12},{5,13},{6,14},{7,15},{8,0},{9,1},... | collective-permute-start | bytes 786440 | tf_op jit(solution)/shard_map/ppermute | solution.py:45
  294.4 32.2 %collective-permute-start.79 = (bf16[128,1024]{1,0:T(8,128)(2,1)S(1)}, bf16[128,1024]{1,0:T(8,128)(2,1)S(1)}, u32[]{:S(2)}, u32[]{:S(2)}) collective-permute-start(bf16[128,1024]{1,0:T(8,128)(2,1)S(1)} %pad_maximum_fusion.24), channel_id=1, source_target_pairs={{0,4},{1,5},{2,6},{3,7},{4,0},{5,1},{6,2},{7,3},{8,12},{9,13},{10,... | collective-permute-start | bytes 786440 | tf_op jit(solution)/shard_map/ppermute | solution.py:45
  294.9 31.7 %collective-permute-start.78 = (bf16[128,1024]{1,0:T(8,128)(2,1)S(1)}, bf16[128,1024]{1,0:T(8,128)(2,1)S(1)}, u32[]{:S(2)}, u32[]{:S(2)}) collective-permute-start(bf16[128,1024]{1,0:T(8,128)(2,1)S(1)} %pad_maximum_fusion.23), channel_id=1, source_target_pairs={{0,2},{1,3},{2,0},{3,1},{4,6},{5,7},{6,4},{7,5},{8,10},{9,11},{10,... | collective-permute-start | bytes 786440 | tf_op jit(solution)/shard_map/ppermute | solution.py:45
  302.3 19.5 %collective-permute-start.83 = (bf16[32,1024]{1,0:T(8,128)(2,1)S(1)}, bf16[32,1024]{1,0:T(8,128)(2,1)S(1)}, u32[]{:S(2)}, u32[]{:S(2)}) collective-permute-start(bf16[32,1024]{1,0:T(8,128)(2,1)S(1)} %get-tuple-element.203), channel_id=1, source_target_pairs={{16,0},{9,1},{2,2},{26,3},{19,4},{12,5},{5,6},{29,7},{22,8},{15,9}... | collective-permute-start | bytes 196616 | tf_op jit(solution)/shard_map/ppermute | solution.py:472
  307.7 7.8 %collective-permute-start.84 = (bf16[32,1024]{1,0:T(8,128)(2,1)S(1)}, bf16[32,1024]{1,0:T(8,128)(2,1)S(1)}, u32[]{:S(2)}, u32[]{:S(2)}) collective-permute-start(bf16[32,1024]{1,0:T(8,128)(2,1)S(1)} %get-tuple-element.200), channel_id=1, source_target_pairs={{0,0},{8,1},{16,2},{24,3},{1,4},{9,5},{17,6},{25,7},{2,8},{10,9},{... | collective-permute-start | bytes 196616 | tf_op jit(solution)/shard_map/ppermute | solution.py:470
  309.7 16.0 %collective-permute-start.82 = (bf16[32,1024]{1,0:T(8,128)(2,1)S(1)}, bf16[32,1024]{1,0:T(8,128)(2,1)S(1)}, u32[]{:S(2)}, u32[]{:S(2)}) collective-permute-start(bf16[32,1024]{1,0:T(8,128)(2,1)S(1)} %get-tuple-element.202), channel_id=1, source_target_pairs={{8,0},{1,1},{25,2},{18,3},{11,4},{4,5},{28,6},{21,7},{14,8},{7,9},... | collective-permute-start | bytes 196616 | tf_op jit(solution)/shard_map/ppermute | solution.py:472
  315.6 10.2 %collective-permute-start.81 = (bf16[32,1024]{1,0:T(8,128)(2,1)S(1)}, bf16[32,1024]{1,0:T(8,128)(2,1)S(1)}, u32[]{:S(2)}, u32[]{:S(2)}) collective-permute-start(bf16[32,1024]{1,0:T(8,128)(2,1)S(1)} %get-tuple-element.201), channel_id=1, source_target_pairs={{0,0},{24,1},{17,2},{10,3},{3,4},{27,5},{20,6},{13,7},{6,8},{30,9}... | collective-permute-start | bytes 196616 | tf_op jit(solution)/shard_map/ppermute | solution.py:472
  321.9 12.4 %collective-permute-start.86 = (bf16[128,1024]{1,0:T(8,128)(2,1)S(1)}, bf16[128,1024]{1,0:T(8,128)(2,1)S(1)}, u32[]{:S(2)}, u32[]{:S(2)}) collective-permute-start(bf16[128,1024]{1,0:T(8,128)(2,1)S(1)} %fusion.38), channel_id=1, source_target_pairs={{0,0},{16,1},{1,2},{17,3},{2,4},{18,5},{3,6},{19,7},{4,8},{20,9},{... | collective-permute-start | bytes 786440 | tf_op jit(solution)/shard_map/ppermute | solution.py:453
  (66 other events, 538.4 us)
